TPU v7x, 32 devices: a whole 2x2x4 slice. The times are simulated.
32 devices in a mesh: tilt: 2 (over y), dom: 16 (over z, x, core).
Axes of the slice: x: 2, y: 2, z: 4, core: 2. Of those that a mesh axis runs over, the one named last changes fastest.
Arguments:
- sections: bfloat16 [32, 256, 256], P('dom'), may hold values from -6 to 6
- images: bfloat16 [32, 4, 256, 256], P('dom', 'tilt'), may hold values from -6 to 6
- slice_rows: bfloat16 [4, 256, 256], P('tilt'), may hold values from -0.375 to 0.375
- slice_cols: bfloat16 [4, 256, 256], P('tilt'), may hold values from -0.375 to 0.375
- ctf_filter: bfloat16 [4, 256, 256], P('tilt'), may hold values from -0.375 to 0.375
- nbr_owner: int32 [32, 2, 8], P('dom'), may hold values from 0 to 15, all different within a row; in each aligned block of 4 rows (0 to 3, 4 to 7, ..., all dimensions but the last counted through in order) at most 4 rows name the same one
- nbr_local: int32 [32, 16], P('dom'), may hold values from 0 to 1
- nbr_side: int32 [32, 16], P('dom'), may hold values from 0 to 1
- nbr_weight: float32 [32, 16], P('dom'), may hold values from 0.25 to 2
Outputs:
- section_grad: float32 [32, 256, 256], P('dom', 'tilt')
- scores: float32 [32], P('dom')
Inputs may be any that keep to these rules, and one draw needn't show every extreme that they name: `nbr_owner`: among the 32 neighbour entries of one spatial block's particles, at most 4 name the same owner block; some blocks reach 4.
All inputs are finite; a program needn't handle non-finite values.
Results may differ from a plain program's by a relative error of at most 0.013.
Values may be sent and summed in bfloat16 or wider, within the bound.
No kernel may reach another device: no remote copies, remote signals or barrier semaphores. Data moves between devices by JAX's collectives and lax.ppermute only.
A program may use at most 64 MiB of HBM per device.

v0:
```python
import jax
import jax.numpy as jnp
from jax import lax
from jax.sharding import PartitionSpec as P

OVL = 16


def on_device(
    sections, images, slice_rows, slice_cols, ctf_filter, nbr_owner, nbr_local, nbr_side, nbr_weight
):
    own_count = sections.shape[0]
    pixels = sections.shape[1]
    tilt_count = images.shape[1]
    neighbours = nbr_local.shape[1]
    peer_count = lax.axis_size("dom")
    capacity = max(2, 2 * own_count * neighbours // peer_count)
    entries = own_count * neighbours
    owners = nbr_owner.reshape(entries)
    wanted = nbr_local.reshape(entries)
    side_list = nbr_side.reshape(entries)
    entry_order = jnp.arange(entries)
    same_owner = (owners[:, None] == owners[None, :]) & (
        entry_order[None, :] < entry_order[:, None]
    )
    slot_rank = jnp.sum(same_owner.astype(jnp.int32), axis=1)
    slot_index = owners * capacity + slot_rank
    request_identifier = wanted * 2 + side_list
    slot_hits = slot_index[:, None] == jnp.arange(peer_count * capacity)[None, :]
    requests = jnp.sum(jnp.where(slot_hits, request_identifier[:, None], 0), axis=0).reshape(
        peer_count, capacity
    )
    halfway = jnp.einsum(
        "kij,tlj->ktil", sections, slice_cols, preferred_element_type=jnp.float32
    ).astype(jnp.bfloat16)
    projected = jnp.einsum(
        "tai,ktil->ktal", slice_rows, halfway, preferred_element_type=jnp.float32
    ).astype(jnp.bfloat16)
    border_rows = jnp.stack((projected[:, :, :OVL], projected[:, :, pixels - OVL :]), axis=1)
    code_table = lax.all_to_all(requests, "dom", split_axis=0, concat_axis=0, tiled=True)
    picked = border_rows[code_table // 2]
    arrived = lax.all_to_all(picked, "dom", split_axis=0, concat_axis=0, tiled=True)
    arrived_flat = arrived.reshape((peer_count * capacity,) + arrived.shape[2:])[slot_index]
    near_bands = jnp.where(
        (side_list == 0)[:, None, None, None], arrived_flat[:, 0], arrived_flat[:, 1]
    )
    band_data = near_bands.astype(jnp.float32).reshape(
        own_count, neighbours, tilt_count, OVL, pixels
    )
    weight_lower = jnp.where(nbr_side == 0, nbr_weight, 0.0)
    weight_upper = jnp.where(nbr_side == 1, nbr_weight, 0.0)
    lower_part = jnp.einsum("kj,kjtrc->ktrc", weight_lower, band_data)
    upper_part = jnp.einsum("kj,kjtrc->ktrc", weight_upper, band_data)
    residual = images.astype(jnp.float32) - projected.astype(jnp.float32)
    residual = residual.at[:, :, :OVL].add(-upper_part)
    residual = residual.at[:, :, pixels - OVL :].add(-lower_part)
    residual_portion = residual.astype(jnp.bfloat16)
    smoothed_images = jnp.einsum(
        "tab,ktbc->ktac", ctf_filter, residual_portion, preferred_element_type=jnp.float32
    ).astype(jnp.bfloat16)
    filtered_images = jnp.einsum(
        "ktac,tdc->ktad", smoothed_images, ctf_filter, preferred_element_type=jnp.float32
    )
    score_part = jnp.sum(filtered_images * filtered_images, axis=(1, 2, 3))
    tilt_groups = lax.axis_size("tilt")
    scores = 0.5 * lax.psum(score_part, "tilt") / (tilt_count * tilt_groups * pixels * pixels)
    filtered_portion = filtered_images.astype(jnp.bfloat16)
    reverse_pass = jnp.einsum(
        "tab,ktac->ktbc", ctf_filter, filtered_portion, preferred_element_type=jnp.float32
    ).astype(jnp.bfloat16)
    weighted = jnp.einsum(
        "ktbc,tcd->ktbd", reverse_pass, ctf_filter, preferred_element_type=jnp.float32
    ).astype(jnp.bfloat16)
    lower_rows = weighted[:, None, :, pixels - OVL :]
    upper_rows = weighted[:, None, :, :OVL]
    chosen = jnp.where((nbr_side == 0)[:, :, None, None, None], lower_rows, upper_rows)
    sent_back = (nbr_weight[:, :, None, None, None] * chosen.astype(jnp.float32)).astype(
        jnp.bfloat16
    )
    sent_back = sent_back.reshape(entries, tilt_count, OVL, pixels)
    outgoing = (
        jnp.zeros((peer_count * capacity, tilt_count, OVL, pixels), jnp.bfloat16)
        .at[slot_index]
        .set(sent_back)
    )
    returned = lax.all_to_all(
        outgoing.reshape(peer_count, capacity, tilt_count, OVL, pixels),
        "dom",
        split_axis=0,
        concat_axis=0,
        tiled=True,
    )
    served_flat = code_table.reshape(peer_count * capacity)
    owner_hits = (served_flat[None, :] == jnp.arange(2 * own_count)[:, None]).astype(jnp.bfloat16)
    gathered = jnp.dot(
        owner_hits,
        returned.reshape(peer_count * capacity, tilt_count * OVL * pixels),
        preferred_element_type=jnp.float32,
    )
    gathered = gathered.reshape(own_count, 2, tilt_count, OVL, pixels)
    proj_grad = weighted.astype(jnp.float32)
    proj_grad = proj_grad.at[:, :, :OVL].add(gathered[:, 0])
    proj_grad = proj_grad.at[:, :, pixels - OVL :].add(gathered[:, 1])
    proj_half = proj_grad.astype(jnp.bfloat16)
    upward = jnp.einsum(
        "tai,ktal->ktil", slice_rows, proj_half, preferred_element_type=jnp.float32
    ).astype(jnp.bfloat16)
    partial_grad = -jnp.einsum(
        "ktil,tlj->kij", upward, slice_cols, preferred_element_type=jnp.float32
    )
    section_grad = lax.psum_scatter(partial_grad, "tilt", scatter_dimension=1, tiled=True)
    return (section_grad, scores)


def solution(mesh):
    in_specs = (
        P("dom", None, None),
        P("dom", "tilt", None, None),
        P("tilt", None, None),
        P("tilt", None, None),
        P("tilt", None, None),
        P("dom", None, None),
        P("dom", None),
        P("dom", None),
        P("dom", None),
    )
    out_specs = (P("dom", "tilt", None), P("dom"))
    return jax.shard_map(
        on_device, mesh=mesh, in_specs=in_specs, out_specs=out_specs, check_vma=False
    )
```

profile of v0, /device:TPU:0, one launch (start us, length us, event | category | flops | bytes accessed | tf_op | source)
XLA Modules:
  0.0 142.6 jit_solution(16559912707165446920)
XLA Ops:
  7.2 0.8 reshape.331
  8.2 0.7 multiply_add_fusion.1
  9.1 0.7 all_to_all.14
  9.7 7.4 %all-to-all-start = ((s32[16,1,4]{2,1,0:T(1,128)}), s32[16,1,4]{2,1,0:T(1,128)S(1)}, u32[]{:S(2)}, u32[]{:S(2)}) async-start(s32[16,1,4]{2,1,0:T(1,128)} %bitcast.11), calls=%async_computation | async-start | bytes 16384 | tf_op jit(solution)/shard_map/all_to_all | solution.py:40
  17.1 1.8 %convert_subtract_fusion = (f32[2,2,256,256]{3,2,0,1:T(8,128)S(1)}, bf16[2,2,256,256]{3,2,0,1:T(8,128)(2,1)S(1)}) fusion(bf16[2,2,256,256]{3,2,1,0:T(8,128)(2,1)} %param.18, bf16[2,256,256]{2,1,0:T(8,128)(2,1)} %param.19, bf16[2,256,256]{2,1,0:T(8,128)(2,1)} %param.20, bf16[2,256,256]{2,1,0:T(8,128)(2,1)} %param.17), kind=kOutput, calls=%fused_computation.23 | convolution fusion | flops 269746176 | bytes 2883584 | tf_op jit(solution)/shard_map/tai,ktil->ktal/dot_general | solution.py:36
  19.0 4.5 %all-to-all-done = s32[16,1,4]{2,1,0:T(1,128)S(1)} async-done(((s32[16,1,4]{2,1,0:T(1,128)}), s32[16,1,4]{2,1,0:T(1,128)S(1)}, u32[]{:S(2)}, u32[]{:S(2)}) %all-to-all-start) | async-done | bytes 288 | tf_op jit(solution)/shard_map/all_to_all | solution.py:40
  23.7 2.0 %gather_fusion = bf16[64,2,2,16,256]{4,3,2,1,0:T(8,128)(2,1)} fusion(bf16[2,2,2,16,256]{4,3,0,2,1:T(8,128)(2,1)S(1)} %pad_maximum_fusion, s32[1024]{0:T(1024)S(1)} %pad_clamp_fusion.1), kind=kCustom, calls=%fused_computation | custom fusion | bytes 4194560 | tf_op jit(solution)/shard_map/gather | solution.py:41
  25.7 3.8 %all-to-all-start.1 = ((bf16[16,4,2,2,16,256]{5,4,3,2,1,0:T(8,128)(2,1)}), bf16[16,4,2,2,16,256]{5,4,3,2,1,0:T(8,128)(2,1)S(1)}, u32[]{:S(2)}, u32[]{:S(2)}) async-start(bf16[16,4,2,2,16,256]{5,4,3,2,1,0:T(8,128)(2,1)} %bitcast.13), calls=%async_computation.1 | async-start | bytes 4194304 | tf_op jit(solution)/shard_map/all_to_all | solution.py:42
  29.9 40.7 %all-to-all-done.1 = bf16[16,4,2,2,16,256]{5,4,3,2,1,0:T(8,128)(2,1)S(1)} async-done(((bf16[16,4,2,2,16,256]{5,4,3,2,1,0:T(8,128)(2,1)}), bf16[16,4,2,2,16,256]{5,4,3,2,1,0:T(8,128)(2,1)S(1)}, u32[]{:S(2)}, u32[]{:S(2)}) %all-to-all-start.1) | async-done | bytes 2097184 | tf_op jit(solution)/shard_map/all_to_all | solution.py:42
  70.6 1.6 %gather_fusion.1 = bf16[32,2,2,16,256]{4,3,2,1,0:T(8,128)(2,1)} fusion(bf16[64,2,2,16,256]{4,3,2,1,0:T(8,128)(2,1)S(1)} %bitcast.166, s32[1024]{0:T(1024)S(1)} %pad_clamp_fusion), kind=kCustom, calls=%fused_computation.1 | custom fusion | bytes 2097280 | tf_op jit(solution)/shard_map/gather | solution.py:43
  72.2 1.3 fusion.48
  74.5 0.7 multiply_reduce_fusion
  75.2 0.6 fusion.55
  76.0 1.1 broadcast_in_dim.76
  77.1 4.4 %scatter_fusion = bf16[64,2,16,256]{3,2,1,0:T(8,128)(2,1)} fusion(bf16[64,2,16,256]{3,2,1,0:T(8,128)(2,1)} %broadcast_in_dim.76, s32[32]{0:T(128)S(1)} %fusion.47, bf16[32,2,16,256]{3,2,1,0:T(8,128)(2,1)S(1)} %multiply_convert_fusion), kind=kCustom, calls=%fused_computation.2 | custom fusion | bytes 1572992 | tf_op jit(solution)/shard_map/scatter | solution.py:84
  81.5 11.2 %all-to-all-start.2 = ((bf16[16,4,2,16,256]{4,3,2,1,0:T(8,128)(2,1)}), bf16[16,4,2,16,256]{4,3,2,1,0:T(8,128)(2,1)S(1)}, u32[]{:S(2)}, u32[]{:S(2)}) async-start(bf16[16,4,2,16,256]{4,3,2,1,0:T(8,128)(2,1)} %bitcast.33), calls=%async_computation.2 | async-start | bytes 2097152 | tf_op jit(solution)/shard_map/all_to_all | solution.py:86
  92.7 0.5 broadcast.225
  93.2 0.7 reduce.12
  94.0 21.6 %all-to-all-done.2 = bf16[16,4,2,16,256]{4,3,2,1,0:T(8,128)(2,1)S(1)} async-done(((bf16[16,4,2,16,256]{4,3,2,1,0:T(8,128)(2,1)}), bf16[16,4,2,16,256]{4,3,2,1,0:T(8,128)(2,1)S(1)}, u32[]{:S(2)}, u32[]{:S(2)}) %all-to-all-start.2) | async-done | bytes 1048608 | tf_op jit(solution)/shard_map/all_to_all | solution.py:86
  116.4 0.7 fusion.8
  117.2 1.5 %fusion.7 = f32[2,256,256]{2,1,0:T(8,128)} fusion(bf16[2,256,256]{2,1,0:T(8,128)(2,1)S(1)} %copy-done.1, bf16[2,256,256]{2,1,0:T(8,128)(2,1)S(1)} %copy-done.2, f32[2,2,256,256]{3,2,0,1:T(8,128)S(1)} %fusion.35), kind=kOutput, calls=%fused_computation.17 | convolution fusion | flops 269090816 | bytes 2097152 | tf_op jit(solution)/shard_map/ktil,tlj->kij/dot_general | solution.py:108
  118.8 4.9 %psum.7 = f32[2]{0:T(128)S(1)} all-reduce(f32[2]{0:T(128)S(1)} %get-tuple-element.65), channel_id=1, replica_groups=mesh['tilt'=2,'dom'=16] {'tilt'}, use_global_device_ids=true, to_apply=%region_5.6 | all-reduce | flops 2 | bytes 16 | tf_op jit(solution)/shard_map/psum | solution.py:66
  123.7 0.5 broadcast_multiply_fusion.1
  124.2 11.5 %reduce-scatter.2.cloned.1.call-done = f32[2,128,256]{2,1,0:T(8,128)} async-done(((f32[2,256,256]{2,1,0:T(8,128)}), f32[2,128,256]{2,1,0:T(8,128)}) %reduce-scatter.2.cloned.1.call-update) | async-done | bytes 262160 | tf_op jit(solution)/shard_map/reduce_scatter | solution.py:111
  (46 shorter events, 3.1 us)
Async XLA Ops:
  7.2 67.3 %copy-start = (bf16[2,256,256]{2,1,0:T(8,128)(2,1)S(1)}, bf16[2,256,256]{2,1,0:T(8,128)(2,1)}, u32[]{:S(2)}) copy-start(bf16[2,256,256]{2,1,0:T(8,128)(2,1)} %param.21) | copy-start | bytes 786436
  9.7 13.7 %all-to-all-start = ((s32[16,1,4]{2,1,0:T(1,128)}), s32[16,1,4]{2,1,0:T(1,128)S(1)}, u32[]{:S(2)}, u32[]{:S(2)}) async-start(s32[16,1,4]{2,1,0:T(1,128)} %bitcast.11), calls=%async_computation | async-start | bytes 16384 | tf_op jit(solution)/shard_map/all_to_all | solution.py:40
  25.7 3.9 %copy-start.3 = (s32[2,2,8]{2,1,0:T(2,128)S(1)}, s32[2,2,8]{2,1,0:T(2,128)}, u32[]{:S(2)}) copy-start(s32[2,2,8]{2,1,0:T(2,128)} %param.22) | copy-start | bytes 388
  25.7 4.0 %copy-start.5 = (f32[2,16]{1,0:T(2,128)S(1)}, f32[2,16]{1,0:T(2,128)}, u32[]{:S(2)}) copy-start(f32[2,16]{1,0:T(2,128)} %param.25) | copy-start | bytes 388
  25.7 4.0 %copy-start.4 = (s32[2,16]{1,0:T(2,128)S(1)}, s32[2,16]{1,0:T(2,128)}, u32[]{:S(2)}) copy-start(s32[2,16]{1,0:T(2,128)} %param.24) | copy-start | bytes 388
  25.7 44.9 %all-to-all-start.1 = ((bf16[16,4,2,2,16,256]{5,4,3,2,1,0:T(8,128)(2,1)}), bf16[16,4,2,2,16,256]{5,4,3,2,1,0:T(8,128)(2,1)S(1)}, u32[]{:S(2)}, u32[]{:S(2)}) async-start(bf16[16,4,2,2,16,256]{5,4,3,2,1,0:T(8,128)(2,1)} %bitcast.13), calls=%async_computation.1 | async-start | bytes 4194304 | tf_op jit(solution)/shard_map/all_to_all | solution.py:42
  81.5 34.1 %all-to-all-start.2 = ((bf16[16,4,2,16,256]{4,3,2,1,0:T(8,128)(2,1)}), bf16[16,4,2,16,256]{4,3,2,1,0:T(8,128)(2,1)S(1)}, u32[]{:S(2)}, u32[]{:S(2)}) async-start(bf16[16,4,2,16,256]{4,3,2,1,0:T(8,128)(2,1)} %bitcast.33), calls=%async_computation.2 | async-start | bytes 2097152 | tf_op jit(solution)/shard_map/all_to_all | solution.py:86
  92.6 43.1 %reduce-scatter.2.cloned.1.call-start = ((), (), s32[]{:S(2)}) async-start(), calls=%async_computation.4 | async-start | bytes 786432 | tf_op jit(solution)/shard_map/reduce_scatter | solution.py:111
  116.1 1.1 copy-start.1
  116.1 1.1 copy-start.2
Sparse Core Ops, SparseCore 0:
  118.9 16.7 reduce-scatter.1
where the time goes:
time: 143 us
  waiting for transfers between devices  78.3 us (55%)
  starting transfers between devices  22.4 us (16%)
  between operations  14.3 us (10%)
  local copies, waits for them, and re-layouts  13.9 us (10%)
  matrix products  6.14 us (4%)
  blocking collectives  4.94 us (3%)
  other arithmetic  2.59 us (2%)
    all_to_all x1, waiting for transfers between devices, on_device(): lax.all_to_all(picked, 'dom', split_axis=0, concat_axis=0, tiled=True)  40.7 us
    all_to_all x1, waiting for transfers between devices, on_device(): lax.all_to_all(outgoing.reshape(peer_count, capacity, tilt_count, OVL, pi...  21.6 us
    reduce_scatter x1, waiting for transfers between devices, on_device(): lax.psum_scatter(partial_grad, 'tilt', scatter_dimension=1, tiled=True)  11.5 us
    all_to_all x1, starting transfers between devices, on_device(): lax.all_to_all(outgoing.reshape(peer_count, capacity, tilt_count, OVL, pi...  11.2 us
    all_to_all x1, starting transfers between devices, on_device(): lax.all_to_all(requests, 'dom', split_axis=0, concat_axis=0, tiled=True)  7.36 us
    psum x1, blocking collectives, on_device(): lax.psum(score_part, 'tilt')  4.94 us
    all_to_all x1, waiting for transfers between devices, on_device(): lax.all_to_all(requests, 'dom', split_axis=0, concat_axis=0, tiled=True)  4.47 us
    scatter x1, local copies, waits for them, and re-layouts, on_device(): outgoing = jnp.zeros((peer_count * capacity, tilt_count, OVL, pixels), jn...  4.36 us
  transfers between devices with their start and end apart: 4, of which 4 were waited for; matrix products, arithmetic and copies ran while one was open for 3% of the time, Pallas kernels for 0%

commit v1 on v0

v1 whole, which is shorter than its diff:
```python
import jax
import jax.numpy as jnp
from jax import lax
from jax.sharding import PartitionSpec as P

OVL = 16


def split_dot(weights, bands):
    hi = weights.astype(jnp.bfloat16)
    rest = weights - hi.astype(jnp.float32)
    mid = rest.astype(jnp.bfloat16)
    low = (rest - mid.astype(jnp.float32)).astype(jnp.bfloat16)
    total = jnp.dot(hi, bands, preferred_element_type=jnp.float32)
    total = total + jnp.dot(mid, bands, preferred_element_type=jnp.float32)
    return total + jnp.dot(low, bands, preferred_element_type=jnp.float32)


def on_device(
    sections, images, slice_rows, slice_cols, ctf_filter, nbr_owner, nbr_local, nbr_side, nbr_weight
):
    own_count = sections.shape[0]
    pixels = sections.shape[1]
    tilt_count = images.shape[1]
    neighbours = nbr_local.shape[1]
    peer_count = lax.axis_size("dom")
    total = own_count * peer_count
    me = lax.axis_index("dom")
    band_size = tilt_count * OVL * pixels

    target = nbr_owner.reshape(own_count, neighbours) * own_count + nbr_local
    every = jnp.arange(total)

    hits = target[:, :, None] == every[None, None, :]
    fwd = [
        jnp.sum(jnp.where(hits & (nbr_side == s)[:, :, None], nbr_weight[:, :, None], 0.0), axis=1)
        for s in (0, 1)
    ]

    target_all = lax.all_gather(target, "dom", axis=0, tiled=True)
    side_all = lax.all_gather(nbr_side, "dom", axis=0, tiled=True)
    weight_all = lax.all_gather(nbr_weight, "dom", axis=0, tiled=True)

    halfway = jnp.einsum(
        "kij,tlj->ktil", sections, slice_cols, preferred_element_type=jnp.float32
    ).astype(jnp.bfloat16)
    projected = jnp.einsum(
        "tai,ktil->ktal", slice_rows, halfway, preferred_element_type=jnp.float32
    ).astype(jnp.bfloat16)
    edges = jnp.stack((projected[:, :, :OVL], projected[:, :, pixels - OVL :]), axis=1)
    edges_all = lax.all_gather(edges, "dom", axis=0, tiled=True)

    lower_part = split_dot(fwd[0], edges_all[:, 0].reshape(total, band_size))
    upper_part = split_dot(fwd[1], edges_all[:, 1].reshape(total, band_size))
    lower_part = lower_part.reshape(own_count, tilt_count, OVL, pixels)
    upper_part = upper_part.reshape(own_count, tilt_count, OVL, pixels)

    residual = images.astype(jnp.float32) - projected.astype(jnp.float32)
    residual = residual.at[:, :, :OVL].add(-upper_part)
    residual = residual.at[:, :, pixels - OVL :].add(-lower_part)
    residual_portion = residual.astype(jnp.bfloat16)
    smoothed_images = jnp.einsum(
        "tab,ktbc->ktac", ctf_filter, residual_portion, preferred_element_type=jnp.float32
    ).astype(jnp.bfloat16)
    filtered_images = jnp.einsum(
        "ktac,tdc->ktad", smoothed_images, ctf_filter, preferred_element_type=jnp.float32
    )
    score_part = jnp.sum(filtered_images * filtered_images, axis=(1, 2, 3))
    tilt_groups = lax.axis_size("tilt")
    scores = 0.5 * lax.psum(score_part, "tilt") / (tilt_count * tilt_groups * pixels * pixels)
    filtered_portion = filtered_images.astype(jnp.bfloat16)
    reverse_pass = jnp.einsum(
        "tab,ktac->ktbc", ctf_filter, filtered_portion, preferred_element_type=jnp.float32
    ).astype(jnp.bfloat16)
    weighted = jnp.einsum(
        "ktbc,tcd->ktbd", reverse_pass, ctf_filter, preferred_element_type=jnp.float32
    ).astype(jnp.bfloat16)

    grad_bands = jnp.stack((weighted[:, :, :OVL], weighted[:, :, pixels - OVL :]), axis=1)
    grad_all = lax.all_gather(grad_bands, "dom", axis=0, tiled=True)

    mine = me * own_count + jnp.arange(own_count)
    named = target_all[None, :, :] == mine[:, None, None]
    back = [
        jnp.sum(jnp.where(named & (side_all == s)[None], weight_all[None], 0.0), axis=2)
        for s in (0, 1)
    ]
    add_top = split_dot(back[0], grad_all[:, 1].reshape(total, band_size))
    add_bottom = split_dot(back[1], grad_all[:, 0].reshape(total, band_size))
    add_top = add_top.reshape(own_count, tilt_count, OVL, pixels)
    add_bottom = add_bottom.reshape(own_count, tilt_count, OVL, pixels)

    proj_grad = weighted.astype(jnp.float32)
    proj_grad = proj_grad.at[:, :, :OVL].add(add_top)
    proj_grad = proj_grad.at[:, :, pixels - OVL :].add(add_bottom)
    proj_half = proj_grad.astype(jnp.bfloat16)
    upward = jnp.einsum(
        "tai,ktal->ktil", slice_rows, proj_half, preferred_element_type=jnp.float32
    ).astype(jnp.bfloat16)
    partial_grad = -jnp.einsum(
        "ktil,tlj->kij", upward, slice_cols, preferred_element_type=jnp.float32
    )
    section_grad = lax.psum_scatter(partial_grad, "tilt", scatter_dimension=1, tiled=True)
    return (section_grad, scores)


def solution(mesh):
    in_specs = (
        P("dom", None, None),
        P("dom", "tilt", None, None),
        P("tilt", None, None),
        P("tilt", None, None),
        P("tilt", None, None),
        P("dom", None, None),
        P("dom", None),
        P("dom", None),
        P("dom", None),
    )
    out_specs = (P("dom", "tilt", None), P("dom"))
    return jax.shard_map(
        on_device, mesh=mesh, in_specs=in_specs, out_specs=out_specs, check_vma=False
    )
```

time: 143 us -> 137 us (0.958)
  blocking collectives: 4.94 us -> 60.5 us
  waiting for transfers between devices: 78.3 us -> 45.5 us
  starting transfers between devices: 22.4 us -> 0.12 us
  local copies, waits for them, and re-layouts: 13.9 us -> 7.73 us
    all_to_all x3 -> x0, waiting for transfers between devices: 66.8 us -> none  [the longest x1 40.7 us: on_device(): lax.all_to_all(picked, 'dom', split_axis=0, concat_axis=0, tiled=True)]
    all_gather x0 -> x3, blocking collectives: none -> 55.5 us  [the longest x1 19.3 us: on_device(): weight_all = lax.all_gather(nbr_weight, 'dom', axis=0, tiled=True)]
    all_gather x0 -> x2, waiting for transfers between devices: none -> 38.9 us  [the longest x1 38.9 us: on_device(): edges_all = lax.all_gather(edges, 'dom', axis=0, tiled=True)]
    all_to_all x3 -> x0, starting transfers between devices: 22.4 us -> none  [the longest x1 11.2 us: on_device(): lax.all_to_all(outgoing.reshape(peer_count, capacity, tilt_count, OVL, pi...]
    reduce_scatter x1, waiting for transfers between devices: 11.5 us -> 6.51 us  [on_device(): lax.psum_scatter(partial_grad, 'tilt', scatter_dimension=1, tiled=True)]
    scatter x1 -> x0, local copies, waits for them, and re-layouts: 4.36 us -> none  [on_device(): outgoing = jnp.zeros((peer_count * capacity, tilt_count, OVL, pixels), jn...]
    gather x2 -> x0, local copies, waits for them, and re-layouts: 3.59 us -> none  [the longest x1 2.01 us: on_device(): picked = border_rows[code_table // 2]]
    unnamed x13 -> x20, local copies, waits for them, and re-layouts: 0.29 us -> 3.68 us
  transfers between devices with their start and end apart: 4 -> 3, of which waited for: 4 -> 2; matrix products, arithmetic and copies ran while one was open for 3% -> 1% of each run, Pallas kernels for 0% -> 0%
where the time goes in v1:
time: 137 us
  blocking collectives  60.5 us (44%)
  waiting for transfers between devices  45.5 us (33%)
  between operations  14 us (10%)
  local copies, waits for them, and re-layouts  7.73 us (6%)
  matrix products  6.92 us (5%)
  other arithmetic  2.08 us (2%)
    all_gather x1, waiting for transfers between devices, on_device(): edges_all = lax.all_gather(edges, 'dom', axis=0, tiled=True)  38.9 us
    all_gather x1, blocking collectives, on_device(): weight_all = lax.all_gather(nbr_weight, 'dom', axis=0, tiled=True)  19.3 us
    all_gather x1, blocking collectives, on_device(): side_all = lax.all_gather(nbr_side, 'dom', axis=0, tiled=True)  18.8 us
    all_gather x1, blocking collectives, on_device(): target_all = lax.all_gather(target, 'dom', axis=0, tiled=True)  17.4 us
    reduce_scatter x1, waiting for transfers between devices, on_device(): lax.psum_scatter(partial_grad, 'tilt', scatter_dimension=1, tiled=True)  6.51 us
    psum x1, blocking collectives, on_device(): lax.psum(score_part, 'tilt')  4.94 us
    unnamed x20, local copies, waits for them, and re-layouts  3.68 us
  transfers between devices with their start and end apart: 3, of which 2 were waited for; matrix products, arithmetic and copies ran while one was open for 1% of the time, Pallas kernels for 0%

profile of v1, /device:TPU:0, one launch (start us, length us, event | category | flops | bytes accessed | tf_op | source)
XLA Modules:
  0.0 136.8 jit_solution(1483881849874437)
XLA Ops:
  7.2 1.9 %convert_subtract_fusion = (f32[2,2,256,256]{3,2,0,1:T(8,128)S(1)}, bf16[2,2,256,256]{3,2,0,1:T(8,128)(2,1)S(1)}) fusion(bf16[2,2,256,256]{3,2,1,0:T(8,128)(2,1)} %param.18, bf16[2,256,256]{2,1,0:T(8,128)(2,1)} %param.19, bf16[2,256,256]{2,1,0:T(8,128)(2,1)} %param.20, bf16[2,256,256]{2,1,0:T(8,128)(2,1)} %param.17), kind=kOutput, calls=%fused_computation.26 | convolution fusion | flops 269746176 | bytes 2883584 | tf_op jit(solution)/shard_map/tai,ktil->ktal/dot_general | solution.py:47
  9.1 0.6 pad_maximum_fusion
  9.8 0.6 copy-done.5
  10.5 0.6 copy-done.6
  11.1 0.7 copy-done.4
  11.8 0.7 copy-done.3
  12.6 38.9 %all-gather.6.cloned.1.call-done = bf16[32,2,2,16,256]{4,3,0,2,1:T(8,128)(2,1)} async-done(((bf16[2,2,2,16,256]{4,3,0,2,1:T(8,128)(2,1)}), bf16[32,2,2,16,256]{4,3,0,2,1:T(8,128)(2,1)}) %all-gather.6.cloned.1.call-update) | async-done | bytes 1048592 | tf_op jit(solution)/shard_map/all_gather | solution.py:51
  51.5 1.3 fusion.53
  52.8 0.2 reshape_squeeze.12
  53.7 0.2 reshape_squeeze.13
  54.6 0.7 multiply_reduce_fusion
  55.3 0.6 fusion.58
  55.9 0.6 pad_maximum_fusion.1
  56.7 19.3 %all-gather.2 = f32[16,2,16]{2,1,0:T(2,128)S(1)} all-gather(f32[1,2,16]{2,1,0:T(2,128)S(1)} %bitcast.146), channel_id=1, replica_groups=mesh['tilt'=2,'dom'=16] {'dom'}, dimensions={0}, use_global_device_ids=true | all-gather | bytes 2176 | tf_op jit(solution)/shard_map/all_gather | solution.py:42
  76.1 17.4 %all-gather = s32[16,2,16]{2,1,0:T(2,128)S(1)} all-gather(s32[1,2,16]{2,1,0:T(2,128)S(1)} %bitcast.145), channel_id=1, replica_groups=mesh['tilt'=2,'dom'=16] {'dom'}, dimensions={0}, use_global_device_ids=true | all-gather | bytes 2176 | tf_op jit(solution)/shard_map/all_gather | solution.py:40
  93.5 18.8 %all-gather.1 = s32[16,2,16]{2,1,0:T(2,128)S(1)} all-gather(s32[1,2,16]{2,1,0:T(2,128)S(1)} %bitcast.147), channel_id=1, replica_groups=mesh['tilt'=2,'dom'=16] {'dom'}, dimensions={0}, use_global_device_ids=true | all-gather | bytes 2176 | tf_op jit(solution)/shard_map/all_gather | solution.py:41
  112.7 1.3 fusion.52
  114.0 0.2 reshape_squeeze.14
  114.9 0.2 reshape_squeeze.15
  115.9 0.9 copy-done.1
  116.8 1.5 %fusion.9 = f32[2,256,256]{2,1,0:T(8,128)} fusion(bf16[2,256,256]{2,1,0:T(8,128)(2,1)S(1)} %copy-done.1, bf16[2,256,256]{2,1,0:T(8,128)(2,1)S(1)} %copy-done.2, f32[2,2,256,256]{3,2,0,1:T(8,128)S(1)} %fusion.30), kind=kOutput, calls=%fused_computation.24 | convolution fusion | flops 269090816 | bytes 2097152 | tf_op jit(solution)/shard_map/ktil,tlj->kij/dot_general | solution.py:100
  118.3 4.9 %psum.7 = f32[2]{0:T(128)S(1)} all-reduce(f32[2]{0:T(128)S(1)} %get-tuple-element.70), channel_id=1, replica_groups=mesh['tilt'=2,'dom'=16] {'tilt'}, use_global_device_ids=true, to_apply=%region_6.7 | all-reduce | flops 2 | bytes 16 | tf_op jit(solution)/shard_map/psum | solution.py:70
  123.3 0.5 broadcast_multiply_fusion.1
  123.8 6.5 %reduce-scatter.2.cloned.1.call-done = f32[2,128,256]{2,1,0:T(8,128)} async-done(((f32[2,256,256]{2,1,0:T(8,128)}), f32[2,128,256]{2,1,0:T(8,128)}) %reduce-scatter.2.cloned.1.call-update) | async-done | bytes 262160 | tf_op jit(solution)/shard_map/reduce_scatter | solution.py:103
  (56 shorter events, 3.5 us)
Async XLA Ops:
  7.2 47.4 %copy-start = (bf16[2,256,256]{2,1,0:T(8,128)(2,1)S(1)}, bf16[2,256,256]{2,1,0:T(8,128)(2,1)}, u32[]{:S(2)}) copy-start(bf16[2,256,256]{2,1,0:T(8,128)(2,1)} %param.21) | copy-start | bytes 786436
  7.2 44.3 %all-gather.6.cloned.1.call-start = ((), (), s32[]{:S(2)}) async-start(), calls=%async_computation.1 | async-start | bytes 1114112 | tf_op jit(solution)/shard_map/all_gather | solution.py:51
  9.7 0.7 copy-start.5
  9.8 102.9 %all-gather.8.cloned.1.call-start = ((), (), s32[]{:S(2)}) async-start(), calls=%async_computation.2 | async-start | bytes 1114112 | tf_op jit(solution)/shard_map/all_gather | solution.py:80
  10.4 0.7 copy-start.6
  11.1 0.7 copy-start.4
  11.8 0.7 copy-start.3
  56.6 73.7 %reduce-scatter.2.cloned.1.call-start = ((), (), s32[]{:S(2)}) async-start(), calls=%async_computation.3 | async-start | bytes 786432 | tf_op jit(solution)/shard_map/reduce_scatter | solution.py:103
  115.8 1.0 copy-start.1
  115.8 1.0 copy-start.2
Sparse Core Ops, SparseCore 0:
  10.8 40.6 all-gather.5
  56.7 36.8 all-gather.7
  118.5 11.8 reduce-scatter.1

commit v2 on v1

--- a/solution.py
+++ b/solution.py
@@ -37,10 +37,6 @@
         for s in (0, 1)
     ]
 
-    target_all = lax.all_gather(target, "dom", axis=0, tiled=True)
-    side_all = lax.all_gather(nbr_side, "dom", axis=0, tiled=True)
-    weight_all = lax.all_gather(nbr_weight, "dom", axis=0, tiled=True)
-
     halfway = jnp.einsum(
         "kij,tlj->ktil", sections, slice_cols, preferred_element_type=jnp.float32
     ).astype(jnp.bfloat16)
@@ -48,7 +44,15 @@
         "tai,ktil->ktal", slice_rows, halfway, preferred_element_type=jnp.float32
     ).astype(jnp.bfloat16)
     edges = jnp.stack((projected[:, :, :OVL], projected[:, :, pixels - OVL :]), axis=1)
-    edges_all = lax.all_gather(edges, "dom", axis=0, tiled=True)
+    edges_all = lax.all_to_all(
+        jnp.broadcast_to(edges[None], (peer_count,) + edges.shape).reshape(
+            (total,) + edges.shape[1:]
+        ),
+        "dom",
+        split_axis=0,
+        concat_axis=0,
+        tiled=True,
+    )
 
     lower_part = split_dot(fwd[0], edges_all[:, 0].reshape(total, band_size))
     upper_part = split_dot(fwd[1], edges_all[:, 1].reshape(total, band_size))
@@ -67,7 +71,6 @@
     )
     score_part = jnp.sum(filtered_images * filtered_images, axis=(1, 2, 3))
     tilt_groups = lax.axis_size("tilt")
-    scores = 0.5 * lax.psum(score_part, "tilt") / (tilt_count * tilt_groups * pixels * pixels)
     filtered_portion = filtered_images.astype(jnp.bfloat16)
     reverse_pass = jnp.einsum(
         "tab,ktac->ktbc", ctf_filter, filtered_portion, preferred_element_type=jnp.float32
@@ -76,19 +79,17 @@
         "ktbc,tcd->ktbd", reverse_pass, ctf_filter, preferred_element_type=jnp.float32
     ).astype(jnp.bfloat16)
 
-    grad_bands = jnp.stack((weighted[:, :, :OVL], weighted[:, :, pixels - OVL :]), axis=1)
-    grad_all = lax.all_gather(grad_bands, "dom", axis=0, tiled=True)
-
-    mine = me * own_count + jnp.arange(own_count)
-    named = target_all[None, :, :] == mine[:, None, None]
-    back = [
-        jnp.sum(jnp.where(named & (side_all == s)[None], weight_all[None], 0.0), axis=2)
-        for s in (0, 1)
-    ]
-    add_top = split_dot(back[0], grad_all[:, 1].reshape(total, band_size))
-    add_bottom = split_dot(back[1], grad_all[:, 0].reshape(total, band_size))
-    add_top = add_top.reshape(own_count, tilt_count, OVL, pixels)
-    add_bottom = add_bottom.reshape(own_count, tilt_count, OVL, pixels)
+    bottom_rows = weighted[:, :, pixels - OVL :].reshape(own_count, band_size)
+    top_rows = weighted[:, :, :OVL].reshape(own_count, band_size)
+    to_top = split_dot(fwd[0].T, bottom_rows)
+    to_bottom = split_dot(fwd[1].T, top_rows)
+    outgoing = jnp.stack((to_top, to_bottom), axis=1).astype(jnp.bfloat16)
+    returned = lax.all_to_all(outgoing, "dom", split_axis=0, concat_axis=0, tiled=True)
+    returned = jnp.sum(
+        returned.reshape(peer_count, own_count, 2, band_size).astype(jnp.float32), axis=0
+    )
+    add_top = returned[:, 0].reshape(own_count, tilt_count, OVL, pixels)
+    add_bottom = returned[:, 1].reshape(own_count, tilt_count, OVL, pixels)
 
     proj_grad = weighted.astype(jnp.float32)
     proj_grad = proj_grad.at[:, :, :OVL].add(add_top)
@@ -100,7 +101,19 @@
     partial_grad = -jnp.einsum(
         "ktil,tlj->kij", upward, slice_cols, preferred_element_type=jnp.float32
     )
-    section_grad = lax.psum_scatter(partial_grad, "tilt", scatter_dimension=1, tiled=True)
+    scale = 0.5 / (tilt_count * tilt_groups * pixels * pixels)
+    if tilt_groups != 2:
+        scores = scale * lax.psum(score_part, "tilt")
+        section_grad = lax.psum_scatter(partial_grad, "tilt", scatter_dimension=1, tiled=True)
+        return (section_grad, scores)
+    half = pixels // 2
+    side = lax.axis_index("tilt")
+    kept = lax.dynamic_slice_in_dim(partial_grad, side * half, half, axis=1)
+    given = lax.dynamic_slice_in_dim(partial_grad, (1 - side) * half, half, axis=1)
+    parcel = jnp.concatenate((given.reshape(-1), score_part))
+    parcel = lax.ppermute(parcel, "tilt", [(0, 1), (1, 0)])
+    section_grad = kept + parcel[: given.size].reshape(given.shape)
+    scores = scale * (score_part + parcel[given.size :])
     return (section_grad, scores)
 
 

time: 137 us -> 85.1 us (0.62)
  blocking collectives: 60.5 us -> 0 us
  starting transfers between devices: 0.12 us -> 15.9 us
  between operations: 14 us -> 1 us
  waiting for transfers between devices: 45.5 us -> 53 us
  local copies, waits for them, and re-layouts: 7.73 us -> 4.7 us
    all_gather x3 -> x0, blocking collectives: 55.5 us -> none  [the longest x1 19.3 us: on_device(): weight_all = lax.all_gather(nbr_weight, 'dom', axis=0, tiled=True)]
    all_to_all x0 -> x2, waiting for transfers between devices: none -> 45.6 us  [the longest x1 22.9 us: on_device(): lax.all_to_all(outgoing, 'dom', split_axis=0, concat_axis=0, tiled=True)]
    all_gather x2 -> x0, waiting for transfers between devices: 38.9 us -> none  [the longest x1 38.9 us: on_device(): edges_all = lax.all_gather(edges, 'dom', axis=0, tiled=True)]
    all_to_all x0 -> x2, starting transfers between devices: none -> 14.4 us  [the longest x1 7.5 us: on_device(): lax.all_to_all(jnp.broadcast_to(edges[None], (peer_count,) + edges.shape)...]
    ppermute x0 -> x1, waiting for transfers between devices: none -> 7.39 us  [on_device(): parcel = lax.ppermute(parcel, 'tilt', [(0, 1), (1, 0)])]
    reduce_scatter x1 -> x0, waiting for transfers between devices: 6.51 us -> none  [on_device(): lax.psum_scatter(partial_grad, 'tilt', scatter_dimension=1, tiled=True)]
    psum x1 -> x0, blocking collectives: 4.94 us -> none  [on_device(): lax.psum(score_part, 'tilt')]
    unnamed x20 -> x23, local copies, waits for them, and re-layouts: 3.68 us -> 0.86 us
  transfers between devices with their start and end apart: 3 -> 3, of which waited for: 2 -> 3; matrix products, arithmetic and copies ran while one was open for 1% -> 0% of each run, Pallas kernels for 0% -> 0%
where the time goes in v2:
time: 85.1 us; the launch traced here: 84.3 us
  waiting for transfers between devices  53 us (62%)
  starting transfers between devices  15.9 us (19%)
  matrix products  7.11 us (8%)
  local copies, waits for them, and re-layouts  4.7 us (6%)
  other arithmetic  2.51 us (3%)
  between operations  1 us (1%)
    all_to_all x1, waiting for transfers between devices, on_device(): lax.all_to_all(outgoing, 'dom', split_axis=0, concat_axis=0, tiled=True)  22.9 us
    all_to_all x1, waiting for transfers between devices, on_device(): lax.all_to_all(jnp.broadcast_to(edges[None], (peer_count,) + edges.shape)...  22.7 us
    all_to_all x1, starting transfers between devices, on_device(): lax.all_to_all(jnp.broadcast_to(edges[None], (peer_count,) + edges.shape)...  7.5 us
    ppermute x1, waiting for transfers between devices, on_device(): parcel = lax.ppermute(parcel, 'tilt', [(0, 1), (1, 0)])  7.39 us
    all_to_all x1, starting transfers between devices, on_device(): lax.all_to_all(outgoing, 'dom', split_axis=0, concat_axis=0, tiled=True)  6.86 us
    another operation x1, local copies, waits for them, and re-layouts, on_device(): outgoing = jnp.stack((to_top, to_bottom), axis=1).astype(jnp.bfloat16)  2.05 us
    dot_general x1, matrix products, on_device(): jnp.einsum('tai,ktil->ktal', slice_rows, halfway, preferred_element_type=...  1.86 us
  transfers between devices with their start and end apart: 3, of which 3 were waited for; matrix products, arithmetic and copies ran while one was open for 0% of the time, Pallas kernels for 0%

profile of v2, /device:TPU:0, one launch (start us, length us, event | category | flops | bytes accessed | tf_op | source)
XLA Modules:
  0.0 84.3 jit_solution(656313760681576977)
XLA Ops:
  0.6 1.9 %convert_subtract_fusion = (f32[2,2,256,256]{3,2,0,1:T(8,128)S(1)}, bf16[2,2,256,256]{3,2,0,1:T(8,128)(2,1)S(1)}) fusion(bf16[2,2,256,256]{3,2,1,0:T(8,128)(2,1)} %param.18, bf16[2,256,256]{2,1,0:T(8,128)(2,1)} %param.19, bf16[2,256,256]{2,1,0:T(8,128)(2,1)} %param.20, bf16[2,256,256]{2,1,0:T(8,128)(2,1)} %param.17), kind=kOutput, calls=%fused_computation.32 | convolution fusion | flops 269746176 | bytes 2883584 | tf_op jit(solution)/shard_map/tai,ktil->ktal/dot_general | solution.py:43
  2.6 1.1 %broadcast_in_dim.30 = bf16[16,2,2,2,16,256]{5,4,3,2,1,0:T(8,128)(2,1)} broadcast(bf16[2,2,2,16,256]{4,3,2,1,0:T(8,128)(2,1)S(1)} %copy.55), dimensions={1,2,3,4,5} | broadcast | bytes 1114112 | tf_op jit(solution)/shard_map/broadcast_in_dim | solution.py:48
  3.7 7.5 %all-to-all-start = ((bf16[32,2,2,16,256]{4,3,2,1,0:T(8,128)(2,1)}), bf16[32,2,2,16,256]{4,3,2,1,0:T(8,128)(2,1)S(1)}, u32[]{:S(2)}, u32[]{:S(2)}) async-start(bf16[32,2,2,16,256]{4,3,2,1,0:T(8,128)(2,1)} %bitcast.9), calls=%async_computation | async-start | bytes 2097152 | tf_op jit(solution)/shard_map/all_to_all | solution.py:47
  11.4 22.7 %all-to-all-done = bf16[32,2,2,16,256]{4,3,2,1,0:T(8,128)(2,1)S(1)} async-done(((bf16[32,2,2,16,256]{4,3,2,1,0:T(8,128)(2,1)}), bf16[32,2,2,16,256]{4,3,2,1,0:T(8,128)(2,1)S(1)}, u32[]{:S(2)}, u32[]{:S(2)}) %all-to-all-start) | async-done | bytes 1048608 | tf_op jit(solution)/shard_map/all_to_all | solution.py:47
  34.2 0.3 copy.81
  35.1 0.3 copy.83
  36.0 0.7 multiply_reduce_fusion
  36.7 0.6 fusion.67
  37.4 0.3 fusion.72
  37.8 0.3 convolution_add_fusion.1
  38.1 0.3 fusion.2
  38.5 0.3 fusion.74
  38.9 0.4 convolution_add_fusion.3
  39.3 0.3 fusion.3
  39.7 2.0 %copy.64 = bf16[32,2,8192]{2,1,0:T(2,128)(2,1)} copy(bf16[32,2,8192]{2,0,1:T(8,128)(2,1)S(1)} %pad_maximum_fusion) | data formatting | bytes 2097152 | tf_op jit(solution)/shard_map/stack | solution.py:86
  41.8 6.9 %all-to-all-start.1 = ((bf16[32,2,8192]{2,1,0:T(2,128)(2,1)}), bf16[32,2,8192]{2,1,0:T(2,128)(2,1)S(1)}, u32[]{:S(2)}, u32[]{:S(2)}) async-start(bf16[32,2,8192]{2,1,0:T(2,128)(2,1)} %copy.64), calls=%async_computation.1 | async-start | bytes 2097152 | tf_op jit(solution)/shard_map/all_to_all | solution.py:87
  48.6 22.9 %all-to-all-done.1 = bf16[32,2,8192]{2,1,0:T(2,128)(2,1)S(1)} async-done(((bf16[32,2,8192]{2,1,0:T(2,128)(2,1)}), bf16[32,2,8192]{2,1,0:T(2,128)(2,1)S(1)}, u32[]{:S(2)}, u32[]{:S(2)}) %all-to-all-start.1) | async-done | bytes 1048608 | tf_op jit(solution)/shard_map/all_to_all | solution.py:87
  71.6 0.9 %convert_reduce_fusion = f32[2,2,8192]{2,1,0:T(2,128)S(1)} fusion(bf16[16,2,2,8192]{3,2,1,0:T(2,128)(2,1)S(1)} %bitcast.187), kind=kLoop, calls=%fused_computation.14 | loop fusion | flops 1015808 | bytes 1179648 | tf_op jit(solution)/shard_map/reduce_sum | solution.py:88
  72.5 0.4 slice_reduce_fusion
  73.0 0.7 fusion.13
  74.0 1.6 %collective-permute-start = (f32[65538]{0:T(1024)S(1)}, f32[65538]{0:T(1024)S(1)}, u32[]{:S(2)}, u32[]{:S(2)}) collective-permute-start(f32[65538]{0:T(1024)S(1)} %pad_maximum_fusion.1), channel_id=1, source_target_pairs={{0,16},{16,0},{1,17},{17,1},{2,18},{18,2},{3,19},{19,3},{4,20},{20... | collective-permute-start | bytes 786464 | tf_op jit(solution)/shard_map/ppermute | solution.py:114
  75.6 7.4 %collective-permute-done = f32[65538]{0:T(1024)S(1)} collective-permute-done((f32[65538]{0:T(1024)S(1)}, f32[65538]{0:T(1024)S(1)}, u32[]{:S(2)}, u32[]{:S(2)}) %collective-permute-start) | collective-permute-done | bytes 262184 | tf_op jit(solution)/shard_map/ppermute | solution.py:114
  83.0 0.7 dynamic-slice_add_fusion
  83.8 0.5 fusion.54
  (48 shorter events, 2.0 us)
Async XLA Ops:
  0.6 35.4 %copy-start = (bf16[2,256,256]{2,1,0:T(8,128)(2,1)S(1)}, bf16[2,256,256]{2,1,0:T(8,128)(2,1)}, u32[]{:S(2)}) copy-start(bf16[2,256,256]{2,1,0:T(8,128)(2,1)} %param.21) | copy-start | bytes 786436
  3.7 7.5 %copy-start.3 = (s32[2,2,8]{2,1,0:T(2,128)S(1)}, s32[2,2,8]{2,1,0:T(2,128)}, u32[]{:S(2)}) copy-start(s32[2,2,8]{2,1,0:T(2,128)} %param.22) | copy-start | bytes 388
  3.7 7.6 %copy-start.4 = (s32[2,16]{1,0:T(2,128)S(1)}, s32[2,16]{1,0:T(2,128)}, u32[]{:S(2)}) copy-start(s32[2,16]{1,0:T(2,128)} %param.23) | copy-start | bytes 388
  3.7 7.6 %copy-start.6 = (s32[2,16]{1,0:T(2,128)S(1)}, s32[2,16]{1,0:T(2,128)}, u32[]{:S(2)}) copy-start(s32[2,16]{1,0:T(2,128)} %param.24) | copy-start | bytes 388
  3.7 7.6 %copy-start.5 = (f32[2,16]{1,0:T(2,128)S(1)}, f32[2,16]{1,0:T(2,128)}, u32[]{:S(2)}) copy-start(f32[2,16]{1,0:T(2,128)} %param.25) | copy-start | bytes 388
  3.7 30.5 %all-to-all-start = ((bf16[32,2,2,16,256]{4,3,2,1,0:T(8,128)(2,1)}), bf16[32,2,2,16,256]{4,3,2,1,0:T(8,128)(2,1)S(1)}, u32[]{:S(2)}, u32[]{:S(2)}) async-start(bf16[32,2,2,16,256]{4,3,2,1,0:T(8,128)(2,1)} %bitcast.9), calls=%async_computation | async-start | bytes 2097152 | tf_op jit(solution)/shard_map/all_to_all | solution.py:47
  41.8 29.8 %all-to-all-start.1 = ((bf16[32,2,8192]{2,1,0:T(2,128)(2,1)}), bf16[32,2,8192]{2,1,0:T(2,128)(2,1)S(1)}, u32[]{:S(2)}, u32[]{:S(2)}) async-start(bf16[32,2,8192]{2,1,0:T(2,128)(2,1)} %copy.64), calls=%async_computation.1 | async-start | bytes 2097152 | tf_op jit(solution)/shard_map/all_to_all | solution.py:87
  71.6 1.4 %copy-start.1 = (bf16[2,256,256]{2,1,0:T(8,128)(2,1)S(1)}, bf16[2,256,256]{2,1,0:T(8,128)(2,1)}, u32[]{:S(2)}) copy-start(bf16[2,256,256]{2,1,0:T(8,128)(2,1)} %param.19) | copy-start | bytes 786436
  71.6 1.4 %copy-start.2 = (bf16[2,256,256]{2,1,0:T(8,128)(2,1)S(1)}, bf16[2,256,256]{2,1,0:T(8,128)(2,1)}, u32[]{:S(2)}) copy-start(bf16[2,256,256]{2,1,0:T(8,128)(2,1)} %param.20) | copy-start | bytes 786436
  74.0 9.0 %collective-permute-start = (f32[65538]{0:T(1024)S(1)}, f32[65538]{0:T(1024)S(1)}, u32[]{:S(2)}, u32[]{:S(2)}) collective-permute-start(f32[65538]{0:T(1024)S(1)} %pad_maximum_fusion.1), channel_id=1, source_target_pairs={{0,16},{16,0},{1,17},{17,1},{2,18},{18,2},{3,19},{19,3},{4,20},{20... | collective-permute-start | bytes 786464 | tf_op jit(solution)/shard_map/ppermute | solution.py:114

commit v3 on v2

--- a/solution.py
+++ b/solution.py
@@ -28,14 +28,18 @@
     me = lax.axis_index("dom")
     band_size = tilt_count * OVL * pixels
 
-    target = nbr_owner.reshape(own_count, neighbours) * own_count + nbr_local
+    steps = peer_count.bit_length() - 1
+    relative = nbr_owner.reshape(own_count, neighbours) ^ me
+    flipped = sum(((relative >> (steps - 1 - b)) & 1) << b for b in range(steps))
     every = jnp.arange(total)
 
-    hits = target[:, :, None] == every[None, None, :]
-    fwd = [
-        jnp.sum(jnp.where(hits & (nbr_side == s)[:, :, None], nbr_weight[:, :, None], 0.0), axis=1)
-        for s in (0, 1)
-    ]
+    def weights_for(blocks, side):
+        hits = (blocks * own_count + nbr_local)[:, :, None] == every[None, None, :]
+        hits = hits & (nbr_side == side)[:, :, None]
+        return jnp.sum(jnp.where(hits, nbr_weight[:, :, None], 0.0), axis=1)
+
+    fwd = [weights_for(flipped, s) for s in (0, 1)]
+    back = [weights_for(relative, s) for s in (0, 1)]
 
     halfway = jnp.einsum(
         "kij,tlj->ktil", sections, slice_cols, preferred_element_type=jnp.float32
@@ -44,15 +48,11 @@
         "tai,ktil->ktal", slice_rows, halfway, preferred_element_type=jnp.float32
     ).astype(jnp.bfloat16)
     edges = jnp.stack((projected[:, :, :OVL], projected[:, :, pixels - OVL :]), axis=1)
-    edges_all = lax.all_to_all(
-        jnp.broadcast_to(edges[None], (peer_count,) + edges.shape).reshape(
-            (total,) + edges.shape[1:]
-        ),
-        "dom",
-        split_axis=0,
-        concat_axis=0,
-        tiled=True,
-    )
+    edges_all = edges
+    for b in range(steps):
+        stride = peer_count >> (b + 1)
+        pairs = [(i, i ^ stride) for i in range(peer_count)]
+        edges_all = jnp.concatenate((edges_all, lax.ppermute(edges_all, "dom", pairs)), axis=0)
 
     lower_part = split_dot(fwd[0], edges_all[:, 0].reshape(total, band_size))
     upper_part = split_dot(fwd[1], edges_all[:, 1].reshape(total, band_size))
@@ -81,13 +81,18 @@
 
     bottom_rows = weighted[:, :, pixels - OVL :].reshape(own_count, band_size)
     top_rows = weighted[:, :, :OVL].reshape(own_count, band_size)
-    to_top = split_dot(fwd[0].T, bottom_rows)
-    to_bottom = split_dot(fwd[1].T, top_rows)
-    outgoing = jnp.stack((to_top, to_bottom), axis=1).astype(jnp.bfloat16)
-    returned = lax.all_to_all(outgoing, "dom", split_axis=0, concat_axis=0, tiled=True)
-    returned = jnp.sum(
-        returned.reshape(peer_count, own_count, 2, band_size).astype(jnp.float32), axis=0
+    to_top = split_dot(back[0].T, bottom_rows)
+    to_bottom = split_dot(back[1].T, top_rows)
+    returned = jnp.stack((to_top, to_bottom), axis=1).reshape(
+        (2,) * steps + (own_count, 2, band_size)
     )
+    for b in range(steps):
+        stride = 1 << b
+        pairs = [(i, i ^ stride) for i in range(peer_count)]
+        axis = steps - 1 - b
+        kept = lax.index_in_dim(returned, 0, axis, keepdims=False)
+        given = lax.index_in_dim(returned, 1, axis, keepdims=False).astype(jnp.bfloat16)
+        returned = kept + lax.ppermute(given, "dom", pairs).astype(jnp.float32)
     add_top = returned[:, 0].reshape(own_count, tilt_count, OVL, pixels)
     add_bottom = returned[:, 1].reshape(own_count, tilt_count, OVL, pixels)
 
@@ -110,10 +115,17 @@
     side = lax.axis_index("tilt")
     kept = lax.dynamic_slice_in_dim(partial_grad, side * half, half, axis=1)
     given = lax.dynamic_slice_in_dim(partial_grad, (1 - side) * half, half, axis=1)
-    parcel = jnp.concatenate((given.reshape(-1), score_part))
-    parcel = lax.ppermute(parcel, "tilt", [(0, 1), (1, 0)])
+    score_hi = score_part.astype(jnp.bfloat16)
+    score_rest = score_part - score_hi.astype(jnp.float32)
+    score_mid = score_rest.astype(jnp.bfloat16)
+    score_low = (score_rest - score_mid.astype(jnp.float32)).astype(jnp.bfloat16)
+    parcel = jnp.concatenate(
+        (given.reshape(-1).astype(jnp.bfloat16), score_hi, score_mid, score_low)
+    )
+    parcel = lax.ppermute(parcel, "tilt", [(0, 1), (1, 0)]).astype(jnp.float32)
     section_grad = kept + parcel[: given.size].reshape(given.shape)
-    scores = scale * (score_part + parcel[given.size :])
+    parts = parcel[given.size :].reshape(3, own_count)
+    scores = scale * (score_part + (parts[0] + (parts[1] + parts[2])))
     return (section_grad, scores)
 
 

time: 85.1 us -> 68.4 us (0.80)
  waiting for transfers between devices: 53 us -> 30.8 us
  local copies, waits for them, and re-layouts: 4.7 us -> 8.6 us
  other arithmetic: 2.51 us -> 5.98 us
  starting transfers between devices: 15.9 us -> 14.6 us
    all_to_all x2 -> x0, waiting for transfers between devices: 45.6 us -> none  [the longest x1 22.9 us: on_device(): lax.all_to_all(outgoing, 'dom', split_axis=0, concat_axis=0, tiled=True)]
    ppermute x1 -> x9, waiting for transfers between devices: 7.39 us -> 30.8 us  [the longest x4 14.8 us: on_device(): returned = kept + lax.ppermute(given, 'dom', pairs).astype(jnp.float32)]
    all_to_all x2 -> x0, starting transfers between devices: 14.4 us -> none  [the longest x1 7.5 us: on_device(): lax.all_to_all(jnp.broadcast_to(edges[None], (peer_count,) + edges.shape)...]
    ppermute x1 -> x9, starting transfers between devices: 1.58 us -> 14.6 us  [the longest x4 6.52 us: on_device(): returned = kept + lax.ppermute(given, 'dom', pairs).astype(jnp.float32)]
    another operation x1, other arithmetic: 0.1 us -> 2.59 us  [on_device(): jnp.stack((to_top, to_bottom), axis=1)]
    unnamed x23 -> x24, local copies, waits for them, and re-layouts: 0.86 us -> 2.29 us
    slice x1 -> x2, local copies, waits for them, and re-layouts: 0.08 us -> 1.33 us  [on_device(): lower_part = split_dot(fwd[0], edges_all[:, 0].reshape(total, band_size))]
    concatenate x0 -> x2, local copies, waits for them, and re-layouts: none -> 1.15 us  [the longest x1 0.84 us: on_device(): jnp.concatenate((edges_all, lax.ppermute(edges_all, 'dom', pairs)), axis=0)]
  transfers between devices with their start and end apart: 3 -> 9, of which waited for: 3 -> 8; matrix products, arithmetic and copies ran while one was open for 0% -> 3% of each run, Pallas kernels for 0% -> 0%
where the time goes in v3:
time: 68.4 us; the launch traced here: 68.2 us
  waiting for transfers between devices  30.8 us (45%)
  starting transfers between devices  14.6 us (21%)
  local copies, waits for them, and re-layouts  8.6 us (13%)
  matrix products  7.12 us (10%)
  other arithmetic  5.98 us (9%)
  between operations  1.11 us (2%)
    ppermute x4, waiting for transfers between devices, on_device(): returned = kept + lax.ppermute(given, 'dom', pairs).astype(jnp.float32)  14.8 us
    ppermute x4, waiting for transfers between devices, on_device(): lax.ppermute(edges_all, 'dom', pairs)  12.5 us
    ppermute x4, starting transfers between devices, on_device(): returned = kept + lax.ppermute(given, 'dom', pairs).astype(jnp.float32)  6.52 us
    ppermute x4, starting transfers between devices, on_device(): lax.ppermute(edges_all, 'dom', pairs)  6.51 us
    ppermute x1, waiting for transfers between devices, on_device(): parcel = lax.ppermute(parcel, 'tilt', [(0, 1), (1, 0)]).astype(jnp.float32)  3.47 us
    another operation x1, other arithmetic, on_device(): jnp.stack((to_top, to_bottom), axis=1)  2.59 us
    unnamed x24, local copies, waits for them, and re-layouts  2.29 us
    another operation x2, local copies, waits for them, and re-layouts, on_device(): jnp.stack((to_top, to_bottom), axis=1)  2.22 us
  transfers between devices with their start and end apart: 9, of which 8 were waited for; matrix products, arithmetic and copies ran while one was open for 3% of the time, Pallas kernels for 0%

profile of v3, /device:TPU:0, one launch (start us, length us, event | category | flops | bytes accessed | tf_op | source)
XLA Modules:
  0.0 68.2 jit_solution(3276465617243493783)
XLA Ops:
  0.7 1.9 %convert_subtract_fusion = (f32[2,2,256,256]{3,2,0,1:T(8,128)S(1)}, bf16[2,2,256,256]{3,2,0,1:T(8,128)(2,1)S(1)}) fusion(bf16[2,2,256,256]{3,2,1,0:T(8,128)(2,1)} %param.18, bf16[2,256,256]{2,1,0:T(8,128)(2,1)} %param.19, bf16[2,256,256]{2,1,0:T(8,128)(2,1)} %param.20, bf16[2,256,256]{2,1,0:T(8,128)(2,1)} %param.17), kind=kOutput, calls=%fused_computation.30 | convolution fusion | flops 269746176 | bytes 2883584 | tf_op jit(solution)/shard_map/tai,ktil->ktal/dot_general | solution.py:47
  3.2 4.0 %collective-permute-start = (bf16[2,2,2,16,256]{4,3,0,2,1:T(8,128)(2,1)S(1)}, bf16[2,2,2,16,256]{4,3,0,2,1:T(8,128)(2,1)S(1)}, u32[]{:S(2)}, u32[]{:S(2)}) collective-permute-start(bf16[2,2,2,16,256]{4,3,0,2,1:T(8,128)(2,1)S(1)} %get-tuple-element.64), channel_id=1, source_target_pairs={{0,8},{1,9},{2,10},{3,11},{4,12},{5,13},{6,14},{7,15},{8,0},{9,1},... | collective-permute-start | bytes 196616 | tf_op jit(solution)/shard_map/ppermute | solution.py:55
  7.3 3.6 %collective-permute-done = bf16[2,2,2,16,256]{4,3,0,2,1:T(8,128)(2,1)S(1)} collective-permute-done((bf16[2,2,2,16,256]{4,3,0,2,1:T(8,128)(2,1)S(1)}, bf16[2,2,2,16,256]{4,3,0,2,1:T(8,128)(2,1)S(1)}, u32[]{:S(2)}, u32[]{:S(2)}) %collective-permute-start) | collective-permute-done | bytes 65568 | tf_op jit(solution)/shard_map/ppermute | solution.py:55
  11.6 4.4 %collective-permute-done.1 = bf16[4,2,2,16,256]{4,3,0,2,1:T(8,128)(2,1)S(1)} collective-permute-done((bf16[4,2,2,16,256]{4,3,0,2,1:T(8,128)(2,1)S(1)}, bf16[4,2,2,16,256]{4,3,0,2,1:T(8,128)(2,1)S(1)}, u32[]{:S(2)}, u32[]{:S(2)}) %collective-permute-start.1) | collective-permute-done | bytes 131104 | tf_op jit(solution)/shard_map/ppermute | solution.py:55
  16.0 1.8 %collective-permute-start.2 = (bf16[8,2,2,16,256]{4,3,0,2,1:T(8,128)(2,1)S(1)}, bf16[8,2,2,16,256]{4,3,0,2,1:T(8,128)(2,1)S(1)}, u32[]{:S(2)}, u32[]{:S(2)}) collective-permute-start(bf16[8,2,2,16,256]{4,3,0,2,1:T(8,128)(2,1)S(1)} %pad_maximum_fusion.2), channel_id=1, source_target_pairs={{0,2},{1,3},{2,0},{3,1},{4,6},{5,7},{6,4},{7,5},{8,10},{9,11},{10,... | collective-permute-start | bytes 786440 | tf_op jit(solution)/shard_map/ppermute | solution.py:55
  18.0 4.5 %collective-permute-done.2 = bf16[8,2,2,16,256]{4,3,0,2,1:T(8,128)(2,1)S(1)} collective-permute-done((bf16[8,2,2,16,256]{4,3,0,2,1:T(8,128)(2,1)S(1)}, bf16[8,2,2,16,256]{4,3,0,2,1:T(8,128)(2,1)S(1)}, u32[]{:S(2)}, u32[]{:S(2)}) %collective-permute-start.2) | collective-permute-done | bytes 262176 | tf_op jit(solution)/shard_map/ppermute | solution.py:55
  23.4 0.7 constant_dynamic-update-slice_fusion.2
  24.0 0.8 %constant_dynamic-update-slice_fusion.1 = bf16[32,2,2,16,256]{4,3,0,2,1:T(8,128)(2,1)} fusion(bf16[32,2,2,16,256]{4,3,0,2,1:T(8,128)(2,1)} %constant_dynamic-update-slice_fusion.2, bf16[8,2,2,16,256]{4,3,0,2,1:T(8,128)(2,1)S(1)} %collective-permute-done.2), kind=kLoop, calls=%fused_computation.82 | loop fusion | bytes 524288
  24.8 0.8 %constant_dynamic-update-slice_fusion = bf16[32,2,2,16,256]{4,3,0,2,1:T(8,128)(2,1)} fusion(bf16[32,2,2,16,256]{4,3,0,2,1:T(8,128)(2,1)} %constant_dynamic-update-slice_fusion.1, bf16[16,2,2,16,256]{4,3,0,2,1:T(8,128)(2,1)S(1)} %collective-permute-done.3), kind=kLoop, calls=%fused_computation.81 | loop fusion | bytes 1048576 | tf_op jit(solution)/shard_map/concatenate | solution.py:55
  25.6 1.3 %fusion.66 = (bf16[32,1,2,16,256]{4,3,0,2,1:T(8,128)(2,1)S(1)}, bf16[32,1,2,16,256]{4,3,0,2,1:T(8,128)(2,1)S(1)}) fusion(bf16[32,2,2,16,256]{4,3,0,2,1:T(8,128)(2,1)} %constant_dynamic-update-slice_fusion), kind=kLoop, calls=%fused_computation.117 | loop fusion | bytes 2097152 | tf_op jit(solution)/shard_map/slice | solution.py:57
  28.8 0.7 %multiply_reduce_fusion = (f32[2]{0:T(128)S(1)}, bf16[2,2,256,256]{3,2,1,0:T(8,128)(2,1)S(1)}) fusion(bf16[2,256,256]{2,1,0:T(8,128)(2,1)S(1)} %copy-done, f32[2,2,256,256]{3,2,0,1:T(8,128)S(1)} %fusion.40), kind=kOutput, calls=%fused_computation.29 | convolution fusion | flops 269746176 | bytes 1835016 | tf_op jit(solution)/shard_map/ktac,tdc->ktad/dot_general | solution.py:69
  33.0 1.6 %stack.21 = f32[2,2,2,2,2,1,8192]{6,4,3,2,1,0,5:T(2,128)} reshape(f32[32,8192]{1,0:T(8,128)S(1)} %convolution_add_fusion.2) | data formatting | bytes 2097152 | tf_op jit(solution)/shard_map/stack | solution.py:86
  34.6 2.6 %pad_maximum_fusion = f32[2,2,2,2,2,2,8192]{6,4,3,2,1,0,5:T(2,128)S(1)} fusion(f32[2,2,2,2,2,1,8192]{6,4,3,2,1,0,5:T(2,128)S(1)} %stack.22, f32[2,2,2,2,2,1,8192]{6,4,3,2,1,0,5:T(2,128)} %stack.21), kind=kLoop, calls=%fused_computation.10 | loop fusion | flops 524288 | bytes 4194304 | tf_op jit(solution)/shard_map/stack | solution.py:86
  38.1 1.5 %collective-permute-done.4 = bf16[2,2,2,2,2,8192]{5,3,4,0,1,2:T(2,128)(2,1)S(1)} collective-permute-done((bf16[2,2,2,2,2,8192]{5,3,4,0,1,2:T(2,128)(2,1)S(1)}, bf16[2,2,2,2,2,8192]{5,3,4,0,1,2:T(2,128)(2,1)S(1)}, u32[]{:S(2)}, u32[]{:S(2)}) %collective-permute-start.4) | collective-permute-done | bytes 524320 | tf_op jit(solution)/shard_map/ppermute | solution.py:95
  40.5 1.8 %collective-permute-start.5 = (bf16[2,2,2,2,8192]{4,2,3,0,1:T(2,128)(2,1)S(1)}, bf16[2,2,2,2,8192]{4,2,3,0,1:T(2,128)(2,1)S(1)}, u32[]{:S(2)}, u32[]{:S(2)}) collective-permute-start(bf16[2,2,2,2,8192]{4,2,3,0,1:T(2,128)(2,1)S(1)} %fusion.21), channel_id=1, source_target_pairs={{0,2},{1,3},{2,0},{3,1},{4,6},{5,7},{6,4},{7,5},{8,10},{9,11},{10,... | collective-permute-start | bytes 786440 | tf_op jit(solution)/shard_map/ppermute | solution.py:95
  42.3 6.9 %collective-permute-done.5 = bf16[2,2,2,2,8192]{4,2,3,0,1:T(2,128)(2,1)S(1)} collective-permute-done((bf16[2,2,2,2,8192]{4,2,3,0,1:T(2,128)(2,1)S(1)}, bf16[2,2,2,2,8192]{4,2,3,0,1:T(2,128)(2,1)S(1)}, u32[]{:S(2)}, u32[]{:S(2)}) %collective-permute-start.5) | collective-permute-done | bytes 262176 | tf_op jit(solution)/shard_map/ppermute | solution.py:95
  49.5 0.9 %collective-permute-start.6 = (bf16[2,2,2,8192]{3,1,2,0:T(2,128)(2,1)S(1)}, bf16[2,2,2,8192]{3,1,2,0:T(2,128)(2,1)S(1)}, u32[]{:S(2)}, u32[]{:S(2)}) collective-permute-start(bf16[2,2,2,8192]{3,1,2,0:T(2,128)(2,1)S(1)} %fusion.35), channel_id=1, source_target_pairs={{0,4},{1,5},{2,6},{3,7},{4,0},{5,1},{6,2},{7,3},{8,12},{9,13},{10,... | collective-permute-start | bytes 393224 | tf_op jit(solution)/shard_map/ppermute | solution.py:95
  50.4 4.2 %collective-permute-done.6 = bf16[2,2,2,8192]{3,1,2,0:T(2,128)(2,1)S(1)} collective-permute-done((bf16[2,2,2,8192]{3,1,2,0:T(2,128)(2,1)S(1)}, bf16[2,2,2,8192]{3,1,2,0:T(2,128)(2,1)S(1)}, u32[]{:S(2)}, u32[]{:S(2)}) %collective-permute-start.6) | collective-permute-done | bytes 131104 | tf_op jit(solution)/shard_map/ppermute | solution.py:95
  54.8 3.3 %collective-permute-start.7 = (bf16[2,2,8192]{2,0,1:T(2,128)(2,1)S(1)}, bf16[2,2,8192]{2,0,1:T(2,128)(2,1)S(1)}, u32[]{:S(2)}, u32[]{:S(2)}) collective-permute-start(bf16[2,2,8192]{2,0,1:T(2,128)(2,1)S(1)} %fusion.37), channel_id=1, source_target_pairs={{0,8},{1,9},{2,10},{3,11},{4,12},{5,13},{6,14},{7,15},{8,0},{9,1},... | collective-permute-start | bytes 196616 | tf_op jit(solution)/shard_map/ppermute | solution.py:95
  58.1 2.2 %collective-permute-done.7 = bf16[2,2,8192]{2,0,1:T(2,128)(2,1)S(1)} collective-permute-done((bf16[2,2,8192]{2,0,1:T(2,128)(2,1)S(1)}, bf16[2,2,8192]{2,0,1:T(2,128)(2,1)S(1)}, u32[]{:S(2)}, u32[]{:S(2)}) %collective-permute-start.7) | collective-permute-done | bytes 65568 | tf_op jit(solution)/shard_map/ppermute | solution.py:95
  60.5 0.7 %fusion.9 = f32[2,256,256]{2,1,0:T(8,128)S(1)} fusion(bf16[2,256,256]{2,1,0:T(8,128)(2,1)S(1)} %copy-done.1, bf16[2,256,256]{2,1,0:T(8,128)(2,1)S(1)} %copy-done.2, f32[2,2,256,256]{3,2,0,1:T(8,128)S(1)} %fusion.38), kind=kOutput, calls=%fused_computation.25 | convolution fusion | flops 269090816 | bytes 2097152 | tf_op jit(solution)/shard_map/ktil,tlj->kij/dot_general | solution.py:106
  61.7 1.5 %collective-permute-start.8 = (bf16[65542]{0:T(1024)(128)(2,1)S(1)}, bf16[65542]{0:T(1024)(128)(2,1)S(1)}, u32[]{:S(2)}, u32[]{:S(2)}) collective-permute-start(bf16[65542]{0:T(1024)(128)(2,1)S(1)} %concatenate.31), channel_id=1, source_target_pairs={{0,16},{16,0},{1,17},{17,1},{2,18},{18,2},{3,19},{19,3},{4,20},{20... | collective-permute-start | bytes 393260 | tf_op jit(solution)/shard_map/ppermute | solution.py:125
  63.2 3.5 %collective-permute-done.8 = bf16[65542]{0:T(1024)(128)(2,1)S(1)} collective-permute-done((bf16[65542]{0:T(1024)(128)(2,1)S(1)}, bf16[65542]{0:T(1024)(128)(2,1)S(1)}, u32[]{:S(2)}, u32[]{:S(2)}) %collective-permute-start.8) | collective-permute-done | bytes 131116 | tf_op jit(solution)/shard_map/ppermute | solution.py:125
  67.4 0.7 %dynamic-slice_add_fusion = f32[2,128,256]{2,1,0:T(8,128)} fusion(f32[2,128,256]{2,1,0:T(8,128)S(1)} %reshape.213, f32[2,256,256]{2,1,0:T(8,128)S(1)} %fusion.9, s32[]{:T(128)S(6)} %select_n.23), kind=kLoop, calls=%fused_computation.53 | loop fusion | flops 65536 | bytes 786436 | tf_op jit(solution)/shard_map/add | solution.py:126
  (78 shorter events, 11.2 us)
Async XLA Ops:
  0.6 28.1 %copy-start = (bf16[2,256,256]{2,1,0:T(8,128)(2,1)S(1)}, bf16[2,256,256]{2,1,0:T(8,128)(2,1)}, u32[]{:S(2)}) copy-start(bf16[2,256,256]{2,1,0:T(8,128)(2,1)} %param.21) | copy-start | bytes 786436
  0.6 17.1 %copy-start.3 = (s32[2,2,8]{2,1,0:T(2,128)S(1)}, s32[2,2,8]{2,1,0:T(2,128)}, u32[]{:S(2)}) copy-start(s32[2,2,8]{2,1,0:T(2,128)} %param.22) | copy-start | bytes 388
  0.7 17.3 %copy-start.4 = (s32[2,16]{1,0:T(2,128)S(1)}, s32[2,16]{1,0:T(2,128)}, u32[]{:S(2)}) copy-start(s32[2,16]{1,0:T(2,128)} %param.23) | copy-start | bytes 388
  0.7 21.9 %copy-start.5 = (s32[2,16]{1,0:T(2,128)S(1)}, s32[2,16]{1,0:T(2,128)}, u32[]{:S(2)}) copy-start(s32[2,16]{1,0:T(2,128)} %param.24) | copy-start | bytes 388
  0.7 21.9 %copy-start.6 = (f32[2,16]{1,0:T(2,128)S(1)}, f32[2,16]{1,0:T(2,128)}, u32[]{:S(2)}) copy-start(f32[2,16]{1,0:T(2,128)} %param.25) | copy-start | bytes 388
  3.2 7.7 %collective-permute-start = (bf16[2,2,2,16,256]{4,3,0,2,1:T(8,128)(2,1)S(1)}, bf16[2,2,2,16,256]{4,3,0,2,1:T(8,128)(2,1)S(1)}, u32[]{:S(2)}, u32[]{:S(2)}) collective-permute-start(bf16[2,2,2,16,256]{4,3,0,2,1:T(8,128)(2,1)S(1)} %get-tuple-element.64), channel_id=1, source_target_pairs={{0,8},{1,9},{2,10},{3,11},{4,12},{5,13},{6,14},{7,15},{8,0},{9,1},... | collective-permute-start | bytes 196616 | tf_op jit(solution)/shard_map/ppermute | solution.py:55
  10.9 5.0 %collective-permute-start.1 = (bf16[4,2,2,16,256]{4,3,0,2,1:T(8,128)(2,1)S(1)}, bf16[4,2,2,16,256]{4,3,0,2,1:T(8,128)(2,1)S(1)}, u32[]{:S(2)}, u32[]{:S(2)}) collective-permute-start(bf16[4,2,2,16,256]{4,3,0,2,1:T(8,128)(2,1)S(1)} %pad_maximum_fusion.3), channel_id=1, source_target_pairs={{0,4},{1,5},{2,6},{3,7},{4,0},{5,1},{6,2},{7,3},{8,12},{9,13},{10,... | collective-permute-start | bytes 393224 | tf_op jit(solution)/shard_map/ppermute | solution.py:55
  16.0 6.4 %collective-permute-start.2 = (bf16[8,2,2,16,256]{4,3,0,2,1:T(8,128)(2,1)S(1)}, bf16[8,2,2,16,256]{4,3,0,2,1:T(8,128)(2,1)S(1)}, u32[]{:S(2)}, u32[]{:S(2)}) collective-permute-start(bf16[8,2,2,16,256]{4,3,0,2,1:T(8,128)(2,1)S(1)} %pad_maximum_fusion.2), channel_id=1, source_target_pairs={{0,2},{1,3},{2,0},{3,1},{4,6},{5,7},{6,4},{7,5},{8,10},{9,11},{10,... | collective-permute-start | bytes 786440 | tf_op jit(solution)/shard_map/ppermute | solution.py:55
  22.5 2.3 %collective-permute-start.3 = (bf16[16,2,2,16,256]{4,3,0,2,1:T(8,128)(2,1)S(1)}, bf16[16,2,2,16,256]{4,3,0,2,1:T(8,128)(2,1)S(1)}, u32[]{:S(2)}, u32[]{:S(2)}) collective-permute-start(bf16[16,2,2,16,256]{4,3,0,2,1:T(8,128)(2,1)S(1)} %pad_maximum_fusion.1), channel_id=1, source_target_pairs={{0,1},{1,0},{2,3},{3,2},{4,5},{5,4},{6,7},{7,6},{8,9},{9,8},{10,11... | collective-permute-start | bytes 1572872 | tf_op jit(solution)/shard_map/ppermute | solution.py:55
  37.6 2.1 %collective-permute-start.4 = (bf16[2,2,2,2,2,8192]{5,3,4,0,1,2:T(2,128)(2,1)S(1)}, bf16[2,2,2,2,2,8192]{5,3,4,0,1,2:T(2,128)(2,1)S(1)}, u32[]{:S(2)}, u32[]{:S(2)}) collective-permute-start(bf16[2,2,2,2,2,8192]{5,3,4,0,1,2:T(2,128)(2,1)S(1)} %fusion.11), channel_id=1, source_target_pairs={{0,1},{1,0},{2,3},{3,2},{4,5},{5,4},{6,7},{7,6},{8,9},{9,8},{10,11... | collective-permute-start | bytes 1572872 | tf_op jit(solution)/shard_map/ppermute | solution.py:95
  40.3 20.2 %copy-start.1 = (bf16[2,256,256]{2,1,0:T(8,128)(2,1)S(1)}, bf16[2,256,256]{2,1,0:T(8,128)(2,1)}, u32[]{:S(2)}) copy-start(bf16[2,256,256]{2,1,0:T(8,128)(2,1)} %param.19) | copy-start | bytes 786436
  40.3 20.2 %copy-start.2 = (bf16[2,256,256]{2,1,0:T(8,128)(2,1)S(1)}, bf16[2,256,256]{2,1,0:T(8,128)(2,1)}, u32[]{:S(2)}) copy-start(bf16[2,256,256]{2,1,0:T(8,128)(2,1)} %param.20) | copy-start | bytes 786436
  40.5 8.7 %collective-permute-start.5 = (bf16[2,2,2,2,8192]{4,2,3,0,1:T(2,128)(2,1)S(1)}, bf16[2,2,2,2,8192]{4,2,3,0,1:T(2,128)(2,1)S(1)}, u32[]{:S(2)}, u32[]{:S(2)}) collective-permute-start(bf16[2,2,2,2,8192]{4,2,3,0,1:T(2,128)(2,1)S(1)} %fusion.21), channel_id=1, source_target_pairs={{0,2},{1,3},{2,0},{3,1},{4,6},{5,7},{6,4},{7,5},{8,10},{9,11},{10,... | collective-permute-start | bytes 786440 | tf_op jit(solution)/shard_map/ppermute | solution.py:95
  49.5 5.0 %collective-permute-start.6 = (bf16[2,2,2,8192]{3,1,2,0:T(2,128)(2,1)S(1)}, bf16[2,2,2,8192]{3,1,2,0:T(2,128)(2,1)S(1)}, u32[]{:S(2)}, u32[]{:S(2)}) collective-permute-start(bf16[2,2,2,8192]{3,1,2,0:T(2,128)(2,1)S(1)} %fusion.35), channel_id=1, source_target_pairs={{0,4},{1,5},{2,6},{3,7},{4,0},{5,1},{6,2},{7,3},{8,12},{9,13},{10,... | collective-permute-start | bytes 393224 | tf_op jit(solution)/shard_map/ppermute | solution.py:95
  54.8 5.6 %collective-permute-start.7 = (bf16[2,2,8192]{2,0,1:T(2,128)(2,1)S(1)}, bf16[2,2,8192]{2,0,1:T(2,128)(2,1)S(1)}, u32[]{:S(2)}, u32[]{:S(2)}) collective-permute-start(bf16[2,2,8192]{2,0,1:T(2,128)(2,1)S(1)} %fusion.37), channel_id=1, source_target_pairs={{0,8},{1,9},{2,10},{3,11},{4,12},{5,13},{6,14},{7,15},{8,0},{9,1},... | collective-permute-start | bytes 196616 | tf_op jit(solution)/shard_map/ppermute | solution.py:95
  61.7 5.0 %collective-permute-start.8 = (bf16[65542]{0:T(1024)(128)(2,1)S(1)}, bf16[65542]{0:T(1024)(128)(2,1)S(1)}, u32[]{:S(2)}, u32[]{:S(2)}) collective-permute-start(bf16[65542]{0:T(1024)(128)(2,1)S(1)} %concatenate.31), channel_id=1, source_target_pairs={{0,16},{16,0},{1,17},{17,1},{2,18},{18,2},{3,19},{19,3},{4,20},{20... | collective-permute-start | bytes 393260 | tf_op jit(solution)/shard_map/ppermute | solution.py:125

commit v4 on v3

--- a/solution.py
+++ b/solution.py
@@ -1,6 +1,8 @@
 import jax
 import jax.numpy as jnp
 from jax import lax
+from jax.experimental import pallas as pl
+from jax.experimental.pallas import tpu as pltpu
 from jax.sharding import PartitionSpec as P
 
 OVL = 16
@@ -14,6 +16,92 @@
     total = jnp.dot(hi, bands, preferred_element_type=jnp.float32)
     total = total + jnp.dot(mid, bands, preferred_element_type=jnp.float32)
     return total + jnp.dot(low, bands, preferred_element_type=jnp.float32)
+
+
+def middle_kernel(
+    fwd_ref, back_ref, image_ref, proj_ref, edge_ref, ctf_ref,
+    weighted_ref, score_ref, return_ref, residual_ref,
+):
+    k = pl.program_id(1)
+    own_count = pl.num_programs(1)
+    total = edge_ref.shape[0]
+    pixels = image_ref.shape[-1]
+
+    def band_sum(q, carry):
+        lower, upper = carry
+        lower = lower + fwd_ref[k * total + q] * edge_ref[q, 0, 0].astype(jnp.float32)
+        upper = upper + fwd_ref[(own_count + k) * total + q] * edge_ref[q, 1, 0].astype(jnp.float32)
+        return lower, upper
+
+    zero = jnp.zeros((OVL, pixels), jnp.float32)
+    lower, upper = lax.fori_loop(0, total, band_sum, (zero, zero))
+    residual_ref[...] = image_ref[0, 0].astype(jnp.float32) - proj_ref[0, 0].astype(jnp.float32)
+    residual_ref[:OVL] = residual_ref[:OVL] - upper
+    residual_ref[pixels - OVL :] = residual_ref[pixels - OVL :] - lower
+    residual = residual_ref[...].astype(jnp.bfloat16)
+    ctf = ctf_ref[0]
+    smoothed = jnp.dot(ctf, residual, preferred_element_type=jnp.float32).astype(jnp.bfloat16)
+    filtered = lax.dot_general(
+        smoothed, ctf, (((1,), (1,)), ((), ())), preferred_element_type=jnp.float32
+    )
+    score_ref[...] = jnp.full(score_ref.shape, jnp.sum(filtered * filtered), jnp.float32)
+    reverse = lax.dot_general(
+        ctf, filtered.astype(jnp.bfloat16), (((0,), (0,)), ((), ())),
+        preferred_element_type=jnp.float32,
+    ).astype(jnp.bfloat16)
+    weighted = jnp.dot(reverse, ctf, preferred_element_type=jnp.float32).astype(jnp.bfloat16)
+    weighted_ref[0, 0] = weighted
+
+    @pl.when(k == 0)
+    def _():
+        return_ref[...] = jnp.zeros_like(return_ref)
+
+    bottom_rows = weighted[pixels - OVL :].astype(jnp.float32)
+    top_rows = weighted[:OVL].astype(jnp.float32)
+
+    def give_back(q, carry):
+        return_ref[q, 0, 0] = return_ref[q, 0, 0] + back_ref[k * total + q] * bottom_rows
+        return_ref[q, 1, 0] = return_ref[q, 1, 0] + back_ref[(own_count + k) * total + q] * top_rows
+        return carry
+
+    lax.fori_loop(0, total, give_back, 0)
+
+
+def middle(fwd, back, images, projected, edges_all, ctf_filter):
+    own_count, tilt_count, pixels, _ = images.shape
+    total = edges_all.shape[0]
+    tile = pl.BlockSpec((1, 1, pixels, pixels), lambda t, k: (k, t, 0, 0))
+    bands = pl.BlockSpec((total, 2, 1, OVL, pixels), lambda t, k: (0, 0, t, 0, 0))
+    smem = pl.BlockSpec(memory_space=pltpu.SMEM)
+    flops = own_count * tilt_count * (8 * pixels**3 + 8 * total * OVL * pixels)
+    moved = 2 * images.size * 3 + 2 * edges_all.size + 4 * edges_all.size + 2 * ctf_filter.size
+    return pl.pallas_call(
+        middle_kernel,
+        grid=(tilt_count, own_count),
+        in_specs=[
+            smem,
+            smem,
+            tile,
+            tile,
+            bands,
+            pl.BlockSpec((1, pixels, pixels), lambda t, k: (t, 0, 0)),
+        ],
+        out_specs=[
+            tile,
+            pl.BlockSpec((1, 1, 8, 128), lambda t, k: (t, k, 0, 0)),
+            bands,
+        ],
+        out_shape=[
+            jax.ShapeDtypeStruct(images.shape, jnp.bfloat16),
+            jax.ShapeDtypeStruct((tilt_count, own_count, 8, 128), jnp.float32),
+            jax.ShapeDtypeStruct(edges_all.shape, jnp.float32),
+        ],
+        scratch_shapes=[pltpu.VMEM((pixels, pixels), jnp.float32)],
+        compiler_params=pltpu.CompilerParams(
+            dimension_semantics=("arbitrary", "arbitrary")
+        ),
+        cost_estimate=pl.CostEstimate(flops=flops, transcendentals=0, bytes_accessed=moved),
+    )(fwd.reshape(-1), back.reshape(-1), images, projected, edges_all, ctf_filter)
 
 
 def on_device(
@@ -54,38 +142,13 @@
         pairs = [(i, i ^ stride) for i in range(peer_count)]
         edges_all = jnp.concatenate((edges_all, lax.ppermute(edges_all, "dom", pairs)), axis=0)
 
-    lower_part = split_dot(fwd[0], edges_all[:, 0].reshape(total, band_size))
-    upper_part = split_dot(fwd[1], edges_all[:, 1].reshape(total, band_size))
-    lower_part = lower_part.reshape(own_count, tilt_count, OVL, pixels)
-    upper_part = upper_part.reshape(own_count, tilt_count, OVL, pixels)
-
-    residual = images.astype(jnp.float32) - projected.astype(jnp.float32)
-    residual = residual.at[:, :, :OVL].add(-upper_part)
-    residual = residual.at[:, :, pixels - OVL :].add(-lower_part)
-    residual_portion = residual.astype(jnp.bfloat16)
-    smoothed_images = jnp.einsum(
-        "tab,ktbc->ktac", ctf_filter, residual_portion, preferred_element_type=jnp.float32
-    ).astype(jnp.bfloat16)
-    filtered_images = jnp.einsum(
-        "ktac,tdc->ktad", smoothed_images, ctf_filter, preferred_element_type=jnp.float32
-    )
-    score_part = jnp.sum(filtered_images * filtered_images, axis=(1, 2, 3))
+    weighted, score_tiles, returned = middle(
+        jnp.stack(fwd), jnp.stack(back), images, projected, edges_all, ctf_filter
+    )
+    score_part = jnp.sum(score_tiles[:, :, 0, 0], axis=0)
     tilt_groups = lax.axis_size("tilt")
-    filtered_portion = filtered_images.astype(jnp.bfloat16)
-    reverse_pass = jnp.einsum(
-        "tab,ktac->ktbc", ctf_filter, filtered_portion, preferred_element_type=jnp.float32
-    ).astype(jnp.bfloat16)
-    weighted = jnp.einsum(
-        "ktbc,tcd->ktbd", reverse_pass, ctf_filter, preferred_element_type=jnp.float32
-    ).astype(jnp.bfloat16)
-
-    bottom_rows = weighted[:, :, pixels - OVL :].reshape(own_count, band_size)
-    top_rows = weighted[:, :, :OVL].reshape(own_count, band_size)
-    to_top = split_dot(back[0].T, bottom_rows)
-    to_bottom = split_dot(back[1].T, top_rows)
-    returned = jnp.stack((to_top, to_bottom), axis=1).reshape(
-        (2,) * steps + (own_count, 2, band_size)
-    )
+
+    returned = returned.reshape((2,) * steps + (own_count, 2, band_size))
     for b in range(steps):
         stride = 1 << b
         pairs = [(i, i ^ stride) for i in range(peer_count)]

time: 68.4 us -> 68.2 us (level)
  Pallas kernels: 0 us -> 7.88 us
  matrix products: 7.12 us -> 3.06 us
  other arithmetic: 5.98 us -> 3.64 us
  local copies, waits for them, and re-layouts: 8.6 us -> 7.7 us
    pallas_call x0 -> x1, Pallas kernels: none -> 7.88 us  [middle(): pl.pallas_call(middle_kernel, grid=(tilt_count, own_count), in_specs=[sme...]
    reshape x0 -> x3, local copies, waits for them, and re-layouts: none -> 3.83 us  [the longest x1 2.63 us: on_device(): returned = returned.reshape((2,) * steps + (own_count, 2, band_size))]
    dot_general x14 -> x1, matrix products: 4.52 us -> 1.28 us  [on_device(): jnp.einsum('kij,tlj->ktil', sections, slice_cols, preferred_element_type=...]
    another operation x4 -> x0, local copies, waits for them, and re-layouts: 2.71 us -> none  [the longest x2 2.22 us: on_device(): jnp.stack((to_top, to_bottom), axis=1)]
    another operation x1 -> x2, other arithmetic: 2.59 us -> 0.01 us  [the longest x1 0.01 us: on_device(): jnp.stack(back)]
    slice x6 -> x0, local copies, waits for them, and re-layouts: 1.4 us -> none  [the longest x2 1.33 us: on_device(): lower_part = split_dot(fwd[0], edges_all[:, 0].reshape(total, band_size))]
    ppermute x4, waiting for transfers between devices: 14.8 us -> 14 us  [on_device(): returned = kept + lax.ppermute(given, 'dom', pairs).astype(jnp.float32)]
    reduce_sum x0 -> x1, other arithmetic: none -> 0.82 us  [on_device(): score_part = jnp.sum(score_tiles[:, :, 0, 0], axis=0)]
  transfers between devices with their start and end apart: 9 -> 9, of which waited for: 8 -> 9; matrix products, arithmetic and copies ran while one was open for 3% -> 4% of each run, Pallas kernels for 0% -> 0%
where the time goes in v4:
time: 68.2 us; the launch traced here: 67.9 us
  waiting for transfers between devices  30.5 us (45%)
  starting transfers between devices  14.2 us (21%)
  Pallas kernels  7.88 us (12%)
  local copies, waits for them, and re-layouts  7.7 us (11%)
  other arithmetic  3.64 us (5%)
  matrix products  3.06 us (4%)
  between operations  0.96 us (1%)
    ppermute x4, waiting for transfers between devices, on_device(): returned = kept + lax.ppermute(given, 'dom', pairs).astype(jnp.float32)  14 us
    ppermute x4, waiting for transfers between devices, on_device(): lax.ppermute(edges_all, 'dom', pairs)  13.1 us
    pallas_call x1, Pallas kernels, middle(): pl.pallas_call(middle_kernel, grid=(tilt_count, own_count), in_specs=[sme...  7.88 us
    ppermute x4, starting transfers between devices, on_device(): lax.ppermute(edges_all, 'dom', pairs)  6.56 us
    ppermute x4, starting transfers between devices, on_device(): returned = kept + lax.ppermute(given, 'dom', pairs).astype(jnp.float32)  6.06 us
    ppermute x1, waiting for transfers between devices, on_device(): parcel = lax.ppermute(parcel, 'tilt', [(0, 1), (1, 0)]).astype(jnp.float32)  3.45 us
    reshape x1, local copies, waits for them, and re-layouts, on_device(): returned = returned.reshape((2,) * steps + (own_count, 2, band_size))  2.63 us
    unnamed x24, local copies, waits for them, and re-layouts  2.09 us
  transfers between devices with their start and end apart: 9, of which 9 were waited for; matrix products, arithmetic and copies ran while one was open for 4% of the time, Pallas kernels for 0%

profile of v4, /device:TPU:0, one launch (start us, length us, event | category | flops | bytes accessed | tf_op | source)
XLA Modules:
  0.0 67.9 jit_solution(7623098266535166266)
XLA Ops:
  0.7 0.9 %copy-done = bf16[2,256,256]{2,1,0:T(8,128)(2,1)S(1)} copy-done((bf16[2,256,256]{2,1,0:T(8,128)(2,1)S(1)}, bf16[2,256,256]{2,1,0:T(8,128)(2,1)}, u32[]{:S(2)}) %copy-start) | copy-done | bytes 262168
  1.6 1.3 %fusion = bf16[2,2,256,256]{3,2,0,1:T(8,128)(2,1)S(1)} fusion(bf16[2,256,256]{2,1,0:T(8,128)(2,1)S(1)} %copy-done, bf16[2,256,256]{2,1,0:T(8,128)(2,1)} %param.13), kind=kOutput, calls=%fused_computation.3 | convolution fusion | flops 134479872 | bytes 1048576 | tf_op jit(solution)/shard_map/kij,tlj->ktil/dot_general | solution.py:132
  2.9 1.3 %fusion.2.proj_ref = bf16[2,2,256,256]{3,2,1,0:T(8,128)(2,1)S(1)} fusion(bf16[2,2,256,256]{3,2,0,1:T(8,128)(2,1)S(1)} %fusion, bf16[2,256,256]{2,1,0:T(8,128)(2,1)} %param.15), kind=kOutput, calls=%fused_computation.5 | convolution fusion | flops 134479872 | bytes 1310720 | tf_op jit(solution)/shard_map/tai,ktil->ktal/dot_general | solution.py:135
  4.2 4.1 %collective-permute-start = (bf16[2,2,2,16,256]{4,3,2,1,0:T(8,128)(2,1)S(1)}, bf16[2,2,2,16,256]{4,3,2,1,0:T(8,128)(2,1)S(1)}, u32[]{:S(2)}, u32[]{:S(2)}) collective-permute-start(bf16[2,2,2,16,256]{4,3,2,1,0:T(8,128)(2,1)S(1)} %get-tuple-element.42), channel_id=1, source_target_pairs={{0,8},{1,9},{2,10},{3,11},{4,12},{5,13},{6,14},{7,15},{8,0},{9,1},... | collective-permute-start | bytes 196616 | tf_op jit(solution)/shard_map/ppermute | solution.py:143
  8.5 3.5 %collective-permute-done = bf16[2,2,2,16,256]{4,3,2,1,0:T(8,128)(2,1)S(1)} collective-permute-done((bf16[2,2,2,16,256]{4,3,2,1,0:T(8,128)(2,1)S(1)}, bf16[2,2,2,16,256]{4,3,2,1,0:T(8,128)(2,1)S(1)}, u32[]{:S(2)}, u32[]{:S(2)}) %collective-permute-start) | collective-permute-done | bytes 65568 | tf_op jit(solution)/shard_map/ppermute | solution.py:143
  11.9 0.6 collective-permute-start.1
  12.6 4.4 %collective-permute-done.1 = bf16[4,2,2,16,256]{4,3,2,1,0:T(8,128)(2,1)S(1)} collective-permute-done((bf16[4,2,2,16,256]{4,3,2,1,0:T(8,128)(2,1)S(1)}, bf16[4,2,2,16,256]{4,3,2,1,0:T(8,128)(2,1)S(1)}, u32[]{:S(2)}, u32[]{:S(2)}) %collective-permute-start.1) | collective-permute-done | bytes 131104 | tf_op jit(solution)/shard_map/ppermute | solution.py:143
  17.0 1.8 %collective-permute-start.2 = (bf16[8,2,2,16,256]{4,3,2,1,0:T(8,128)(2,1)S(1)}, bf16[8,2,2,16,256]{4,3,2,1,0:T(8,128)(2,1)S(1)}, u32[]{:S(2)}, u32[]{:S(2)}) collective-permute-start(bf16[8,2,2,16,256]{4,3,2,1,0:T(8,128)(2,1)S(1)} %pad_maximum_fusion.1), channel_id=1, source_target_pairs={{0,2},{1,3},{2,0},{3,1},{4,6},{5,7},{6,4},{7,5},{8,10},{9,11},{10,... | collective-permute-start | bytes 786440 | tf_op jit(solution)/shard_map/ppermute | solution.py:143
  18.9 4.5 %collective-permute-done.2 = bf16[8,2,2,16,256]{4,3,2,1,0:T(8,128)(2,1)S(1)} collective-permute-done((bf16[8,2,2,16,256]{4,3,2,1,0:T(8,128)(2,1)S(1)}, bf16[8,2,2,16,256]{4,3,2,1,0:T(8,128)(2,1)S(1)}, u32[]{:S(2)}, u32[]{:S(2)}) %collective-permute-start.2) | collective-permute-done | bytes 262176 | tf_op jit(solution)/shard_map/ppermute | solution.py:143
  24.9 0.6 collective-permute-done.3
  25.6 1.0 %copy-done.2 = bf16[32,2,2,16,256]{4,3,2,1,0:T(8,128)(2,1)} copy-done((bf16[32,2,2,16,256]{4,3,2,1,0:T(8,128)(2,1)}, bf16[32,2,2,16,256]{4,3,2,1,0:T(8,128)(2,1)S(1)}, u32[]{:S(2)}) %copy-start.2) | copy-done | bytes 1048600
  26.6 7.9 %shard_map.104 = (bf16[2,2,256,256]{3,2,1,0:T(8,128)(2,1)}, f32[2,2,8,128]{3,2,1,0:T(8,128)}, f32[32,2,2,16,256]{4,3,2,1,0:T(8,128)}) custom-call(f32[128]{0:T(128)} %reshape.137.fwd_ref, f32[128]{0:T(128)} %reshape.138.back_ref, bf16[2,2,256,256]{3,2,1,0:T(8,128)(2,1)} %image_ref.1, bf16[2,2,256,256]{3,2,1,0:T(8,128)(2,1)} %copy-done.1, ...), custom_call_target="tpu_custom_call" | custom-call | flops 541065216 | bytes 4980736 | tf_op jit(solution)/shard_map/pallas_call | solution.py:78
  34.4 2.6 %reshape.139 = f32[2,2,2,2,2,2,8192]{6,5,4,3,2,1,0:T(2,128)S(1)} reshape(f32[32,2,2,16,256]{4,3,2,1,0:T(8,128)} %get-tuple-element.30) | data formatting | bytes 4194304 | tf_op jit(solution)/shard_map/reshape | solution.py:151
  37.7 1.8 %collective-permute-done.4 = bf16[2,2,2,2,2,8192]{5,4,3,2,1,0:T(2,128)(2,1)S(1)} collective-permute-done((bf16[2,2,2,2,2,8192]{5,4,3,2,1,0:T(2,128)(2,1)S(1)}, bf16[2,2,2,2,2,8192]{5,4,3,2,1,0:T(2,128)(2,1)S(1)}, u32[]{:S(2)}, u32[]{:S(2)}) %collective-permute-start.4) | collective-permute-done | bytes 524320 | tf_op jit(solution)/shard_map/ppermute | solution.py:158
  40.3 1.8 %collective-permute-start.5 = (bf16[2,2,2,2,8192]{4,3,2,1,0:T(2,128)(2,1)S(1)}, bf16[2,2,2,2,8192]{4,3,2,1,0:T(2,128)(2,1)S(1)}, u32[]{:S(2)}, u32[]{:S(2)}) collective-permute-start(bf16[2,2,2,2,8192]{4,3,2,1,0:T(2,128)(2,1)S(1)} %fusion.10), channel_id=1, source_target_pairs={{0,2},{1,3},{2,0},{3,1},{4,6},{5,7},{6,4},{7,5},{8,10},{9,11},{10,... | collective-permute-start | bytes 786440 | tf_op jit(solution)/shard_map/ppermute | solution.py:158
  42.1 6.7 %collective-permute-done.5 = bf16[2,2,2,2,8192]{4,3,2,1,0:T(2,128)(2,1)S(1)} collective-permute-done((bf16[2,2,2,2,8192]{4,3,2,1,0:T(2,128)(2,1)S(1)}, bf16[2,2,2,2,8192]{4,3,2,1,0:T(2,128)(2,1)S(1)}, u32[]{:S(2)}, u32[]{:S(2)}) %collective-permute-start.5) | collective-permute-done | bytes 262176 | tf_op jit(solution)/shard_map/ppermute | solution.py:158
  49.1 0.8 %collective-permute-start.6 = (bf16[2,2,2,8192]{3,2,1,0:T(2,128)(2,1)S(1)}, bf16[2,2,2,8192]{3,2,1,0:T(2,128)(2,1)S(1)}, u32[]{:S(2)}, u32[]{:S(2)}) collective-permute-start(bf16[2,2,2,8192]{3,2,1,0:T(2,128)(2,1)S(1)} %fusion.18), channel_id=1, source_target_pairs={{0,4},{1,5},{2,6},{3,7},{4,0},{5,1},{6,2},{7,3},{8,12},{9,13},{10,... | collective-permute-start | bytes 393224 | tf_op jit(solution)/shard_map/ppermute | solution.py:158
  49.9 0.8 %slice_reduce_fusion.2 = f32[2]{0:T(128)S(1)} fusion(f32[2,2,8,128]{3,2,1,0:T(8,128)} %get-tuple-element.31), kind=kLoop, calls=%fused_computation.63 | loop fusion | flops 2 | bytes 24 | tf_op jit(solution)/shard_map/reduce_sum | solution.py:148
  50.8 3.4 %collective-permute-done.6 = bf16[2,2,2,8192]{3,2,1,0:T(2,128)(2,1)S(1)} collective-permute-done((bf16[2,2,2,8192]{3,2,1,0:T(2,128)(2,1)S(1)}, bf16[2,2,2,8192]{3,2,1,0:T(2,128)(2,1)S(1)}, u32[]{:S(2)}, u32[]{:S(2)}) %collective-permute-start.6) | collective-permute-done | bytes 131104 | tf_op jit(solution)/shard_map/ppermute | solution.py:158
  54.3 3.3 %collective-permute-start.7 = (bf16[2,2,8192]{2,1,0:T(2,128)(2,1)S(1)}, bf16[2,2,8192]{2,1,0:T(2,128)(2,1)S(1)}, u32[]{:S(2)}, u32[]{:S(2)}) collective-permute-start(bf16[2,2,8192]{2,1,0:T(2,128)(2,1)S(1)} %fusion.20), channel_id=1, source_target_pairs={{0,8},{1,9},{2,10},{3,11},{4,12},{5,13},{6,14},{7,15},{8,0},{9,1},... | collective-permute-start | bytes 196616 | tf_op jit(solution)/shard_map/ppermute | solution.py:158
  57.7 2.1 %collective-permute-done.7 = bf16[2,2,8192]{2,1,0:T(2,128)(2,1)S(1)} collective-permute-done((bf16[2,2,8192]{2,1,0:T(2,128)(2,1)S(1)}, bf16[2,2,8192]{2,1,0:T(2,128)(2,1)S(1)}, u32[]{:S(2)}, u32[]{:S(2)}) %collective-permute-start.7) | collective-permute-done | bytes 65568 | tf_op jit(solution)/shard_map/ppermute | solution.py:158
  61.4 1.5 %collective-permute-start.8 = (bf16[65542]{0:T(1024)(128)(2,1)S(1)}, bf16[65542]{0:T(1024)(128)(2,1)S(1)}, u32[]{:S(2)}, u32[]{:S(2)}) collective-permute-start(bf16[65542]{0:T(1024)(128)(2,1)S(1)} %concatenate.26), channel_id=1, source_target_pairs={{0,16},{16,0},{1,17},{17,1},{2,18},{18,2},{3,19},{19,3},{4,20},{20... | collective-permute-start | bytes 393260 | tf_op jit(solution)/shard_map/ppermute | solution.py:188
  62.9 3.5 %collective-permute-done.8 = bf16[65542]{0:T(1024)(128)(2,1)S(1)} collective-permute-done((bf16[65542]{0:T(1024)(128)(2,1)S(1)}, bf16[65542]{0:T(1024)(128)(2,1)S(1)}, u32[]{:S(2)}, u32[]{:S(2)}) %collective-permute-start.8) | collective-permute-done | bytes 131116 | tf_op jit(solution)/shard_map/ppermute | solution.py:188
  67.1 0.7 %dynamic-slice_add_fusion = f32[2,128,256]{2,1,0:T(8,128)} fusion(f32[2,128,256]{2,1,0:T(8,128)S(1)} %reshape.142, f32[2,256,256]{2,1,0:T(8,128)S(1)} %fusion.3, s32[]{:T(128)S(6)} %select_n.23), kind=kLoop, calls=%fused_computation.29 | loop fusion | flops 65536 | bytes 786436 | tf_op jit(solution)/shard_map/add | solution.py:189
  (60 shorter events, 6.1 us)
Async XLA Ops:
  0.6 1.0 %copy-start = (bf16[2,256,256]{2,1,0:T(8,128)(2,1)S(1)}, bf16[2,256,256]{2,1,0:T(8,128)(2,1)}, u32[]{:S(2)}) copy-start(bf16[2,256,256]{2,1,0:T(8,128)(2,1)} %param.16) | copy-start | bytes 786436
  0.6 7.6 %copy-start.5 = (s32[2,2,8]{2,1,0:T(2,128)S(1)}, s32[2,2,8]{2,1,0:T(2,128)}, u32[]{:S(2)}) copy-start(s32[2,2,8]{2,1,0:T(2,128)} %param.18) | copy-start | bytes 388
  0.7 11.9 %copy-start.6 = (s32[2,16]{1,0:T(2,128)S(1)}, s32[2,16]{1,0:T(2,128)}, u32[]{:S(2)}) copy-start(s32[2,16]{1,0:T(2,128)} %param.19) | copy-start | bytes 388
  0.7 18.1 %copy-start.7 = (s32[2,16]{1,0:T(2,128)S(1)}, s32[2,16]{1,0:T(2,128)}, u32[]{:S(2)}) copy-start(s32[2,16]{1,0:T(2,128)} %param.20) | copy-start | bytes 388
  0.7 18.1 %copy-start.8 = (f32[2,16]{1,0:T(2,128)S(1)}, f32[2,16]{1,0:T(2,128)}, u32[]{:S(2)}) copy-start(f32[2,16]{1,0:T(2,128)} %param.21) | copy-start | bytes 388
  4.1 21.4 %copy-start.1 = (bf16[2,2,256,256]{3,2,1,0:T(8,128)(2,1)}, bf16[2,2,256,256]{3,2,1,0:T(8,128)(2,1)S(1)}, u32[]{:S(2)}) copy-start(bf16[2,2,256,256]{3,2,1,0:T(8,128)(2,1)S(1)} %fusion.2.proj_ref) | copy-start | bytes 1572868
  4.2 7.8 %collective-permute-start = (bf16[2,2,2,16,256]{4,3,2,1,0:T(8,128)(2,1)S(1)}, bf16[2,2,2,16,256]{4,3,2,1,0:T(8,128)(2,1)S(1)}, u32[]{:S(2)}, u32[]{:S(2)}) collective-permute-start(bf16[2,2,2,16,256]{4,3,2,1,0:T(8,128)(2,1)S(1)} %get-tuple-element.42), channel_id=1, source_target_pairs={{0,8},{1,9},{2,10},{3,11},{4,12},{5,13},{6,14},{7,15},{8,0},{9,1},... | collective-permute-start | bytes 196616 | tf_op jit(solution)/shard_map/ppermute | solution.py:143
  11.9 5.0 %collective-permute-start.1 = (bf16[4,2,2,16,256]{4,3,2,1,0:T(8,128)(2,1)S(1)}, bf16[4,2,2,16,256]{4,3,2,1,0:T(8,128)(2,1)S(1)}, u32[]{:S(2)}, u32[]{:S(2)}) collective-permute-start(bf16[4,2,2,16,256]{4,3,2,1,0:T(8,128)(2,1)S(1)} %pad_maximum_fusion.2), channel_id=1, source_target_pairs={{0,4},{1,5},{2,6},{3,7},{4,0},{5,1},{6,2},{7,3},{8,12},{9,13},{10,... | collective-permute-start | bytes 393224 | tf_op jit(solution)/shard_map/ppermute | solution.py:143
  17.0 6.4 %collective-permute-start.2 = (bf16[8,2,2,16,256]{4,3,2,1,0:T(8,128)(2,1)S(1)}, bf16[8,2,2,16,256]{4,3,2,1,0:T(8,128)(2,1)S(1)}, u32[]{:S(2)}, u32[]{:S(2)}) collective-permute-start(bf16[8,2,2,16,256]{4,3,2,1,0:T(8,128)(2,1)S(1)} %pad_maximum_fusion.1), channel_id=1, source_target_pairs={{0,2},{1,3},{2,0},{3,1},{4,6},{5,7},{6,4},{7,5},{8,10},{9,11},{10,... | collective-permute-start | bytes 786440 | tf_op jit(solution)/shard_map/ppermute | solution.py:143
  23.5 2.0 %collective-permute-start.3 = (bf16[16,2,2,16,256]{4,3,2,1,0:T(8,128)(2,1)S(1)}, bf16[16,2,2,16,256]{4,3,2,1,0:T(8,128)(2,1)S(1)}, u32[]{:S(2)}, u32[]{:S(2)}) collective-permute-start(bf16[16,2,2,16,256]{4,3,2,1,0:T(8,128)(2,1)S(1)} %pad_maximum_fusion), channel_id=1, source_target_pairs={{0,1},{1,0},{2,3},{3,2},{4,5},{5,4},{6,7},{7,6},{8,9},{9,8},{10,11... | collective-permute-start | bytes 1572872 | tf_op jit(solution)/shard_map/ppermute | solution.py:143
  25.5 1.0 %copy-start.2 = (bf16[32,2,2,16,256]{4,3,2,1,0:T(8,128)(2,1)}, bf16[32,2,2,16,256]{4,3,2,1,0:T(8,128)(2,1)S(1)}, u32[]{:S(2)}) copy-start(bf16[32,2,2,16,256]{4,3,2,1,0:T(8,128)(2,1)S(1)} %constant_dynamic-update-slice_fusion.edge_ref) | copy-start | bytes 3145732
  37.5 2.0 %collective-permute-start.4 = (bf16[2,2,2,2,2,8192]{5,4,3,2,1,0:T(2,128)(2,1)S(1)}, bf16[2,2,2,2,2,8192]{5,4,3,2,1,0:T(2,128)(2,1)S(1)}, u32[]{:S(2)}, u32[]{:S(2)}) collective-permute-start(bf16[2,2,2,2,2,8192]{5,4,3,2,1,0:T(2,128)(2,1)S(1)} %fusion.5), channel_id=1, source_target_pairs={{0,1},{1,0},{2,3},{3,2},{4,5},{5,4},{6,7},{7,6},{8,9},{9,8},{10,11... | collective-permute-start | bytes 1572872 | tf_op jit(solution)/shard_map/ppermute | solution.py:158
  40.1 17.5 %copy-start.4 = (bf16[2,2,256,256]{3,2,1,0:T(8,128)(2,1)S(1)}, bf16[2,2,256,256]{3,2,1,0:T(8,128)(2,1)}, u32[]{:S(2)}) copy-start(bf16[2,2,256,256]{3,2,1,0:T(8,128)(2,1)} %get-tuple-element.29) | copy-start | bytes 1572868
  40.3 8.4 %collective-permute-start.5 = (bf16[2,2,2,2,8192]{4,3,2,1,0:T(2,128)(2,1)S(1)}, bf16[2,2,2,2,8192]{4,3,2,1,0:T(2,128)(2,1)S(1)}, u32[]{:S(2)}, u32[]{:S(2)}) collective-permute-start(bf16[2,2,2,2,8192]{4,3,2,1,0:T(2,128)(2,1)S(1)} %fusion.10), channel_id=1, source_target_pairs={{0,2},{1,3},{2,0},{3,1},{4,6},{5,7},{6,4},{7,5},{8,10},{9,11},{10,... | collective-permute-start | bytes 786440 | tf_op jit(solution)/shard_map/ppermute | solution.py:158
  49.0 11.4 %copy-start.3 = (bf16[2,256,256]{2,1,0:T(8,128)(2,1)S(1)}, bf16[2,256,256]{2,1,0:T(8,128)(2,1)}, u32[]{:S(2)}) copy-start(bf16[2,256,256]{2,1,0:T(8,128)(2,1)} %param.15) | copy-start | bytes 786436
  49.1 5.0 %collective-permute-start.6 = (bf16[2,2,2,8192]{3,2,1,0:T(2,128)(2,1)S(1)}, bf16[2,2,2,8192]{3,2,1,0:T(2,128)(2,1)S(1)}, u32[]{:S(2)}, u32[]{:S(2)}) collective-permute-start(bf16[2,2,2,8192]{3,2,1,0:T(2,128)(2,1)S(1)} %fusion.18), channel_id=1, source_target_pairs={{0,4},{1,5},{2,6},{3,7},{4,0},{5,1},{6,2},{7,3},{8,12},{9,13},{10,... | collective-permute-start | bytes 393224 | tf_op jit(solution)/shard_map/ppermute | solution.py:158
  54.3 5.5 %collective-permute-start.7 = (bf16[2,2,8192]{2,1,0:T(2,128)(2,1)S(1)}, bf16[2,2,8192]{2,1,0:T(2,128)(2,1)S(1)}, u32[]{:S(2)}, u32[]{:S(2)}) collective-permute-start(bf16[2,2,8192]{2,1,0:T(2,128)(2,1)S(1)} %fusion.20), channel_id=1, source_target_pairs={{0,8},{1,9},{2,10},{3,11},{4,12},{5,13},{6,14},{7,15},{8,0},{9,1},... | collective-permute-start | bytes 196616 | tf_op jit(solution)/shard_map/ppermute | solution.py:158
  61.4 5.0 %collective-permute-start.8 = (bf16[65542]{0:T(1024)(128)(2,1)S(1)}, bf16[65542]{0:T(1024)(128)(2,1)S(1)}, u32[]{:S(2)}, u32[]{:S(2)}) collective-permute-start(bf16[65542]{0:T(1024)(128)(2,1)S(1)} %concatenate.26), channel_id=1, source_target_pairs={{0,16},{16,0},{1,17},{17,1},{2,18},{18,2},{3,19},{19,3},{4,20},{20... | collective-permute-start | bytes 393260 | tf_op jit(solution)/shard_map/ppermute | solution.py:188

commit v5 on v4

--- a/solution.py
+++ b/solution.py
@@ -23,14 +23,13 @@
     weighted_ref, score_ref, return_ref, residual_ref,
 ):
     k = pl.program_id(1)
-    own_count = pl.num_programs(1)
     total = edge_ref.shape[0]
     pixels = image_ref.shape[-1]
 
     def band_sum(q, carry):
         lower, upper = carry
-        lower = lower + fwd_ref[k * total + q] * edge_ref[q, 0, 0].astype(jnp.float32)
-        upper = upper + fwd_ref[(own_count + k) * total + q] * edge_ref[q, 1, 0].astype(jnp.float32)
+        lower = lower + fwd_ref[0, k, q] * edge_ref[q, 0, 0].astype(jnp.float32)
+        upper = upper + fwd_ref[1, k, q] * edge_ref[q, 1, 0].astype(jnp.float32)
         return lower, upper
 
     zero = jnp.zeros((OVL, pixels), jnp.float32)
@@ -60,8 +59,8 @@
     top_rows = weighted[:OVL].astype(jnp.float32)
 
     def give_back(q, carry):
-        return_ref[q, 0, 0] = return_ref[q, 0, 0] + back_ref[k * total + q] * bottom_rows
-        return_ref[q, 1, 0] = return_ref[q, 1, 0] + back_ref[(own_count + k) * total + q] * top_rows
+        return_ref[q, 0, 0] = return_ref[q, 0, 0] + back_ref[0, k, q] * bottom_rows
+        return_ref[q, 1, 0] = return_ref[q, 1, 0] + back_ref[1, k, q] * top_rows
         return carry
 
     lax.fori_loop(0, total, give_back, 0)
@@ -101,7 +100,7 @@
             dimension_semantics=("arbitrary", "arbitrary")
         ),
         cost_estimate=pl.CostEstimate(flops=flops, transcendentals=0, bytes_accessed=moved),
-    )(fwd.reshape(-1), back.reshape(-1), images, projected, edges_all, ctf_filter)
+    )(fwd, back, images, projected, edges_all, ctf_filter)
 
 
 def on_device(
@@ -148,7 +147,7 @@
     score_part = jnp.sum(score_tiles[:, :, 0, 0], axis=0)
     tilt_groups = lax.axis_size("tilt")
 
-    returned = returned.reshape((2,) * steps + (own_count, 2, band_size))
+    returned = returned.reshape((2,) * steps + (own_count,) + returned.shape[1:])
     for b in range(steps):
         stride = 1 << b
         pairs = [(i, i ^ stride) for i in range(peer_count)]
@@ -156,8 +155,8 @@
         kept = lax.index_in_dim(returned, 0, axis, keepdims=False)
         given = lax.index_in_dim(returned, 1, axis, keepdims=False).astype(jnp.bfloat16)
         returned = kept + lax.ppermute(given, "dom", pairs).astype(jnp.float32)
-    add_top = returned[:, 0].reshape(own_count, tilt_count, OVL, pixels)
-    add_bottom = returned[:, 1].reshape(own_count, tilt_count, OVL, pixels)
+    add_top = returned[:, 0]
+    add_bottom = returned[:, 1]
 
     proj_grad = weighted.astype(jnp.float32)
     proj_grad = proj_grad.at[:, :, :OVL].add(add_top)

time: 68.2 us -> 66.6 us (0.977)
  local copies, waits for them, and re-layouts: 7.7 us -> 4.04 us
  other arithmetic: 3.64 us -> 4.66 us
    reshape x3 -> x0, local copies, waits for them, and re-layouts: 3.83 us -> none  [the longest x1 2.63 us: on_device(): returned = returned.reshape((2,) * steps + (own_count, 2, band_size))]
    unnamed x24 -> x22, local copies, waits for them, and re-layouts: 2.09 us -> 2.04 us
  transfers between devices with their start and end apart: 9 -> 9, of which waited for: 9 -> 9; matrix products, arithmetic and copies ran while one was open for 4% -> 3% of each run, Pallas kernels for 0% -> 0%
where the time goes in v5:
time: 66.6 us; the launch traced here: 66.2 us
  waiting for transfers between devices  31.1 us (47%)
  starting transfers between devices  14.2 us (21%)
  Pallas kernels  8.29 us (12%)
  other arithmetic  4.66 us (7%)
  local copies, waits for them, and re-layouts  4.04 us (6%)
  matrix products  3.06 us (5%)
  between operations  0.93 us (1%)
    ppermute x4, waiting for transfers between devices, on_device(): returned = kept + lax.ppermute(given, 'dom', pairs).astype(jnp.float32)  13.9 us
    ppermute x4, waiting for transfers between devices, on_device(): lax.ppermute(edges_all, 'dom', pairs)  13.6 us
    pallas_call x1, Pallas kernels, middle(): pl.pallas_call(middle_kernel, grid=(tilt_count, own_count), in_specs=[sme...  8.29 us
    ppermute x4, starting transfers between devices, on_device(): lax.ppermute(edges_all, 'dom', pairs)  6.57 us
    ppermute x4, starting transfers between devices, on_device(): returned = kept + lax.ppermute(given, 'dom', pairs).astype(jnp.float32)  6.09 us
    ppermute x1, waiting for transfers between devices, on_device(): parcel = lax.ppermute(parcel, 'tilt', [(0, 1), (1, 0)]).astype(jnp.float32)  3.47 us
    unnamed x22, local copies, waits for them, and re-layouts  2.04 us
    ppermute x1, starting transfers between devices, on_device(): parcel = lax.ppermute(parcel, 'tilt', [(0, 1), (1, 0)]).astype(jnp.float32)  1.52 us
  transfers between devices with their start and end apart: 9, of which 9 were waited for; matrix products, arithmetic and copies ran while one was open for 3% of the time, Pallas kernels for 0%

profile of v5, /device:TPU:0, one launch (start us, length us, event | category | flops | bytes accessed | tf_op | source)
XLA Modules:
  0.0 66.2 jit_solution(12420796239878132697)
XLA Ops:
  0.7 0.9 %copy-done = bf16[2,256,256]{2,1,0:T(8,128)(2,1)S(1)} copy-done((bf16[2,256,256]{2,1,0:T(8,128)(2,1)S(1)}, bf16[2,256,256]{2,1,0:T(8,128)(2,1)}, u32[]{:S(2)}) %copy-start) | copy-done | bytes 262168
  1.6 1.3 %fusion = bf16[2,2,256,256]{3,2,0,1:T(8,128)(2,1)S(1)} fusion(bf16[2,256,256]{2,1,0:T(8,128)(2,1)S(1)} %copy-done, bf16[2,256,256]{2,1,0:T(8,128)(2,1)} %param.13), kind=kOutput, calls=%fused_computation.3 | convolution fusion | flops 134479872 | bytes 1048576 | tf_op jit(solution)/shard_map/kij,tlj->ktil/dot_general | solution.py:131
  2.9 1.3 %fusion.2.proj_ref = bf16[2,2,256,256]{3,2,1,0:T(8,128)(2,1)S(1)} fusion(bf16[2,2,256,256]{3,2,0,1:T(8,128)(2,1)S(1)} %fusion, bf16[2,256,256]{2,1,0:T(8,128)(2,1)} %param.15), kind=kOutput, calls=%fused_computation.5 | convolution fusion | flops 134479872 | bytes 1310720 | tf_op jit(solution)/shard_map/tai,ktil->ktal/dot_general | solution.py:134
  4.2 4.1 %collective-permute-start = (bf16[2,2,2,16,256]{4,3,2,1,0:T(8,128)(2,1)S(1)}, bf16[2,2,2,16,256]{4,3,2,1,0:T(8,128)(2,1)S(1)}, u32[]{:S(2)}, u32[]{:S(2)}) collective-permute-start(bf16[2,2,2,16,256]{4,3,2,1,0:T(8,128)(2,1)S(1)} %get-tuple-element.40), channel_id=1, source_target_pairs={{0,8},{1,9},{2,10},{3,11},{4,12},{5,13},{6,14},{7,15},{8,0},{9,1},... | collective-permute-start | bytes 196616 | tf_op jit(solution)/shard_map/ppermute | solution.py:142
  8.3 3.6 %collective-permute-done = bf16[2,2,2,16,256]{4,3,2,1,0:T(8,128)(2,1)S(1)} collective-permute-done((bf16[2,2,2,16,256]{4,3,2,1,0:T(8,128)(2,1)S(1)}, bf16[2,2,2,16,256]{4,3,2,1,0:T(8,128)(2,1)S(1)}, u32[]{:S(2)}, u32[]{:S(2)}) %collective-permute-start) | collective-permute-done | bytes 65568 | tf_op jit(solution)/shard_map/ppermute | solution.py:142
  12.6 4.4 %collective-permute-done.1 = bf16[4,2,2,16,256]{4,3,2,1,0:T(8,128)(2,1)S(1)} collective-permute-done((bf16[4,2,2,16,256]{4,3,2,1,0:T(8,128)(2,1)S(1)}, bf16[4,2,2,16,256]{4,3,2,1,0:T(8,128)(2,1)S(1)}, u32[]{:S(2)}, u32[]{:S(2)}) %collective-permute-start.1) | collective-permute-done | bytes 131104 | tf_op jit(solution)/shard_map/ppermute | solution.py:142
  17.0 1.8 %collective-permute-start.2 = (bf16[8,2,2,16,256]{4,3,2,1,0:T(8,128)(2,1)S(1)}, bf16[8,2,2,16,256]{4,3,2,1,0:T(8,128)(2,1)S(1)}, u32[]{:S(2)}, u32[]{:S(2)}) collective-permute-start(bf16[8,2,2,16,256]{4,3,2,1,0:T(8,128)(2,1)S(1)} %pad_maximum_fusion.1), channel_id=1, source_target_pairs={{0,2},{1,3},{2,0},{3,1},{4,6},{5,7},{6,4},{7,5},{8,10},{9,11},{10,... | collective-permute-start | bytes 786440 | tf_op jit(solution)/shard_map/ppermute | solution.py:142
  19.0 4.5 %collective-permute-done.2 = bf16[8,2,2,16,256]{4,3,2,1,0:T(8,128)(2,1)S(1)} collective-permute-done((bf16[8,2,2,16,256]{4,3,2,1,0:T(8,128)(2,1)S(1)}, bf16[8,2,2,16,256]{4,3,2,1,0:T(8,128)(2,1)S(1)}, u32[]{:S(2)}, u32[]{:S(2)}) %collective-permute-start.2) | collective-permute-done | bytes 262176 | tf_op jit(solution)/shard_map/ppermute | solution.py:142
  24.4 1.1 %collective-permute-done.3 = bf16[16,2,2,16,256]{4,3,2,1,0:T(8,128)(2,1)S(1)} collective-permute-done((bf16[16,2,2,16,256]{4,3,2,1,0:T(8,128)(2,1)S(1)}, bf16[16,2,2,16,256]{4,3,2,1,0:T(8,128)(2,1)S(1)}, u32[]{:S(2)}, u32[]{:S(2)}) %collective-permute-start.3) | collective-permute-done | bytes 524320 | tf_op jit(solution)/shard_map/ppermute | solution.py:142
  25.5 1.0 %copy-done.2 = bf16[32,2,2,16,256]{4,3,2,1,0:T(8,128)(2,1)} copy-done((bf16[32,2,2,16,256]{4,3,2,1,0:T(8,128)(2,1)}, bf16[32,2,2,16,256]{4,3,2,1,0:T(8,128)(2,1)S(1)}, u32[]{:S(2)}) %copy-start.2) | copy-done | bytes 1048600
  26.5 8.3 %shard_map.104 = (bf16[2,2,256,256]{3,2,1,0:T(8,128)(2,1)}, f32[2,2,8,128]{3,2,1,0:T(8,128)}, f32[32,2,2,16,256]{4,3,2,1,0:T(8,128)}) custom-call(f32[2,2,32]{2,1,0:T(2,128)} %get-tuple-element.51.fwd_ref, f32[2,2,32]{2,1,0:T(2,128)} %get-tuple-element.52.back_ref, bf16[2,2,256,256]{3,2,1,0:T(8,128)(2,1)} %image_ref.1, bf16[2,2,256,256]{3,2,1,0:T(8,128)(2,1)} %copy-done.1, ...), custom_call_target="tpu_custom_call" | custom-call | flops 541065216 | bytes 4980736 | tf_op jit(solution)/shard_map/pallas_call | solution.py:77
  34.8 1.3 %fusion.5 = bf16[2,2,2,2,2,2,16,256]{7,6,5,3,4,0,1,2:T(8,128)(2,1)S(1)} fusion(f32[2,2,2,2,2,2,2,16,256]{8,7,6,5,4,3,2,1,0:T(8,128)} %bitcast.78), kind=kLoop, calls=%fused_computation.11 | loop fusion | bytes 1048576 | tf_op jit(solution)/shard_map/convert_element_type | solution.py:156
  36.3 1.8 %collective-permute-done.4 = bf16[2,2,2,2,2,2,16,256]{7,6,5,3,4,0,1,2:T(8,128)(2,1)S(1)} collective-permute-done((bf16[2,2,2,2,2,2,16,256]{7,6,5,3,4,0,1,2:T(8,128)(2,1)S(1)}, bf16[2,2,2,2,2,2,16,256]{7,6,5,3,4,0,1,2:T(8,128)(2,1)S(1)}, u32[]{:S(2)}, u32[]{:S(2)}) %collective-permute-start.4) | collective-permute-done | bytes 524320 | tf_op jit(solution)/shard_map/ppermute | solution.py:157
  38.1 1.4 %fusion.4 = f32[2,2,2,2,2,2,16,256]{7,6,5,3,4,0,1,2:T(8,128)S(1)} fusion(bf16[2,2,2,2,2,2,16,256]{7,6,5,3,4,0,1,2:T(8,128)(2,1)S(1)} %collective-permute-done.4, f32[2,2,2,2,2,2,2,16,256]{8,7,6,5,4,3,2,1,0:T(8,128)} %bitcast.79), kind=kLoop, calls=%fused_computation.10 | loop fusion | flops 524288 | bytes 2621440 | tf_op jit(solution)/shard_map/add | solution.py:157
  39.6 1.8 %collective-permute-start.5 = (bf16[2,2,2,2,2,16,256]{6,5,4,2,3,0,1:T(8,128)(2,1)S(1)}, bf16[2,2,2,2,2,16,256]{6,5,4,2,3,0,1:T(8,128)(2,1)S(1)}, u32[]{:S(2)}, u32[]{:S(2)}) collective-permute-start(bf16[2,2,2,2,2,16,256]{6,5,4,2,3,0,1:T(8,128)(2,1)S(1)} %fusion.10), channel_id=1, source_target_pairs={{0,2},{1,3},{2,0},{3,1},{4,6},{5,7},{6,4},{7,5},{8,10},{9,11},{10,... | collective-permute-start | bytes 786440 | tf_op jit(solution)/shard_map/ppermute | solution.py:157
  41.3 6.6 %collective-permute-done.5 = bf16[2,2,2,2,2,16,256]{6,5,4,2,3,0,1:T(8,128)(2,1)S(1)} collective-permute-done((bf16[2,2,2,2,2,16,256]{6,5,4,2,3,0,1:T(8,128)(2,1)S(1)}, bf16[2,2,2,2,2,16,256]{6,5,4,2,3,0,1:T(8,128)(2,1)S(1)}, u32[]{:S(2)}, u32[]{:S(2)}) %collective-permute-start.5) | collective-permute-done | bytes 262176 | tf_op jit(solution)/shard_map/ppermute | solution.py:157
  48.1 0.8 %collective-permute-start.6 = (bf16[2,2,2,2,16,256]{5,4,3,1,2,0:T(8,128)(2,1)S(1)}, bf16[2,2,2,2,16,256]{5,4,3,1,2,0:T(8,128)(2,1)S(1)}, u32[]{:S(2)}, u32[]{:S(2)}) collective-permute-start(bf16[2,2,2,2,16,256]{5,4,3,1,2,0:T(8,128)(2,1)S(1)} %fusion.18), channel_id=1, source_target_pairs={{0,4},{1,5},{2,6},{3,7},{4,0},{5,1},{6,2},{7,3},{8,12},{9,13},{10,... | collective-permute-start | bytes 393224 | tf_op jit(solution)/shard_map/ppermute | solution.py:157
  48.9 0.8 %slice_reduce_fusion = f32[2]{0:T(128)S(1)} fusion(f32[2,2,8,128]{3,2,1,0:T(8,128)} %get-tuple-element.31), kind=kLoop, calls=%fused_computation.63 | loop fusion | flops 2 | bytes 24 | tf_op jit(solution)/shard_map/reduce_sum | solution.py:147
  49.7 3.4 %collective-permute-done.6 = bf16[2,2,2,2,16,256]{5,4,3,1,2,0:T(8,128)(2,1)S(1)} collective-permute-done((bf16[2,2,2,2,16,256]{5,4,3,1,2,0:T(8,128)(2,1)S(1)}, bf16[2,2,2,2,16,256]{5,4,3,1,2,0:T(8,128)(2,1)S(1)}, u32[]{:S(2)}, u32[]{:S(2)}) %collective-permute-start.6) | collective-permute-done | bytes 131104 | tf_op jit(solution)/shard_map/ppermute | solution.py:157
  53.2 3.3 %collective-permute-start.7 = (bf16[2,2,2,16,256]{4,3,2,0,1:T(8,128)(2,1)S(1)}, bf16[2,2,2,16,256]{4,3,2,0,1:T(8,128)(2,1)S(1)}, u32[]{:S(2)}, u32[]{:S(2)}) collective-permute-start(bf16[2,2,2,16,256]{4,3,2,0,1:T(8,128)(2,1)S(1)} %fusion.20), channel_id=1, source_target_pairs={{0,8},{1,9},{2,10},{3,11},{4,12},{5,13},{6,14},{7,15},{8,0},{9,1},... | collective-permute-start | bytes 196616 | tf_op jit(solution)/shard_map/ppermute | solution.py:157
  56.6 2.1 %collective-permute-done.7 = bf16[2,2,2,16,256]{4,3,2,0,1:T(8,128)(2,1)S(1)} collective-permute-done((bf16[2,2,2,16,256]{4,3,2,0,1:T(8,128)(2,1)S(1)}, bf16[2,2,2,16,256]{4,3,2,0,1:T(8,128)(2,1)S(1)}, u32[]{:S(2)}, u32[]{:S(2)}) %collective-permute-start.7) | collective-permute-done | bytes 65568 | tf_op jit(solution)/shard_map/ppermute | solution.py:157
  59.8 1.5 %collective-permute-start.8 = (bf16[65542]{0:T(1024)(128)(2,1)S(1)}, bf16[65542]{0:T(1024)(128)(2,1)S(1)}, u32[]{:S(2)}, u32[]{:S(2)}) collective-permute-start(bf16[65542]{0:T(1024)(128)(2,1)S(1)} %concatenate.26), channel_id=1, source_target_pairs={{0,16},{16,0},{1,17},{17,1},{2,18},{18,2},{3,19},{19,3},{4,20},{20... | collective-permute-start | bytes 393260 | tf_op jit(solution)/shard_map/ppermute | solution.py:187
  61.3 3.5 %collective-permute-done.8 = bf16[65542]{0:T(1024)(128)(2,1)S(1)} collective-permute-done((bf16[65542]{0:T(1024)(128)(2,1)S(1)}, bf16[65542]{0:T(1024)(128)(2,1)S(1)}, u32[]{:S(2)}, u32[]{:S(2)}) %collective-permute-start.8) | collective-permute-done | bytes 131116 | tf_op jit(solution)/shard_map/ppermute | solution.py:187
  65.5 0.7 %dynamic-slice_add_fusion = f32[2,128,256]{2,1,0:T(8,128)} fusion(f32[2,128,256]{2,1,0:T(8,128)S(1)} %reshape.134, f32[2,256,256]{2,1,0:T(8,128)S(1)} %fusion.3, s32[]{:T(128)S(6)} %select_n.23), kind=kLoop, calls=%fused_computation.29 | loop fusion | flops 65536 | bytes 786436 | tf_op jit(solution)/shard_map/add | solution.py:188
  (53 shorter events, 4.0 us)
Async XLA Ops:
  0.6 1.0 %copy-start = (bf16[2,256,256]{2,1,0:T(8,128)(2,1)S(1)}, bf16[2,256,256]{2,1,0:T(8,128)(2,1)}, u32[]{:S(2)}) copy-start(bf16[2,256,256]{2,1,0:T(8,128)(2,1)} %param.16) | copy-start | bytes 786436
  0.6 11.9 %copy-start.5 = (s32[2,2,8]{2,1,0:T(2,128)S(1)}, s32[2,2,8]{2,1,0:T(2,128)}, u32[]{:S(2)}) copy-start(s32[2,2,8]{2,1,0:T(2,128)} %param.18) | copy-start | bytes 388
  0.7 18.1 %copy-start.7 = (s32[2,16]{1,0:T(2,128)S(1)}, s32[2,16]{1,0:T(2,128)}, u32[]{:S(2)}) copy-start(s32[2,16]{1,0:T(2,128)} %param.20) | copy-start | bytes 388
  0.7 18.3 %copy-start.6 = (s32[2,16]{1,0:T(2,128)S(1)}, s32[2,16]{1,0:T(2,128)}, u32[]{:S(2)}) copy-start(s32[2,16]{1,0:T(2,128)} %param.19) | copy-start | bytes 388
  0.7 22.9 %copy-start.8 = (f32[2,16]{1,0:T(2,128)S(1)}, f32[2,16]{1,0:T(2,128)}, u32[]{:S(2)}) copy-start(f32[2,16]{1,0:T(2,128)} %param.21) | copy-start | bytes 388
  4.1 21.4 %copy-start.1 = (bf16[2,2,256,256]{3,2,1,0:T(8,128)(2,1)}, bf16[2,2,256,256]{3,2,1,0:T(8,128)(2,1)S(1)}, u32[]{:S(2)}) copy-start(bf16[2,2,256,256]{3,2,1,0:T(8,128)(2,1)S(1)} %fusion.2.proj_ref) | copy-start | bytes 1572868
  4.2 7.8 %collective-permute-start = (bf16[2,2,2,16,256]{4,3,2,1,0:T(8,128)(2,1)S(1)}, bf16[2,2,2,16,256]{4,3,2,1,0:T(8,128)(2,1)S(1)}, u32[]{:S(2)}, u32[]{:S(2)}) collective-permute-start(bf16[2,2,2,16,256]{4,3,2,1,0:T(8,128)(2,1)S(1)} %get-tuple-element.40), channel_id=1, source_target_pairs={{0,8},{1,9},{2,10},{3,11},{4,12},{5,13},{6,14},{7,15},{8,0},{9,1},... | collective-permute-start | bytes 196616 | tf_op jit(solution)/shard_map/ppermute | solution.py:142
  11.9 5.0 %collective-permute-start.1 = (bf16[4,2,2,16,256]{4,3,2,1,0:T(8,128)(2,1)S(1)}, bf16[4,2,2,16,256]{4,3,2,1,0:T(8,128)(2,1)S(1)}, u32[]{:S(2)}, u32[]{:S(2)}) collective-permute-start(bf16[4,2,2,16,256]{4,3,2,1,0:T(8,128)(2,1)S(1)} %pad_maximum_fusion.2), channel_id=1, source_target_pairs={{0,4},{1,5},{2,6},{3,7},{4,0},{5,1},{6,2},{7,3},{8,12},{9,13},{10,... | collective-permute-start | bytes 393224 | tf_op jit(solution)/shard_map/ppermute | solution.py:142
  17.0 6.4 %collective-permute-start.2 = (bf16[8,2,2,16,256]{4,3,2,1,0:T(8,128)(2,1)S(1)}, bf16[8,2,2,16,256]{4,3,2,1,0:T(8,128)(2,1)S(1)}, u32[]{:S(2)}, u32[]{:S(2)}) collective-permute-start(bf16[8,2,2,16,256]{4,3,2,1,0:T(8,128)(2,1)S(1)} %pad_maximum_fusion.1), channel_id=1, source_target_pairs={{0,2},{1,3},{2,0},{3,1},{4,6},{5,7},{6,4},{7,5},{8,10},{9,11},{10,... | collective-permute-start | bytes 786440 | tf_op jit(solution)/shard_map/ppermute | solution.py:142
  23.5 2.0 %collective-permute-start.3 = (bf16[16,2,2,16,256]{4,3,2,1,0:T(8,128)(2,1)S(1)}, bf16[16,2,2,16,256]{4,3,2,1,0:T(8,128)(2,1)S(1)}, u32[]{:S(2)}, u32[]{:S(2)}) collective-permute-start(bf16[16,2,2,16,256]{4,3,2,1,0:T(8,128)(2,1)S(1)} %pad_maximum_fusion), channel_id=1, source_target_pairs={{0,1},{1,0},{2,3},{3,2},{4,5},{5,4},{6,7},{7,6},{8,9},{9,8},{10,11... | collective-permute-start | bytes 1572872 | tf_op jit(solution)/shard_map/ppermute | solution.py:142
  25.5 1.0 %copy-start.2 = (bf16[32,2,2,16,256]{4,3,2,1,0:T(8,128)(2,1)}, bf16[32,2,2,16,256]{4,3,2,1,0:T(8,128)(2,1)S(1)}, u32[]{:S(2)}) copy-start(bf16[32,2,2,16,256]{4,3,2,1,0:T(8,128)(2,1)S(1)} %constant_dynamic-update-slice_fusion.edge_ref) | copy-start | bytes 3145732
  36.1 2.0 %collective-permute-start.4 = (bf16[2,2,2,2,2,2,16,256]{7,6,5,3,4,0,1,2:T(8,128)(2,1)S(1)}, bf16[2,2,2,2,2,2,16,256]{7,6,5,3,4,0,1,2:T(8,128)(2,1)S(1)}, u32[]{:S(2)}, u32[]{:S(2)}) collective-permute-start(bf16[2,2,2,2,2,2,16,256]{7,6,5,3,4,0,1,2:T(8,128)(2,1)S(1)} %fusion.5), channel_id=1, source_target_pairs={{0,1},{1,0},{2,3},{3,2},{4,5},{5,4},{6,7},{7,6},{8,9},{9,8},{10,11... | collective-permute-start | bytes 1572872 | tf_op jit(solution)/shard_map/ppermute | solution.py:157
  39.5 17.0 %copy-start.4 = (bf16[2,2,256,256]{3,2,1,0:T(8,128)(2,1)S(1)}, bf16[2,2,256,256]{3,2,1,0:T(8,128)(2,1)}, u32[]{:S(2)}) copy-start(bf16[2,2,256,256]{3,2,1,0:T(8,128)(2,1)} %get-tuple-element.29) | copy-start | bytes 1572868
  39.5 19.2 %copy-start.3 = (bf16[2,256,256]{2,1,0:T(8,128)(2,1)S(1)}, bf16[2,256,256]{2,1,0:T(8,128)(2,1)}, u32[]{:S(2)}) copy-start(bf16[2,256,256]{2,1,0:T(8,128)(2,1)} %param.15) | copy-start | bytes 786436
  39.6 8.4 %collective-permute-start.5 = (bf16[2,2,2,2,2,16,256]{6,5,4,2,3,0,1:T(8,128)(2,1)S(1)}, bf16[2,2,2,2,2,16,256]{6,5,4,2,3,0,1:T(8,128)(2,1)S(1)}, u32[]{:S(2)}, u32[]{:S(2)}) collective-permute-start(bf16[2,2,2,2,2,16,256]{6,5,4,2,3,0,1:T(8,128)(2,1)S(1)} %fusion.10), channel_id=1, source_target_pairs={{0,2},{1,3},{2,0},{3,1},{4,6},{5,7},{6,4},{7,5},{8,10},{9,11},{10,... | collective-permute-start | bytes 786440 | tf_op jit(solution)/shard_map/ppermute | solution.py:157
  48.1 5.0 %collective-permute-start.6 = (bf16[2,2,2,2,16,256]{5,4,3,1,2,0:T(8,128)(2,1)S(1)}, bf16[2,2,2,2,16,256]{5,4,3,1,2,0:T(8,128)(2,1)S(1)}, u32[]{:S(2)}, u32[]{:S(2)}) collective-permute-start(bf16[2,2,2,2,16,256]{5,4,3,1,2,0:T(8,128)(2,1)S(1)} %fusion.18), channel_id=1, source_target_pairs={{0,4},{1,5},{2,6},{3,7},{4,0},{5,1},{6,2},{7,3},{8,12},{9,13},{10,... | collective-permute-start | bytes 393224 | tf_op jit(solution)/shard_map/ppermute | solution.py:157
  53.2 5.5 %collective-permute-start.7 = (bf16[2,2,2,16,256]{4,3,2,0,1:T(8,128)(2,1)S(1)}, bf16[2,2,2,16,256]{4,3,2,0,1:T(8,128)(2,1)S(1)}, u32[]{:S(2)}, u32[]{:S(2)}) collective-permute-start(bf16[2,2,2,16,256]{4,3,2,0,1:T(8,128)(2,1)S(1)} %fusion.20), channel_id=1, source_target_pairs={{0,8},{1,9},{2,10},{3,11},{4,12},{5,13},{6,14},{7,15},{8,0},{9,1},... | collective-permute-start | bytes 196616 | tf_op jit(solution)/shard_map/ppermute | solution.py:157
  59.8 5.0 %collective-permute-start.8 = (bf16[65542]{0:T(1024)(128)(2,1)S(1)}, bf16[65542]{0:T(1024)(128)(2,1)S(1)}, u32[]{:S(2)}, u32[]{:S(2)}) collective-permute-start(bf16[65542]{0:T(1024)(128)(2,1)S(1)} %concatenate.26), channel_id=1, source_target_pairs={{0,16},{16,0},{1,17},{17,1},{2,18},{18,2},{3,19},{19,3},{4,20},{20... | collective-permute-start | bytes 393260 | tf_op jit(solution)/shard_map/ppermute | solution.py:187

commit v6 on v5

--- a/solution.py
+++ b/solution.py
@@ -33,7 +33,7 @@
         return lower, upper
 
     zero = jnp.zeros((OVL, pixels), jnp.float32)
-    lower, upper = lax.fori_loop(0, total, band_sum, (zero, zero))
+    lower, upper = lax.fori_loop(0, total, band_sum, (zero, zero), unroll=8)
     residual_ref[...] = image_ref[0, 0].astype(jnp.float32) - proj_ref[0, 0].astype(jnp.float32)
     residual_ref[:OVL] = residual_ref[:OVL] - upper
     residual_ref[pixels - OVL :] = residual_ref[pixels - OVL :] - lower
@@ -63,7 +63,7 @@
         return_ref[q, 1, 0] = return_ref[q, 1, 0] + back_ref[1, k, q] * top_rows
         return carry
 
-    lax.fori_loop(0, total, give_back, 0)
+    lax.fori_loop(0, total, give_back, 0, unroll=8)
 
 
 def middle(fwd, back, images, projected, edges_all, ctf_filter):
@@ -126,7 +126,6 @@
         return jnp.sum(jnp.where(hits, nbr_weight[:, :, None], 0.0), axis=1)
 
     fwd = [weights_for(flipped, s) for s in (0, 1)]
-    back = [weights_for(relative, s) for s in (0, 1)]
 
     halfway = jnp.einsum(
         "kij,tlj->ktil", sections, slice_cols, preferred_element_type=jnp.float32
@@ -142,19 +141,17 @@
         edges_all = jnp.concatenate((edges_all, lax.ppermute(edges_all, "dom", pairs)), axis=0)
 
     weighted, score_tiles, returned = middle(
-        jnp.stack(fwd), jnp.stack(back), images, projected, edges_all, ctf_filter
+        jnp.stack(fwd), jnp.stack(fwd), images, projected, edges_all, ctf_filter
     )
     score_part = jnp.sum(score_tiles[:, :, 0, 0], axis=0)
     tilt_groups = lax.axis_size("tilt")
 
-    returned = returned.reshape((2,) * steps + (own_count,) + returned.shape[1:])
     for b in range(steps):
         stride = 1 << b
         pairs = [(i, i ^ stride) for i in range(peer_count)]
-        axis = steps - 1 - b
-        kept = lax.index_in_dim(returned, 0, axis, keepdims=False)
-        given = lax.index_in_dim(returned, 1, axis, keepdims=False).astype(jnp.bfloat16)
-        returned = kept + lax.ppermute(given, "dom", pairs).astype(jnp.float32)
+        half = returned.shape[0] // 2
+        given = returned[half:].astype(jnp.bfloat16)
+        returned = returned[:half] + lax.ppermute(given, "dom", pairs).astype(jnp.float32)
     add_top = returned[:, 0]
     add_bottom = returned[:, 1]
 

time: 66.6 us -> 64.7 us (0.971)
  Pallas kernels: 8.29 us -> 6.35 us
    pallas_call x1, Pallas kernels: 8.29 us -> 6.35 us  [middle(): pl.pallas_call(middle_kernel, grid=(tilt_count, own_count), in_specs=[sme...]
    convert_element_type x4 -> x0, local copies, waits for them, and re-layouts: 1.37 us -> none  [on_device(): lax.index_in_dim(returned, 1, axis, keepdims=False).astype(jnp.bfloat16)]
    slice x0 -> x4, local copies, waits for them, and re-layouts: none -> 1.37 us  [on_device(): given = returned[half:].astype(jnp.bfloat16)]
where the time goes in v6:
time: 64.7 us; the launch traced here: 64.3 us
  waiting for transfers between devices  31.2 us (48%)
  starting transfers between devices  14.2 us (22%)
  Pallas kernels  6.35 us (10%)
  other arithmetic  4.64 us (7%)
  local copies, waits for them, and re-layouts  3.96 us (6%)
  matrix products  3.06 us (5%)
  between operations  0.93 us (1%)
    ppermute x4, waiting for transfers between devices, on_device(): lax.ppermute(given, 'dom', pairs).astype(jnp.float32)  13.9 us
    ppermute x4, waiting for transfers between devices, on_device(): lax.ppermute(edges_all, 'dom', pairs)  13.7 us
    ppermute x4, starting transfers between devices, on_device(): lax.ppermute(edges_all, 'dom', pairs)  6.57 us
    pallas_call x1, Pallas kernels, middle(): pl.pallas_call(middle_kernel, grid=(tilt_count, own_count), in_specs=[sme...  6.35 us
    ppermute x4, starting transfers between devices, on_device(): lax.ppermute(given, 'dom', pairs).astype(jnp.float32)  6.09 us
    ppermute x1, waiting for transfers between devices, on_device(): parcel = lax.ppermute(parcel, 'tilt', [(0, 1), (1, 0)]).astype(jnp.float32)  3.46 us
    unnamed x22, local copies, waits for them, and re-layouts  2.04 us
    ppermute x1, starting transfers between devices, on_device(): parcel = lax.ppermute(parcel, 'tilt', [(0, 1), (1, 0)]).astype(jnp.float32)  1.53 us
  transfers between devices with their start and end apart: 9, of which 9 were waited for; matrix products, arithmetic and copies ran while one was open for 3% of the time, Pallas kernels for 0%

profile of v6, /device:TPU:0, one launch (start us, length us, event | category | flops | bytes accessed | tf_op | source)
XLA Modules:
  0.0 64.3 jit_solution(148849925059529633)
XLA Ops:
  0.7 0.9 %copy-done = bf16[2,256,256]{2,1,0:T(8,128)(2,1)S(1)} copy-done((bf16[2,256,256]{2,1,0:T(8,128)(2,1)S(1)}, bf16[2,256,256]{2,1,0:T(8,128)(2,1)}, u32[]{:S(2)}) %copy-start) | copy-done | bytes 262168
  1.6 1.3 %fusion = bf16[2,2,256,256]{3,2,0,1:T(8,128)(2,1)S(1)} fusion(bf16[2,256,256]{2,1,0:T(8,128)(2,1)S(1)} %copy-done, bf16[2,256,256]{2,1,0:T(8,128)(2,1)} %param.13), kind=kOutput, calls=%fused_computation.3 | convolution fusion | flops 134479872 | bytes 1048576 | tf_op jit(solution)/shard_map/kij,tlj->ktil/dot_general | solution.py:130
  2.9 1.3 %fusion.2.proj_ref = bf16[2,2,256,256]{3,2,1,0:T(8,128)(2,1)S(1)} fusion(bf16[2,2,256,256]{3,2,0,1:T(8,128)(2,1)S(1)} %fusion, bf16[2,256,256]{2,1,0:T(8,128)(2,1)} %param.15), kind=kOutput, calls=%fused_computation.5 | convolution fusion | flops 134479872 | bytes 1310720 | tf_op jit(solution)/shard_map/tai,ktil->ktal/dot_general | solution.py:133
  4.2 4.1 %collective-permute-start = (bf16[2,2,2,16,256]{4,3,2,1,0:T(8,128)(2,1)S(1)}, bf16[2,2,2,16,256]{4,3,2,1,0:T(8,128)(2,1)S(1)}, u32[]{:S(2)}, u32[]{:S(2)}) collective-permute-start(bf16[2,2,2,16,256]{4,3,2,1,0:T(8,128)(2,1)S(1)} %get-tuple-element.36), channel_id=1, source_target_pairs={{0,8},{1,9},{2,10},{3,11},{4,12},{5,13},{6,14},{7,15},{8,0},{9,1},... | collective-permute-start | bytes 196616 | tf_op jit(solution)/shard_map/ppermute | solution.py:141
  8.3 3.6 %collective-permute-done = bf16[2,2,2,16,256]{4,3,2,1,0:T(8,128)(2,1)S(1)} collective-permute-done((bf16[2,2,2,16,256]{4,3,2,1,0:T(8,128)(2,1)S(1)}, bf16[2,2,2,16,256]{4,3,2,1,0:T(8,128)(2,1)S(1)}, u32[]{:S(2)}, u32[]{:S(2)}) %collective-permute-start) | collective-permute-done | bytes 65568 | tf_op jit(solution)/shard_map/ppermute | solution.py:141
  12.6 4.4 %collective-permute-done.1 = bf16[4,2,2,16,256]{4,3,2,1,0:T(8,128)(2,1)S(1)} collective-permute-done((bf16[4,2,2,16,256]{4,3,2,1,0:T(8,128)(2,1)S(1)}, bf16[4,2,2,16,256]{4,3,2,1,0:T(8,128)(2,1)S(1)}, u32[]{:S(2)}, u32[]{:S(2)}) %collective-permute-start.1) | collective-permute-done | bytes 131104 | tf_op jit(solution)/shard_map/ppermute | solution.py:141
  17.0 1.8 %collective-permute-start.2 = (bf16[8,2,2,16,256]{4,3,2,1,0:T(8,128)(2,1)S(1)}, bf16[8,2,2,16,256]{4,3,2,1,0:T(8,128)(2,1)S(1)}, u32[]{:S(2)}, u32[]{:S(2)}) collective-permute-start(bf16[8,2,2,16,256]{4,3,2,1,0:T(8,128)(2,1)S(1)} %pad_maximum_fusion.1), channel_id=1, source_target_pairs={{0,2},{1,3},{2,0},{3,1},{4,6},{5,7},{6,4},{7,5},{8,10},{9,11},{10,... | collective-permute-start | bytes 786440 | tf_op jit(solution)/shard_map/ppermute | solution.py:141
  18.9 4.6 %collective-permute-done.2 = bf16[8,2,2,16,256]{4,3,2,1,0:T(8,128)(2,1)S(1)} collective-permute-done((bf16[8,2,2,16,256]{4,3,2,1,0:T(8,128)(2,1)S(1)}, bf16[8,2,2,16,256]{4,3,2,1,0:T(8,128)(2,1)S(1)}, u32[]{:S(2)}, u32[]{:S(2)}) %collective-permute-start.2) | collective-permute-done | bytes 262176 | tf_op jit(solution)/shard_map/ppermute | solution.py:141
  24.3 1.1 %collective-permute-done.3 = bf16[16,2,2,16,256]{4,3,2,1,0:T(8,128)(2,1)S(1)} collective-permute-done((bf16[16,2,2,16,256]{4,3,2,1,0:T(8,128)(2,1)S(1)}, bf16[16,2,2,16,256]{4,3,2,1,0:T(8,128)(2,1)S(1)}, u32[]{:S(2)}, u32[]{:S(2)}) %collective-permute-start.3) | collective-permute-done | bytes 524320 | tf_op jit(solution)/shard_map/ppermute | solution.py:141
  25.5 1.0 %copy-done.2 = bf16[32,2,2,16,256]{4,3,2,1,0:T(8,128)(2,1)} copy-done((bf16[32,2,2,16,256]{4,3,2,1,0:T(8,128)(2,1)}, bf16[32,2,2,16,256]{4,3,2,1,0:T(8,128)(2,1)S(1)}, u32[]{:S(2)}) %copy-start.2) | copy-done | bytes 1048600
  26.5 6.4 %shard_map.104 = (bf16[2,2,256,256]{3,2,1,0:T(8,128)(2,1)}, f32[2,2,8,128]{3,2,1,0:T(8,128)}, f32[32,2,2,16,256]{4,3,2,1,0:T(8,128)}) custom-call(f32[2,2,32]{2,1,0:T(2,128)} %pad_maximum_fusion.4.fwd_ref.back_ref, f32[2,2,32]{2,1,0:T(2,128)} %pad_maximum_fusion.4.fwd_ref.back_ref, bf16[2,2,256,256]{3,2,1,0:T(8,128)(2,1)} %image_ref.1, ...), custom_call_target="tpu_custom_call" | custom-call | flops 541065216 | bytes 4980736 | tf_op jit(solution)/shard_map/pallas_call | solution.py:77
  32.9 1.3 %slice.192 = bf16[16,2,2,16,256]{4,3,2,1,0:T(8,128)(2,1)S(1)} slice(f32[32,2,2,16,256]{4,3,2,1,0:T(8,128)} %get-tuple-element.30), slice={[16:32], [0:2], [0:2], [0:16], [0:256]} | slice | bytes 1048576 | tf_op jit(solution)/shard_map/slice | solution.py:153
  34.4 1.8 %collective-permute-done.4 = bf16[16,2,2,16,256]{4,3,2,1,0:T(8,128)(2,1)S(1)} collective-permute-done((bf16[16,2,2,16,256]{4,3,2,1,0:T(8,128)(2,1)S(1)}, bf16[16,2,2,16,256]{4,3,2,1,0:T(8,128)(2,1)S(1)}, u32[]{:S(2)}, u32[]{:S(2)}) %collective-permute-start.4) | collective-permute-done | bytes 524320 | tf_op jit(solution)/shard_map/ppermute | solution.py:154
  36.1 1.4 %convert_add_fusion = f32[16,2,2,16,256]{4,3,2,1,0:T(8,128)S(1)} fusion(bf16[16,2,2,16,256]{4,3,2,1,0:T(8,128)(2,1)S(1)} %collective-permute-done.4, f32[32,2,2,16,256]{4,3,2,1,0:T(8,128)} %get-tuple-element.30), kind=kLoop, calls=%fused_computation.9 | loop fusion | flops 524288 | bytes 2621440 | tf_op jit(solution)/shard_map/add | solution.py:154
  37.6 1.8 %collective-permute-start.5 = (bf16[8,2,2,16,256]{4,3,2,1,0:T(8,128)(2,1)S(1)}, bf16[8,2,2,16,256]{4,3,2,1,0:T(8,128)(2,1)S(1)}, u32[]{:S(2)}, u32[]{:S(2)}) collective-permute-start(bf16[8,2,2,16,256]{4,3,2,1,0:T(8,128)(2,1)S(1)} %slice.193), channel_id=1, source_target_pairs={{0,2},{1,3},{2,0},{3,1},{4,6},{5,7},{6,4},{7,5},{8,10},{9,11},{10,... | collective-permute-start | bytes 786440 | tf_op jit(solution)/shard_map/ppermute | solution.py:154
  39.4 6.6 %collective-permute-done.5 = bf16[8,2,2,16,256]{4,3,2,1,0:T(8,128)(2,1)S(1)} collective-permute-done((bf16[8,2,2,16,256]{4,3,2,1,0:T(8,128)(2,1)S(1)}, bf16[8,2,2,16,256]{4,3,2,1,0:T(8,128)(2,1)S(1)}, u32[]{:S(2)}, u32[]{:S(2)}) %collective-permute-start.5) | collective-permute-done | bytes 262176 | tf_op jit(solution)/shard_map/ppermute | solution.py:154
  46.1 0.8 %collective-permute-start.6 = (bf16[4,2,2,16,256]{4,3,2,1,0:T(8,128)(2,1)S(1)}, bf16[4,2,2,16,256]{4,3,2,1,0:T(8,128)(2,1)S(1)}, u32[]{:S(2)}, u32[]{:S(2)}) collective-permute-start(bf16[4,2,2,16,256]{4,3,2,1,0:T(8,128)(2,1)S(1)} %slice.194), channel_id=1, source_target_pairs={{0,4},{1,5},{2,6},{3,7},{4,0},{5,1},{6,2},{7,3},{8,12},{9,13},{10,... | collective-permute-start | bytes 393224 | tf_op jit(solution)/shard_map/ppermute | solution.py:154
  47.0 0.8 %slice_reduce_fusion = f32[2]{0:T(128)S(1)} fusion(f32[2,2,8,128]{3,2,1,0:T(8,128)} %get-tuple-element.31), kind=kLoop, calls=%fused_computation.49 | loop fusion | flops 2 | bytes 24 | tf_op jit(solution)/shard_map/reduce_sum | solution.py:146
  47.8 3.4 %collective-permute-done.6 = bf16[4,2,2,16,256]{4,3,2,1,0:T(8,128)(2,1)S(1)} collective-permute-done((bf16[4,2,2,16,256]{4,3,2,1,0:T(8,128)(2,1)S(1)}, bf16[4,2,2,16,256]{4,3,2,1,0:T(8,128)(2,1)S(1)}, u32[]{:S(2)}, u32[]{:S(2)}) %collective-permute-start.6) | collective-permute-done | bytes 131104 | tf_op jit(solution)/shard_map/ppermute | solution.py:154
  51.2 3.3 %collective-permute-start.7 = (bf16[2,2,2,16,256]{4,3,2,1,0:T(8,128)(2,1)S(1)}, bf16[2,2,2,16,256]{4,3,2,1,0:T(8,128)(2,1)S(1)}, u32[]{:S(2)}, u32[]{:S(2)}) collective-permute-start(bf16[2,2,2,16,256]{4,3,2,1,0:T(8,128)(2,1)S(1)} %slice.195), channel_id=1, source_target_pairs={{0,8},{1,9},{2,10},{3,11},{4,12},{5,13},{6,14},{7,15},{8,0},{9,1},... | collective-permute-start | bytes 196616 | tf_op jit(solution)/shard_map/ppermute | solution.py:154
  54.6 2.1 %collective-permute-done.7 = bf16[2,2,2,16,256]{4,3,2,1,0:T(8,128)(2,1)S(1)} collective-permute-done((bf16[2,2,2,16,256]{4,3,2,1,0:T(8,128)(2,1)S(1)}, bf16[2,2,2,16,256]{4,3,2,1,0:T(8,128)(2,1)S(1)}, u32[]{:S(2)}, u32[]{:S(2)}) %collective-permute-start.7) | collective-permute-done | bytes 65568 | tf_op jit(solution)/shard_map/ppermute | solution.py:154
  57.8 1.5 %collective-permute-start.8 = (bf16[65542]{0:T(1024)(128)(2,1)S(1)}, bf16[65542]{0:T(1024)(128)(2,1)S(1)}, u32[]{:S(2)}, u32[]{:S(2)}) collective-permute-start(bf16[65542]{0:T(1024)(128)(2,1)S(1)} %concatenate.26), channel_id=1, source_target_pairs={{0,16},{16,0},{1,17},{17,1},{2,18},{18,2},{3,19},{19,3},{4,20},{20... | collective-permute-start | bytes 393260 | tf_op jit(solution)/shard_map/ppermute | solution.py:184
  59.4 3.5 %collective-permute-done.8 = bf16[65542]{0:T(1024)(128)(2,1)S(1)} collective-permute-done((bf16[65542]{0:T(1024)(128)(2,1)S(1)}, bf16[65542]{0:T(1024)(128)(2,1)S(1)}, u32[]{:S(2)}, u32[]{:S(2)}) %collective-permute-start.8) | collective-permute-done | bytes 131116 | tf_op jit(solution)/shard_map/ppermute | solution.py:184
  63.5 0.7 %dynamic-slice_add_fusion = f32[2,128,256]{2,1,0:T(8,128)} fusion(f32[2,128,256]{2,1,0:T(8,128)S(1)} %reshape.123, f32[2,256,256]{2,1,0:T(8,128)S(1)} %fusion.3, s32[]{:T(128)S(6)} %select_n.15), kind=kLoop, calls=%fused_computation.24 | loop fusion | flops 65536 | bytes 786436 | tf_op jit(solution)/shard_map/add | solution.py:185
  (52 shorter events, 3.9 us)
Async XLA Ops:
  0.6 1.0 %copy-start = (bf16[2,256,256]{2,1,0:T(8,128)(2,1)S(1)}, bf16[2,256,256]{2,1,0:T(8,128)(2,1)}, u32[]{:S(2)}) copy-start(bf16[2,256,256]{2,1,0:T(8,128)(2,1)} %param.16) | copy-start | bytes 786436
  0.6 18.1 %copy-start.5 = (s32[2,2,8]{2,1,0:T(2,128)S(1)}, s32[2,2,8]{2,1,0:T(2,128)}, u32[]{:S(2)}) copy-start(s32[2,2,8]{2,1,0:T(2,128)} %param.18) | copy-start | bytes 388
  0.7 18.2 %copy-start.6 = (s32[2,16]{1,0:T(2,128)S(1)}, s32[2,16]{1,0:T(2,128)}, u32[]{:S(2)}) copy-start(s32[2,16]{1,0:T(2,128)} %param.19) | copy-start | bytes 388
  0.7 18.2 %copy-start.8 = (s32[2,16]{1,0:T(2,128)S(1)}, s32[2,16]{1,0:T(2,128)}, u32[]{:S(2)}) copy-start(s32[2,16]{1,0:T(2,128)} %param.20) | copy-start | bytes 388
  0.7 22.9 %copy-start.7 = (f32[2,16]{1,0:T(2,128)S(1)}, f32[2,16]{1,0:T(2,128)}, u32[]{:S(2)}) copy-start(f32[2,16]{1,0:T(2,128)} %param.21) | copy-start | bytes 388
  4.1 21.4 %copy-start.1 = (bf16[2,2,256,256]{3,2,1,0:T(8,128)(2,1)}, bf16[2,2,256,256]{3,2,1,0:T(8,128)(2,1)S(1)}, u32[]{:S(2)}) copy-start(bf16[2,2,256,256]{3,2,1,0:T(8,128)(2,1)S(1)} %fusion.2.proj_ref) | copy-start | bytes 1572868
  4.2 7.8 %collective-permute-start = (bf16[2,2,2,16,256]{4,3,2,1,0:T(8,128)(2,1)S(1)}, bf16[2,2,2,16,256]{4,3,2,1,0:T(8,128)(2,1)S(1)}, u32[]{:S(2)}, u32[]{:S(2)}) collective-permute-start(bf16[2,2,2,16,256]{4,3,2,1,0:T(8,128)(2,1)S(1)} %get-tuple-element.36), channel_id=1, source_target_pairs={{0,8},{1,9},{2,10},{3,11},{4,12},{5,13},{6,14},{7,15},{8,0},{9,1},... | collective-permute-start | bytes 196616 | tf_op jit(solution)/shard_map/ppermute | solution.py:141
  11.9 5.0 %collective-permute-start.1 = (bf16[4,2,2,16,256]{4,3,2,1,0:T(8,128)(2,1)S(1)}, bf16[4,2,2,16,256]{4,3,2,1,0:T(8,128)(2,1)S(1)}, u32[]{:S(2)}, u32[]{:S(2)}) collective-permute-start(bf16[4,2,2,16,256]{4,3,2,1,0:T(8,128)(2,1)S(1)} %pad_maximum_fusion.2), channel_id=1, source_target_pairs={{0,4},{1,5},{2,6},{3,7},{4,0},{5,1},{6,2},{7,3},{8,12},{9,13},{10,... | collective-permute-start | bytes 393224 | tf_op jit(solution)/shard_map/ppermute | solution.py:141
  17.0 6.4 %collective-permute-start.2 = (bf16[8,2,2,16,256]{4,3,2,1,0:T(8,128)(2,1)S(1)}, bf16[8,2,2,16,256]{4,3,2,1,0:T(8,128)(2,1)S(1)}, u32[]{:S(2)}, u32[]{:S(2)}) collective-permute-start(bf16[8,2,2,16,256]{4,3,2,1,0:T(8,128)(2,1)S(1)} %pad_maximum_fusion.1), channel_id=1, source_target_pairs={{0,2},{1,3},{2,0},{3,1},{4,6},{5,7},{6,4},{7,5},{8,10},{9,11},{10,... | collective-permute-start | bytes 786440 | tf_op jit(solution)/shard_map/ppermute | solution.py:141
  23.5 2.0 %collective-permute-start.3 = (bf16[16,2,2,16,256]{4,3,2,1,0:T(8,128)(2,1)S(1)}, bf16[16,2,2,16,256]{4,3,2,1,0:T(8,128)(2,1)S(1)}, u32[]{:S(2)}, u32[]{:S(2)}) collective-permute-start(bf16[16,2,2,16,256]{4,3,2,1,0:T(8,128)(2,1)S(1)} %pad_maximum_fusion), channel_id=1, source_target_pairs={{0,1},{1,0},{2,3},{3,2},{4,5},{5,4},{6,7},{7,6},{8,9},{9,8},{10,11... | collective-permute-start | bytes 1572872 | tf_op jit(solution)/shard_map/ppermute | solution.py:141
  25.5 1.0 %copy-start.2 = (bf16[32,2,2,16,256]{4,3,2,1,0:T(8,128)(2,1)}, bf16[32,2,2,16,256]{4,3,2,1,0:T(8,128)(2,1)S(1)}, u32[]{:S(2)}) copy-start(bf16[32,2,2,16,256]{4,3,2,1,0:T(8,128)(2,1)S(1)} %constant_dynamic-update-slice_fusion.edge_ref) | copy-start | bytes 3145732
  34.2 2.0 %collective-permute-start.4 = (bf16[16,2,2,16,256]{4,3,2,1,0:T(8,128)(2,1)S(1)}, bf16[16,2,2,16,256]{4,3,2,1,0:T(8,128)(2,1)S(1)}, u32[]{:S(2)}, u32[]{:S(2)}) collective-permute-start(bf16[16,2,2,16,256]{4,3,2,1,0:T(8,128)(2,1)S(1)} %slice.192), channel_id=1, source_target_pairs={{0,1},{1,0},{2,3},{3,2},{4,5},{5,4},{6,7},{7,6},{8,9},{9,8},{10,11... | collective-permute-start | bytes 1572872 | tf_op jit(solution)/shard_map/ppermute | solution.py:154
  37.6 17.0 %copy-start.4 = (bf16[2,2,256,256]{3,2,1,0:T(8,128)(2,1)S(1)}, bf16[2,2,256,256]{3,2,1,0:T(8,128)(2,1)}, u32[]{:S(2)}) copy-start(bf16[2,2,256,256]{3,2,1,0:T(8,128)(2,1)} %get-tuple-element.29) | copy-start | bytes 1572868
  37.6 19.2 %copy-start.3 = (bf16[2,256,256]{2,1,0:T(8,128)(2,1)S(1)}, bf16[2,256,256]{2,1,0:T(8,128)(2,1)}, u32[]{:S(2)}) copy-start(bf16[2,256,256]{2,1,0:T(8,128)(2,1)} %param.15) | copy-start | bytes 786436
  37.6 8.4 %collective-permute-start.5 = (bf16[8,2,2,16,256]{4,3,2,1,0:T(8,128)(2,1)S(1)}, bf16[8,2,2,16,256]{4,3,2,1,0:T(8,128)(2,1)S(1)}, u32[]{:S(2)}, u32[]{:S(2)}) collective-permute-start(bf16[8,2,2,16,256]{4,3,2,1,0:T(8,128)(2,1)S(1)} %slice.193), channel_id=1, source_target_pairs={{0,2},{1,3},{2,0},{3,1},{4,6},{5,7},{6,4},{7,5},{8,10},{9,11},{10,... | collective-permute-start | bytes 786440 | tf_op jit(solution)/shard_map/ppermute | solution.py:154
  46.1 5.0 %collective-permute-start.6 = (bf16[4,2,2,16,256]{4,3,2,1,0:T(8,128)(2,1)S(1)}, bf16[4,2,2,16,256]{4,3,2,1,0:T(8,128)(2,1)S(1)}, u32[]{:S(2)}, u32[]{:S(2)}) collective-permute-start(bf16[4,2,2,16,256]{4,3,2,1,0:T(8,128)(2,1)S(1)} %slice.194), channel_id=1, source_target_pairs={{0,4},{1,5},{2,6},{3,7},{4,0},{5,1},{6,2},{7,3},{8,12},{9,13},{10,... | collective-permute-start | bytes 393224 | tf_op jit(solution)/shard_map/ppermute | solution.py:154
  51.2 5.5 %collective-permute-start.7 = (bf16[2,2,2,16,256]{4,3,2,1,0:T(8,128)(2,1)S(1)}, bf16[2,2,2,16,256]{4,3,2,1,0:T(8,128)(2,1)S(1)}, u32[]{:S(2)}, u32[]{:S(2)}) collective-permute-start(bf16[2,2,2,16,256]{4,3,2,1,0:T(8,128)(2,1)S(1)} %slice.195), channel_id=1, source_target_pairs={{0,8},{1,9},{2,10},{3,11},{4,12},{5,13},{6,14},{7,15},{8,0},{9,1},... | collective-permute-start | bytes 196616 | tf_op jit(solution)/shard_map/ppermute | solution.py:154
  57.8 5.0 %collective-permute-start.8 = (bf16[65542]{0:T(1024)(128)(2,1)S(1)}, bf16[65542]{0:T(1024)(128)(2,1)S(1)}, u32[]{:S(2)}, u32[]{:S(2)}) collective-permute-start(bf16[65542]{0:T(1024)(128)(2,1)S(1)} %concatenate.26), channel_id=1, source_target_pairs={{0,16},{16,0},{1,17},{17,1},{2,18},{18,2},{3,19},{19,3},{4,20},{20... | collective-permute-start | bytes 393260 | tf_op jit(solution)/shard_map/ppermute | solution.py:184

commit v7 on v6

--- a/solution.py
+++ b/solution.py
@@ -8,32 +8,27 @@
 OVL = 16
 
 
-def split_dot(weights, bands):
-    hi = weights.astype(jnp.bfloat16)
-    rest = weights - hi.astype(jnp.float32)
-    mid = rest.astype(jnp.bfloat16)
-    low = (rest - mid.astype(jnp.float32)).astype(jnp.bfloat16)
-    total = jnp.dot(hi, bands, preferred_element_type=jnp.float32)
-    total = total + jnp.dot(mid, bands, preferred_element_type=jnp.float32)
-    return total + jnp.dot(low, bands, preferred_element_type=jnp.float32)
-
-
 def middle_kernel(
-    fwd_ref, back_ref, image_ref, proj_ref, edge_ref, ctf_ref,
-    weighted_ref, score_ref, return_ref, residual_ref,
+    place_ref, side_ref, weight_ref, image_ref, proj_ref, edge_ref, ctf_ref,
+    weighted_ref, score_ref, kept_ref, sent_ref, residual_ref,
 ):
     k = pl.program_id(1)
-    total = edge_ref.shape[0]
+    neighbours = place_ref.shape[1]
+    half = kept_ref.shape[0]
     pixels = image_ref.shape[-1]
 
-    def band_sum(q, carry):
+    def band_sum(j, carry):
         lower, upper = carry
-        lower = lower + fwd_ref[0, k, q] * edge_ref[q, 0, 0].astype(jnp.float32)
-        upper = upper + fwd_ref[1, k, q] * edge_ref[q, 1, 0].astype(jnp.float32)
+        q = place_ref[k, j]
+        s = side_ref[k, j]
+        w = weight_ref[k, j]
+        band = edge_ref[q, s, 0].astype(jnp.float32)
+        lower = lower + jnp.where(s == 0, w, 0.0) * band
+        upper = upper + jnp.where(s == 1, w, 0.0) * band
         return lower, upper
 
     zero = jnp.zeros((OVL, pixels), jnp.float32)
-    lower, upper = lax.fori_loop(0, total, band_sum, (zero, zero), unroll=8)
+    lower, upper = lax.fori_loop(0, neighbours, band_sum, (zero, zero), unroll=True)
     residual_ref[...] = image_ref[0, 0].astype(jnp.float32) - proj_ref[0, 0].astype(jnp.float32)
     residual_ref[:OVL] = residual_ref[:OVL] - upper
     residual_ref[pixels - OVL :] = residual_ref[pixels - OVL :] - lower
@@ -53,31 +48,46 @@
 
     @pl.when(k == 0)
     def _():
-        return_ref[...] = jnp.zeros_like(return_ref)
+        kept_ref[...] = jnp.zeros_like(kept_ref)
+        sent_ref[...] = jnp.zeros_like(sent_ref)
 
     bottom_rows = weighted[pixels - OVL :].astype(jnp.float32)
     top_rows = weighted[:OVL].astype(jnp.float32)
 
-    def give_back(q, carry):
-        return_ref[q, 0, 0] = return_ref[q, 0, 0] + back_ref[0, k, q] * bottom_rows
-        return_ref[q, 1, 0] = return_ref[q, 1, 0] + back_ref[1, k, q] * top_rows
+    def give_back(j, carry):
+        q = place_ref[k, j]
+        s = side_ref[k, j]
+        rows = jnp.where(s == 0, bottom_rows, top_rows)
+        part = (weight_ref[k, j] * rows).astype(jnp.bfloat16).astype(jnp.float32)
+
+        @pl.when(q < half)
+        def _():
+            kept_ref[q, s, 0] = kept_ref[q, s, 0] + part
+
+        @pl.when(q >= half)
+        def _():
+            sent_ref[q - half, s, 0] = sent_ref[q - half, s, 0] + part
+
         return carry
 
-    lax.fori_loop(0, total, give_back, 0, unroll=8)
-
-
-def middle(fwd, back, images, projected, edges_all, ctf_filter):
+    lax.fori_loop(0, neighbours, give_back, 0, unroll=True)
+
+
+def middle(place, side, weight, images, projected, edges_all, ctf_filter):
     own_count, tilt_count, pixels, _ = images.shape
     total = edges_all.shape[0]
+    half = total // 2
     tile = pl.BlockSpec((1, 1, pixels, pixels), lambda t, k: (k, t, 0, 0))
     bands = pl.BlockSpec((total, 2, 1, OVL, pixels), lambda t, k: (0, 0, t, 0, 0))
+    halves = pl.BlockSpec((half, 2, 1, OVL, pixels), lambda t, k: (0, 0, t, 0, 0))
     smem = pl.BlockSpec(memory_space=pltpu.SMEM)
-    flops = own_count * tilt_count * (8 * pixels**3 + 8 * total * OVL * pixels)
+    flops = own_count * tilt_count * 8 * pixels**3
     moved = 2 * images.size * 3 + 2 * edges_all.size + 4 * edges_all.size + 2 * ctf_filter.size
     return pl.pallas_call(
         middle_kernel,
         grid=(tilt_count, own_count),
         in_specs=[
+            smem,
             smem,
             smem,
             tile,
@@ -88,19 +98,21 @@
         out_specs=[
             tile,
             pl.BlockSpec((1, 1, 8, 128), lambda t, k: (t, k, 0, 0)),
-            bands,
+            halves,
+            halves,
         ],
         out_shape=[
             jax.ShapeDtypeStruct(images.shape, jnp.bfloat16),
             jax.ShapeDtypeStruct((tilt_count, own_count, 8, 128), jnp.float32),
-            jax.ShapeDtypeStruct(edges_all.shape, jnp.float32),
+            jax.ShapeDtypeStruct((half,) + edges_all.shape[1:], jnp.float32),
+            jax.ShapeDtypeStruct((half,) + edges_all.shape[1:], jnp.float32),
         ],
         scratch_shapes=[pltpu.VMEM((pixels, pixels), jnp.float32)],
         compiler_params=pltpu.CompilerParams(
             dimension_semantics=("arbitrary", "arbitrary")
         ),
         cost_estimate=pl.CostEstimate(flops=flops, transcendentals=0, bytes_accessed=moved),
-    )(fwd, back, images, projected, edges_all, ctf_filter)
+    )(place, side, weight, images, projected, edges_all, ctf_filter)
 
 
 def on_device(
@@ -118,14 +130,7 @@
     steps = peer_count.bit_length() - 1
     relative = nbr_owner.reshape(own_count, neighbours) ^ me
     flipped = sum(((relative >> (steps - 1 - b)) & 1) << b for b in range(steps))
-    every = jnp.arange(total)
-
-    def weights_for(blocks, side):
-        hits = (blocks * own_count + nbr_local)[:, :, None] == every[None, None, :]
-        hits = hits & (nbr_side == side)[:, :, None]
-        return jnp.sum(jnp.where(hits, nbr_weight[:, :, None], 0.0), axis=1)
-
-    fwd = [weights_for(flipped, s) for s in (0, 1)]
+    place = flipped * own_count + nbr_local
 
     halfway = jnp.einsum(
         "kij,tlj->ktil", sections, slice_cols, preferred_element_type=jnp.float32
@@ -140,13 +145,17 @@
         pairs = [(i, i ^ stride) for i in range(peer_count)]
         edges_all = jnp.concatenate((edges_all, lax.ppermute(edges_all, "dom", pairs)), axis=0)
 
-    weighted, score_tiles, returned = middle(
-        jnp.stack(fwd), jnp.stack(fwd), images, projected, edges_all, ctf_filter
+    weighted, score_tiles, kept_half, sent_half = middle(
+        place, nbr_side, nbr_weight, images, projected, edges_all, ctf_filter
     )
     score_part = jnp.sum(score_tiles[:, :, 0, 0], axis=0)
     tilt_groups = lax.axis_size("tilt")
 
-    for b in range(steps):
+    pairs = [(i, i ^ 1) for i in range(peer_count)]
+    returned = kept_half + lax.ppermute(sent_half.astype(jnp.bfloat16), "dom", pairs).astype(
+        jnp.float32
+    )
+    for b in range(1, steps):
         stride = 1 << b
         pairs = [(i, i ^ stride) for i in range(peer_count)]
         half = returned.shape[0] // 2

time: 64.7 us -> 63 us (0.974)
  matrix products: 3.06 us -> 2.12 us
  local copies, waits for them, and re-layouts: 3.96 us -> 3.28 us
    ppermute x4 -> x3, waiting for transfers between devices: 13.9 us -> 12.2 us  [on_device(): lax.ppermute(given, 'dom', pairs).astype(jnp.float32)]
    ppermute x0 -> x1, waiting for transfers between devices: none -> 1.77 us  [on_device(): lax.ppermute(sent_half.astype(jnp.bfloat16), 'dom', pairs)]
    add x4 -> x3, other arithmetic: 1.52 us -> 0.12 us  [on_device(): returned[:half] + lax.ppermute(given, 'dom', pairs).astype(jnp.float32)]
    convert_element_type x0 -> x1, other arithmetic: none -> 1.38 us  [on_device(): sent_half.astype(jnp.bfloat16)]
    slice x4 -> x3, local copies, waits for them, and re-layouts: 1.37 us -> 0.07 us  [on_device(): given = returned[half:].astype(jnp.bfloat16)]
    dot_general x1, matrix products: 1.25 us -> 0.3 us  [on_device(): jnp.einsum('tai,ktil->ktal', slice_rows, halfway, preferred_element_type=...]
    add x1 -> x2, other arithmetic: 0.01 us -> 0.75 us  [the longest x1 0.54 us: on_device(): place = flipped * own_count + nbr_local]
    unnamed x22 -> x20, local copies, waits for them, and re-layouts: 2.04 us -> 2.66 us
where the time goes in v7:
time: 63 us; the launch traced here: 62.7 us
  waiting for transfers between devices  30.7 us (49%)
  starting transfers between devices  14.2 us (23%)
  Pallas kernels  6.82 us (11%)
  other arithmetic  4.67 us (7%)
  local copies, waits for them, and re-layouts  3.28 us (5%)
  matrix products  2.12 us (3%)
  between operations  0.91 us (1%)
    ppermute x4, waiting for transfers between devices, on_device(): lax.ppermute(edges_all, 'dom', pairs)  13.3 us
    ppermute x3, waiting for transfers between devices, on_device(): lax.ppermute(given, 'dom', pairs).astype(jnp.float32)  12.2 us
    pallas_call x1, Pallas kernels, middle(): pl.pallas_call(middle_kernel, grid=(tilt_count, own_count), in_specs=[sme...  6.82 us
    ppermute x4, starting transfers between devices, on_device(): lax.ppermute(edges_all, 'dom', pairs)  6.57 us
    ppermute x3, starting transfers between devices, on_device(): lax.ppermute(given, 'dom', pairs).astype(jnp.float32)  5.93 us
    ppermute x1, waiting for transfers between devices, on_device(): parcel = lax.ppermute(parcel, 'tilt', [(0, 1), (1, 0)]).astype(jnp.float32)  3.49 us
    unnamed x20, local copies, waits for them, and re-layouts  2.66 us
    ppermute x1, waiting for transfers between devices, on_device(): lax.ppermute(sent_half.astype(jnp.bfloat16), 'dom', pairs)  1.77 us
  transfers between devices with their start and end apart: 9, of which 9 were waited for; matrix products, arithmetic and copies ran while one was open for 3% of the time, Pallas kernels for 0%

profile of v7, /device:TPU:0, one launch (start us, length us, event | category | flops | bytes accessed | tf_op | source)
XLA Modules:
  0.0 62.7 jit_solution(8262322397044652597)
XLA Ops:
  0.7 0.9 %copy-done = bf16[2,256,256]{2,1,0:T(8,128)(2,1)S(1)} copy-done((bf16[2,256,256]{2,1,0:T(8,128)(2,1)S(1)}, bf16[2,256,256]{2,1,0:T(8,128)(2,1)}, u32[]{:S(2)}) %copy-start) | copy-done | bytes 262168
  1.6 1.3 %fusion = bf16[2,2,256,256]{3,2,0,1:T(8,128)(2,1)S(1)} fusion(bf16[2,256,256]{2,1,0:T(8,128)(2,1)S(1)} %copy-done, bf16[2,256,256]{2,1,0:T(8,128)(2,1)} %param.13), kind=kOutput, calls=%fused_computation.3 | convolution fusion | flops 134479872 | bytes 1048576 | tf_op jit(solution)/shard_map/kij,tlj->ktil/dot_general | solution.py:135
  3.2 4.1 %collective-permute-start = (bf16[2,2,2,16,256]{4,3,2,1,0:T(8,128)(2,1)S(1)}, bf16[2,2,2,16,256]{4,3,2,1,0:T(8,128)(2,1)S(1)}, u32[]{:S(2)}, u32[]{:S(2)}) collective-permute-start(bf16[2,2,2,16,256]{4,3,2,1,0:T(8,128)(2,1)S(1)} %get-tuple-element.36), channel_id=1, source_target_pairs={{0,8},{1,9},{2,10},{3,11},{4,12},{5,13},{6,14},{7,15},{8,0},{9,1},... | collective-permute-start | bytes 196616 | tf_op jit(solution)/shard_map/ppermute | solution.py:146
  7.3 3.6 %collective-permute-done = bf16[2,2,2,16,256]{4,3,2,1,0:T(8,128)(2,1)S(1)} collective-permute-done((bf16[2,2,2,16,256]{4,3,2,1,0:T(8,128)(2,1)S(1)}, bf16[2,2,2,16,256]{4,3,2,1,0:T(8,128)(2,1)S(1)}, u32[]{:S(2)}, u32[]{:S(2)}) %collective-permute-start) | collective-permute-done | bytes 65568 | tf_op jit(solution)/shard_map/ppermute | solution.py:146
  11.0 0.6 %collective-permute-start.1 = (bf16[4,2,2,16,256]{4,3,2,1,0:T(8,128)(2,1)S(1)}, bf16[4,2,2,16,256]{4,3,2,1,0:T(8,128)(2,1)S(1)}, u32[]{:S(2)}, u32[]{:S(2)}) collective-permute-start(bf16[4,2,2,16,256]{4,3,2,1,0:T(8,128)(2,1)S(1)} %pad_maximum_fusion.2), channel_id=1, source_target_pairs={{0,4},{1,5},{2,6},{3,7},{4,0},{5,1},{6,2},{7,3},{8,12},{9,13},{10,... | collective-permute-start | bytes 393224 | tf_op jit(solution)/shard_map/ppermute | solution.py:146
  11.6 4.4 %collective-permute-done.1 = bf16[4,2,2,16,256]{4,3,2,1,0:T(8,128)(2,1)S(1)} collective-permute-done((bf16[4,2,2,16,256]{4,3,2,1,0:T(8,128)(2,1)S(1)}, bf16[4,2,2,16,256]{4,3,2,1,0:T(8,128)(2,1)S(1)}, u32[]{:S(2)}, u32[]{:S(2)}) %collective-permute-start.1) | collective-permute-done | bytes 131104 | tf_op jit(solution)/shard_map/ppermute | solution.py:146
  16.1 1.8 %collective-permute-start.2 = (bf16[8,2,2,16,256]{4,3,2,1,0:T(8,128)(2,1)S(1)}, bf16[8,2,2,16,256]{4,3,2,1,0:T(8,128)(2,1)S(1)}, u32[]{:S(2)}, u32[]{:S(2)}) collective-permute-start(bf16[8,2,2,16,256]{4,3,2,1,0:T(8,128)(2,1)S(1)} %pad_maximum_fusion.1), channel_id=1, source_target_pairs={{0,2},{1,3},{2,0},{3,1},{4,6},{5,7},{6,4},{7,5},{8,10},{9,11},{10,... | collective-permute-start | bytes 786440 | tf_op jit(solution)/shard_map/ppermute | solution.py:146
  17.8 4.7 %collective-permute-done.2 = bf16[8,2,2,16,256]{4,3,2,1,0:T(8,128)(2,1)S(1)} collective-permute-done((bf16[8,2,2,16,256]{4,3,2,1,0:T(8,128)(2,1)S(1)}, bf16[8,2,2,16,256]{4,3,2,1,0:T(8,128)(2,1)S(1)}, u32[]{:S(2)}, u32[]{:S(2)}) %collective-permute-start.2) | collective-permute-done | bytes 262176 | tf_op jit(solution)/shard_map/ppermute | solution.py:146
  24.0 0.6 collective-permute-done.3
  24.6 1.0 %copy-done.2 = bf16[32,2,2,16,256]{4,3,2,1,0:T(8,128)(2,1)} copy-done((bf16[32,2,2,16,256]{4,3,2,1,0:T(8,128)(2,1)}, bf16[32,2,2,16,256]{4,3,2,1,0:T(8,128)(2,1)S(1)}, u32[]{:S(2)}) %copy-start.2) | copy-done | bytes 1048600
  25.6 6.8 %shard_map.104 = (bf16[2,2,256,256]{3,2,1,0:T(8,128)(2,1)}, f32[2,2,8,128]{3,2,1,0:T(8,128)}, f32[16,2,2,16,256]{4,3,2,1,0:T(8,128)}, f32[16,2,2,16,256]{4,3,2,1,0:T(8,128)}) custom-call(s32[2,16]{1,0:T(2,128)} %add.59.place_ref, s32[2,16]{1,0:T(2,128)} %side_ref.1, f32[2,16]{1,0:T(2,128)} %weight_ref.1, bf16[2,2,256,256]{3,2,1,0:T(8,128)(2,1)} %image_ref.1, ...), custom_call_target="tpu_custom_call" | custom-call | flops 536870912 | bytes 4980736 | tf_op jit(solution)/shard_map/pallas_call | solution.py:86
  32.4 1.4 %convert_element_type.70 = bf16[16,2,2,16,256]{4,3,2,1,0:T(8,128)(2,1)S(1)} convert(f32[16,2,2,16,256]{4,3,2,1,0:T(8,128)} %get-tuple-element.32) | non-fusion elementwise | flops 262144 | bytes 1572864 | tf_op jit(solution)/shard_map/convert_element_type | solution.py:155
  34.0 1.8 %collective-permute-done.4 = bf16[16,2,2,16,256]{4,3,2,1,0:T(8,128)(2,1)S(1)} collective-permute-done((bf16[16,2,2,16,256]{4,3,2,1,0:T(8,128)(2,1)S(1)}, bf16[16,2,2,16,256]{4,3,2,1,0:T(8,128)(2,1)S(1)}, u32[]{:S(2)}, u32[]{:S(2)}) %collective-permute-start.4) | collective-permute-done | bytes 524320 | tf_op jit(solution)/shard_map/ppermute | solution.py:155
  36.0 1.8 %collective-permute-start.5 = (bf16[8,2,2,16,256]{4,3,2,1,0:T(8,128)(2,1)S(1)}, bf16[8,2,2,16,256]{4,3,2,1,0:T(8,128)(2,1)S(1)}, u32[]{:S(2)}, u32[]{:S(2)}) collective-permute-start(bf16[8,2,2,16,256]{4,3,2,1,0:T(8,128)(2,1)S(1)} %slice.180), channel_id=1, source_target_pairs={{0,2},{1,3},{2,0},{3,1},{4,6},{5,7},{6,4},{7,5},{8,10},{9,11},{10,... | collective-permute-start | bytes 786440 | tf_op jit(solution)/shard_map/ppermute | solution.py:163
  37.8 6.6 %collective-permute-done.5 = bf16[8,2,2,16,256]{4,3,2,1,0:T(8,128)(2,1)S(1)} collective-permute-done((bf16[8,2,2,16,256]{4,3,2,1,0:T(8,128)(2,1)S(1)}, bf16[8,2,2,16,256]{4,3,2,1,0:T(8,128)(2,1)S(1)}, u32[]{:S(2)}, u32[]{:S(2)}) %collective-permute-start.5) | collective-permute-done | bytes 262176 | tf_op jit(solution)/shard_map/ppermute | solution.py:163
  44.6 0.8 %collective-permute-start.6 = (bf16[4,2,2,16,256]{4,3,2,1,0:T(8,128)(2,1)S(1)}, bf16[4,2,2,16,256]{4,3,2,1,0:T(8,128)(2,1)S(1)}, u32[]{:S(2)}, u32[]{:S(2)}) collective-permute-start(bf16[4,2,2,16,256]{4,3,2,1,0:T(8,128)(2,1)S(1)} %slice.181), channel_id=1, source_target_pairs={{0,4},{1,5},{2,6},{3,7},{4,0},{5,1},{6,2},{7,3},{8,12},{9,13},{10,... | collective-permute-start | bytes 393224 | tf_op jit(solution)/shard_map/ppermute | solution.py:163
  45.4 0.8 %slice_reduce_fusion = f32[2]{0:T(128)S(1)} fusion(f32[2,2,8,128]{3,2,1,0:T(8,128)} %get-tuple-element.33), kind=kLoop, calls=%fused_computation.42 | loop fusion | flops 2 | bytes 24 | tf_op jit(solution)/shard_map/reduce_sum | solution.py:151
  46.2 3.4 %collective-permute-done.6 = bf16[4,2,2,16,256]{4,3,2,1,0:T(8,128)(2,1)S(1)} collective-permute-done((bf16[4,2,2,16,256]{4,3,2,1,0:T(8,128)(2,1)S(1)}, bf16[4,2,2,16,256]{4,3,2,1,0:T(8,128)(2,1)S(1)}, u32[]{:S(2)}, u32[]{:S(2)}) %collective-permute-start.6) | collective-permute-done | bytes 131104 | tf_op jit(solution)/shard_map/ppermute | solution.py:163
  49.7 3.3 %collective-permute-start.7 = (bf16[2,2,2,16,256]{4,3,2,1,0:T(8,128)(2,1)S(1)}, bf16[2,2,2,16,256]{4,3,2,1,0:T(8,128)(2,1)S(1)}, u32[]{:S(2)}, u32[]{:S(2)}) collective-permute-start(bf16[2,2,2,16,256]{4,3,2,1,0:T(8,128)(2,1)S(1)} %slice.182), channel_id=1, source_target_pairs={{0,8},{1,9},{2,10},{3,11},{4,12},{5,13},{6,14},{7,15},{8,0},{9,1},... | collective-permute-start | bytes 196616 | tf_op jit(solution)/shard_map/ppermute | solution.py:163
  53.1 2.1 %collective-permute-done.7 = bf16[2,2,2,16,256]{4,3,2,1,0:T(8,128)(2,1)S(1)} collective-permute-done((bf16[2,2,2,16,256]{4,3,2,1,0:T(8,128)(2,1)S(1)}, bf16[2,2,2,16,256]{4,3,2,1,0:T(8,128)(2,1)S(1)}, u32[]{:S(2)}, u32[]{:S(2)}) %collective-permute-start.7) | collective-permute-done | bytes 65568 | tf_op jit(solution)/shard_map/ppermute | solution.py:163
  56.3 1.5 %collective-permute-start.8 = (bf16[65542]{0:T(1024)(128)(2,1)S(1)}, bf16[65542]{0:T(1024)(128)(2,1)S(1)}, u32[]{:S(2)}, u32[]{:S(2)}) collective-permute-start(bf16[65542]{0:T(1024)(128)(2,1)S(1)} %concatenate.26), channel_id=1, source_target_pairs={{0,16},{16,0},{1,17},{17,1},{2,18},{18,2},{3,19},{19,3},{4,20},{20... | collective-permute-start | bytes 393260 | tf_op jit(solution)/shard_map/ppermute | solution.py:193
  57.8 3.5 %collective-permute-done.8 = bf16[65542]{0:T(1024)(128)(2,1)S(1)} collective-permute-done((bf16[65542]{0:T(1024)(128)(2,1)S(1)}, bf16[65542]{0:T(1024)(128)(2,1)S(1)}, u32[]{:S(2)}, u32[]{:S(2)}) %collective-permute-start.8) | collective-permute-done | bytes 131116 | tf_op jit(solution)/shard_map/ppermute | solution.py:193
  61.3 0.6 fusion.19
  62.0 0.7 %dynamic-slice_add_fusion = f32[2,128,256]{2,1,0:T(8,128)} fusion(f32[2,128,256]{2,1,0:T(8,128)S(1)} %reshape.119, f32[2,256,256]{2,1,0:T(8,128)S(1)} %fusion.3, s32[]{:T(128)S(6)} %select_n.6), kind=kLoop, calls=%fused_computation.23 | loop fusion | flops 65536 | bytes 786436 | tf_op jit(solution)/shard_map/add | solution.py:194
  (47 shorter events, 3.6 us)
Async XLA Ops:
  0.6 1.0 %copy-start = (bf16[2,256,256]{2,1,0:T(8,128)(2,1)S(1)}, bf16[2,256,256]{2,1,0:T(8,128)(2,1)}, u32[]{:S(2)}) copy-start(bf16[2,256,256]{2,1,0:T(8,128)(2,1)} %param.16) | copy-start | bytes 786436
  0.6 2.2 %copy-start.4 = (bf16[2,256,256]{2,1,0:T(8,128)(2,1)S(1)}, bf16[2,256,256]{2,1,0:T(8,128)(2,1)}, u32[]{:S(2)}) copy-start(bf16[2,256,256]{2,1,0:T(8,128)(2,1)} %param.15) | copy-start | bytes 786436
  3.2 12.9 %copy-start.1 = (bf16[2,2,256,256]{3,2,1,0:T(8,128)(2,1)}, bf16[2,2,256,256]{3,2,1,0:T(8,128)(2,1)S(1)}, u32[]{:S(2)}) copy-start(bf16[2,2,256,256]{3,2,1,0:T(8,128)(2,1)S(1)} %fusion.2.proj_ref) | copy-start | bytes 1572868
  3.2 7.7 %collective-permute-start = (bf16[2,2,2,16,256]{4,3,2,1,0:T(8,128)(2,1)S(1)}, bf16[2,2,2,16,256]{4,3,2,1,0:T(8,128)(2,1)S(1)}, u32[]{:S(2)}, u32[]{:S(2)}) collective-permute-start(bf16[2,2,2,16,256]{4,3,2,1,0:T(8,128)(2,1)S(1)} %get-tuple-element.36), channel_id=1, source_target_pairs={{0,8},{1,9},{2,10},{3,11},{4,12},{5,13},{6,14},{7,15},{8,0},{9,1},... | collective-permute-start | bytes 196616 | tf_op jit(solution)/shard_map/ppermute | solution.py:146
  11.0 5.0 %collective-permute-start.1 = (bf16[4,2,2,16,256]{4,3,2,1,0:T(8,128)(2,1)S(1)}, bf16[4,2,2,16,256]{4,3,2,1,0:T(8,128)(2,1)S(1)}, u32[]{:S(2)}, u32[]{:S(2)}) collective-permute-start(bf16[4,2,2,16,256]{4,3,2,1,0:T(8,128)(2,1)S(1)} %pad_maximum_fusion.2), channel_id=1, source_target_pairs={{0,4},{1,5},{2,6},{3,7},{4,0},{5,1},{6,2},{7,3},{8,12},{9,13},{10,... | collective-permute-start | bytes 393224 | tf_op jit(solution)/shard_map/ppermute | solution.py:146
  16.1 6.4 %collective-permute-start.2 = (bf16[8,2,2,16,256]{4,3,2,1,0:T(8,128)(2,1)S(1)}, bf16[8,2,2,16,256]{4,3,2,1,0:T(8,128)(2,1)S(1)}, u32[]{:S(2)}, u32[]{:S(2)}) collective-permute-start(bf16[8,2,2,16,256]{4,3,2,1,0:T(8,128)(2,1)S(1)} %pad_maximum_fusion.1), channel_id=1, source_target_pairs={{0,2},{1,3},{2,0},{3,1},{4,6},{5,7},{6,4},{7,5},{8,10},{9,11},{10,... | collective-permute-start | bytes 786440 | tf_op jit(solution)/shard_map/ppermute | solution.py:146
  17.8 4.8 %copy-start.6 = (s32[2,2,8]{2,1,0:T(2,128)S(1)}, s32[2,2,8]{2,1,0:T(2,128)}, u32[]{:S(2)}) copy-start(s32[2,2,8]{2,1,0:T(2,128)} %param.18) | copy-start | bytes 388
  22.6 2.0 %collective-permute-start.3 = (bf16[16,2,2,16,256]{4,3,2,1,0:T(8,128)(2,1)S(1)}, bf16[16,2,2,16,256]{4,3,2,1,0:T(8,128)(2,1)S(1)}, u32[]{:S(2)}, u32[]{:S(2)}) collective-permute-start(bf16[16,2,2,16,256]{4,3,2,1,0:T(8,128)(2,1)S(1)} %pad_maximum_fusion), channel_id=1, source_target_pairs={{0,1},{1,0},{2,3},{3,2},{4,5},{5,4},{6,7},{7,6},{8,9},{9,8},{10,11... | collective-permute-start | bytes 1572872 | tf_op jit(solution)/shard_map/ppermute | solution.py:146
  22.7 0.7 %copy-start.7 = (s32[2,16]{1,0:T(2,128)S(1)}, s32[2,16]{1,0:T(2,128)}, u32[]{:S(2)}) copy-start(s32[2,16]{1,0:T(2,128)} %param.19) | copy-start | bytes 388
  24.6 1.0 %copy-start.2 = (bf16[32,2,2,16,256]{4,3,2,1,0:T(8,128)(2,1)}, bf16[32,2,2,16,256]{4,3,2,1,0:T(8,128)(2,1)S(1)}, u32[]{:S(2)}) copy-start(bf16[32,2,2,16,256]{4,3,2,1,0:T(8,128)(2,1)S(1)} %constant_dynamic-update-slice_fusion.edge_ref) | copy-start | bytes 3145732
  32.4 3.4 %copy-start.3 = (f32[16,2,2,16,256]{4,3,2,1,0:T(8,128)S(1)}, f32[16,2,2,16,256]{4,3,2,1,0:T(8,128)}, u32[]{:S(2)}) copy-start(f32[16,2,2,16,256]{4,3,2,1,0:T(8,128)} %get-tuple-element.31) | copy-start | bytes 3145732
  33.8 2.0 %collective-permute-start.4 = (bf16[16,2,2,16,256]{4,3,2,1,0:T(8,128)(2,1)S(1)}, bf16[16,2,2,16,256]{4,3,2,1,0:T(8,128)(2,1)S(1)}, u32[]{:S(2)}, u32[]{:S(2)}) collective-permute-start(bf16[16,2,2,16,256]{4,3,2,1,0:T(8,128)(2,1)S(1)} %convert_element_type.70), channel_id=1, source_target_pairs={{0,1},{1,0},{2,3},{3,2},{4,5},{5,4},{6,7},{7,6},{8,9},{9,8},{10,11... | collective-permute-start | bytes 1572872 | tf_op jit(solution)/shard_map/ppermute | solution.py:155
  36.0 8.4 %collective-permute-start.5 = (bf16[8,2,2,16,256]{4,3,2,1,0:T(8,128)(2,1)S(1)}, bf16[8,2,2,16,256]{4,3,2,1,0:T(8,128)(2,1)S(1)}, u32[]{:S(2)}, u32[]{:S(2)}) collective-permute-start(bf16[8,2,2,16,256]{4,3,2,1,0:T(8,128)(2,1)S(1)} %slice.180), channel_id=1, source_target_pairs={{0,2},{1,3},{2,0},{3,1},{4,6},{5,7},{6,4},{7,5},{8,10},{9,11},{10,... | collective-permute-start | bytes 786440 | tf_op jit(solution)/shard_map/ppermute | solution.py:163
  44.5 8.4 %copy-start.5 = (bf16[2,2,256,256]{3,2,1,0:T(8,128)(2,1)S(1)}, bf16[2,2,256,256]{3,2,1,0:T(8,128)(2,1)}, u32[]{:S(2)}) copy-start(bf16[2,2,256,256]{3,2,1,0:T(8,128)(2,1)} %get-tuple-element.30) | copy-start | bytes 1572868
  44.6 5.0 %collective-permute-start.6 = (bf16[4,2,2,16,256]{4,3,2,1,0:T(8,128)(2,1)S(1)}, bf16[4,2,2,16,256]{4,3,2,1,0:T(8,128)(2,1)S(1)}, u32[]{:S(2)}, u32[]{:S(2)}) collective-permute-start(bf16[4,2,2,16,256]{4,3,2,1,0:T(8,128)(2,1)S(1)} %slice.181), channel_id=1, source_target_pairs={{0,4},{1,5},{2,6},{3,7},{4,0},{5,1},{6,2},{7,3},{8,12},{9,13},{10,... | collective-permute-start | bytes 393224 | tf_op jit(solution)/shard_map/ppermute | solution.py:163
  49.7 5.6 %collective-permute-start.7 = (bf16[2,2,2,16,256]{4,3,2,1,0:T(8,128)(2,1)S(1)}, bf16[2,2,2,16,256]{4,3,2,1,0:T(8,128)(2,1)S(1)}, u32[]{:S(2)}, u32[]{:S(2)}) collective-permute-start(bf16[2,2,2,16,256]{4,3,2,1,0:T(8,128)(2,1)S(1)} %slice.182), channel_id=1, source_target_pairs={{0,8},{1,9},{2,10},{3,11},{4,12},{5,13},{6,14},{7,15},{8,0},{9,1},... | collective-permute-start | bytes 196616 | tf_op jit(solution)/shard_map/ppermute | solution.py:163
  56.3 5.0 %collective-permute-start.8 = (bf16[65542]{0:T(1024)(128)(2,1)S(1)}, bf16[65542]{0:T(1024)(128)(2,1)S(1)}, u32[]{:S(2)}, u32[]{:S(2)}) collective-permute-start(bf16[65542]{0:T(1024)(128)(2,1)S(1)} %concatenate.26), channel_id=1, source_target_pairs={{0,16},{16,0},{1,17},{17,1},{2,18},{18,2},{3,19},{19,3},{4,20},{20... | collective-permute-start | bytes 393260 | tf_op jit(solution)/shard_map/ppermute | solution.py:193

commit v8 on v7

--- a/solution.py
+++ b/solution.py
@@ -10,94 +10,88 @@
 
 def middle_kernel(
     place_ref, side_ref, weight_ref, image_ref, proj_ref, edge_ref, ctf_ref,
-    weighted_ref, score_ref, kept_ref, sent_ref, residual_ref,
+    weighted_ref, score_ref, kept_ref, sent_ref, residual_ref, return_ref,
 ):
-    k = pl.program_id(1)
-    neighbours = place_ref.shape[1]
+    own_count, neighbours = place_ref.shape
     half = kept_ref.shape[0]
     pixels = image_ref.shape[-1]
-
-    def band_sum(j, carry):
-        lower, upper = carry
-        q = place_ref[k, j]
-        s = side_ref[k, j]
-        w = weight_ref[k, j]
-        band = edge_ref[q, s, 0].astype(jnp.float32)
-        lower = lower + jnp.where(s == 0, w, 0.0) * band
-        upper = upper + jnp.where(s == 1, w, 0.0) * band
-        return lower, upper
-
+    ctf = ctf_ref[0]
     zero = jnp.zeros((OVL, pixels), jnp.float32)
-    lower, upper = lax.fori_loop(0, neighbours, band_sum, (zero, zero), unroll=True)
-    residual_ref[...] = image_ref[0, 0].astype(jnp.float32) - proj_ref[0, 0].astype(jnp.float32)
-    residual_ref[:OVL] = residual_ref[:OVL] - upper
-    residual_ref[pixels - OVL :] = residual_ref[pixels - OVL :] - lower
-    residual = residual_ref[...].astype(jnp.bfloat16)
-    ctf = ctf_ref[0]
-    smoothed = jnp.dot(ctf, residual, preferred_element_type=jnp.float32).astype(jnp.bfloat16)
-    filtered = lax.dot_general(
-        smoothed, ctf, (((1,), (1,)), ((), ())), preferred_element_type=jnp.float32
-    )
-    score_ref[...] = jnp.full(score_ref.shape, jnp.sum(filtered * filtered), jnp.float32)
-    reverse = lax.dot_general(
-        ctf, filtered.astype(jnp.bfloat16), (((0,), (0,)), ((), ())),
-        preferred_element_type=jnp.float32,
-    ).astype(jnp.bfloat16)
-    weighted = jnp.dot(reverse, ctf, preferred_element_type=jnp.float32).astype(jnp.bfloat16)
-    weighted_ref[0, 0] = weighted
-
-    @pl.when(k == 0)
-    def _():
-        kept_ref[...] = jnp.zeros_like(kept_ref)
-        sent_ref[...] = jnp.zeros_like(sent_ref)
-
-    bottom_rows = weighted[pixels - OVL :].astype(jnp.float32)
-    top_rows = weighted[:OVL].astype(jnp.float32)
-
-    def give_back(j, carry):
-        q = place_ref[k, j]
-        s = side_ref[k, j]
-        rows = jnp.where(s == 0, bottom_rows, top_rows)
-        part = (weight_ref[k, j] * rows).astype(jnp.bfloat16).astype(jnp.float32)
-
-        @pl.when(q < half)
-        def _():
-            kept_ref[q, s, 0] = kept_ref[q, s, 0] + part
-
-        @pl.when(q >= half)
-        def _():
-            sent_ref[q - half, s, 0] = sent_ref[q - half, s, 0] + part
-
-        return carry
-
-    lax.fori_loop(0, neighbours, give_back, 0, unroll=True)
+    edge_rows = []
+    for k in range(own_count):
+
+        def band_sum(j, carry, k=k):
+            lower, upper = carry
+            q = place_ref[k, j]
+            s = side_ref[k, j]
+            w = weight_ref[k, j]
+            band = edge_ref[q, s, 0].astype(jnp.float32)
+            lower = lower + jnp.where(s == 0, w, 0.0) * band
+            upper = upper + jnp.where(s == 1, w, 0.0) * band
+            return lower, upper
+
+        lower, upper = lax.fori_loop(0, neighbours, band_sum, (zero, zero), unroll=True)
+        residual_ref[k] = image_ref[k, 0].astype(jnp.float32) - proj_ref[k, 0].astype(jnp.float32)
+        residual_ref[k, :OVL] = residual_ref[k, :OVL] - upper
+        residual_ref[k, pixels - OVL :] = residual_ref[k, pixels - OVL :] - lower
+        residual = residual_ref[k].astype(jnp.bfloat16)
+        smoothed = jnp.dot(ctf, residual, preferred_element_type=jnp.float32).astype(jnp.bfloat16)
+        filtered = lax.dot_general(
+            smoothed, ctf, (((1,), (1,)), ((), ())), preferred_element_type=jnp.float32
+        )
+        score_ref[0, k] = jnp.full(score_ref.shape[2:], jnp.sum(filtered * filtered), jnp.float32)
+        reverse = lax.dot_general(
+            ctf, filtered.astype(jnp.bfloat16), (((0,), (0,)), ((), ())),
+            preferred_element_type=jnp.float32,
+        ).astype(jnp.bfloat16)
+        weighted = jnp.dot(reverse, ctf, preferred_element_type=jnp.float32).astype(jnp.bfloat16)
+        weighted_ref[k, 0] = weighted
+        edge_rows.append(
+            (weighted[pixels - OVL :].astype(jnp.float32), weighted[:OVL].astype(jnp.float32))
+        )
+
+    return_ref[...] = jnp.zeros_like(return_ref)
+    for k in range(own_count):
+        bottom_rows, top_rows = edge_rows[k]
+
+        def give_back(j, carry, k=k, bottom_rows=bottom_rows, top_rows=top_rows):
+            q = place_ref[k, j]
+            s = side_ref[k, j]
+            rows = jnp.where(s == 0, bottom_rows, top_rows)
+            part = (weight_ref[k, j] * rows).astype(jnp.bfloat16).astype(jnp.float32)
+            return_ref[q, s] = return_ref[q, s] + part
+            return carry
+
+        lax.fori_loop(0, neighbours, give_back, 0, unroll=True)
+    kept_ref[:, :, 0] = return_ref[:half]
+    sent_ref[:, :, 0] = return_ref[half:].astype(jnp.bfloat16)
 
 
 def middle(place, side, weight, images, projected, edges_all, ctf_filter):
     own_count, tilt_count, pixels, _ = images.shape
     total = edges_all.shape[0]
     half = total // 2
-    tile = pl.BlockSpec((1, 1, pixels, pixels), lambda t, k: (k, t, 0, 0))
-    bands = pl.BlockSpec((total, 2, 1, OVL, pixels), lambda t, k: (0, 0, t, 0, 0))
-    halves = pl.BlockSpec((half, 2, 1, OVL, pixels), lambda t, k: (0, 0, t, 0, 0))
+    tiles = pl.BlockSpec((own_count, 1, pixels, pixels), lambda t: (0, t, 0, 0))
+    bands = pl.BlockSpec((total, 2, 1, OVL, pixels), lambda t: (0, 0, t, 0, 0))
+    halves = pl.BlockSpec((half, 2, 1, OVL, pixels), lambda t: (0, 0, t, 0, 0))
     smem = pl.BlockSpec(memory_space=pltpu.SMEM)
     flops = own_count * tilt_count * 8 * pixels**3
-    moved = 2 * images.size * 3 + 2 * edges_all.size + 4 * edges_all.size + 2 * ctf_filter.size
+    moved = 2 * images.size * 3 + 2 * edges_all.size + 3 * edges_all.size + 2 * ctf_filter.size
     return pl.pallas_call(
         middle_kernel,
-        grid=(tilt_count, own_count),
+        grid=(tilt_count,),
         in_specs=[
             smem,
             smem,
             smem,
-            tile,
-            tile,
+            tiles,
+            tiles,
             bands,
-            pl.BlockSpec((1, pixels, pixels), lambda t, k: (t, 0, 0)),
+            pl.BlockSpec((1, pixels, pixels), lambda t: (t, 0, 0)),
         ],
         out_specs=[
-            tile,
-            pl.BlockSpec((1, 1, 8, 128), lambda t, k: (t, k, 0, 0)),
+            tiles,
+            pl.BlockSpec((1, own_count, 8, 128), lambda t: (t, 0, 0, 0)),
             halves,
             halves,
         ],
@@ -105,12 +99,13 @@
             jax.ShapeDtypeStruct(images.shape, jnp.bfloat16),
             jax.ShapeDtypeStruct((tilt_count, own_count, 8, 128), jnp.float32),
             jax.ShapeDtypeStruct((half,) + edges_all.shape[1:], jnp.float32),
-            jax.ShapeDtypeStruct((half,) + edges_all.shape[1:], jnp.float32),
-        ],
-        scratch_shapes=[pltpu.VMEM((pixels, pixels), jnp.float32)],
-        compiler_params=pltpu.CompilerParams(
-            dimension_semantics=("arbitrary", "arbitrary")
-        ),
+            jax.ShapeDtypeStruct((half,) + edges_all.shape[1:], jnp.bfloat16),
+        ],
+        scratch_shapes=[
+            pltpu.VMEM((own_count, pixels, pixels), jnp.float32),
+            pltpu.VMEM((total, 2, OVL, pixels), jnp.float32),
+        ],
+        compiler_params=pltpu.CompilerParams(dimension_semantics=("arbitrary",)),
         cost_estimate=pl.CostEstimate(flops=flops, transcendentals=0, bytes_accessed=moved),
     )(place, side, weight, images, projected, edges_all, ctf_filter)
 
@@ -152,9 +147,7 @@
     tilt_groups = lax.axis_size("tilt")
 
     pairs = [(i, i ^ 1) for i in range(peer_count)]
-    returned = kept_half + lax.ppermute(sent_half.astype(jnp.bfloat16), "dom", pairs).astype(
-        jnp.float32
-    )
+    returned = kept_half + lax.ppermute(sent_half, "dom", pairs).astype(jnp.float32)
     for b in range(1, steps):
         stride = 1 << b
         pairs = [(i, i ^ stride) for i in range(peer_count)]

time: 63 us -> 61 us (0.968)
  Pallas kernels: 6.82 us -> 4.85 us
    pallas_call x1, Pallas kernels: 6.82 us -> 4.85 us  [middle(): pl.pallas_call(middle_kernel, grid=(tilt_count,), in_specs=[smem, smem, s...]
    convert_element_type x1 -> x0, other arithmetic: 1.38 us -> none  [on_device(): sent_half.astype(jnp.bfloat16)]
    add x1, other arithmetic: 0.2 us -> 1.4 us  [on_device(): kept_half + lax.ppermute(sent_half, 'dom', pairs).astype(jnp.float32)]
    unnamed x20 -> x18, local copies, waits for them, and re-layouts: 2.66 us -> 2.66 us
where the time goes in v8:
time: 61 us; the launch traced here: 60.7 us
  waiting for transfers between devices  30.9 us (51%)
  starting transfers between devices  14.1 us (23%)
  Pallas kernels  4.85 us (8%)
  other arithmetic  4.5 us (7%)
  local copies, waits for them, and re-layouts  3.28 us (5%)
  matrix products  2.12 us (3%)
  between operations  0.9 us (1%)
    ppermute x4, waiting for transfers between devices, on_device(): lax.ppermute(edges_all, 'dom', pairs)  13.3 us
    ppermute x3, waiting for transfers between devices, on_device(): lax.ppermute(given, 'dom', pairs).astype(jnp.float32)  12.2 us
    ppermute x4, starting transfers between devices, on_device(): lax.ppermute(edges_all, 'dom', pairs)  6.57 us
    ppermute x3, starting transfers between devices, on_device(): lax.ppermute(given, 'dom', pairs).astype(jnp.float32)  5.92 us
    pallas_call x1, Pallas kernels, middle(): pl.pallas_call(middle_kernel, grid=(tilt_count,), in_specs=[smem, smem, s...  4.85 us
    ppermute x1, waiting for transfers between devices, on_device(): parcel = lax.ppermute(parcel, 'tilt', [(0, 1), (1, 0)]).astype(jnp.float32)  3.49 us
    unnamed x18, local copies, waits for them, and re-layouts  2.66 us
    ppermute x1, waiting for transfers between devices, on_device(): lax.ppermute(sent_half, 'dom', pairs).astype(jnp.float32)  1.99 us
  transfers between devices with their start and end apart: 9, of which 9 were waited for; matrix products, arithmetic and copies ran while one was open for 3% of the time, Pallas kernels for 0%

profile of v8, /device:TPU:0, one launch (start us, length us, event | category | flops | bytes accessed | tf_op | source)
XLA Modules:
  0.0 60.7 jit_solution(4790686153986752321)
XLA Ops:
  0.7 0.9 %copy-done = bf16[2,256,256]{2,1,0:T(8,128)(2,1)S(1)} copy-done((bf16[2,256,256]{2,1,0:T(8,128)(2,1)S(1)}, bf16[2,256,256]{2,1,0:T(8,128)(2,1)}, u32[]{:S(2)}) %copy-start) | copy-done | bytes 262168
  1.6 1.3 %fusion = bf16[2,2,256,256]{3,2,0,1:T(8,128)(2,1)S(1)} fusion(bf16[2,256,256]{2,1,0:T(8,128)(2,1)S(1)} %copy-done, bf16[2,256,256]{2,1,0:T(8,128)(2,1)} %param.13), kind=kOutput, calls=%fused_computation.3 | convolution fusion | flops 134479872 | bytes 1048576 | tf_op jit(solution)/shard_map/kij,tlj->ktil/dot_general | solution.py:130
  3.2 4.1 %collective-permute-start = (bf16[2,2,2,16,256]{4,3,2,1,0:T(8,128)(2,1)S(1)}, bf16[2,2,2,16,256]{4,3,2,1,0:T(8,128)(2,1)S(1)}, u32[]{:S(2)}, u32[]{:S(2)}) collective-permute-start(bf16[2,2,2,16,256]{4,3,2,1,0:T(8,128)(2,1)S(1)} %get-tuple-element.36), channel_id=1, source_target_pairs={{0,8},{1,9},{2,10},{3,11},{4,12},{5,13},{6,14},{7,15},{8,0},{9,1},... | collective-permute-start | bytes 196616 | tf_op jit(solution)/shard_map/ppermute | solution.py:141
  7.3 3.6 %collective-permute-done = bf16[2,2,2,16,256]{4,3,2,1,0:T(8,128)(2,1)S(1)} collective-permute-done((bf16[2,2,2,16,256]{4,3,2,1,0:T(8,128)(2,1)S(1)}, bf16[2,2,2,16,256]{4,3,2,1,0:T(8,128)(2,1)S(1)}, u32[]{:S(2)}, u32[]{:S(2)}) %collective-permute-start) | collective-permute-done | bytes 65568 | tf_op jit(solution)/shard_map/ppermute | solution.py:141
  11.0 0.6 %collective-permute-start.1 = (bf16[4,2,2,16,256]{4,3,2,1,0:T(8,128)(2,1)S(1)}, bf16[4,2,2,16,256]{4,3,2,1,0:T(8,128)(2,1)S(1)}, u32[]{:S(2)}, u32[]{:S(2)}) collective-permute-start(bf16[4,2,2,16,256]{4,3,2,1,0:T(8,128)(2,1)S(1)} %pad_maximum_fusion.2), channel_id=1, source_target_pairs={{0,4},{1,5},{2,6},{3,7},{4,0},{5,1},{6,2},{7,3},{8,12},{9,13},{10,... | collective-permute-start | bytes 393224 | tf_op jit(solution)/shard_map/ppermute | solution.py:141
  11.6 4.4 %collective-permute-done.1 = bf16[4,2,2,16,256]{4,3,2,1,0:T(8,128)(2,1)S(1)} collective-permute-done((bf16[4,2,2,16,256]{4,3,2,1,0:T(8,128)(2,1)S(1)}, bf16[4,2,2,16,256]{4,3,2,1,0:T(8,128)(2,1)S(1)}, u32[]{:S(2)}, u32[]{:S(2)}) %collective-permute-start.1) | collective-permute-done | bytes 131104 | tf_op jit(solution)/shard_map/ppermute | solution.py:141
  16.1 1.8 %collective-permute-start.2 = (bf16[8,2,2,16,256]{4,3,2,1,0:T(8,128)(2,1)S(1)}, bf16[8,2,2,16,256]{4,3,2,1,0:T(8,128)(2,1)S(1)}, u32[]{:S(2)}, u32[]{:S(2)}) collective-permute-start(bf16[8,2,2,16,256]{4,3,2,1,0:T(8,128)(2,1)S(1)} %pad_maximum_fusion.1), channel_id=1, source_target_pairs={{0,2},{1,3},{2,0},{3,1},{4,6},{5,7},{6,4},{7,5},{8,10},{9,11},{10,... | collective-permute-start | bytes 786440 | tf_op jit(solution)/shard_map/ppermute | solution.py:141
  17.8 4.7 %collective-permute-done.2 = bf16[8,2,2,16,256]{4,3,2,1,0:T(8,128)(2,1)S(1)} collective-permute-done((bf16[8,2,2,16,256]{4,3,2,1,0:T(8,128)(2,1)S(1)}, bf16[8,2,2,16,256]{4,3,2,1,0:T(8,128)(2,1)S(1)}, u32[]{:S(2)}, u32[]{:S(2)}) %collective-permute-start.2) | collective-permute-done | bytes 262176 | tf_op jit(solution)/shard_map/ppermute | solution.py:141
  22.8 0.6 copy-done.6
  24.6 1.0 %copy-done.2 = bf16[32,2,2,16,256]{4,3,2,1,0:T(8,128)(2,1)} copy-done((bf16[32,2,2,16,256]{4,3,2,1,0:T(8,128)(2,1)}, bf16[32,2,2,16,256]{4,3,2,1,0:T(8,128)(2,1)S(1)}, u32[]{:S(2)}) %copy-start.2) | copy-done | bytes 1048600
  25.6 4.8 %shard_map.104 = (bf16[2,2,256,256]{3,2,1,0:T(8,128)(2,1)}, f32[2,2,8,128]{3,2,1,0:T(8,128)}, f32[16,2,2,16,256]{4,3,2,1,0:T(8,128)}, bf16[16,2,2,16,256]{4,3,2,1,0:T(8,128)(2,1)}) custom-call(s32[2,16]{1,0:T(2,128)} %add.59.place_ref, s32[2,16]{1,0:T(2,128)} %side_ref.1, f32[2,16]{1,0:T(2,128)} %weight_ref.1, bf16[2,2,256,256]{3,2,1,0:T(8,128)(2,1)} %image_ref.1, ...), custom_call_target="tpu_custom_call" | custom-call | flops 536870912 | bytes 4456448 | tf_op jit(solution)/shard_map/pallas_call | solution.py:80
  30.6 2.0 %collective-permute-done.4 = bf16[16,2,2,16,256]{4,3,2,1,0:T(8,128)(2,1)S(1)} collective-permute-done((bf16[16,2,2,16,256]{4,3,2,1,0:T(8,128)(2,1)}, bf16[16,2,2,16,256]{4,3,2,1,0:T(8,128)(2,1)S(1)}, u32[]{:S(2)}, u32[]{:S(2)}) %collective-permute-start.4) | collective-permute-done | bytes 524320 | tf_op jit(solution)/shard_map/ppermute | solution.py:150
  32.6 1.4 %convert_add_fusion = f32[16,2,2,16,256]{4,3,2,1,0:T(8,128)S(1)} fusion(f32[16,2,2,16,256]{4,3,2,1,0:T(8,128)} %get-tuple-element.31, bf16[16,2,2,16,256]{4,3,2,1,0:T(8,128)(2,1)S(1)} %collective-permute-done.4), kind=kLoop, calls=%fused_computation.8 | loop fusion | flops 524288 | bytes 2621440 | tf_op jit(solution)/shard_map/add | solution.py:150
  34.0 1.8 %collective-permute-start.5 = (bf16[8,2,2,16,256]{4,3,2,1,0:T(8,128)(2,1)S(1)}, bf16[8,2,2,16,256]{4,3,2,1,0:T(8,128)(2,1)S(1)}, u32[]{:S(2)}, u32[]{:S(2)}) collective-permute-start(bf16[8,2,2,16,256]{4,3,2,1,0:T(8,128)(2,1)S(1)} %slice.180), channel_id=1, source_target_pairs={{0,2},{1,3},{2,0},{3,1},{4,6},{5,7},{6,4},{7,5},{8,10},{9,11},{10,... | collective-permute-start | bytes 786440 | tf_op jit(solution)/shard_map/ppermute | solution.py:156
  35.8 6.6 %collective-permute-done.5 = bf16[8,2,2,16,256]{4,3,2,1,0:T(8,128)(2,1)S(1)} collective-permute-done((bf16[8,2,2,16,256]{4,3,2,1,0:T(8,128)(2,1)S(1)}, bf16[8,2,2,16,256]{4,3,2,1,0:T(8,128)(2,1)S(1)}, u32[]{:S(2)}, u32[]{:S(2)}) %collective-permute-start.5) | collective-permute-done | bytes 262176 | tf_op jit(solution)/shard_map/ppermute | solution.py:156
  42.6 0.8 %collective-permute-start.6 = (bf16[4,2,2,16,256]{4,3,2,1,0:T(8,128)(2,1)S(1)}, bf16[4,2,2,16,256]{4,3,2,1,0:T(8,128)(2,1)S(1)}, u32[]{:S(2)}, u32[]{:S(2)}) collective-permute-start(bf16[4,2,2,16,256]{4,3,2,1,0:T(8,128)(2,1)S(1)} %slice.181), channel_id=1, source_target_pairs={{0,4},{1,5},{2,6},{3,7},{4,0},{5,1},{6,2},{7,3},{8,12},{9,13},{10,... | collective-permute-start | bytes 393224 | tf_op jit(solution)/shard_map/ppermute | solution.py:156
  43.4 0.8 %slice_reduce_fusion = f32[2]{0:T(128)S(1)} fusion(f32[2,2,8,128]{3,2,1,0:T(8,128)} %get-tuple-element.33), kind=kLoop, calls=%fused_computation.42 | loop fusion | flops 2 | bytes 24 | tf_op jit(solution)/shard_map/reduce_sum | solution.py:146
  44.2 3.4 %collective-permute-done.6 = bf16[4,2,2,16,256]{4,3,2,1,0:T(8,128)(2,1)S(1)} collective-permute-done((bf16[4,2,2,16,256]{4,3,2,1,0:T(8,128)(2,1)S(1)}, bf16[4,2,2,16,256]{4,3,2,1,0:T(8,128)(2,1)S(1)}, u32[]{:S(2)}, u32[]{:S(2)}) %collective-permute-start.6) | collective-permute-done | bytes 131104 | tf_op jit(solution)/shard_map/ppermute | solution.py:156
  47.6 3.3 %collective-permute-start.7 = (bf16[2,2,2,16,256]{4,3,2,1,0:T(8,128)(2,1)S(1)}, bf16[2,2,2,16,256]{4,3,2,1,0:T(8,128)(2,1)S(1)}, u32[]{:S(2)}, u32[]{:S(2)}) collective-permute-start(bf16[2,2,2,16,256]{4,3,2,1,0:T(8,128)(2,1)S(1)} %slice.182), channel_id=1, source_target_pairs={{0,8},{1,9},{2,10},{3,11},{4,12},{5,13},{6,14},{7,15},{8,0},{9,1},... | collective-permute-start | bytes 196616 | tf_op jit(solution)/shard_map/ppermute | solution.py:156
  51.0 2.1 %collective-permute-done.7 = bf16[2,2,2,16,256]{4,3,2,1,0:T(8,128)(2,1)S(1)} collective-permute-done((bf16[2,2,2,16,256]{4,3,2,1,0:T(8,128)(2,1)S(1)}, bf16[2,2,2,16,256]{4,3,2,1,0:T(8,128)(2,1)S(1)}, u32[]{:S(2)}, u32[]{:S(2)}) %collective-permute-start.7) | collective-permute-done | bytes 65568 | tf_op jit(solution)/shard_map/ppermute | solution.py:156
  54.3 1.5 %collective-permute-start.8 = (bf16[65542]{0:T(1024)(128)(2,1)S(1)}, bf16[65542]{0:T(1024)(128)(2,1)S(1)}, u32[]{:S(2)}, u32[]{:S(2)}) collective-permute-start(bf16[65542]{0:T(1024)(128)(2,1)S(1)} %concatenate.26), channel_id=1, source_target_pairs={{0,16},{16,0},{1,17},{17,1},{2,18},{18,2},{3,19},{19,3},{4,20},{20... | collective-permute-start | bytes 393260 | tf_op jit(solution)/shard_map/ppermute | solution.py:186
  55.8 3.5 %collective-permute-done.8 = bf16[65542]{0:T(1024)(128)(2,1)S(1)} collective-permute-done((bf16[65542]{0:T(1024)(128)(2,1)S(1)}, bf16[65542]{0:T(1024)(128)(2,1)S(1)}, u32[]{:S(2)}, u32[]{:S(2)}) %collective-permute-start.8) | collective-permute-done | bytes 131116 | tf_op jit(solution)/shard_map/ppermute | solution.py:186
  59.3 0.6 fusion.19
  60.0 0.7 %dynamic-slice_add_fusion = f32[2,128,256]{2,1,0:T(8,128)} fusion(f32[2,128,256]{2,1,0:T(8,128)S(1)} %reshape.119, f32[2,256,256]{2,1,0:T(8,128)S(1)} %fusion.3, s32[]{:T(128)S(6)} %select_n.6), kind=kLoop, calls=%fused_computation.23 | loop fusion | flops 65536 | bytes 786436 | tf_op jit(solution)/shard_map/add | solution.py:187
  (44 shorter events, 3.4 us)
Async XLA Ops:
  0.6 1.0 %copy-start = (bf16[2,256,256]{2,1,0:T(8,128)(2,1)S(1)}, bf16[2,256,256]{2,1,0:T(8,128)(2,1)}, u32[]{:S(2)}) copy-start(bf16[2,256,256]{2,1,0:T(8,128)(2,1)} %param.16) | copy-start | bytes 786436
  0.6 2.2 %copy-start.3 = (bf16[2,256,256]{2,1,0:T(8,128)(2,1)S(1)}, bf16[2,256,256]{2,1,0:T(8,128)(2,1)}, u32[]{:S(2)}) copy-start(bf16[2,256,256]{2,1,0:T(8,128)(2,1)} %param.15) | copy-start | bytes 786436
  3.2 12.9 %copy-start.1 = (bf16[2,2,256,256]{3,2,1,0:T(8,128)(2,1)}, bf16[2,2,256,256]{3,2,1,0:T(8,128)(2,1)S(1)}, u32[]{:S(2)}) copy-start(bf16[2,2,256,256]{3,2,1,0:T(8,128)(2,1)S(1)} %fusion.2.proj_ref) | copy-start | bytes 1572868
  3.2 7.7 %collective-permute-start = (bf16[2,2,2,16,256]{4,3,2,1,0:T(8,128)(2,1)S(1)}, bf16[2,2,2,16,256]{4,3,2,1,0:T(8,128)(2,1)S(1)}, u32[]{:S(2)}, u32[]{:S(2)}) collective-permute-start(bf16[2,2,2,16,256]{4,3,2,1,0:T(8,128)(2,1)S(1)} %get-tuple-element.36), channel_id=1, source_target_pairs={{0,8},{1,9},{2,10},{3,11},{4,12},{5,13},{6,14},{7,15},{8,0},{9,1},... | collective-permute-start | bytes 196616 | tf_op jit(solution)/shard_map/ppermute | solution.py:141
  11.0 5.0 %collective-permute-start.1 = (bf16[4,2,2,16,256]{4,3,2,1,0:T(8,128)(2,1)S(1)}, bf16[4,2,2,16,256]{4,3,2,1,0:T(8,128)(2,1)S(1)}, u32[]{:S(2)}, u32[]{:S(2)}) collective-permute-start(bf16[4,2,2,16,256]{4,3,2,1,0:T(8,128)(2,1)S(1)} %pad_maximum_fusion.2), channel_id=1, source_target_pairs={{0,4},{1,5},{2,6},{3,7},{4,0},{5,1},{6,2},{7,3},{8,12},{9,13},{10,... | collective-permute-start | bytes 393224 | tf_op jit(solution)/shard_map/ppermute | solution.py:141
  16.1 6.4 %collective-permute-start.2 = (bf16[8,2,2,16,256]{4,3,2,1,0:T(8,128)(2,1)S(1)}, bf16[8,2,2,16,256]{4,3,2,1,0:T(8,128)(2,1)S(1)}, u32[]{:S(2)}, u32[]{:S(2)}) collective-permute-start(bf16[8,2,2,16,256]{4,3,2,1,0:T(8,128)(2,1)S(1)} %pad_maximum_fusion.1), channel_id=1, source_target_pairs={{0,2},{1,3},{2,0},{3,1},{4,6},{5,7},{6,4},{7,5},{8,10},{9,11},{10,... | collective-permute-start | bytes 786440 | tf_op jit(solution)/shard_map/ppermute | solution.py:141
  17.8 4.8 %copy-start.5 = (s32[2,2,8]{2,1,0:T(2,128)S(1)}, s32[2,2,8]{2,1,0:T(2,128)}, u32[]{:S(2)}) copy-start(s32[2,2,8]{2,1,0:T(2,128)} %param.18) | copy-start | bytes 388
  22.6 2.0 %collective-permute-start.3 = (bf16[16,2,2,16,256]{4,3,2,1,0:T(8,128)(2,1)S(1)}, bf16[16,2,2,16,256]{4,3,2,1,0:T(8,128)(2,1)S(1)}, u32[]{:S(2)}, u32[]{:S(2)}) collective-permute-start(bf16[16,2,2,16,256]{4,3,2,1,0:T(8,128)(2,1)S(1)} %pad_maximum_fusion), channel_id=1, source_target_pairs={{0,1},{1,0},{2,3},{3,2},{4,5},{5,4},{6,7},{7,6},{8,9},{9,8},{10,11... | collective-permute-start | bytes 1572872 | tf_op jit(solution)/shard_map/ppermute | solution.py:141
  22.7 0.7 %copy-start.6 = (s32[2,16]{1,0:T(2,128)S(1)}, s32[2,16]{1,0:T(2,128)}, u32[]{:S(2)}) copy-start(s32[2,16]{1,0:T(2,128)} %param.19) | copy-start | bytes 388
  24.6 1.0 %copy-start.2 = (bf16[32,2,2,16,256]{4,3,2,1,0:T(8,128)(2,1)}, bf16[32,2,2,16,256]{4,3,2,1,0:T(8,128)(2,1)S(1)}, u32[]{:S(2)}) copy-start(bf16[32,2,2,16,256]{4,3,2,1,0:T(8,128)(2,1)S(1)} %constant_dynamic-update-slice_fusion.edge_ref) | copy-start | bytes 3145732
  30.4 2.1 %collective-permute-start.4 = (bf16[16,2,2,16,256]{4,3,2,1,0:T(8,128)(2,1)}, bf16[16,2,2,16,256]{4,3,2,1,0:T(8,128)(2,1)S(1)}, u32[]{:S(2)}, u32[]{:S(2)}) collective-permute-start(bf16[16,2,2,16,256]{4,3,2,1,0:T(8,128)(2,1)} %get-tuple-element.32), channel_id=1, source_target_pairs={{0,1},{1,0},{2,3},{3,2},{4,5},{5,4},{6,7},{7,6},{8,9},{9,8},{10,11... | collective-permute-start | bytes 1572872 | tf_op jit(solution)/shard_map/ppermute | solution.py:150
  34.0 8.4 %collective-permute-start.5 = (bf16[8,2,2,16,256]{4,3,2,1,0:T(8,128)(2,1)S(1)}, bf16[8,2,2,16,256]{4,3,2,1,0:T(8,128)(2,1)S(1)}, u32[]{:S(2)}, u32[]{:S(2)}) collective-permute-start(bf16[8,2,2,16,256]{4,3,2,1,0:T(8,128)(2,1)S(1)} %slice.180), channel_id=1, source_target_pairs={{0,2},{1,3},{2,0},{3,1},{4,6},{5,7},{6,4},{7,5},{8,10},{9,11},{10,... | collective-permute-start | bytes 786440 | tf_op jit(solution)/shard_map/ppermute | solution.py:156
  42.5 8.4 %copy-start.4 = (bf16[2,2,256,256]{3,2,1,0:T(8,128)(2,1)S(1)}, bf16[2,2,256,256]{3,2,1,0:T(8,128)(2,1)}, u32[]{:S(2)}) copy-start(bf16[2,2,256,256]{3,2,1,0:T(8,128)(2,1)} %get-tuple-element.30) | copy-start | bytes 1572868
  42.6 5.0 %collective-permute-start.6 = (bf16[4,2,2,16,256]{4,3,2,1,0:T(8,128)(2,1)S(1)}, bf16[4,2,2,16,256]{4,3,2,1,0:T(8,128)(2,1)S(1)}, u32[]{:S(2)}, u32[]{:S(2)}) collective-permute-start(bf16[4,2,2,16,256]{4,3,2,1,0:T(8,128)(2,1)S(1)} %slice.181), channel_id=1, source_target_pairs={{0,4},{1,5},{2,6},{3,7},{4,0},{5,1},{6,2},{7,3},{8,12},{9,13},{10,... | collective-permute-start | bytes 393224 | tf_op jit(solution)/shard_map/ppermute | solution.py:156
  47.6 5.6 %collective-permute-start.7 = (bf16[2,2,2,16,256]{4,3,2,1,0:T(8,128)(2,1)S(1)}, bf16[2,2,2,16,256]{4,3,2,1,0:T(8,128)(2,1)S(1)}, u32[]{:S(2)}, u32[]{:S(2)}) collective-permute-start(bf16[2,2,2,16,256]{4,3,2,1,0:T(8,128)(2,1)S(1)} %slice.182), channel_id=1, source_target_pairs={{0,8},{1,9},{2,10},{3,11},{4,12},{5,13},{6,14},{7,15},{8,0},{9,1},... | collective-permute-start | bytes 196616 | tf_op jit(solution)/shard_map/ppermute | solution.py:156
  54.3 5.0 %collective-permute-start.8 = (bf16[65542]{0:T(1024)(128)(2,1)S(1)}, bf16[65542]{0:T(1024)(128)(2,1)S(1)}, u32[]{:S(2)}, u32[]{:S(2)}) collective-permute-start(bf16[65542]{0:T(1024)(128)(2,1)S(1)} %concatenate.26), channel_id=1, source_target_pairs={{0,16},{16,0},{1,17},{17,1},{2,18},{18,2},{3,19},{19,3},{4,20},{20... | collective-permute-start | bytes 393260 | tf_op jit(solution)/shard_map/ppermute | solution.py:186

commit v9 on v8

--- a/solution.py
+++ b/solution.py
@@ -110,6 +110,16 @@
     )(place, side, weight, images, projected, edges_all, ctf_filter)
 
 
+def gather_stages(peer_count):
+    steps = peer_count.bit_length() - 1
+    strides = [peer_count >> (b + 1) for b in range(steps)]
+    if steps <= 2:
+        return [(stride,) for stride in strides]
+    middle_strides = strides[1:-1]
+    pairs = [tuple(middle_strides[i : i + 2]) for i in range(0, len(middle_strides), 2)]
+    return [(strides[0],)] + pairs + [(strides[-1],)]
+
+
 def on_device(
     sections, images, slice_rows, slice_cols, ctf_filter, nbr_owner, nbr_local, nbr_side, nbr_weight
 ):
@@ -134,11 +144,15 @@
         "tai,ktil->ktal", slice_rows, halfway, preferred_element_type=jnp.float32
     ).astype(jnp.bfloat16)
     edges = jnp.stack((projected[:, :, :OVL], projected[:, :, pixels - OVL :]), axis=1)
+    stages = gather_stages(peer_count)
     edges_all = edges
-    for b in range(steps):
-        stride = peer_count >> (b + 1)
-        pairs = [(i, i ^ stride) for i in range(peer_count)]
-        edges_all = jnp.concatenate((edges_all, lax.ppermute(edges_all, "dom", pairs)), axis=0)
+    for stage in stages:
+        pieces = [edges_all]
+        for g in range(1, 2 ** len(stage)):
+            offset = sum(stride for i, stride in enumerate(stage) if (g >> i) & 1)
+            pairs = [(i, i ^ offset) for i in range(peer_count)]
+            pieces.append(lax.ppermute(edges_all, "dom", pairs))
+        edges_all = jnp.concatenate(pieces, axis=0)
 
     weighted, score_tiles, kept_half, sent_half = middle(
         place, nbr_side, nbr_weight, images, projected, edges_all, ctf_filter
@@ -148,12 +162,18 @@
 
     pairs = [(i, i ^ 1) for i in range(peer_count)]
     returned = kept_half + lax.ppermute(sent_half, "dom", pairs).astype(jnp.float32)
-    for b in range(1, steps):
-        stride = 1 << b
-        pairs = [(i, i ^ stride) for i in range(peer_count)]
-        half = returned.shape[0] // 2
-        given = returned[half:].astype(jnp.bfloat16)
-        returned = returned[:half] + lax.ppermute(given, "dom", pairs).astype(jnp.float32)
+    for stage in [tuple(reversed(stage)) for stage in reversed(stages[:-1])]:
+        count = 2 ** len(stage)
+        share = returned.shape[0] // count
+        kept = returned[:share]
+        for g in range(1, count):
+            offset = sum(
+                stride for i, stride in enumerate(stage) if (g >> (len(stage) - 1 - i)) & 1
+            )
+            pairs = [(i, i ^ offset) for i in range(peer_count)]
+            given = returned[g * share : (g + 1) * share].astype(jnp.bfloat16)
+            kept = kept + lax.ppermute(given, "dom", pairs).astype(jnp.float32)
+        returned = kept
     add_top = returned[:, 0]
     add_bottom = returned[:, 1]
 

time: 61 us -> 54.9 us (0.900)
  waiting for transfers between devices: 30.9 us -> 21.7 us
  starting transfers between devices: 14.1 us -> 16.6 us
  local copies, waits for them, and re-layouts: 3.28 us -> 3.98 us
    ppermute x7 -> x9, waiting for transfers between devices: 25.4 us -> 16.5 us  [the longest x5 8.81 us: on_device(): pieces.append(lax.ppermute(edges_all, 'dom', pairs))]
    ppermute x7 -> x9, starting transfers between devices: 12.5 us -> 14.5 us  [the longest x5 7.72 us: on_device(): pieces.append(lax.ppermute(edges_all, 'dom', pairs))]
    add x4 -> x2, other arithmetic: 1.52 us -> 0.09 us  [on_device(): kept = kept + lax.ppermute(given, 'dom', pairs).astype(jnp.float32)]
    another operation x1, other arithmetic: 0.01 us -> 1.41 us  [on_device(): jnp.stack((projected[:, :, :OVL], projected[:, :, pixels - OVL:]), axis=1)]
    unnamed x18, local copies, waits for them, and re-layouts: 2.66 us -> 3.36 us
  transfers between devices with their start and end apart: 9 -> 11, of which waited for: 9 -> 9; matrix products, arithmetic and copies ran while one was open for 3% -> 3% of each run, Pallas kernels for 0% -> 0%
where the time goes in v9:
time: 54.9 us; the launch traced here: 54.6 us
  waiting for transfers between devices  21.7 us (40%)
  starting transfers between devices  16.6 us (30%)
  Pallas kernels  4.85 us (9%)
  other arithmetic  4.43 us (8%)
  local copies, waits for them, and re-layouts  3.98 us (7%)
  matrix products  2.12 us (4%)
  between operations  0.88 us (2%)
    ppermute x5, waiting for transfers between devices, on_device(): pieces.append(lax.ppermute(edges_all, 'dom', pairs))  8.81 us
    ppermute x5, starting transfers between devices, on_device(): pieces.append(lax.ppermute(edges_all, 'dom', pairs))  7.72 us
    ppermute x4, waiting for transfers between devices, on_device(): kept = kept + lax.ppermute(given, 'dom', pairs).astype(jnp.float32)  7.71 us
    ppermute x4, starting transfers between devices, on_device(): kept = kept + lax.ppermute(given, 'dom', pairs).astype(jnp.float32)  6.81 us
    pallas_call x1, Pallas kernels, middle(): pl.pallas_call(middle_kernel, grid=(tilt_count,), in_specs=[smem, smem, s...  4.85 us
    ppermute x1, waiting for transfers between devices, on_device(): parcel = lax.ppermute(parcel, 'tilt', [(0, 1), (1, 0)]).astype(jnp.float32)  3.46 us
    unnamed x18, local copies, waits for them, and re-layouts  3.36 us
    ppermute x1, waiting for transfers between devices, on_device(): lax.ppermute(sent_half, 'dom', pairs).astype(jnp.float32)  1.75 us
  transfers between devices with their start and end apart: 11, of which 9 were waited for; matrix products, arithmetic and copies ran while one was open for 3% of the time, Pallas kernels for 0%

profile of v9, /device:TPU:0, one launch (start us, length us, event | category | flops | bytes accessed | tf_op | source)
XLA Modules:
  0.0 54.6 jit_solution(13608174756352052174)
XLA Ops:
  0.7 0.9 %copy-done = bf16[2,256,256]{2,1,0:T(8,128)(2,1)S(1)} copy-done((bf16[2,256,256]{2,1,0:T(8,128)(2,1)S(1)}, bf16[2,256,256]{2,1,0:T(8,128)(2,1)}, u32[]{:S(2)}) %copy-start) | copy-done | bytes 262168
  1.6 1.3 %fusion = bf16[2,2,256,256]{3,2,0,1:T(8,128)(2,1)S(1)} fusion(bf16[2,256,256]{2,1,0:T(8,128)(2,1)S(1)} %copy-done, bf16[2,256,256]{2,1,0:T(8,128)(2,1)} %param.13), kind=kOutput, calls=%fused_computation.3 | convolution fusion | flops 134479872 | bytes 1048576 | tf_op jit(solution)/shard_map/kij,tlj->ktil/dot_general | solution.py:140
  3.2 4.1 %collective-permute-start = (bf16[2,2,2,16,256]{4,3,2,1,0:T(8,128)(2,1)S(1)}, bf16[2,2,2,16,256]{4,3,2,1,0:T(8,128)(2,1)S(1)}, u32[]{:S(2)}, u32[]{:S(2)}) collective-permute-start(bf16[2,2,2,16,256]{4,3,2,1,0:T(8,128)(2,1)S(1)} %get-tuple-element.51), channel_id=1, source_target_pairs={{0,8},{1,9},{2,10},{3,11},{4,12},{5,13},{6,14},{7,15},{8,0},{9,1},... | collective-permute-start | bytes 196616 | tf_op jit(solution)/shard_map/ppermute | solution.py:154
  7.3 3.6 %collective-permute-done = bf16[2,2,2,16,256]{4,3,2,1,0:T(8,128)(2,1)S(1)} collective-permute-done((bf16[2,2,2,16,256]{4,3,2,1,0:T(8,128)(2,1)S(1)}, bf16[2,2,2,16,256]{4,3,2,1,0:T(8,128)(2,1)S(1)}, u32[]{:S(2)}, u32[]{:S(2)}) %collective-permute-start) | collective-permute-done | bytes 65568 | tf_op jit(solution)/shard_map/ppermute | solution.py:154
  11.6 1.5 %collective-permute-start.2 = (bf16[4,2,2,16,256]{4,3,2,1,0:T(8,128)(2,1)S(1)}, bf16[4,2,2,16,256]{4,3,2,1,0:T(8,128)(2,1)S(1)}, u32[]{:S(2)}, u32[]{:S(2)}) collective-permute-start(bf16[4,2,2,16,256]{4,3,2,1,0:T(8,128)(2,1)S(1)} %pad_maximum_fusion), channel_id=1, source_target_pairs={{0,2},{1,3},{2,0},{3,1},{4,6},{5,7},{6,4},{7,5},{8,10},{9,11},{10,... | collective-permute-start | bytes 393224 | tf_op jit(solution)/shard_map/ppermute | solution.py:154
  13.1 1.4 %collective-permute-start.3 = (bf16[4,2,2,16,256]{4,3,2,1,0:T(8,128)(2,1)S(1)}, bf16[4,2,2,16,256]{4,3,2,1,0:T(8,128)(2,1)S(1)}, u32[]{:S(2)}, u32[]{:S(2)}) collective-permute-start(bf16[4,2,2,16,256]{4,3,2,1,0:T(8,128)(2,1)S(1)} %pad_maximum_fusion), channel_id=1, source_target_pairs={{0,6},{1,7},{2,4},{3,5},{4,2},{5,3},{6,0},{7,1},{8,14},{9,15},{10,... | collective-permute-start | bytes 393224 | tf_op jit(solution)/shard_map/ppermute | solution.py:154
  14.6 2.8 %collective-permute-done.1 = bf16[4,2,2,16,256]{4,3,2,1,0:T(8,128)(2,1)S(1)} collective-permute-done((bf16[4,2,2,16,256]{4,3,2,1,0:T(8,128)(2,1)S(1)}, bf16[4,2,2,16,256]{4,3,2,1,0:T(8,128)(2,1)S(1)}, u32[]{:S(2)}, u32[]{:S(2)}) %collective-permute-start.1) | collective-permute-done | bytes 131104 | tf_op jit(solution)/shard_map/ppermute | solution.py:154
  17.4 0.7 %collective-permute-done.2 = bf16[4,2,2,16,256]{4,3,2,1,0:T(8,128)(2,1)S(1)} collective-permute-done((bf16[4,2,2,16,256]{4,3,2,1,0:T(8,128)(2,1)S(1)}, bf16[4,2,2,16,256]{4,3,2,1,0:T(8,128)(2,1)S(1)}, u32[]{:S(2)}, u32[]{:S(2)}) %collective-permute-start.2) | collective-permute-done | bytes 131104 | tf_op jit(solution)/shard_map/ppermute | solution.py:154
  18.2 1.6 %collective-permute-done.3 = bf16[4,2,2,16,256]{4,3,2,1,0:T(8,128)(2,1)S(1)} collective-permute-done((bf16[4,2,2,16,256]{4,3,2,1,0:T(8,128)(2,1)S(1)}, bf16[4,2,2,16,256]{4,3,2,1,0:T(8,128)(2,1)S(1)}, u32[]{:S(2)}, u32[]{:S(2)}) %collective-permute-start.3) | collective-permute-done | bytes 131104 | tf_op jit(solution)/shard_map/ppermute | solution.py:154
  21.9 1.0 %copy-done.2 = bf16[32,2,2,16,256]{4,3,2,1,0:T(8,128)(2,1)} copy-done((bf16[32,2,2,16,256]{4,3,2,1,0:T(8,128)(2,1)}, bf16[32,2,2,16,256]{4,3,2,1,0:T(8,128)(2,1)S(1)}, u32[]{:S(2)}) %copy-start.2) | copy-done | bytes 1048600
  22.9 4.9 %shard_map.104 = (bf16[2,2,256,256]{3,2,1,0:T(8,128)(2,1)}, f32[2,2,8,128]{3,2,1,0:T(8,128)}, f32[16,2,2,16,256]{4,3,2,1,0:T(8,128)}, bf16[16,2,2,16,256]{4,3,2,1,0:T(8,128)(2,1)}) custom-call(s32[2,16]{1,0:T(2,128)} %add.62.place_ref, s32[2,16]{1,0:T(2,128)} %side_ref.1, f32[2,16]{1,0:T(2,128)} %weight_ref.1, bf16[2,2,256,256]{3,2,1,0:T(8,128)(2,1)} %image_ref.1, ...), custom_call_target="tpu_custom_call" | custom-call | flops 536870912 | bytes 4456448 | tf_op jit(solution)/shard_map/pallas_call | solution.py:80
  28.3 1.7 %collective-permute-done.5 = bf16[16,2,2,16,256]{4,3,2,1,0:T(8,128)(2,1)S(1)} collective-permute-done((bf16[16,2,2,16,256]{4,3,2,1,0:T(8,128)(2,1)}, bf16[16,2,2,16,256]{4,3,2,1,0:T(8,128)(2,1)S(1)}, u32[]{:S(2)}, u32[]{:S(2)}) %collective-permute-start.5) | collective-permute-done | bytes 524320 | tf_op jit(solution)/shard_map/ppermute | solution.py:164
  30.0 1.4 %fusion.23 = (bf16[16,2,2,16,256]{4,3,2,1,0:T(8,128)(2,1)S(1)}, f32[16,2,2,16,256]{4,3,2,1,0:T(8,128)S(1)}) fusion(f32[16,2,2,16,256]{4,3,2,1,0:T(8,128)} %get-tuple-element.31, bf16[16,2,2,16,256]{4,3,2,1,0:T(8,128)(2,1)S(1)} %collective-permute-done.5), kind=kLoop, calls=%fused_computation.53 | loop fusion | flops 786432 | bytes 3145728 | tf_op jit(solution)/shard_map/convert.3
  31.5 1.0 %collective-permute-start.6 = (bf16[4,2,2,16,256]{4,3,2,1,0:T(8,128)(2,1)S(1)}, bf16[4,2,2,16,256]{4,3,2,1,0:T(8,128)(2,1)S(1)}, u32[]{:S(2)}, u32[]{:S(2)}) collective-permute-start(bf16[4,2,2,16,256]{4,3,2,1,0:T(8,128)(2,1)S(1)} %get-tuple-element.36), channel_id=1, source_target_pairs={{0,4},{1,5},{2,6},{3,7},{4,0},{5,1},{6,2},{7,3},{8,12},{9,13},{10,... | collective-permute-start | bytes 393224 | tf_op jit(solution)/shard_map/ppermute | solution.py:175
  32.5 1.0 %collective-permute-start.7 = (bf16[4,2,2,16,256]{4,3,2,1,0:T(8,128)(2,1)S(1)}, bf16[4,2,2,16,256]{4,3,2,1,0:T(8,128)(2,1)S(1)}, u32[]{:S(2)}, u32[]{:S(2)}) collective-permute-start(bf16[4,2,2,16,256]{4,3,2,1,0:T(8,128)(2,1)S(1)} %get-tuple-element.38), channel_id=1, source_target_pairs={{0,2},{1,3},{2,0},{3,1},{4,6},{5,7},{6,4},{7,5},{8,10},{9,11},{10,... | collective-permute-start | bytes 393224 | tf_op jit(solution)/shard_map/ppermute | solution.py:175
  33.5 1.6 %collective-permute-start.8 = (bf16[4,2,2,16,256]{4,3,2,1,0:T(8,128)(2,1)S(1)}, bf16[4,2,2,16,256]{4,3,2,1,0:T(8,128)(2,1)S(1)}, u32[]{:S(2)}, u32[]{:S(2)}) collective-permute-start(bf16[4,2,2,16,256]{4,3,2,1,0:T(8,128)(2,1)S(1)} %get-tuple-element.37), channel_id=1, source_target_pairs={{0,6},{1,7},{2,4},{3,5},{4,2},{5,3},{6,0},{7,1},{8,14},{9,15},{10,... | collective-permute-start | bytes 393224 | tf_op jit(solution)/shard_map/ppermute | solution.py:175
  35.1 0.8 %slice_reduce_fusion = f32[2]{0:T(128)S(1)} fusion(f32[2,2,8,128]{3,2,1,0:T(8,128)} %get-tuple-element.33), kind=kLoop, calls=%fused_computation.45 | loop fusion | flops 2 | bytes 24 | tf_op jit(solution)/shard_map/reduce_sum | solution.py:160
  35.9 2.0 %collective-permute-done.6 = bf16[4,2,2,16,256]{4,3,2,1,0:T(8,128)(2,1)S(1)} collective-permute-done((bf16[4,2,2,16,256]{4,3,2,1,0:T(8,128)(2,1)S(1)}, bf16[4,2,2,16,256]{4,3,2,1,0:T(8,128)(2,1)S(1)}, u32[]{:S(2)}, u32[]{:S(2)}) %collective-permute-start.6) | collective-permute-done | bytes 131104 | tf_op jit(solution)/shard_map/ppermute | solution.py:175
  37.9 2.9 %collective-permute-done.7 = bf16[4,2,2,16,256]{4,3,2,1,0:T(8,128)(2,1)S(1)} collective-permute-done((bf16[4,2,2,16,256]{4,3,2,1,0:T(8,128)(2,1)S(1)}, bf16[4,2,2,16,256]{4,3,2,1,0:T(8,128)(2,1)S(1)}, u32[]{:S(2)}, u32[]{:S(2)}) %collective-permute-start.7) | collective-permute-done | bytes 131104 | tf_op jit(solution)/shard_map/ppermute | solution.py:175
  40.8 3.2 %collective-permute-start.9 = (bf16[2,2,2,16,256]{4,3,2,1,0:T(8,128)(2,1)S(1)}, bf16[2,2,2,16,256]{4,3,2,1,0:T(8,128)(2,1)S(1)}, u32[]{:S(2)}, u32[]{:S(2)}) collective-permute-start(bf16[2,2,2,16,256]{4,3,2,1,0:T(8,128)(2,1)S(1)} %slice.182), channel_id=1, source_target_pairs={{0,8},{1,9},{2,10},{3,11},{4,12},{5,13},{6,14},{7,15},{8,0},{9,1},... | collective-permute-start | bytes 196616 | tf_op jit(solution)/shard_map/ppermute | solution.py:175
  44.2 2.8 %collective-permute-done.9 = bf16[2,2,2,16,256]{4,3,2,1,0:T(8,128)(2,1)S(1)} collective-permute-done((bf16[2,2,2,16,256]{4,3,2,1,0:T(8,128)(2,1)S(1)}, bf16[2,2,2,16,256]{4,3,2,1,0:T(8,128)(2,1)S(1)}, u32[]{:S(2)}, u32[]{:S(2)}) %collective-permute-start.9) | collective-permute-done | bytes 65568 | tf_op jit(solution)/shard_map/ppermute | solution.py:175
  48.1 1.5 %collective-permute-start.10 = (bf16[65542]{0:T(1024)(128)(2,1)S(1)}, bf16[65542]{0:T(1024)(128)(2,1)S(1)}, u32[]{:S(2)}, u32[]{:S(2)}) collective-permute-start(bf16[65542]{0:T(1024)(128)(2,1)S(1)} %concatenate.21), channel_id=1, source_target_pairs={{0,16},{16,0},{1,17},{17,1},{2,18},{18,2},{3,19},{19,3},{4,20},{20... | collective-permute-start | bytes 393260 | tf_op jit(solution)/shard_map/ppermute | solution.py:206
  49.6 3.5 %collective-permute-done.10 = bf16[65542]{0:T(1024)(128)(2,1)S(1)} collective-permute-done((bf16[65542]{0:T(1024)(128)(2,1)S(1)}, bf16[65542]{0:T(1024)(128)(2,1)S(1)}, u32[]{:S(2)}, u32[]{:S(2)}) %collective-permute-start.10) | collective-permute-done | bytes 131116 | tf_op jit(solution)/shard_map/ppermute | solution.py:206
  53.8 0.7 %dynamic-slice_add_fusion = f32[2,128,256]{2,1,0:T(8,128)} fusion(f32[2,128,256]{2,1,0:T(8,128)S(1)} %reshape.119, f32[2,256,256]{2,1,0:T(8,128)S(1)} %fusion.3, s32[]{:T(128)S(6)} %select_n.6), kind=kLoop, calls=%fused_computation.20 | loop fusion | flops 65536 | bytes 786436 | tf_op jit(solution)/shard_map/add | solution.py:207
  (45 shorter events, 5.6 us)
Async XLA Ops:
  0.6 1.0 %copy-start = (bf16[2,256,256]{2,1,0:T(8,128)(2,1)S(1)}, bf16[2,256,256]{2,1,0:T(8,128)(2,1)}, u32[]{:S(2)}) copy-start(bf16[2,256,256]{2,1,0:T(8,128)(2,1)} %param.16) | copy-start | bytes 786436
  0.6 2.2 %copy-start.3 = (bf16[2,256,256]{2,1,0:T(8,128)(2,1)S(1)}, bf16[2,256,256]{2,1,0:T(8,128)(2,1)}, u32[]{:S(2)}) copy-start(bf16[2,256,256]{2,1,0:T(8,128)(2,1)} %param.15) | copy-start | bytes 786436
  3.2 14.2 %copy-start.1 = (bf16[2,2,256,256]{3,2,1,0:T(8,128)(2,1)}, bf16[2,2,256,256]{3,2,1,0:T(8,128)(2,1)S(1)}, u32[]{:S(2)}) copy-start(bf16[2,2,256,256]{3,2,1,0:T(8,128)(2,1)S(1)} %fusion.2.proj_ref) | copy-start | bytes 1572868
  3.2 7.7 %collective-permute-start = (bf16[2,2,2,16,256]{4,3,2,1,0:T(8,128)(2,1)S(1)}, bf16[2,2,2,16,256]{4,3,2,1,0:T(8,128)(2,1)S(1)}, u32[]{:S(2)}, u32[]{:S(2)}) collective-permute-start(bf16[2,2,2,16,256]{4,3,2,1,0:T(8,128)(2,1)S(1)} %get-tuple-element.51), channel_id=1, source_target_pairs={{0,8},{1,9},{2,10},{3,11},{4,12},{5,13},{6,14},{7,15},{8,0},{9,1},... | collective-permute-start | bytes 196616 | tf_op jit(solution)/shard_map/ppermute | solution.py:154
  11.0 6.4 %collective-permute-start.1 = (bf16[4,2,2,16,256]{4,3,2,1,0:T(8,128)(2,1)S(1)}, bf16[4,2,2,16,256]{4,3,2,1,0:T(8,128)(2,1)S(1)}, u32[]{:S(2)}, u32[]{:S(2)}) collective-permute-start(bf16[4,2,2,16,256]{4,3,2,1,0:T(8,128)(2,1)S(1)} %pad_maximum_fusion), channel_id=1, source_target_pairs={{0,4},{1,5},{2,6},{3,7},{4,0},{5,1},{6,2},{7,3},{8,12},{9,13},{10,... | collective-permute-start | bytes 393224 | tf_op jit(solution)/shard_map/ppermute | solution.py:154
  11.6 6.5 %collective-permute-start.2 = (bf16[4,2,2,16,256]{4,3,2,1,0:T(8,128)(2,1)S(1)}, bf16[4,2,2,16,256]{4,3,2,1,0:T(8,128)(2,1)S(1)}, u32[]{:S(2)}, u32[]{:S(2)}) collective-permute-start(bf16[4,2,2,16,256]{4,3,2,1,0:T(8,128)(2,1)S(1)} %pad_maximum_fusion), channel_id=1, source_target_pairs={{0,2},{1,3},{2,0},{3,1},{4,6},{5,7},{6,4},{7,5},{8,10},{9,11},{10,... | collective-permute-start | bytes 393224 | tf_op jit(solution)/shard_map/ppermute | solution.py:154
  13.1 6.7 %collective-permute-start.3 = (bf16[4,2,2,16,256]{4,3,2,1,0:T(8,128)(2,1)S(1)}, bf16[4,2,2,16,256]{4,3,2,1,0:T(8,128)(2,1)S(1)}, u32[]{:S(2)}, u32[]{:S(2)}) collective-permute-start(bf16[4,2,2,16,256]{4,3,2,1,0:T(8,128)(2,1)S(1)} %pad_maximum_fusion), channel_id=1, source_target_pairs={{0,6},{1,7},{2,4},{3,5},{4,2},{5,3},{6,0},{7,1},{8,14},{9,15},{10,... | collective-permute-start | bytes 393224 | tf_op jit(solution)/shard_map/ppermute | solution.py:154
  19.8 2.1 %collective-permute-start.4 = (bf16[16,2,2,16,256]{4,3,2,1,0:T(8,128)(2,1)S(1)}, bf16[16,2,2,16,256]{4,3,2,1,0:T(8,128)(2,1)S(1)}, u32[]{:S(2)}, u32[]{:S(2)}) collective-permute-start(bf16[16,2,2,16,256]{4,3,2,1,0:T(8,128)(2,1)S(1)} %get-tuple-element.41), channel_id=1, source_target_pairs={{0,1},{1,0},{2,3},{3,2},{4,5},{5,4},{6,7},{7,6},{8,9},{9,8},{10,11... | collective-permute-start | bytes 1572872 | tf_op jit(solution)/shard_map/ppermute | solution.py:154
  19.9 0.7 %copy-start.5 = (s32[2,2,8]{2,1,0:T(2,128)S(1)}, s32[2,2,8]{2,1,0:T(2,128)}, u32[]{:S(2)}) copy-start(s32[2,2,8]{2,1,0:T(2,128)} %param.18) | copy-start | bytes 388
  20.6 0.7 %copy-start.6 = (s32[2,16]{1,0:T(2,128)S(1)}, s32[2,16]{1,0:T(2,128)}, u32[]{:S(2)}) copy-start(s32[2,16]{1,0:T(2,128)} %param.19) | copy-start | bytes 388
  21.9 1.0 %copy-start.2 = (bf16[32,2,2,16,256]{4,3,2,1,0:T(8,128)(2,1)}, bf16[32,2,2,16,256]{4,3,2,1,0:T(8,128)(2,1)S(1)}, u32[]{:S(2)}) copy-start(bf16[32,2,2,16,256]{4,3,2,1,0:T(8,128)(2,1)S(1)} %constant_dynamic-update-slice_fusion.5.edge_ref) | copy-start | bytes 3145732
  27.8 2.3 %collective-permute-start.5 = (bf16[16,2,2,16,256]{4,3,2,1,0:T(8,128)(2,1)}, bf16[16,2,2,16,256]{4,3,2,1,0:T(8,128)(2,1)S(1)}, u32[]{:S(2)}, u32[]{:S(2)}) collective-permute-start(bf16[16,2,2,16,256]{4,3,2,1,0:T(8,128)(2,1)} %get-tuple-element.32), channel_id=1, source_target_pairs={{0,1},{1,0},{2,3},{3,2},{4,5},{5,4},{6,7},{7,6},{8,9},{9,8},{10,11... | collective-permute-start | bytes 1572872 | tf_op jit(solution)/shard_map/ppermute | solution.py:164
  31.5 6.4 %collective-permute-start.6 = (bf16[4,2,2,16,256]{4,3,2,1,0:T(8,128)(2,1)S(1)}, bf16[4,2,2,16,256]{4,3,2,1,0:T(8,128)(2,1)S(1)}, u32[]{:S(2)}, u32[]{:S(2)}) collective-permute-start(bf16[4,2,2,16,256]{4,3,2,1,0:T(8,128)(2,1)S(1)} %get-tuple-element.36), channel_id=1, source_target_pairs={{0,4},{1,5},{2,6},{3,7},{4,0},{5,1},{6,2},{7,3},{8,12},{9,13},{10,... | collective-permute-start | bytes 393224 | tf_op jit(solution)/shard_map/ppermute | solution.py:175
  32.5 8.3 %collective-permute-start.7 = (bf16[4,2,2,16,256]{4,3,2,1,0:T(8,128)(2,1)S(1)}, bf16[4,2,2,16,256]{4,3,2,1,0:T(8,128)(2,1)S(1)}, u32[]{:S(2)}, u32[]{:S(2)}) collective-permute-start(bf16[4,2,2,16,256]{4,3,2,1,0:T(8,128)(2,1)S(1)} %get-tuple-element.38), channel_id=1, source_target_pairs={{0,2},{1,3},{2,0},{3,1},{4,6},{5,7},{6,4},{7,5},{8,10},{9,11},{10,... | collective-permute-start | bytes 393224 | tf_op jit(solution)/shard_map/ppermute | solution.py:175
  33.5 7.3 %collective-permute-start.8 = (bf16[4,2,2,16,256]{4,3,2,1,0:T(8,128)(2,1)S(1)}, bf16[4,2,2,16,256]{4,3,2,1,0:T(8,128)(2,1)S(1)}, u32[]{:S(2)}, u32[]{:S(2)}) collective-permute-start(bf16[4,2,2,16,256]{4,3,2,1,0:T(8,128)(2,1)S(1)} %get-tuple-element.37), channel_id=1, source_target_pairs={{0,6},{1,7},{2,4},{3,5},{4,2},{5,3},{6,0},{7,1},{8,14},{9,15},{10,... | collective-permute-start | bytes 393224 | tf_op jit(solution)/shard_map/ppermute | solution.py:175
  40.7 3.4 %copy-start.4 = (bf16[2,2,256,256]{3,2,1,0:T(8,128)(2,1)S(1)}, bf16[2,2,256,256]{3,2,1,0:T(8,128)(2,1)}, u32[]{:S(2)}) copy-start(bf16[2,2,256,256]{3,2,1,0:T(8,128)(2,1)} %get-tuple-element.30) | copy-start | bytes 1572868
  40.8 6.2 %collective-permute-start.9 = (bf16[2,2,2,16,256]{4,3,2,1,0:T(8,128)(2,1)S(1)}, bf16[2,2,2,16,256]{4,3,2,1,0:T(8,128)(2,1)S(1)}, u32[]{:S(2)}, u32[]{:S(2)}) collective-permute-start(bf16[2,2,2,16,256]{4,3,2,1,0:T(8,128)(2,1)S(1)} %slice.182), channel_id=1, source_target_pairs={{0,8},{1,9},{2,10},{3,11},{4,12},{5,13},{6,14},{7,15},{8,0},{9,1},... | collective-permute-start | bytes 196616 | tf_op jit(solution)/shard_map/ppermute | solution.py:175
  48.1 5.0 %collective-permute-start.10 = (bf16[65542]{0:T(1024)(128)(2,1)S(1)}, bf16[65542]{0:T(1024)(128)(2,1)S(1)}, u32[]{:S(2)}, u32[]{:S(2)}) collective-permute-start(bf16[65542]{0:T(1024)(128)(2,1)S(1)} %concatenate.21), channel_id=1, source_target_pairs={{0,16},{16,0},{1,17},{17,1},{2,18},{18,2},{3,19},{19,3},{4,20},{20... | collective-permute-start | bytes 393260 | tf_op jit(solution)/shard_map/ppermute | solution.py:206

commit v10 on v9

--- a/solution.py
+++ b/solution.py
@@ -9,28 +9,37 @@
 
 
 def middle_kernel(
-    place_ref, side_ref, weight_ref, image_ref, proj_ref, edge_ref, ctf_ref,
-    weighted_ref, score_ref, kept_ref, sent_ref, residual_ref, return_ref,
+    owner_ref, local_ref, side_ref, weight_ref, image_ref, proj_ref, low_ref, high_ref,
+    ctf_ref, weighted_ref, score_ref, kept_ref, sent_ref, residual_ref, return_ref,
 ):
-    own_count, neighbours = place_ref.shape
+    own_count, neighbours = local_ref.shape
+    group = owner_ref.shape[2]
     half = kept_ref.shape[0]
     pixels = image_ref.shape[-1]
+    peer_count = lax.axis_size("dom")
+    steps = peer_count.bit_length() - 1
+    me = lax.axis_index("dom")
     ctf = ctf_ref[0]
     zero = jnp.zeros((OVL, pixels), jnp.float32)
+
+    def place_of(k, j):
+        relative = owner_ref[k, j // group, j % group] ^ me
+        flipped = sum(((relative >> (steps - 1 - b)) & 1) << b for b in range(steps))
+        return flipped * own_count + local_ref[k, j]
+
+    places = [[place_of(k, j) for j in range(neighbours)] for k in range(own_count)]
     edge_rows = []
     for k in range(own_count):
-
-        def band_sum(j, carry, k=k):
-            lower, upper = carry
-            q = place_ref[k, j]
+        lower, upper = zero, zero
+        for j in range(neighbours):
+            q = places[k][j]
             s = side_ref[k, j]
             w = weight_ref[k, j]
-            band = edge_ref[q, s, 0].astype(jnp.float32)
+            low_band = low_ref[jnp.minimum(q, half - 1), s, 0]
+            high_band = high_ref[jnp.maximum(q - half, 0), s, 0]
+            band = jnp.where(q < half, low_band, high_band).astype(jnp.float32)
             lower = lower + jnp.where(s == 0, w, 0.0) * band
             upper = upper + jnp.where(s == 1, w, 0.0) * band
-            return lower, upper
-
-        lower, upper = lax.fori_loop(0, neighbours, band_sum, (zero, zero), unroll=True)
         residual_ref[k] = image_ref[k, 0].astype(jnp.float32) - proj_ref[k, 0].astype(jnp.float32)
         residual_ref[k, :OVL] = residual_ref[k, :OVL] - upper
         residual_ref[k, pixels - OVL :] = residual_ref[k, pixels - OVL :] - lower
@@ -54,29 +63,25 @@
     for k in range(own_count):
         bottom_rows, top_rows = edge_rows[k]
 
-        def give_back(j, carry, k=k, bottom_rows=bottom_rows, top_rows=top_rows):
-            q = place_ref[k, j]
+        for j in range(neighbours):
+            q = places[k][j]
             s = side_ref[k, j]
             rows = jnp.where(s == 0, bottom_rows, top_rows)
             part = (weight_ref[k, j] * rows).astype(jnp.bfloat16).astype(jnp.float32)
             return_ref[q, s] = return_ref[q, s] + part
-            return carry
-
-        lax.fori_loop(0, neighbours, give_back, 0, unroll=True)
     kept_ref[:, :, 0] = return_ref[:half]
     sent_ref[:, :, 0] = return_ref[half:].astype(jnp.bfloat16)
 
 
-def middle(place, side, weight, images, projected, edges_all, ctf_filter):
+def middle(owner, local, side, weight, images, projected, edges_low, edges_high, ctf_filter):
     own_count, tilt_count, pixels, _ = images.shape
-    total = edges_all.shape[0]
-    half = total // 2
+    half = edges_low.shape[0]
+    total = 2 * half
     tiles = pl.BlockSpec((own_count, 1, pixels, pixels), lambda t: (0, t, 0, 0))
-    bands = pl.BlockSpec((total, 2, 1, OVL, pixels), lambda t: (0, 0, t, 0, 0))
     halves = pl.BlockSpec((half, 2, 1, OVL, pixels), lambda t: (0, 0, t, 0, 0))
     smem = pl.BlockSpec(memory_space=pltpu.SMEM)
     flops = own_count * tilt_count * 8 * pixels**3
-    moved = 2 * images.size * 3 + 2 * edges_all.size + 3 * edges_all.size + 2 * ctf_filter.size
+    moved = 2 * images.size * 3 + 10 * edges_low.size + 2 * ctf_filter.size
     return pl.pallas_call(
         middle_kernel,
         grid=(tilt_count,),
@@ -84,9 +89,11 @@
             smem,
             smem,
             smem,
+            smem,
             tiles,
             tiles,
-            bands,
+            halves,
+            halves,
             pl.BlockSpec((1, pixels, pixels), lambda t: (t, 0, 0)),
         ],
         out_specs=[
@@ -98,8 +105,8 @@
         out_shape=[
             jax.ShapeDtypeStruct(images.shape, jnp.bfloat16),
             jax.ShapeDtypeStruct((tilt_count, own_count, 8, 128), jnp.float32),
-            jax.ShapeDtypeStruct((half,) + edges_all.shape[1:], jnp.float32),
-            jax.ShapeDtypeStruct((half,) + edges_all.shape[1:], jnp.bfloat16),
+            jax.ShapeDtypeStruct(edges_low.shape, jnp.float32),
+            jax.ShapeDtypeStruct(edges_low.shape, jnp.bfloat16),
         ],
         scratch_shapes=[
             pltpu.VMEM((own_count, pixels, pixels), jnp.float32),
@@ -107,7 +114,7 @@
         ],
         compiler_params=pltpu.CompilerParams(dimension_semantics=("arbitrary",)),
         cost_estimate=pl.CostEstimate(flops=flops, transcendentals=0, bytes_accessed=moved),
-    )(place, side, weight, images, projected, edges_all, ctf_filter)
+    )(owner, local, side, weight, images, projected, edges_low, edges_high, ctf_filter)
 
 
 def gather_stages(peer_count):
@@ -132,11 +139,6 @@
     me = lax.axis_index("dom")
     band_size = tilt_count * OVL * pixels
 
-    steps = peer_count.bit_length() - 1
-    relative = nbr_owner.reshape(own_count, neighbours) ^ me
-    flipped = sum(((relative >> (steps - 1 - b)) & 1) << b for b in range(steps))
-    place = flipped * own_count + nbr_local
-
     halfway = jnp.einsum(
         "kij,tlj->ktil", sections, slice_cols, preferred_element_type=jnp.float32
     ).astype(jnp.bfloat16)
@@ -146,16 +148,18 @@
     edges = jnp.stack((projected[:, :, :OVL], projected[:, :, pixels - OVL :]), axis=1)
     stages = gather_stages(peer_count)
     edges_all = edges
-    for stage in stages:
+    for stage in stages[:-1]:
         pieces = [edges_all]
         for g in range(1, 2 ** len(stage)):
             offset = sum(stride for i, stride in enumerate(stage) if (g >> i) & 1)
             pairs = [(i, i ^ offset) for i in range(peer_count)]
             pieces.append(lax.ppermute(edges_all, "dom", pairs))
         edges_all = jnp.concatenate(pieces, axis=0)
+    edges_high = lax.ppermute(edges_all, "dom", [(i, i ^ 1) for i in range(peer_count)])
 
     weighted, score_tiles, kept_half, sent_half = middle(
-        place, nbr_side, nbr_weight, images, projected, edges_all, ctf_filter
+        nbr_owner, nbr_local, nbr_side, nbr_weight, images, projected, edges_all, edges_high,
+        ctf_filter,
     )
     score_part = jnp.sum(score_tiles[:, :, 0, 0], axis=0)
     tilt_groups = lax.axis_size("tilt")

time: 54.9 us -> 54.6 us (level)
  waiting for transfers between devices: 21.7 us -> 23.7 us
  local copies, waits for them, and re-layouts: 3.98 us -> 2.36 us
  other arithmetic: 4.43 us -> 3.82 us
    ppermute x0 -> x1, waiting for transfers between devices: none -> 1.9 us  [on_device(): lax.ppermute(edges_all, 'dom', [(i, i ^ 1) for i in range(peer_count)])]
    unnamed x18 -> x16, local copies, waits for them, and re-layouts: 3.36 us -> 1.88 us
    add x1 -> x0, other arithmetic: 0.59 us -> none  [on_device(): place = flipped * own_count + nbr_local]
    ppermute x5 -> x4, starting transfers between devices: 7.72 us -> 7.65 us  [on_device(): pieces.append(lax.ppermute(edges_all, 'dom', pairs))]
    ppermute x5 -> x4, waiting for transfers between devices: 8.81 us -> 8.84 us  [on_device(): pieces.append(lax.ppermute(edges_all, 'dom', pairs))]
    another operation x1 -> x2, other arithmetic: 1.41 us -> 1.43 us
  transfers between devices with their start and end apart: 11 -> 11, of which waited for: 9 -> 10; matrix products, arithmetic and copies ran while one was open for 3% -> 2% of each run, Pallas kernels for 0% -> 0%
where the time goes in v10:
time: 54.6 us; the launch traced here: 54.4 us
  waiting for transfers between devices  23.7 us (43%)
  starting transfers between devices  16.2 us (30%)
  Pallas kernels  5.33 us (10%)
  other arithmetic  3.82 us (7%)
  local copies, waits for them, and re-layouts  2.36 us (4%)
  matrix products  2.12 us (4%)
  between operations  0.85 us (2%)
    ppermute x4, waiting for transfers between devices, on_device(): pieces.append(lax.ppermute(edges_all, 'dom', pairs))  8.84 us
    ppermute x4, starting transfers between devices, on_device(): pieces.append(lax.ppermute(edges_all, 'dom', pairs))  7.65 us
    ppermute x4, waiting for transfers between devices, on_device(): kept = kept + lax.ppermute(given, 'dom', pairs).astype(jnp.float32)  7.5 us
    ppermute x4, starting transfers between devices, on_device(): kept = kept + lax.ppermute(given, 'dom', pairs).astype(jnp.float32)  6.8 us
    pallas_call x1, Pallas kernels, middle(): pl.pallas_call(middle_kernel, grid=(tilt_count,), in_specs=[smem, smem, s...  5.33 us
    ppermute x1, waiting for transfers between devices, on_device(): parcel = lax.ppermute(parcel, 'tilt', [(0, 1), (1, 0)]).astype(jnp.float32)  3.46 us
    ppermute x1, waiting for transfers between devices, on_device(): lax.ppermute(sent_half, 'dom', pairs).astype(jnp.float32)  1.97 us
    ppermute x1, waiting for transfers between devices, on_device(): lax.ppermute(edges_all, 'dom', [(i, i ^ 1) for i in range(peer_count)])  1.9 us
  transfers between devices with their start and end apart: 11, of which 10 were waited for; matrix products, arithmetic and copies ran while one was open for 2% of the time, Pallas kernels for 0%

profile of v10, /device:TPU:0, one launch (start us, length us, event | category | flops | bytes accessed | tf_op | source)
XLA Modules:
  0.0 54.4 jit_solution(11517557955712748382)
XLA Ops:
  0.7 0.9 %copy-done = bf16[2,256,256]{2,1,0:T(8,128)(2,1)S(1)} copy-done((bf16[2,256,256]{2,1,0:T(8,128)(2,1)S(1)}, bf16[2,256,256]{2,1,0:T(8,128)(2,1)}, u32[]{:S(2)}) %copy-start) | copy-done | bytes 262168
  1.6 1.3 %fusion = bf16[2,2,256,256]{3,2,0,1:T(8,128)(2,1)S(1)} fusion(bf16[2,256,256]{2,1,0:T(8,128)(2,1)S(1)} %copy-done, bf16[2,256,256]{2,1,0:T(8,128)(2,1)} %param.13), kind=kOutput, calls=%fused_computation.3 | convolution fusion | flops 134479872 | bytes 1048576 | tf_op jit(solution)/shard_map/kij,tlj->ktil/dot_general | solution.py:142
  3.2 4.1 %collective-permute-start = (bf16[2,2,2,16,256]{4,3,2,1,0:T(8,128)(2,1)S(1)}, bf16[2,2,2,16,256]{4,3,2,1,0:T(8,128)(2,1)S(1)}, u32[]{:S(2)}, u32[]{:S(2)}) collective-permute-start(bf16[2,2,2,16,256]{4,3,2,1,0:T(8,128)(2,1)S(1)} %get-tuple-element.41), channel_id=1, source_target_pairs={{0,8},{1,9},{2,10},{3,11},{4,12},{5,13},{6,14},{7,15},{8,0},{9,1},... | collective-permute-start | bytes 196616 | tf_op jit(solution)/shard_map/ppermute | solution.py:156
  7.3 3.6 %collective-permute-done = bf16[2,2,2,16,256]{4,3,2,1,0:T(8,128)(2,1)S(1)} collective-permute-done((bf16[2,2,2,16,256]{4,3,2,1,0:T(8,128)(2,1)S(1)}, bf16[2,2,2,16,256]{4,3,2,1,0:T(8,128)(2,1)S(1)}, u32[]{:S(2)}, u32[]{:S(2)}) %collective-permute-start) | collective-permute-done | bytes 65568 | tf_op jit(solution)/shard_map/ppermute | solution.py:156
  11.6 1.5 %collective-permute-start.2 = (bf16[4,2,2,16,256]{4,3,2,1,0:T(8,128)(2,1)S(1)}, bf16[4,2,2,16,256]{4,3,2,1,0:T(8,128)(2,1)S(1)}, u32[]{:S(2)}, u32[]{:S(2)}) collective-permute-start(bf16[4,2,2,16,256]{4,3,2,1,0:T(8,128)(2,1)S(1)} %pad_maximum_fusion), channel_id=1, source_target_pairs={{0,2},{1,3},{2,0},{3,1},{4,6},{5,7},{6,4},{7,5},{8,10},{9,11},{10,... | collective-permute-start | bytes 393224 | tf_op jit(solution)/shard_map/ppermute | solution.py:156
  13.1 1.4 %collective-permute-start.3 = (bf16[4,2,2,16,256]{4,3,2,1,0:T(8,128)(2,1)S(1)}, bf16[4,2,2,16,256]{4,3,2,1,0:T(8,128)(2,1)S(1)}, u32[]{:S(2)}, u32[]{:S(2)}) collective-permute-start(bf16[4,2,2,16,256]{4,3,2,1,0:T(8,128)(2,1)S(1)} %pad_maximum_fusion), channel_id=1, source_target_pairs={{0,6},{1,7},{2,4},{3,5},{4,2},{5,3},{6,0},{7,1},{8,14},{9,15},{10,... | collective-permute-start | bytes 393224 | tf_op jit(solution)/shard_map/ppermute | solution.py:156
  14.6 2.8 %collective-permute-done.1 = bf16[4,2,2,16,256]{4,3,2,1,0:T(8,128)(2,1)S(1)} collective-permute-done((bf16[4,2,2,16,256]{4,3,2,1,0:T(8,128)(2,1)S(1)}, bf16[4,2,2,16,256]{4,3,2,1,0:T(8,128)(2,1)S(1)}, u32[]{:S(2)}, u32[]{:S(2)}) %collective-permute-start.1) | collective-permute-done | bytes 131104 | tf_op jit(solution)/shard_map/ppermute | solution.py:156
  17.4 0.8 %collective-permute-done.2 = bf16[4,2,2,16,256]{4,3,2,1,0:T(8,128)(2,1)S(1)} collective-permute-done((bf16[4,2,2,16,256]{4,3,2,1,0:T(8,128)(2,1)S(1)}, bf16[4,2,2,16,256]{4,3,2,1,0:T(8,128)(2,1)S(1)}, u32[]{:S(2)}, u32[]{:S(2)}) %collective-permute-start.2) | collective-permute-done | bytes 131104 | tf_op jit(solution)/shard_map/ppermute | solution.py:156
  18.2 1.6 %collective-permute-done.3 = bf16[4,2,2,16,256]{4,3,2,1,0:T(8,128)(2,1)S(1)} collective-permute-done((bf16[4,2,2,16,256]{4,3,2,1,0:T(8,128)(2,1)S(1)}, bf16[4,2,2,16,256]{4,3,2,1,0:T(8,128)(2,1)S(1)}, u32[]{:S(2)}, u32[]{:S(2)}) %collective-permute-start.3) | collective-permute-done | bytes 131104 | tf_op jit(solution)/shard_map/ppermute | solution.py:156
  19.9 1.9 %collective-permute-done.4.high_ref = bf16[16,2,2,16,256]{4,3,2,1,0:T(8,128)(2,1)S(1)} collective-permute-done((bf16[16,2,2,16,256]{4,3,2,1,0:T(8,128)(2,1)S(1)}, bf16[16,2,2,16,256]{4,3,2,1,0:T(8,128)(2,1)S(1)}, u32[]{:S(2)}, u32[]{:S(2)}) %collective-permute-start.4) | collective-permute-done | bytes 524320 | tf_op jit(solution)/shard_map/ppermute | solution.py:158
  21.8 0.8 %copy-done.5 = bf16[16,2,2,16,256]{4,3,2,1,0:T(8,128)(2,1)} copy-done((bf16[16,2,2,16,256]{4,3,2,1,0:T(8,128)(2,1)}, bf16[16,2,2,16,256]{4,3,2,1,0:T(8,128)(2,1)S(1)}, u32[]{:S(2)}) %copy-start.5) | copy-done | bytes 524312
  22.6 5.3 %shard_map.104 = (bf16[2,2,256,256]{3,2,1,0:T(8,128)(2,1)}, f32[2,2,8,128]{3,2,1,0:T(8,128)}, f32[16,2,2,16,256]{4,3,2,1,0:T(8,128)}, bf16[16,2,2,16,256]{4,3,2,1,0:T(8,128)(2,1)}) custom-call(s32[2,2,8]{2,1,0:T(2,128)} %owner_ref.1, s32[2,16]{1,0:T(2,128)} %local_ref.1, s32[2,16]{1,0:T(2,128)} %side_ref.1, f32[2,16]{1,0:T(2,128)} %weight_ref.1, ...), custom_call_target="tpu_custom_call" | custom-call | flops 536870912 | bytes 4456448 | tf_op jit(solution)/shard_map/pallas_call | solution.py:85
  28.1 2.0 %collective-permute-done.5 = bf16[16,2,2,16,256]{4,3,2,1,0:T(8,128)(2,1)S(1)} collective-permute-done((bf16[16,2,2,16,256]{4,3,2,1,0:T(8,128)(2,1)}, bf16[16,2,2,16,256]{4,3,2,1,0:T(8,128)(2,1)S(1)}, u32[]{:S(2)}, u32[]{:S(2)}) %collective-permute-start.5) | collective-permute-done | bytes 524320 | tf_op jit(solution)/shard_map/ppermute | solution.py:168
  30.1 1.4 %fusion.23 = (bf16[16,2,2,16,256]{4,3,2,1,0:T(8,128)(2,1)S(1)}, f32[16,2,2,16,256]{4,3,2,1,0:T(8,128)S(1)}) fusion(f32[16,2,2,16,256]{4,3,2,1,0:T(8,128)} %get-tuple-element.31, bf16[16,2,2,16,256]{4,3,2,1,0:T(8,128)(2,1)S(1)} %collective-permute-done.5), kind=kLoop, calls=%fused_computation.46 | loop fusion | flops 786432 | bytes 3145728 | tf_op jit(solution)/shard_map/convert.3
  31.5 0.9 %collective-permute-start.6 = (bf16[4,2,2,16,256]{4,3,2,1,0:T(8,128)(2,1)S(1)}, bf16[4,2,2,16,256]{4,3,2,1,0:T(8,128)(2,1)S(1)}, u32[]{:S(2)}, u32[]{:S(2)}) collective-permute-start(bf16[4,2,2,16,256]{4,3,2,1,0:T(8,128)(2,1)S(1)} %get-tuple-element.36), channel_id=1, source_target_pairs={{0,4},{1,5},{2,6},{3,7},{4,0},{5,1},{6,2},{7,3},{8,12},{9,13},{10,... | collective-permute-start | bytes 393224 | tf_op jit(solution)/shard_map/ppermute | solution.py:179
  32.5 1.0 %collective-permute-start.7 = (bf16[4,2,2,16,256]{4,3,2,1,0:T(8,128)(2,1)S(1)}, bf16[4,2,2,16,256]{4,3,2,1,0:T(8,128)(2,1)S(1)}, u32[]{:S(2)}, u32[]{:S(2)}) collective-permute-start(bf16[4,2,2,16,256]{4,3,2,1,0:T(8,128)(2,1)S(1)} %get-tuple-element.38), channel_id=1, source_target_pairs={{0,2},{1,3},{2,0},{3,1},{4,6},{5,7},{6,4},{7,5},{8,10},{9,11},{10,... | collective-permute-start | bytes 393224 | tf_op jit(solution)/shard_map/ppermute | solution.py:179
  33.5 1.6 %collective-permute-start.8 = (bf16[4,2,2,16,256]{4,3,2,1,0:T(8,128)(2,1)S(1)}, bf16[4,2,2,16,256]{4,3,2,1,0:T(8,128)(2,1)S(1)}, u32[]{:S(2)}, u32[]{:S(2)}) collective-permute-start(bf16[4,2,2,16,256]{4,3,2,1,0:T(8,128)(2,1)S(1)} %get-tuple-element.37), channel_id=1, source_target_pairs={{0,6},{1,7},{2,4},{3,5},{4,2},{5,3},{6,0},{7,1},{8,14},{9,15},{10,... | collective-permute-start | bytes 393224 | tf_op jit(solution)/shard_map/ppermute | solution.py:179
  35.1 0.8 %slice_reduce_fusion = f32[2]{0:T(128)S(1)} fusion(f32[2,2,8,128]{3,2,1,0:T(8,128)} %get-tuple-element.33), kind=kLoop, calls=%fused_computation.38 | loop fusion | flops 2 | bytes 24 | tf_op jit(solution)/shard_map/reduce_sum | solution.py:164
  35.9 2.0 %collective-permute-done.6 = bf16[4,2,2,16,256]{4,3,2,1,0:T(8,128)(2,1)S(1)} collective-permute-done((bf16[4,2,2,16,256]{4,3,2,1,0:T(8,128)(2,1)S(1)}, bf16[4,2,2,16,256]{4,3,2,1,0:T(8,128)(2,1)S(1)}, u32[]{:S(2)}, u32[]{:S(2)}) %collective-permute-start.6) | collective-permute-done | bytes 131104 | tf_op jit(solution)/shard_map/ppermute | solution.py:179
  37.9 2.6 %collective-permute-done.7 = bf16[4,2,2,16,256]{4,3,2,1,0:T(8,128)(2,1)S(1)} collective-permute-done((bf16[4,2,2,16,256]{4,3,2,1,0:T(8,128)(2,1)S(1)}, bf16[4,2,2,16,256]{4,3,2,1,0:T(8,128)(2,1)S(1)}, u32[]{:S(2)}, u32[]{:S(2)}) %collective-permute-start.7) | collective-permute-done | bytes 131104 | tf_op jit(solution)/shard_map/ppermute | solution.py:179
  40.7 3.2 %collective-permute-start.9 = (bf16[2,2,2,16,256]{4,3,2,1,0:T(8,128)(2,1)S(1)}, bf16[2,2,2,16,256]{4,3,2,1,0:T(8,128)(2,1)S(1)}, u32[]{:S(2)}, u32[]{:S(2)}) collective-permute-start(bf16[2,2,2,16,256]{4,3,2,1,0:T(8,128)(2,1)S(1)} %slice.182), channel_id=1, source_target_pairs={{0,8},{1,9},{2,10},{3,11},{4,12},{5,13},{6,14},{7,15},{8,0},{9,1},... | collective-permute-start | bytes 196616 | tf_op jit(solution)/shard_map/ppermute | solution.py:179
  44.0 2.8 %collective-permute-done.9 = bf16[2,2,2,16,256]{4,3,2,1,0:T(8,128)(2,1)S(1)} collective-permute-done((bf16[2,2,2,16,256]{4,3,2,1,0:T(8,128)(2,1)S(1)}, bf16[2,2,2,16,256]{4,3,2,1,0:T(8,128)(2,1)S(1)}, u32[]{:S(2)}, u32[]{:S(2)}) %collective-permute-start.9) | collective-permute-done | bytes 65568 | tf_op jit(solution)/shard_map/ppermute | solution.py:179
  47.9 1.5 %collective-permute-start.10 = (bf16[65542]{0:T(1024)(128)(2,1)S(1)}, bf16[65542]{0:T(1024)(128)(2,1)S(1)}, u32[]{:S(2)}, u32[]{:S(2)}) collective-permute-start(bf16[65542]{0:T(1024)(128)(2,1)S(1)} %concatenate.16), channel_id=1, source_target_pairs={{0,16},{16,0},{1,17},{17,1},{2,18},{18,2},{3,19},{19,3},{4,20},{20... | collective-permute-start | bytes 393260 | tf_op jit(solution)/shard_map/ppermute | solution.py:210
  49.4 3.5 %collective-permute-done.10 = bf16[65542]{0:T(1024)(128)(2,1)S(1)} collective-permute-done((bf16[65542]{0:T(1024)(128)(2,1)S(1)}, bf16[65542]{0:T(1024)(128)(2,1)S(1)}, u32[]{:S(2)}, u32[]{:S(2)}) %collective-permute-start.10) | collective-permute-done | bytes 131116 | tf_op jit(solution)/shard_map/ppermute | solution.py:210
  (39 shorter events, 4.0 us)
Async XLA Ops:
  0.6 1.0 %copy-start = (bf16[2,256,256]{2,1,0:T(8,128)(2,1)S(1)}, bf16[2,256,256]{2,1,0:T(8,128)(2,1)}, u32[]{:S(2)}) copy-start(bf16[2,256,256]{2,1,0:T(8,128)(2,1)} %param.16) | copy-start | bytes 786436
  0.6 2.2 %copy-start.2 = (bf16[2,256,256]{2,1,0:T(8,128)(2,1)S(1)}, bf16[2,256,256]{2,1,0:T(8,128)(2,1)}, u32[]{:S(2)}) copy-start(bf16[2,256,256]{2,1,0:T(8,128)(2,1)} %param.15) | copy-start | bytes 786436
  3.2 15.0 %copy-start.1 = (bf16[2,2,256,256]{3,2,1,0:T(8,128)(2,1)}, bf16[2,2,256,256]{3,2,1,0:T(8,128)(2,1)S(1)}, u32[]{:S(2)}) copy-start(bf16[2,2,256,256]{3,2,1,0:T(8,128)(2,1)S(1)} %fusion.2.proj_ref) | copy-start | bytes 1572868
  3.2 7.7 %collective-permute-start = (bf16[2,2,2,16,256]{4,3,2,1,0:T(8,128)(2,1)S(1)}, bf16[2,2,2,16,256]{4,3,2,1,0:T(8,128)(2,1)S(1)}, u32[]{:S(2)}, u32[]{:S(2)}) collective-permute-start(bf16[2,2,2,16,256]{4,3,2,1,0:T(8,128)(2,1)S(1)} %get-tuple-element.41), channel_id=1, source_target_pairs={{0,8},{1,9},{2,10},{3,11},{4,12},{5,13},{6,14},{7,15},{8,0},{9,1},... | collective-permute-start | bytes 196616 | tf_op jit(solution)/shard_map/ppermute | solution.py:156
  11.0 6.4 %collective-permute-start.1 = (bf16[4,2,2,16,256]{4,3,2,1,0:T(8,128)(2,1)S(1)}, bf16[4,2,2,16,256]{4,3,2,1,0:T(8,128)(2,1)S(1)}, u32[]{:S(2)}, u32[]{:S(2)}) collective-permute-start(bf16[4,2,2,16,256]{4,3,2,1,0:T(8,128)(2,1)S(1)} %pad_maximum_fusion), channel_id=1, source_target_pairs={{0,4},{1,5},{2,6},{3,7},{4,0},{5,1},{6,2},{7,3},{8,12},{9,13},{10,... | collective-permute-start | bytes 393224 | tf_op jit(solution)/shard_map/ppermute | solution.py:156
  11.6 6.5 %collective-permute-start.2 = (bf16[4,2,2,16,256]{4,3,2,1,0:T(8,128)(2,1)S(1)}, bf16[4,2,2,16,256]{4,3,2,1,0:T(8,128)(2,1)S(1)}, u32[]{:S(2)}, u32[]{:S(2)}) collective-permute-start(bf16[4,2,2,16,256]{4,3,2,1,0:T(8,128)(2,1)S(1)} %pad_maximum_fusion), channel_id=1, source_target_pairs={{0,2},{1,3},{2,0},{3,1},{4,6},{5,7},{6,4},{7,5},{8,10},{9,11},{10,... | collective-permute-start | bytes 393224 | tf_op jit(solution)/shard_map/ppermute | solution.py:156
  13.1 6.7 %collective-permute-start.3 = (bf16[4,2,2,16,256]{4,3,2,1,0:T(8,128)(2,1)S(1)}, bf16[4,2,2,16,256]{4,3,2,1,0:T(8,128)(2,1)S(1)}, u32[]{:S(2)}, u32[]{:S(2)}) collective-permute-start(bf16[4,2,2,16,256]{4,3,2,1,0:T(8,128)(2,1)S(1)} %pad_maximum_fusion), channel_id=1, source_target_pairs={{0,6},{1,7},{2,4},{3,5},{4,2},{5,3},{6,0},{7,1},{8,14},{9,15},{10,... | collective-permute-start | bytes 393224 | tf_op jit(solution)/shard_map/ppermute | solution.py:156
  19.8 2.0 %copy-start.3 = (bf16[16,2,2,16,256]{4,3,2,1,0:T(8,128)(2,1)}, bf16[16,2,2,16,256]{4,3,2,1,0:T(8,128)(2,1)S(1)}, u32[]{:S(2)}) copy-start(bf16[16,2,2,16,256]{4,3,2,1,0:T(8,128)(2,1)S(1)} %constant_dynamic-update-slice_fusion.low_ref) | copy-start | bytes 1572868
  19.8 2.0 %collective-permute-start.4 = (bf16[16,2,2,16,256]{4,3,2,1,0:T(8,128)(2,1)S(1)}, bf16[16,2,2,16,256]{4,3,2,1,0:T(8,128)(2,1)S(1)}, u32[]{:S(2)}, u32[]{:S(2)}) collective-permute-start(bf16[16,2,2,16,256]{4,3,2,1,0:T(8,128)(2,1)S(1)} %constant_dynamic-update-slice_fusion.low_ref), channel_id=1, source_target_pairs={{0,1},{1,0},{2,3},{3,2},{4,5},{5,4},{6,7},{7,6},{8,9},{9,8},{10,11... | collective-permute-start | bytes 1572872 | tf_op jit(solution)/shard_map/ppermute | solution.py:158
  21.8 0.8 %copy-start.5 = (bf16[16,2,2,16,256]{4,3,2,1,0:T(8,128)(2,1)}, bf16[16,2,2,16,256]{4,3,2,1,0:T(8,128)(2,1)S(1)}, u32[]{:S(2)}) copy-start(bf16[16,2,2,16,256]{4,3,2,1,0:T(8,128)(2,1)S(1)} %collective-permute-done.4.high_ref) | copy-start | bytes 1572868
  27.9 2.2 %collective-permute-start.5 = (bf16[16,2,2,16,256]{4,3,2,1,0:T(8,128)(2,1)}, bf16[16,2,2,16,256]{4,3,2,1,0:T(8,128)(2,1)S(1)}, u32[]{:S(2)}, u32[]{:S(2)}) collective-permute-start(bf16[16,2,2,16,256]{4,3,2,1,0:T(8,128)(2,1)} %get-tuple-element.32), channel_id=1, source_target_pairs={{0,1},{1,0},{2,3},{3,2},{4,5},{5,4},{6,7},{7,6},{8,9},{9,8},{10,11... | collective-permute-start | bytes 1572872 | tf_op jit(solution)/shard_map/ppermute | solution.py:168
  31.5 6.4 %collective-permute-start.6 = (bf16[4,2,2,16,256]{4,3,2,1,0:T(8,128)(2,1)S(1)}, bf16[4,2,2,16,256]{4,3,2,1,0:T(8,128)(2,1)S(1)}, u32[]{:S(2)}, u32[]{:S(2)}) collective-permute-start(bf16[4,2,2,16,256]{4,3,2,1,0:T(8,128)(2,1)S(1)} %get-tuple-element.36), channel_id=1, source_target_pairs={{0,4},{1,5},{2,6},{3,7},{4,0},{5,1},{6,2},{7,3},{8,12},{9,13},{10,... | collective-permute-start | bytes 393224 | tf_op jit(solution)/shard_map/ppermute | solution.py:179
  32.5 8.1 %collective-permute-start.7 = (bf16[4,2,2,16,256]{4,3,2,1,0:T(8,128)(2,1)S(1)}, bf16[4,2,2,16,256]{4,3,2,1,0:T(8,128)(2,1)S(1)}, u32[]{:S(2)}, u32[]{:S(2)}) collective-permute-start(bf16[4,2,2,16,256]{4,3,2,1,0:T(8,128)(2,1)S(1)} %get-tuple-element.38), channel_id=1, source_target_pairs={{0,2},{1,3},{2,0},{3,1},{4,6},{5,7},{6,4},{7,5},{8,10},{9,11},{10,... | collective-permute-start | bytes 393224 | tf_op jit(solution)/shard_map/ppermute | solution.py:179
  33.5 7.0 %collective-permute-start.8 = (bf16[4,2,2,16,256]{4,3,2,1,0:T(8,128)(2,1)S(1)}, bf16[4,2,2,16,256]{4,3,2,1,0:T(8,128)(2,1)S(1)}, u32[]{:S(2)}, u32[]{:S(2)}) collective-permute-start(bf16[4,2,2,16,256]{4,3,2,1,0:T(8,128)(2,1)S(1)} %get-tuple-element.37), channel_id=1, source_target_pairs={{0,6},{1,7},{2,4},{3,5},{4,2},{5,3},{6,0},{7,1},{8,14},{9,15},{10,... | collective-permute-start | bytes 393224 | tf_op jit(solution)/shard_map/ppermute | solution.py:179
  40.6 3.4 %copy-start.4 = (bf16[2,2,256,256]{3,2,1,0:T(8,128)(2,1)S(1)}, bf16[2,2,256,256]{3,2,1,0:T(8,128)(2,1)}, u32[]{:S(2)}) copy-start(bf16[2,2,256,256]{3,2,1,0:T(8,128)(2,1)} %get-tuple-element.30) | copy-start | bytes 1572868
  40.7 6.2 %collective-permute-start.9 = (bf16[2,2,2,16,256]{4,3,2,1,0:T(8,128)(2,1)S(1)}, bf16[2,2,2,16,256]{4,3,2,1,0:T(8,128)(2,1)S(1)}, u32[]{:S(2)}, u32[]{:S(2)}) collective-permute-start(bf16[2,2,2,16,256]{4,3,2,1,0:T(8,128)(2,1)S(1)} %slice.182), channel_id=1, source_target_pairs={{0,8},{1,9},{2,10},{3,11},{4,12},{5,13},{6,14},{7,15},{8,0},{9,1},... | collective-permute-start | bytes 196616 | tf_op jit(solution)/shard_map/ppermute | solution.py:179
  47.9 5.0 %collective-permute-start.10 = (bf16[65542]{0:T(1024)(128)(2,1)S(1)}, bf16[65542]{0:T(1024)(128)(2,1)S(1)}, u32[]{:S(2)}, u32[]{:S(2)}) collective-permute-start(bf16[65542]{0:T(1024)(128)(2,1)S(1)} %concatenate.16), channel_id=1, source_target_pairs={{0,16},{16,0},{1,17},{17,1},{2,18},{18,2},{3,19},{19,3},{4,20},{20... | collective-permute-start | bytes 393260 | tf_op jit(solution)/shard_map/ppermute | solution.py:210

commit v11 on v10

--- a/solution.py
+++ b/solution.py
@@ -135,8 +135,6 @@
     tilt_count = images.shape[1]
     neighbours = nbr_local.shape[1]
     peer_count = lax.axis_size("dom")
-    total = own_count * peer_count
-    me = lax.axis_index("dom")
     band_size = tilt_count * OVL * pixels
 
     halfway = jnp.einsum(
@@ -145,39 +143,46 @@
     projected = jnp.einsum(
         "tai,ktil->ktal", slice_rows, halfway, preferred_element_type=jnp.float32
     ).astype(jnp.bfloat16)
-    edges = jnp.stack((projected[:, :, :OVL], projected[:, :, pixels - OVL :]), axis=1)
     stages = gather_stages(peer_count)
-    edges_all = edges
-    for stage in stages[:-1]:
-        pieces = [edges_all]
-        for g in range(1, 2 ** len(stage)):
-            offset = sum(stride for i, stride in enumerate(stage) if (g >> i) & 1)
-            pairs = [(i, i ^ offset) for i in range(peer_count)]
-            pieces.append(lax.ppermute(edges_all, "dom", pairs))
-        edges_all = jnp.concatenate(pieces, axis=0)
-    edges_high = lax.ppermute(edges_all, "dom", [(i, i ^ 1) for i in range(peer_count)])
-
-    weighted, score_tiles, kept_half, sent_half = middle(
-        nbr_owner, nbr_local, nbr_side, nbr_weight, images, projected, edges_all, edges_high,
-        ctf_filter,
-    )
-    score_part = jnp.sum(score_tiles[:, :, 0, 0], axis=0)
+    core_pairs = [(i, i ^ 1) for i in range(peer_count)]
+    chains = []
+    for t in range(tilt_count):
+        tilt = slice(t, t + 1)
+        edges = jnp.stack(
+            (projected[:, tilt, :OVL], projected[:, tilt, pixels - OVL :]), axis=1
+        )
+        edges_all = edges
+        for stage in stages[:-1]:
+            pieces = [edges_all]
+            for g in range(1, 2 ** len(stage)):
+                offset = sum(stride for i, stride in enumerate(stage) if (g >> i) & 1)
+                pairs = [(i, i ^ offset) for i in range(peer_count)]
+                pieces.append(lax.ppermute(edges_all, "dom", pairs))
+            edges_all = jnp.concatenate(pieces, axis=0)
+        edges_high = lax.ppermute(edges_all, "dom", core_pairs)
+        weighted_t, score_t, kept_half, sent_half = middle(
+            nbr_owner, nbr_local, nbr_side, nbr_weight, images[:, tilt], projected[:, tilt],
+            edges_all, edges_high, ctf_filter[tilt],
+        )
+        returned = kept_half + lax.ppermute(sent_half, "dom", core_pairs).astype(jnp.float32)
+        for stage in [tuple(reversed(stage)) for stage in reversed(stages[:-1])]:
+            count = 2 ** len(stage)
+            share = returned.shape[0] // count
+            kept = returned[:share]
+            for g in range(1, count):
+                offset = sum(
+                    stride for i, stride in enumerate(stage) if (g >> (len(stage) - 1 - i)) & 1
+                )
+                pairs = [(i, i ^ offset) for i in range(peer_count)]
+                given = returned[g * share : (g + 1) * share].astype(jnp.bfloat16)
+                kept = kept + lax.ppermute(given, "dom", pairs).astype(jnp.float32)
+            returned = kept
+        chains.append((weighted_t, score_t, returned))
+    weighted = jnp.concatenate([c[0] for c in chains], axis=1)
+    score_part = sum(jnp.sum(c[1][:, :, 0, 0], axis=0) for c in chains)
+    returned = jnp.concatenate([c[2] for c in chains], axis=2)
     tilt_groups = lax.axis_size("tilt")
 
-    pairs = [(i, i ^ 1) for i in range(peer_count)]
-    returned = kept_half + lax.ppermute(sent_half, "dom", pairs).astype(jnp.float32)
-    for stage in [tuple(reversed(stage)) for stage in reversed(stages[:-1])]:
-        count = 2 ** len(stage)
-        share = returned.shape[0] // count
-        kept = returned[:share]
-        for g in range(1, count):
-            offset = sum(
-                stride for i, stride in enumerate(stage) if (g >> (len(stage) - 1 - i)) & 1
-            )
-            pairs = [(i, i ^ offset) for i in range(peer_count)]
-            given = returned[g * share : (g + 1) * share].astype(jnp.bfloat16)
-            kept = kept + lax.ppermute(given, "dom", pairs).astype(jnp.float32)
-        returned = kept
     add_top = returned[:, 0]
     add_bottom = returned[:, 1]
 

time: 54.6 us -> 59.8 us (1.095)
  waiting for transfers between devices: 23.7 us -> 11.6 us
  starting transfers between devices: 16.2 us -> 26.8 us
  local copies, waits for them, and re-layouts: 2.36 us -> 7.1 us
  Pallas kernels: 5.33 us -> 7.26 us
    ppermute x4 -> x8, starting transfers between devices: 6.8 us -> 13.3 us  [on_device(): kept = kept + lax.ppermute(given, 'dom', pairs).astype(jnp.float32)]
    ppermute x4 -> x8, waiting for transfers between devices: 7.5 us -> 2.14 us  [on_device(): kept = kept + lax.ppermute(given, 'dom', pairs).astype(jnp.float32)]
    ppermute x2 -> x4, waiting for transfers between devices: 3.87 us -> 0.01 us  [the longest x2 0.01 us: on_device(): lax.ppermute(sent_half, 'dom', core_pairs).astype(jnp.float32)]
    ppermute x4 -> x8, starting transfers between devices: 7.65 us -> 11.4 us  [on_device(): pieces.append(lax.ppermute(edges_all, 'dom', pairs))]
    ppermute x4 -> x8, waiting for transfers between devices: 8.84 us -> 5.96 us  [on_device(): pieces.append(lax.ppermute(edges_all, 'dom', pairs))]
    slice x0 -> x3, local copies, waits for them, and re-layouts: none -> 2.4 us  [the longest x1 0.84 us: on_device(): projected[:, tilt]]
    pallas_call x1 -> x2, Pallas kernels: 5.33 us -> 7.26 us  [middle(): pl.pallas_call(middle_kernel, grid=(tilt_count,), in_specs=[smem, smem, s...]
    dot_general x1, matrix products: 0.3 us -> 1.61 us  [on_device(): jnp.einsum('tai,ktil->ktal', slice_rows, halfway, preferred_element_type=...]
  transfers between devices with their start and end apart: 11 -> 21, of which waited for: 10 -> 6; matrix products, arithmetic and copies ran while one was open for 2% -> 10% of each run, Pallas kernels for 0% -> 12%
where the time goes in v11:
time: 59.8 us; the launch traced here: 59.4 us
  starting transfers between devices  26.8 us (45%)
  waiting for transfers between devices  11.6 us (19%)
  Pallas kernels  7.26 us (12%)
  local copies, waits for them, and re-layouts  7.1 us (12%)
  other arithmetic  3.6 us (6%)
  matrix products  2.14 us (4%)
  between operations  0.92 us (2%)
    ppermute x8, starting transfers between devices, on_device(): kept = kept + lax.ppermute(given, 'dom', pairs).astype(jnp.float32)  13.3 us
    ppermute x8, starting transfers between devices, on_device(): pieces.append(lax.ppermute(edges_all, 'dom', pairs))  11.4 us
    pallas_call x2, Pallas kernels, middle(): pl.pallas_call(middle_kernel, grid=(tilt_count,), in_specs=[smem, smem, s...  7.26 us
    ppermute x8, waiting for transfers between devices, on_device(): pieces.append(lax.ppermute(edges_all, 'dom', pairs))  5.96 us
    ppermute x1, waiting for transfers between devices, on_device(): parcel = lax.ppermute(parcel, 'tilt', [(0, 1), (1, 0)]).astype(jnp.float32)  3.47 us
    unnamed x25, local copies, waits for them, and re-layouts  2.75 us
    ppermute x8, waiting for transfers between devices, on_device(): kept = kept + lax.ppermute(given, 'dom', pairs).astype(jnp.float32)  2.14 us
    dot_general x1, matrix products, on_device(): jnp.einsum('tai,ktil->ktal', slice_rows, halfway, preferred_element_type=...  1.61 us
  transfers between devices with their start and end apart: 21, of which 6 were waited for; matrix products, arithmetic and copies ran while one was open for 10% of the time, Pallas kernels for 12%

profile of v11, /device:TPU:0, one launch (start us, length us, event | category | flops | bytes accessed | tf_op | source)
XLA Modules:
  0.0 59.4 jit_solution(4387878258397337653)
XLA Ops:
  0.6 0.9 %copy-done = bf16[2,256,256]{2,1,0:T(8,128)(2,1)S(1)} copy-done((bf16[2,256,256]{2,1,0:T(8,128)(2,1)S(1)}, bf16[2,256,256]{2,1,0:T(8,128)(2,1)}, u32[]{:S(2)}) %copy-start) | copy-done | bytes 262168
  1.6 1.6 %fusion.2 = bf16[2,2,256,256]{3,2,0,1:T(8,128)(2,1)S(1)} fusion(bf16[2,256,256]{2,1,0:T(8,128)(2,1)S(1)} %copy-done, bf16[2,256,256]{2,1,0:T(8,128)(2,1)} %param.16, bf16[2,256,256]{2,1,0:T(8,128)(2,1)} %param.13), kind=kOutput, calls=%fused_computation.5 | convolution fusion | flops 268959744 | bytes 1310720 | tf_op jit(solution)/shard_map/tai,ktil->ktal/dot_general | solution.py:143
  3.2 4.1 %collective-permute-start.5 = (bf16[2,2,1,16,256]{4,3,2,1,0:T(8,128)(2,1)S(1)}, bf16[2,2,1,16,256]{4,3,2,1,0:T(8,128)(2,1)S(1)}, u32[]{:S(2)}, u32[]{:S(2)}) collective-permute-start(bf16[2,2,1,16,256]{4,3,2,1,0:T(8,128)(2,1)S(1)} %get-tuple-element.64), channel_id=1, source_target_pairs={{0,8},{1,9},{2,10},{3,11},{4,12},{5,13},{6,14},{7,15},{8,0},{9,1},... | collective-permute-start | bytes 98312 | tf_op jit(solution)/shard_map/ppermute | solution.py:160
  7.4 0.8 %slice_bitcast_fusion.1 = (bf16[2,1,256,256]{3,2,1,0:T(8,128)(2,1)}, bf16[2,1,256,256]{3,2,1,0:T(8,128)(2,1)}) fusion(bf16[2,2,256,256]{3,2,0,1:T(8,128)(2,1)S(1)} %fusion.2), kind=kLoop, calls=%fused_computation.13 | loop fusion | bytes 1048576 | tf_op jit(solution)/shard_map/slice | solution.py:164
  8.3 1.3 %collective-permute-done.5 = bf16[2,2,1,16,256]{4,3,2,1,0:T(8,128)(2,1)S(1)} collective-permute-done((bf16[2,2,1,16,256]{4,3,2,1,0:T(8,128)(2,1)S(1)}, bf16[2,2,1,16,256]{4,3,2,1,0:T(8,128)(2,1)S(1)}, u32[]{:S(2)}, u32[]{:S(2)}) %collective-permute-start.5) | collective-permute-done | bytes 32800 | tf_op jit(solution)/shard_map/ppermute | solution.py:160
  9.6 1.7 %collective-permute-start.6 = (bf16[4,2,1,16,256]{4,3,2,1,0:T(8,128)(2,1)S(1)}, bf16[4,2,1,16,256]{4,3,2,1,0:T(8,128)(2,1)S(1)}, u32[]{:S(2)}, u32[]{:S(2)}) collective-permute-start(bf16[4,2,1,16,256]{4,3,2,1,0:T(8,128)(2,1)S(1)} %pad_maximum_fusion.2), channel_id=1, source_target_pairs={{0,4},{1,5},{2,6},{3,7},{4,0},{5,1},{6,2},{7,3},{8,12},{9,13},{10,... | collective-permute-start | bytes 196616 | tf_op jit(solution)/shard_map/ppermute | solution.py:160
  11.3 1.5 %collective-permute-start.7 = (bf16[4,2,1,16,256]{4,3,2,1,0:T(8,128)(2,1)S(1)}, bf16[4,2,1,16,256]{4,3,2,1,0:T(8,128)(2,1)S(1)}, u32[]{:S(2)}, u32[]{:S(2)}) collective-permute-start(bf16[4,2,1,16,256]{4,3,2,1,0:T(8,128)(2,1)S(1)} %pad_maximum_fusion.2), channel_id=1, source_target_pairs={{0,2},{1,3},{2,0},{3,1},{4,6},{5,7},{6,4},{7,5},{8,10},{9,11},{10,... | collective-permute-start | bytes 196616 | tf_op jit(solution)/shard_map/ppermute | solution.py:160
  13.2 1.7 %collective-permute-start.1 = (bf16[4,2,1,16,256]{4,3,0,2,1:T(8,128)(2,1)S(1)}, bf16[4,2,1,16,256]{4,3,0,2,1:T(8,128)(2,1)S(1)}, u32[]{:S(2)}, u32[]{:S(2)}) collective-permute-start(bf16[4,2,1,16,256]{4,3,0,2,1:T(8,128)(2,1)S(1)} %pad_maximum_fusion.1), channel_id=1, source_target_pairs={{0,4},{1,5},{2,6},{3,7},{4,0},{5,1},{6,2},{7,3},{8,12},{9,13},{10,... | collective-permute-start | bytes 196616 | tf_op jit(solution)/shard_map/ppermute | solution.py:160
  14.9 1.5 %collective-permute-start.2 = (bf16[4,2,1,16,256]{4,3,0,2,1:T(8,128)(2,1)S(1)}, bf16[4,2,1,16,256]{4,3,0,2,1:T(8,128)(2,1)S(1)}, u32[]{:S(2)}, u32[]{:S(2)}) collective-permute-start(bf16[4,2,1,16,256]{4,3,0,2,1:T(8,128)(2,1)S(1)} %pad_maximum_fusion.1), channel_id=1, source_target_pairs={{0,2},{1,3},{2,0},{3,1},{4,6},{5,7},{6,4},{7,5},{8,10},{9,11},{10,... | collective-permute-start | bytes 196616 | tf_op jit(solution)/shard_map/ppermute | solution.py:160
  16.8 1.8 %collective-permute-done.8 = bf16[4,2,1,16,256]{4,3,2,1,0:T(8,128)(2,1)S(1)} collective-permute-done((bf16[4,2,1,16,256]{4,3,2,1,0:T(8,128)(2,1)S(1)}, bf16[4,2,1,16,256]{4,3,2,1,0:T(8,128)(2,1)S(1)}, u32[]{:S(2)}, u32[]{:S(2)}) %collective-permute-start.8) | collective-permute-done | bytes 65568 | tf_op jit(solution)/shard_map/ppermute | solution.py:160
  19.3 2.2 %collective-permute-done.3 = bf16[4,2,1,16,256]{4,3,0,2,1:T(8,128)(2,1)S(1)} collective-permute-done((bf16[4,2,1,16,256]{4,3,0,2,1:T(8,128)(2,1)S(1)}, bf16[4,2,1,16,256]{4,3,0,2,1:T(8,128)(2,1)S(1)}, u32[]{:S(2)}, u32[]{:S(2)}) %collective-permute-start.3) | collective-permute-done | bytes 65568 | tf_op jit(solution)/shard_map/ppermute | solution.py:160
  21.7 0.8 %fusion.31 = (bf16[2,1,256,256]{3,2,1,0:T(8,128)(2,1)}, bf16[2,1,256,256]{3,2,1,0:T(8,128)(2,1)}) fusion(bf16[2,2,256,256]{3,2,1,0:T(8,128)(2,1)S(1)} %copy-done.4), kind=kLoop, calls=%fused_computation.69 | loop fusion | bytes 1048576 | tf_op jit(solution)/shard_map/slice | solution.py:164
  24.7 3.6 %shard_map.105 = (bf16[2,1,256,256]{3,2,1,0:T(8,128)(2,1)}, f32[1,2,8,128]{3,2,1,0:T(8,128)}, f32[16,2,1,16,256]{4,3,2,1,0:T(8,128)}, bf16[16,2,1,16,256]{4,3,2,1,0:T(8,128)(2,1)}) custom-call(s32[2,2,8]{2,1,0:T(2,128)} %owner_ref.3, s32[2,16]{1,0:T(2,128)} %local_ref.3, s32[2,16]{1,0:T(2,128)} %side_ref.3, f32[2,16]{1,0:T(2,128)} %weight_ref.3, ...), custom_call_target="tpu_custom_call" | custom-call | flops 268435456 | bytes 2228224 | tf_op jit(solution)/shard_map/pallas_call | solution.py:85
  29.5 3.7 %shard_map.104 = (bf16[2,1,256,256]{3,2,1,0:T(8,128)(2,1)}, f32[1,2,8,128]{3,2,1,0:T(8,128)}, f32[16,2,1,16,256]{4,3,2,1,0:T(8,128)}, bf16[16,2,1,16,256]{4,3,2,1,0:T(8,128)(2,1)}) custom-call(s32[2,2,8]{2,1,0:T(2,128)} %owner_ref.3, s32[2,16]{1,0:T(2,128)} %local_ref.3, s32[2,16]{1,0:T(2,128)} %side_ref.3, f32[2,16]{1,0:T(2,128)} %weight_ref.3, ...), custom_call_target="tpu_custom_call" | custom-call | flops 268435456 | bytes 2228224 | tf_op jit(solution)/shard_map/pallas_call | solution.py:85
  33.3 1.1 %maximum_convert_fusion = f32[2,2,256,256]{3,2,1,0:T(8,128)S(1)} fusion(bf16[2,1,256,256]{3,2,1,0:T(8,128)(2,1)S(1)} %copy-done.8, bf16[2,1,256,256]{3,2,1,0:T(8,128)(2,1)} %get-tuple-element.34), kind=kLoop, calls=%fused_computation.8 | loop fusion | flops 524288 | bytes 1572864 | tf_op jit(solution)/shard_map/convert_element_type | solution.py:189
  34.3 0.8 %add_reduce_fusion = f32[2]{0:T(128)S(1)} fusion(f32[1,2,8,128]{3,2,1,0:T(8,128)} %get-tuple-element.41, f32[1,2,8,128]{3,2,1,0:T(8,128)} %get-tuple-element.40), kind=kLoop, calls=%fused_computation.59 | loop fusion | flops 2 | bytes 24 | tf_op jit(solution)/shard_map/add | solution.py:182
  36.3 2.6 %collective-permute-start.18 = (bf16[4,2,1,16,256]{4,3,2,1,0:T(8,128)(2,1)S(1)}, bf16[4,2,1,16,256]{4,3,2,1,0:T(8,128)(2,1)S(1)}, u32[]{:S(2)}, u32[]{:S(2)}) collective-permute-start(bf16[4,2,1,16,256]{4,3,2,1,0:T(8,128)(2,1)S(1)} %get-tuple-element.55), channel_id=1, source_target_pairs={{0,6},{1,7},{2,4},{3,5},{4,2},{5,3},{6,0},{7,1},{8,14},{9,15},{10,... | collective-permute-start | bytes 196616 | tf_op jit(solution)/shard_map/ppermute | solution.py:178
  40.0 2.6 %collective-permute-start.13 = (bf16[4,2,1,16,256]{4,3,2,1,0:T(8,128)(2,1)S(1)}, bf16[4,2,1,16,256]{4,3,2,1,0:T(8,128)(2,1)S(1)}, u32[]{:S(2)}, u32[]{:S(2)}) collective-permute-start(bf16[4,2,1,16,256]{4,3,2,1,0:T(8,128)(2,1)S(1)} %get-tuple-element.58), channel_id=1, source_target_pairs={{0,6},{1,7},{2,4},{3,5},{4,2},{5,3},{6,0},{7,1},{8,14},{9,15},{10,... | collective-permute-start | bytes 196616 | tf_op jit(solution)/shard_map/ppermute | solution.py:178
  42.6 3.4 %collective-permute-start.19 = (bf16[2,2,1,16,256]{4,3,2,1,0:T(8,128)(2,1)S(1)}, bf16[2,2,1,16,256]{4,3,2,1,0:T(8,128)(2,1)S(1)}, u32[]{:S(2)}, u32[]{:S(2)}) collective-permute-start(bf16[2,2,1,16,256]{4,3,2,1,0:T(8,128)(2,1)S(1)} %slice.270), channel_id=1, source_target_pairs={{0,8},{1,9},{2,10},{3,11},{4,12},{5,13},{6,14},{7,15},{8,0},{9,1},... | collective-permute-start | bytes 98312 | tf_op jit(solution)/shard_map/ppermute | solution.py:178
  46.1 2.7 %collective-permute-start.14 = (bf16[2,2,1,16,256]{4,3,2,1,0:T(8,128)(2,1)S(1)}, bf16[2,2,1,16,256]{4,3,2,1,0:T(8,128)(2,1)S(1)}, u32[]{:S(2)}, u32[]{:S(2)}) collective-permute-start(bf16[2,2,1,16,256]{4,3,2,1,0:T(8,128)(2,1)S(1)} %slice.271), channel_id=1, source_target_pairs={{0,8},{1,9},{2,10},{3,11},{4,12},{5,13},{6,14},{7,15},{8,0},{9,1},... | collective-permute-start | bytes 98312 | tf_op jit(solution)/shard_map/ppermute | solution.py:178
  48.9 2.1 %collective-permute-done.14 = bf16[2,2,1,16,256]{4,3,2,1,0:T(8,128)(2,1)S(1)} collective-permute-done((bf16[2,2,1,16,256]{4,3,2,1,0:T(8,128)(2,1)S(1)}, bf16[2,2,1,16,256]{4,3,2,1,0:T(8,128)(2,1)S(1)}, u32[]{:S(2)}, u32[]{:S(2)}) %collective-permute-start.14) | collective-permute-done | bytes 32800 | tf_op jit(solution)/shard_map/ppermute | solution.py:178
  51.1 0.9 %copy-done.1 = bf16[2,256,256]{2,1,0:T(8,128)(2,1)S(1)} copy-done((bf16[2,256,256]{2,1,0:T(8,128)(2,1)S(1)}, bf16[2,256,256]{2,1,0:T(8,128)(2,1)}, u32[]{:S(2)}) %copy-start.1) | copy-done | bytes 262168
  53.0 1.5 %collective-permute-start.20 = (bf16[65542]{0:T(1024)(128)(2,1)S(1)}, bf16[65542]{0:T(1024)(128)(2,1)S(1)}, u32[]{:S(2)}, u32[]{:S(2)}) collective-permute-start(bf16[65542]{0:T(1024)(128)(2,1)S(1)} %concatenate.33), channel_id=1, source_target_pairs={{0,16},{16,0},{1,17},{17,1},{2,18},{18,2},{3,19},{19,3},{4,20},{20... | collective-permute-start | bytes 393260 | tf_op jit(solution)/shard_map/ppermute | solution.py:215
  54.5 3.5 %collective-permute-done.20 = bf16[65542]{0:T(1024)(128)(2,1)S(1)} collective-permute-done((bf16[65542]{0:T(1024)(128)(2,1)S(1)}, bf16[65542]{0:T(1024)(128)(2,1)S(1)}, u32[]{:S(2)}, u32[]{:S(2)}) %collective-permute-start.20) | collective-permute-done | bytes 131116 | tf_op jit(solution)/shard_map/ppermute | solution.py:215
  (81 shorter events, 10.0 us)
Async XLA Ops:
  3.2 6.3 %collective-permute-start.5 = (bf16[2,2,1,16,256]{4,3,2,1,0:T(8,128)(2,1)S(1)}, bf16[2,2,1,16,256]{4,3,2,1,0:T(8,128)(2,1)S(1)}, u32[]{:S(2)}, u32[]{:S(2)}) collective-permute-start(bf16[2,2,1,16,256]{4,3,2,1,0:T(8,128)(2,1)S(1)} %get-tuple-element.64), channel_id=1, source_target_pairs={{0,8},{1,9},{2,10},{3,11},{4,12},{5,13},{6,14},{7,15},{8,0},{9,1},... | collective-permute-start | bytes 98312 | tf_op jit(solution)/shard_map/ppermute | solution.py:160
  7.3 5.8 %collective-permute-start = (bf16[2,2,1,16,256]{4,3,0,2,1:T(8,128)(2,1)S(1)}, bf16[2,2,1,16,256]{4,3,0,2,1:T(8,128)(2,1)S(1)}, u32[]{:S(2)}, u32[]{:S(2)}) collective-permute-start(bf16[2,2,1,16,256]{4,3,0,2,1:T(8,128)(2,1)S(1)} %get-tuple-element.62), channel_id=1, source_target_pairs={{0,8},{1,9},{2,10},{3,11},{4,12},{5,13},{6,14},{7,15},{8,0},{9,1},... | collective-permute-start | bytes 98312 | tf_op jit(solution)/shard_map/ppermute | solution.py:160
  9.6 12.1 %copy-start.4 = (bf16[2,2,256,256]{3,2,1,0:T(8,128)(2,1)S(1)}, bf16[2,2,256,256]{3,2,1,0:T(8,128)(2,1)}, u32[]{:S(2)}) copy-start(bf16[2,2,256,256]{3,2,1,0:T(8,128)(2,1)} %param.14) | copy-start | bytes 1572868
  9.6 6.8 %collective-permute-start.6 = (bf16[4,2,1,16,256]{4,3,2,1,0:T(8,128)(2,1)S(1)}, bf16[4,2,1,16,256]{4,3,2,1,0:T(8,128)(2,1)S(1)}, u32[]{:S(2)}, u32[]{:S(2)}) collective-permute-start(bf16[4,2,1,16,256]{4,3,2,1,0:T(8,128)(2,1)S(1)} %pad_maximum_fusion.2), channel_id=1, source_target_pairs={{0,4},{1,5},{2,6},{3,7},{4,0},{5,1},{6,2},{7,3},{8,12},{9,13},{10,... | collective-permute-start | bytes 196616 | tf_op jit(solution)/shard_map/ppermute | solution.py:160
  11.3 5.5 %collective-permute-start.7 = (bf16[4,2,1,16,256]{4,3,2,1,0:T(8,128)(2,1)S(1)}, bf16[4,2,1,16,256]{4,3,2,1,0:T(8,128)(2,1)S(1)}, u32[]{:S(2)}, u32[]{:S(2)}) collective-permute-start(bf16[4,2,1,16,256]{4,3,2,1,0:T(8,128)(2,1)S(1)} %pad_maximum_fusion.2), channel_id=1, source_target_pairs={{0,2},{1,3},{2,0},{3,1},{4,6},{5,7},{6,4},{7,5},{8,10},{9,11},{10,... | collective-permute-start | bytes 196616 | tf_op jit(solution)/shard_map/ppermute | solution.py:160
  12.8 5.9 %collective-permute-start.8 = (bf16[4,2,1,16,256]{4,3,2,1,0:T(8,128)(2,1)S(1)}, bf16[4,2,1,16,256]{4,3,2,1,0:T(8,128)(2,1)S(1)}, u32[]{:S(2)}, u32[]{:S(2)}) collective-permute-start(bf16[4,2,1,16,256]{4,3,2,1,0:T(8,128)(2,1)S(1)} %pad_maximum_fusion.2), channel_id=1, source_target_pairs={{0,6},{1,7},{2,4},{3,5},{4,2},{5,3},{6,0},{7,1},{8,14},{9,15},{10,... | collective-permute-start | bytes 196616 | tf_op jit(solution)/shard_map/ppermute | solution.py:160
  13.2 5.6 %collective-permute-start.1 = (bf16[4,2,1,16,256]{4,3,0,2,1:T(8,128)(2,1)S(1)}, bf16[4,2,1,16,256]{4,3,0,2,1:T(8,128)(2,1)S(1)}, u32[]{:S(2)}, u32[]{:S(2)}) collective-permute-start(bf16[4,2,1,16,256]{4,3,0,2,1:T(8,128)(2,1)S(1)} %pad_maximum_fusion.1), channel_id=1, source_target_pairs={{0,4},{1,5},{2,6},{3,7},{4,0},{5,1},{6,2},{7,3},{8,12},{9,13},{10,... | collective-permute-start | bytes 196616 | tf_op jit(solution)/shard_map/ppermute | solution.py:160
  14.9 4.5 %collective-permute-start.2 = (bf16[4,2,1,16,256]{4,3,0,2,1:T(8,128)(2,1)S(1)}, bf16[4,2,1,16,256]{4,3,0,2,1:T(8,128)(2,1)S(1)}, u32[]{:S(2)}, u32[]{:S(2)}) collective-permute-start(bf16[4,2,1,16,256]{4,3,0,2,1:T(8,128)(2,1)S(1)} %pad_maximum_fusion.1), channel_id=1, source_target_pairs={{0,2},{1,3},{2,0},{3,1},{4,6},{5,7},{6,4},{7,5},{8,10},{9,11},{10,... | collective-permute-start | bytes 196616 | tf_op jit(solution)/shard_map/ppermute | solution.py:160
  16.4 5.2 %collective-permute-start.3 = (bf16[4,2,1,16,256]{4,3,0,2,1:T(8,128)(2,1)S(1)}, bf16[4,2,1,16,256]{4,3,0,2,1:T(8,128)(2,1)S(1)}, u32[]{:S(2)}, u32[]{:S(2)}) collective-permute-start(bf16[4,2,1,16,256]{4,3,0,2,1:T(8,128)(2,1)S(1)} %pad_maximum_fusion.1), channel_id=1, source_target_pairs={{0,6},{1,7},{2,4},{3,5},{4,2},{5,3},{6,0},{7,1},{8,14},{9,15},{10,... | collective-permute-start | bytes 196616 | tf_op jit(solution)/shard_map/ppermute | solution.py:160
  18.7 3.9 %copy-start.5 = (bf16[16,2,1,16,256]{4,3,2,1,0:T(8,128)(2,1)}, bf16[16,2,1,16,256]{4,3,2,1,0:T(8,128)(2,1)S(1)}, u32[]{:S(2)}) copy-start(bf16[16,2,1,16,256]{4,3,2,1,0:T(8,128)(2,1)S(1)} %constant_dynamic-update-slice_fusion.5.low_ref) | copy-start | bytes 786436
  18.7 5.4 %collective-permute-start.9 = (bf16[16,2,1,16,256]{4,3,2,1,0:T(8,128)(2,1)S(1)}, bf16[16,2,1,16,256]{4,3,2,1,0:T(8,128)(2,1)S(1)}, u32[]{:S(2)}, u32[]{:S(2)}) collective-permute-start(bf16[16,2,1,16,256]{4,3,2,1,0:T(8,128)(2,1)S(1)} %constant_dynamic-update-slice_fusion.5.low_ref), channel_id=1, source_target_pairs={{0,1},{1,0},{2,3},{3,2},{4,5},{5,4},{6,7},{7,6},{8,9},{9,8},{10,11... | collective-permute-start | bytes 786440 | tf_op jit(solution)/shard_map/ppermute | solution.py:162
  21.6 7.2 %collective-permute-start.4 = (bf16[16,2,1,16,256]{4,3,0,2,1:T(8,128)(2,1)S(1)}, bf16[16,2,1,16,256]{4,3,0,2,1:T(8,128)(2,1)S(1)}, u32[]{:S(2)}, u32[]{:S(2)}) collective-permute-start(bf16[16,2,1,16,256]{4,3,0,2,1:T(8,128)(2,1)S(1)} %constant_dynamic-update-slice_fusion), channel_id=1, source_target_pairs={{0,1},{1,0},{2,3},{3,2},{4,5},{5,4},{6,7},{7,6},{8,9},{9,8},{10,11... | collective-permute-start | bytes 786440 | tf_op jit(solution)/shard_map/ppermute | solution.py:162
  28.3 6.8 %collective-permute-start.15 = (bf16[16,2,1,16,256]{4,3,2,1,0:T(8,128)(2,1)}, bf16[16,2,1,16,256]{4,3,2,1,0:T(8,128)(2,1)S(1)}, u32[]{:S(2)}, u32[]{:S(2)}) collective-permute-start(bf16[16,2,1,16,256]{4,3,2,1,0:T(8,128)(2,1)} %get-tuple-element.39), channel_id=1, source_target_pairs={{0,1},{1,0},{2,3},{3,2},{4,5},{5,4},{6,7},{7,6},{8,9},{9,8},{10,11... | collective-permute-start | bytes 786440 | tf_op jit(solution)/shard_map/ppermute | solution.py:167
  29.5 3.7 %copy-start.8 = (bf16[2,1,256,256]{3,2,1,0:T(8,128)(2,1)S(1)}, bf16[2,1,256,256]{3,2,1,0:T(8,128)(2,1)}, u32[]{:S(2)}) copy-start(bf16[2,1,256,256]{3,2,1,0:T(8,128)(2,1)} %get-tuple-element.35) | copy-start | bytes 786436
  33.2 5.7 %collective-permute-start.10 = (bf16[16,2,1,16,256]{4,3,2,1,0:T(8,128)(2,1)}, bf16[16,2,1,16,256]{4,3,2,1,0:T(8,128)(2,1)S(1)}, u32[]{:S(2)}, u32[]{:S(2)}) collective-permute-start(bf16[16,2,1,16,256]{4,3,2,1,0:T(8,128)(2,1)} %get-tuple-element.37), channel_id=1, source_target_pairs={{0,1},{1,0},{2,3},{3,2},{4,5},{5,4},{6,7},{7,6},{8,9},{9,8},{10,11... | collective-permute-start | bytes 786440 | tf_op jit(solution)/shard_map/ppermute | solution.py:167
  35.3 4.7 %collective-permute-start.16 = (bf16[4,2,1,16,256]{4,3,2,1,0:T(8,128)(2,1)S(1)}, bf16[4,2,1,16,256]{4,3,2,1,0:T(8,128)(2,1)S(1)}, u32[]{:S(2)}, u32[]{:S(2)}) collective-permute-start(bf16[4,2,1,16,256]{4,3,2,1,0:T(8,128)(2,1)S(1)} %get-tuple-element.54), channel_id=1, source_target_pairs={{0,4},{1,5},{2,6},{3,7},{4,0},{5,1},{6,2},{7,3},{8,12},{9,13},{10,... | collective-permute-start | bytes 196616 | tf_op jit(solution)/shard_map/ppermute | solution.py:178
  36.0 6.6 %collective-permute-start.17 = (bf16[4,2,1,16,256]{4,3,2,1,0:T(8,128)(2,1)S(1)}, bf16[4,2,1,16,256]{4,3,2,1,0:T(8,128)(2,1)S(1)}, u32[]{:S(2)}, u32[]{:S(2)}) collective-permute-start(bf16[4,2,1,16,256]{4,3,2,1,0:T(8,128)(2,1)S(1)} %get-tuple-element.56), channel_id=1, source_target_pairs={{0,2},{1,3},{2,0},{3,1},{4,6},{5,7},{6,4},{7,5},{8,10},{9,11},{10,... | collective-permute-start | bytes 196616 | tf_op jit(solution)/shard_map/ppermute | solution.py:178
  36.3 6.3 %collective-permute-start.18 = (bf16[4,2,1,16,256]{4,3,2,1,0:T(8,128)(2,1)S(1)}, bf16[4,2,1,16,256]{4,3,2,1,0:T(8,128)(2,1)S(1)}, u32[]{:S(2)}, u32[]{:S(2)}) collective-permute-start(bf16[4,2,1,16,256]{4,3,2,1,0:T(8,128)(2,1)S(1)} %get-tuple-element.55), channel_id=1, source_target_pairs={{0,6},{1,7},{2,4},{3,5},{4,2},{5,3},{6,0},{7,1},{8,14},{9,15},{10,... | collective-permute-start | bytes 196616 | tf_op jit(solution)/shard_map/ppermute | solution.py:178
  39.0 7.1 %collective-permute-start.11 = (bf16[4,2,1,16,256]{4,3,2,1,0:T(8,128)(2,1)S(1)}, bf16[4,2,1,16,256]{4,3,2,1,0:T(8,128)(2,1)S(1)}, u32[]{:S(2)}, u32[]{:S(2)}) collective-permute-start(bf16[4,2,1,16,256]{4,3,2,1,0:T(8,128)(2,1)S(1)} %get-tuple-element.57), channel_id=1, source_target_pairs={{0,4},{1,5},{2,6},{3,7},{4,0},{5,1},{6,2},{7,3},{8,12},{9,13},{10,... | collective-permute-start | bytes 196616 | tf_op jit(solution)/shard_map/ppermute | solution.py:178
  39.7 6.4 %collective-permute-start.12 = (bf16[4,2,1,16,256]{4,3,2,1,0:T(8,128)(2,1)S(1)}, bf16[4,2,1,16,256]{4,3,2,1,0:T(8,128)(2,1)S(1)}, u32[]{:S(2)}, u32[]{:S(2)}) collective-permute-start(bf16[4,2,1,16,256]{4,3,2,1,0:T(8,128)(2,1)S(1)} %get-tuple-element.59), channel_id=1, source_target_pairs={{0,2},{1,3},{2,0},{3,1},{4,6},{5,7},{6,4},{7,5},{8,10},{9,11},{10,... | collective-permute-start | bytes 196616 | tf_op jit(solution)/shard_map/ppermute | solution.py:178
  40.0 6.1 %collective-permute-start.13 = (bf16[4,2,1,16,256]{4,3,2,1,0:T(8,128)(2,1)S(1)}, bf16[4,2,1,16,256]{4,3,2,1,0:T(8,128)(2,1)S(1)}, u32[]{:S(2)}, u32[]{:S(2)}) collective-permute-start(bf16[4,2,1,16,256]{4,3,2,1,0:T(8,128)(2,1)S(1)} %get-tuple-element.58), channel_id=1, source_target_pairs={{0,6},{1,7},{2,4},{3,5},{4,2},{5,3},{6,0},{7,1},{8,14},{9,15},{10,... | collective-permute-start | bytes 196616 | tf_op jit(solution)/shard_map/ppermute | solution.py:178
  42.6 6.3 %collective-permute-start.19 = (bf16[2,2,1,16,256]{4,3,2,1,0:T(8,128)(2,1)S(1)}, bf16[2,2,1,16,256]{4,3,2,1,0:T(8,128)(2,1)S(1)}, u32[]{:S(2)}, u32[]{:S(2)}) collective-permute-start(bf16[2,2,1,16,256]{4,3,2,1,0:T(8,128)(2,1)S(1)} %slice.270), channel_id=1, source_target_pairs={{0,8},{1,9},{2,10},{3,11},{4,12},{5,13},{6,14},{7,15},{8,0},{9,1},... | collective-permute-start | bytes 98312 | tf_op jit(solution)/shard_map/ppermute | solution.py:178
  46.1 4.9 %collective-permute-start.14 = (bf16[2,2,1,16,256]{4,3,2,1,0:T(8,128)(2,1)S(1)}, bf16[2,2,1,16,256]{4,3,2,1,0:T(8,128)(2,1)S(1)}, u32[]{:S(2)}, u32[]{:S(2)}) collective-permute-start(bf16[2,2,1,16,256]{4,3,2,1,0:T(8,128)(2,1)S(1)} %slice.271), channel_id=1, source_target_pairs={{0,8},{1,9},{2,10},{3,11},{4,12},{5,13},{6,14},{7,15},{8,0},{9,1},... | collective-permute-start | bytes 98312 | tf_op jit(solution)/shard_map/ppermute | solution.py:178
  53.0 5.0 %collective-permute-start.20 = (bf16[65542]{0:T(1024)(128)(2,1)S(1)}, bf16[65542]{0:T(1024)(128)(2,1)S(1)}, u32[]{:S(2)}, u32[]{:S(2)}) collective-permute-start(bf16[65542]{0:T(1024)(128)(2,1)S(1)} %concatenate.33), channel_id=1, source_target_pairs={{0,16},{16,0},{1,17},{17,1},{2,18},{18,2},{3,19},{19,3},{4,20},{20... | collective-permute-start | bytes 393260 | tf_op jit(solution)/shard_map/ppermute | solution.py:215
  (6 other events, 9.2 us)

commit v12 on v10

--- a/solution.py
+++ b/solution.py
@@ -117,6 +117,47 @@
     )(owner, local, side, weight, images, projected, edges_low, edges_high, ctf_filter)
 
 
+def project_kernel(section_ref, rows_ref, cols_ref, projected_ref, edge_ref):
+    own_count = section_ref.shape[0]
+    pixels = section_ref.shape[-1]
+    for k in range(own_count):
+        halfway = lax.dot_general(
+            section_ref[k], cols_ref[0], (((1,), (1,)), ((), ())),
+            preferred_element_type=jnp.float32,
+        ).astype(jnp.bfloat16)
+        projected = jnp.dot(rows_ref[0], halfway, preferred_element_type=jnp.float32).astype(
+            jnp.bfloat16
+        )
+        projected_ref[k, 0] = projected
+        edge_ref[k, 0, 0] = projected[:OVL]
+        edge_ref[k, 1, 0] = projected[pixels - OVL :]
+
+
+def project(sections, slice_rows, slice_cols):
+    own_count, pixels, _ = sections.shape
+    tilt_count = slice_rows.shape[0]
+    per_tilt = pl.BlockSpec((1, pixels, pixels), lambda t: (t, 0, 0))
+    return pl.pallas_call(
+        project_kernel,
+        grid=(tilt_count,),
+        in_specs=[pl.BlockSpec(sections.shape, lambda t: (0, 0, 0)), per_tilt, per_tilt],
+        out_specs=[
+            pl.BlockSpec((own_count, 1, pixels, pixels), lambda t: (0, t, 0, 0)),
+            pl.BlockSpec((own_count, 2, 1, OVL, pixels), lambda t: (0, 0, t, 0, 0)),
+        ],
+        out_shape=[
+            jax.ShapeDtypeStruct((own_count, tilt_count, pixels, pixels), jnp.bfloat16),
+            jax.ShapeDtypeStruct((own_count, 2, tilt_count, OVL, pixels), jnp.bfloat16),
+        ],
+        compiler_params=pltpu.CompilerParams(dimension_semantics=("arbitrary",)),
+        cost_estimate=pl.CostEstimate(
+            flops=4 * own_count * tilt_count * pixels**3,
+            transcendentals=0,
+            bytes_accessed=2 * (sections.size + 2 * slice_rows.size + 2 * own_count * slice_rows.size),
+        ),
+    )(sections, slice_rows, slice_cols)
+
+
 def gather_stages(peer_count):
     steps = peer_count.bit_length() - 1
     strides = [peer_count >> (b + 1) for b in range(steps)]
@@ -139,13 +180,7 @@
     me = lax.axis_index("dom")
     band_size = tilt_count * OVL * pixels
 
-    halfway = jnp.einsum(
-        "kij,tlj->ktil", sections, slice_cols, preferred_element_type=jnp.float32
-    ).astype(jnp.bfloat16)
-    projected = jnp.einsum(
-        "tai,ktil->ktal", slice_rows, halfway, preferred_element_type=jnp.float32
-    ).astype(jnp.bfloat16)
-    edges = jnp.stack((projected[:, :, :OVL], projected[:, :, pixels - OVL :]), axis=1)
+    projected, edges = project(sections, slice_rows, slice_cols)
     stages = gather_stages(peer_count)
     edges_all = edges
     for stage in stages[:-1]:

time: 54.6 us -> 56.4 us (1.033)
  Pallas kernels: 5.33 us -> 8.54 us
  matrix products: 2.12 us -> 0.53 us
  local copies, waits for them, and re-layouts: 2.36 us -> 3.25 us
  waiting for transfers between devices: 23.7 us -> 23 us
    pallas_call x0 -> x1, Pallas kernels: none -> 3.2 us  [project(): pl.pallas_call(project_kernel, grid=(tilt_count,), in_specs=[pl.BlockSpec...]
    dot_general x2 -> x0, matrix products: 1.58 us -> none  [the longest x1 1.28 us: on_device(): jnp.einsum('kij,tlj->ktil', sections, slice_cols, preferred_element_type=...]
    unnamed x16 -> x14, local copies, waits for them, and re-layouts: 1.88 us -> 2.76 us
    another operation x2 -> x1, other arithmetic: 1.43 us -> 1.41 us
  transfers between devices with their start and end apart: 11 -> 11, of which waited for: 10 -> 10; matrix products, arithmetic and copies ran while one was open for 2% -> 3% of each run, Pallas kernels for 0% -> 0%
where the time goes in v12:
time: 56.4 us; the launch traced here: 56.1 us
  waiting for transfers between devices  23 us (41%)
  starting transfers between devices  16.1 us (29%)
  Pallas kernels  8.54 us (15%)
  other arithmetic  3.8 us (7%)
  local copies, waits for them, and re-layouts  3.25 us (6%)
  between operations  0.78 us (1%)
    ppermute x4, waiting for transfers between devices, on_device(): pieces.append(lax.ppermute(edges_all, 'dom', pairs))  8.29 us
    ppermute x4, starting transfers between devices, on_device(): pieces.append(lax.ppermute(edges_all, 'dom', pairs))  7.59 us
    ppermute x4, waiting for transfers between devices, on_device(): kept = kept + lax.ppermute(given, 'dom', pairs).astype(jnp.float32)  7.37 us
    ppermute x4, starting transfers between devices, on_device(): kept = kept + lax.ppermute(given, 'dom', pairs).astype(jnp.float32)  6.79 us
    pallas_call x1, Pallas kernels, middle(): pl.pallas_call(middle_kernel, grid=(tilt_count,), in_specs=[smem, smem, s...  5.34 us
    ppermute x1, waiting for transfers between devices, on_device(): parcel = lax.ppermute(parcel, 'tilt', [(0, 1), (1, 0)]).astype(jnp.float32)  3.46 us
    pallas_call x1, Pallas kernels, project(): pl.pallas_call(project_kernel, grid=(tilt_count,), in_specs=[pl.BlockSpec...  3.2 us
    unnamed x14, local copies, waits for them, and re-layouts  2.76 us
  transfers between devices with their start and end apart: 11, of which 10 were waited for; matrix products, arithmetic and copies ran while one was open for 3% of the time, Pallas kernels for 0%

profile of v12, /device:TPU:0, one launch (start us, length us, event | category | flops | bytes accessed | tf_op | source)
XLA Modules:
  0.0 56.1 jit_solution(13290227230458811705)
XLA Ops:
  0.6 3.2 %shard_map.104 = (bf16[2,2,256,256]{3,2,1,0:T(8,128)(2,1)}, bf16[2,2,2,16,256]{4,3,2,1,0:T(8,128)(2,1)}) custom-call(bf16[2,256,256]{2,1,0:T(8,128)(2,1)} %section_ref.1, bf16[2,256,256]{2,1,0:T(8,128)(2,1)} %rows_ref.1, bf16[2,256,256]{2,1,0:T(8,128)(2,1)} %cols_ref.1), custom_call_target="tpu_custom_call" | custom-call | flops 268435456 | bytes 1835008 | tf_op jit(solution)/shard_map/pallas_call | solution.py:140
  3.8 4.0 %collective-permute-start = (bf16[2,2,2,16,256]{4,3,2,1,0:T(8,128)(2,1)}, bf16[2,2,2,16,256]{4,3,2,1,0:T(8,128)(2,1)S(1)}, u32[]{:S(2)}, u32[]{:S(2)}) collective-permute-start(bf16[2,2,2,16,256]{4,3,2,1,0:T(8,128)(2,1)} %get-tuple-element.33), channel_id=1, source_target_pairs={{0,8},{1,9},{2,10},{3,11},{4,12},{5,13},{6,14},{7,15},{8,0},{9,1},... | collective-permute-start | bytes 196616 | tf_op jit(solution)/shard_map/ppermute | solution.py:191
  7.9 0.9 %constant_dynamic-update-slice_fusion.1 = (bf16[4,2,2,16,256]{4,3,2,1,0:T(8,128)(2,1)S(1)}, bf16[16,2,2,16,256]{4,3,2,1,0:T(8,128)(2,1)S(1)}) fusion(bf16[2,2,2,16,256]{4,3,2,1,0:T(8,128)(2,1)} %get-tuple-element.33), kind=kLoop, calls=%fused_computation.22 | loop fusion | bytes 196608
  8.7 3.0 %collective-permute-done = bf16[2,2,2,16,256]{4,3,2,1,0:T(8,128)(2,1)S(1)} collective-permute-done((bf16[2,2,2,16,256]{4,3,2,1,0:T(8,128)(2,1)}, bf16[2,2,2,16,256]{4,3,2,1,0:T(8,128)(2,1)S(1)}, u32[]{:S(2)}, u32[]{:S(2)}) %collective-permute-start) | collective-permute-done | bytes 65568 | tf_op jit(solution)/shard_map/ppermute | solution.py:191
  12.5 1.5 %collective-permute-start.2 = (bf16[4,2,2,16,256]{4,3,2,1,0:T(8,128)(2,1)S(1)}, bf16[4,2,2,16,256]{4,3,2,1,0:T(8,128)(2,1)S(1)}, u32[]{:S(2)}, u32[]{:S(2)}) collective-permute-start(bf16[4,2,2,16,256]{4,3,2,1,0:T(8,128)(2,1)S(1)} %get-tuple-element.43), channel_id=1, source_target_pairs={{0,2},{1,3},{2,0},{3,1},{4,6},{5,7},{6,4},{7,5},{8,10},{9,11},{10,... | collective-permute-start | bytes 393224 | tf_op jit(solution)/shard_map/ppermute | solution.py:191
  14.0 1.3 %collective-permute-start.3 = (bf16[4,2,2,16,256]{4,3,2,1,0:T(8,128)(2,1)S(1)}, bf16[4,2,2,16,256]{4,3,2,1,0:T(8,128)(2,1)S(1)}, u32[]{:S(2)}, u32[]{:S(2)}) collective-permute-start(bf16[4,2,2,16,256]{4,3,2,1,0:T(8,128)(2,1)S(1)} %get-tuple-element.43), channel_id=1, source_target_pairs={{0,6},{1,7},{2,4},{3,5},{4,2},{5,3},{6,0},{7,1},{8,14},{9,15},{10,... | collective-permute-start | bytes 393224 | tf_op jit(solution)/shard_map/ppermute | solution.py:191
  15.3 2.7 %collective-permute-done.1 = bf16[4,2,2,16,256]{4,3,2,1,0:T(8,128)(2,1)S(1)} collective-permute-done((bf16[4,2,2,16,256]{4,3,2,1,0:T(8,128)(2,1)S(1)}, bf16[4,2,2,16,256]{4,3,2,1,0:T(8,128)(2,1)S(1)}, u32[]{:S(2)}, u32[]{:S(2)}) %collective-permute-start.1) | collective-permute-done | bytes 131104 | tf_op jit(solution)/shard_map/ppermute | solution.py:191
  18.0 1.0 %collective-permute-done.2 = bf16[4,2,2,16,256]{4,3,2,1,0:T(8,128)(2,1)S(1)} collective-permute-done((bf16[4,2,2,16,256]{4,3,2,1,0:T(8,128)(2,1)S(1)}, bf16[4,2,2,16,256]{4,3,2,1,0:T(8,128)(2,1)S(1)}, u32[]{:S(2)}, u32[]{:S(2)}) %collective-permute-start.2) | collective-permute-done | bytes 131104 | tf_op jit(solution)/shard_map/ppermute | solution.py:191
  19.0 1.6 %collective-permute-done.3 = bf16[4,2,2,16,256]{4,3,2,1,0:T(8,128)(2,1)S(1)} collective-permute-done((bf16[4,2,2,16,256]{4,3,2,1,0:T(8,128)(2,1)S(1)}, bf16[4,2,2,16,256]{4,3,2,1,0:T(8,128)(2,1)S(1)}, u32[]{:S(2)}, u32[]{:S(2)}) %collective-permute-start.3) | collective-permute-done | bytes 131104 | tf_op jit(solution)/shard_map/ppermute | solution.py:191
  20.7 1.9 %collective-permute-done.4.high_ref = bf16[16,2,2,16,256]{4,3,2,1,0:T(8,128)(2,1)S(1)} collective-permute-done((bf16[16,2,2,16,256]{4,3,2,1,0:T(8,128)(2,1)S(1)}, bf16[16,2,2,16,256]{4,3,2,1,0:T(8,128)(2,1)S(1)}, u32[]{:S(2)}, u32[]{:S(2)}) %collective-permute-start.4) | collective-permute-done | bytes 524320 | tf_op jit(solution)/shard_map/ppermute | solution.py:193
  23.4 5.3 %shard_map.105 = (bf16[2,2,256,256]{3,2,1,0:T(8,128)(2,1)}, f32[2,2,8,128]{3,2,1,0:T(8,128)}, f32[16,2,2,16,256]{4,3,2,1,0:T(8,128)}, bf16[16,2,2,16,256]{4,3,2,1,0:T(8,128)(2,1)}) custom-call(s32[2,2,8]{2,1,0:T(2,128)} %owner_ref.1, s32[2,16]{1,0:T(2,128)} %local_ref.1, s32[2,16]{1,0:T(2,128)} %side_ref.1, f32[2,16]{1,0:T(2,128)} %weight_ref.1, ...), custom_call_target="tpu_custom_call" | custom-call | flops 536870912 | bytes 4456448 | tf_op jit(solution)/shard_map/pallas_call | solution.py:85
  28.9 2.0 %collective-permute-done.5 = bf16[16,2,2,16,256]{4,3,2,1,0:T(8,128)(2,1)S(1)} collective-permute-done((bf16[16,2,2,16,256]{4,3,2,1,0:T(8,128)(2,1)}, bf16[16,2,2,16,256]{4,3,2,1,0:T(8,128)(2,1)S(1)}, u32[]{:S(2)}, u32[]{:S(2)}) %collective-permute-start.5) | collective-permute-done | bytes 524320 | tf_op jit(solution)/shard_map/ppermute | solution.py:203
  30.9 1.4 %fusion.17 = (bf16[16,2,2,16,256]{4,3,2,1,0:T(8,128)(2,1)S(1)}, f32[16,2,2,16,256]{4,3,2,1,0:T(8,128)S(1)}) fusion(f32[16,2,2,16,256]{4,3,2,1,0:T(8,128)} %get-tuple-element.35, bf16[16,2,2,16,256]{4,3,2,1,0:T(8,128)(2,1)S(1)} %collective-permute-done.5), kind=kLoop, calls=%fused_computation.36 | loop fusion | flops 786432 | bytes 3145728 | tf_op jit(solution)/shard_map/convert.3
  32.4 0.8 %collective-permute-start.6 = (bf16[4,2,2,16,256]{4,3,2,1,0:T(8,128)(2,1)S(1)}, bf16[4,2,2,16,256]{4,3,2,1,0:T(8,128)(2,1)S(1)}, u32[]{:S(2)}, u32[]{:S(2)}) collective-permute-start(bf16[4,2,2,16,256]{4,3,2,1,0:T(8,128)(2,1)S(1)} %get-tuple-element.40), channel_id=1, source_target_pairs={{0,4},{1,5},{2,6},{3,7},{4,0},{5,1},{6,2},{7,3},{8,12},{9,13},{10,... | collective-permute-start | bytes 393224 | tf_op jit(solution)/shard_map/ppermute | solution.py:214
  33.2 1.1 %collective-permute-start.7 = (bf16[4,2,2,16,256]{4,3,2,1,0:T(8,128)(2,1)S(1)}, bf16[4,2,2,16,256]{4,3,2,1,0:T(8,128)(2,1)S(1)}, u32[]{:S(2)}, u32[]{:S(2)}) collective-permute-start(bf16[4,2,2,16,256]{4,3,2,1,0:T(8,128)(2,1)S(1)} %get-tuple-element.42), channel_id=1, source_target_pairs={{0,2},{1,3},{2,0},{3,1},{4,6},{5,7},{6,4},{7,5},{8,10},{9,11},{10,... | collective-permute-start | bytes 393224 | tf_op jit(solution)/shard_map/ppermute | solution.py:214
  34.3 1.7 %collective-permute-start.8 = (bf16[4,2,2,16,256]{4,3,2,1,0:T(8,128)(2,1)S(1)}, bf16[4,2,2,16,256]{4,3,2,1,0:T(8,128)(2,1)S(1)}, u32[]{:S(2)}, u32[]{:S(2)}) collective-permute-start(bf16[4,2,2,16,256]{4,3,2,1,0:T(8,128)(2,1)S(1)} %get-tuple-element.41), channel_id=1, source_target_pairs={{0,6},{1,7},{2,4},{3,5},{4,2},{5,3},{6,0},{7,1},{8,14},{9,15},{10,... | collective-permute-start | bytes 393224 | tf_op jit(solution)/shard_map/ppermute | solution.py:214
  35.9 0.8 %slice_reduce_fusion = f32[2]{0:T(128)S(1)} fusion(f32[2,2,8,128]{3,2,1,0:T(8,128)} %get-tuple-element.37), kind=kLoop, calls=%fused_computation.28 | loop fusion | flops 2 | bytes 24 | tf_op jit(solution)/shard_map/reduce_sum | solution.py:199
  36.8 2.0 %collective-permute-done.6 = bf16[4,2,2,16,256]{4,3,2,1,0:T(8,128)(2,1)S(1)} collective-permute-done((bf16[4,2,2,16,256]{4,3,2,1,0:T(8,128)(2,1)S(1)}, bf16[4,2,2,16,256]{4,3,2,1,0:T(8,128)(2,1)S(1)}, u32[]{:S(2)}, u32[]{:S(2)}) %collective-permute-start.6) | collective-permute-done | bytes 131104 | tf_op jit(solution)/shard_map/ppermute | solution.py:214
  38.8 2.5 %collective-permute-done.7 = bf16[4,2,2,16,256]{4,3,2,1,0:T(8,128)(2,1)S(1)} collective-permute-done((bf16[4,2,2,16,256]{4,3,2,1,0:T(8,128)(2,1)S(1)}, bf16[4,2,2,16,256]{4,3,2,1,0:T(8,128)(2,1)S(1)}, u32[]{:S(2)}, u32[]{:S(2)}) %collective-permute-start.7) | collective-permute-done | bytes 131104 | tf_op jit(solution)/shard_map/ppermute | solution.py:214
  41.4 3.2 %collective-permute-start.9 = (bf16[2,2,2,16,256]{4,3,2,1,0:T(8,128)(2,1)S(1)}, bf16[2,2,2,16,256]{4,3,2,1,0:T(8,128)(2,1)S(1)}, u32[]{:S(2)}, u32[]{:S(2)}) collective-permute-start(bf16[2,2,2,16,256]{4,3,2,1,0:T(8,128)(2,1)S(1)} %slice.170), channel_id=1, source_target_pairs={{0,8},{1,9},{2,10},{3,11},{4,12},{5,13},{6,14},{7,15},{8,0},{9,1},... | collective-permute-start | bytes 196616 | tf_op jit(solution)/shard_map/ppermute | solution.py:214
  44.7 2.8 %collective-permute-done.9 = bf16[2,2,2,16,256]{4,3,2,1,0:T(8,128)(2,1)S(1)} collective-permute-done((bf16[2,2,2,16,256]{4,3,2,1,0:T(8,128)(2,1)S(1)}, bf16[2,2,2,16,256]{4,3,2,1,0:T(8,128)(2,1)S(1)}, u32[]{:S(2)}, u32[]{:S(2)}) %collective-permute-start.9) | collective-permute-done | bytes 65568 | tf_op jit(solution)/shard_map/ppermute | solution.py:214
  47.7 0.9 %copy-done.4 = bf16[2,256,256]{2,1,0:T(8,128)(2,1)S(1)} copy-done((bf16[2,256,256]{2,1,0:T(8,128)(2,1)S(1)}, bf16[2,256,256]{2,1,0:T(8,128)(2,1)}, u32[]{:S(2)}) %copy-start.4) | copy-done | bytes 262168
  49.6 1.5 %collective-permute-start.10 = (bf16[65542]{0:T(1024)(128)(2,1)S(1)}, bf16[65542]{0:T(1024)(128)(2,1)S(1)}, u32[]{:S(2)}, u32[]{:S(2)}) collective-permute-start(bf16[65542]{0:T(1024)(128)(2,1)S(1)} %concatenate.16), channel_id=1, source_target_pairs={{0,16},{16,0},{1,17},{17,1},{2,18},{18,2},{3,19},{19,3},{4,20},{20... | collective-permute-start | bytes 393260 | tf_op jit(solution)/shard_map/ppermute | solution.py:245
  51.1 3.5 %collective-permute-done.10 = bf16[65542]{0:T(1024)(128)(2,1)S(1)} collective-permute-done((bf16[65542]{0:T(1024)(128)(2,1)S(1)}, bf16[65542]{0:T(1024)(128)(2,1)S(1)}, u32[]{:S(2)}, u32[]{:S(2)}) %collective-permute-start.10) | collective-permute-done | bytes 131116 | tf_op jit(solution)/shard_map/ppermute | solution.py:245
  (34 shorter events, 4.6 us)
Async XLA Ops:
  3.8 7.9 %collective-permute-start = (bf16[2,2,2,16,256]{4,3,2,1,0:T(8,128)(2,1)}, bf16[2,2,2,16,256]{4,3,2,1,0:T(8,128)(2,1)S(1)}, u32[]{:S(2)}, u32[]{:S(2)}) collective-permute-start(bf16[2,2,2,16,256]{4,3,2,1,0:T(8,128)(2,1)} %get-tuple-element.33), channel_id=1, source_target_pairs={{0,8},{1,9},{2,10},{3,11},{4,12},{5,13},{6,14},{7,15},{8,0},{9,1},... | collective-permute-start | bytes 196616 | tf_op jit(solution)/shard_map/ppermute | solution.py:191
  11.7 6.3 %collective-permute-start.1 = (bf16[4,2,2,16,256]{4,3,2,1,0:T(8,128)(2,1)S(1)}, bf16[4,2,2,16,256]{4,3,2,1,0:T(8,128)(2,1)S(1)}, u32[]{:S(2)}, u32[]{:S(2)}) collective-permute-start(bf16[4,2,2,16,256]{4,3,2,1,0:T(8,128)(2,1)S(1)} %get-tuple-element.43), channel_id=1, source_target_pairs={{0,4},{1,5},{2,6},{3,7},{4,0},{5,1},{6,2},{7,3},{8,12},{9,13},{10,... | collective-permute-start | bytes 393224 | tf_op jit(solution)/shard_map/ppermute | solution.py:191
  12.5 6.5 %collective-permute-start.2 = (bf16[4,2,2,16,256]{4,3,2,1,0:T(8,128)(2,1)S(1)}, bf16[4,2,2,16,256]{4,3,2,1,0:T(8,128)(2,1)S(1)}, u32[]{:S(2)}, u32[]{:S(2)}) collective-permute-start(bf16[4,2,2,16,256]{4,3,2,1,0:T(8,128)(2,1)S(1)} %get-tuple-element.43), channel_id=1, source_target_pairs={{0,2},{1,3},{2,0},{3,1},{4,6},{5,7},{6,4},{7,5},{8,10},{9,11},{10,... | collective-permute-start | bytes 393224 | tf_op jit(solution)/shard_map/ppermute | solution.py:191
  14.0 6.7 %collective-permute-start.3 = (bf16[4,2,2,16,256]{4,3,2,1,0:T(8,128)(2,1)S(1)}, bf16[4,2,2,16,256]{4,3,2,1,0:T(8,128)(2,1)S(1)}, u32[]{:S(2)}, u32[]{:S(2)}) collective-permute-start(bf16[4,2,2,16,256]{4,3,2,1,0:T(8,128)(2,1)S(1)} %get-tuple-element.43), channel_id=1, source_target_pairs={{0,6},{1,7},{2,4},{3,5},{4,2},{5,3},{6,0},{7,1},{8,14},{9,15},{10,... | collective-permute-start | bytes 393224 | tf_op jit(solution)/shard_map/ppermute | solution.py:191
  20.6 2.0 %copy-start = (bf16[16,2,2,16,256]{4,3,2,1,0:T(8,128)(2,1)}, bf16[16,2,2,16,256]{4,3,2,1,0:T(8,128)(2,1)S(1)}, u32[]{:S(2)}) copy-start(bf16[16,2,2,16,256]{4,3,2,1,0:T(8,128)(2,1)S(1)} %constant_dynamic-update-slice_fusion.2.low_ref) | copy-start | bytes 1572868
  20.7 2.0 %collective-permute-start.4 = (bf16[16,2,2,16,256]{4,3,2,1,0:T(8,128)(2,1)S(1)}, bf16[16,2,2,16,256]{4,3,2,1,0:T(8,128)(2,1)S(1)}, u32[]{:S(2)}, u32[]{:S(2)}) collective-permute-start(bf16[16,2,2,16,256]{4,3,2,1,0:T(8,128)(2,1)S(1)} %constant_dynamic-update-slice_fusion.2.low_ref), channel_id=1, source_target_pairs={{0,1},{1,0},{2,3},{3,2},{4,5},{5,4},{6,7},{7,6},{8,9},{9,8},{10,11... | collective-permute-start | bytes 1572872 | tf_op jit(solution)/shard_map/ppermute | solution.py:193
  22.6 0.8 %copy-start.2 = (bf16[16,2,2,16,256]{4,3,2,1,0:T(8,128)(2,1)}, bf16[16,2,2,16,256]{4,3,2,1,0:T(8,128)(2,1)S(1)}, u32[]{:S(2)}) copy-start(bf16[16,2,2,16,256]{4,3,2,1,0:T(8,128)(2,1)S(1)} %collective-permute-done.4.high_ref) | copy-start | bytes 1572868
  28.8 2.2 %collective-permute-start.5 = (bf16[16,2,2,16,256]{4,3,2,1,0:T(8,128)(2,1)}, bf16[16,2,2,16,256]{4,3,2,1,0:T(8,128)(2,1)S(1)}, u32[]{:S(2)}, u32[]{:S(2)}) collective-permute-start(bf16[16,2,2,16,256]{4,3,2,1,0:T(8,128)(2,1)} %get-tuple-element.36), channel_id=1, source_target_pairs={{0,1},{1,0},{2,3},{3,2},{4,5},{5,4},{6,7},{7,6},{8,9},{9,8},{10,11... | collective-permute-start | bytes 1572872 | tf_op jit(solution)/shard_map/ppermute | solution.py:203
  32.4 6.4 %collective-permute-start.6 = (bf16[4,2,2,16,256]{4,3,2,1,0:T(8,128)(2,1)S(1)}, bf16[4,2,2,16,256]{4,3,2,1,0:T(8,128)(2,1)S(1)}, u32[]{:S(2)}, u32[]{:S(2)}) collective-permute-start(bf16[4,2,2,16,256]{4,3,2,1,0:T(8,128)(2,1)S(1)} %get-tuple-element.40), channel_id=1, source_target_pairs={{0,4},{1,5},{2,6},{3,7},{4,0},{5,1},{6,2},{7,3},{8,12},{9,13},{10,... | collective-permute-start | bytes 393224 | tf_op jit(solution)/shard_map/ppermute | solution.py:214
  33.2 8.1 %collective-permute-start.7 = (bf16[4,2,2,16,256]{4,3,2,1,0:T(8,128)(2,1)S(1)}, bf16[4,2,2,16,256]{4,3,2,1,0:T(8,128)(2,1)S(1)}, u32[]{:S(2)}, u32[]{:S(2)}) collective-permute-start(bf16[4,2,2,16,256]{4,3,2,1,0:T(8,128)(2,1)S(1)} %get-tuple-element.42), channel_id=1, source_target_pairs={{0,2},{1,3},{2,0},{3,1},{4,6},{5,7},{6,4},{7,5},{8,10},{9,11},{10,... | collective-permute-start | bytes 393224 | tf_op jit(solution)/shard_map/ppermute | solution.py:214
  34.3 7.0 %collective-permute-start.8 = (bf16[4,2,2,16,256]{4,3,2,1,0:T(8,128)(2,1)S(1)}, bf16[4,2,2,16,256]{4,3,2,1,0:T(8,128)(2,1)S(1)}, u32[]{:S(2)}, u32[]{:S(2)}) collective-permute-start(bf16[4,2,2,16,256]{4,3,2,1,0:T(8,128)(2,1)S(1)} %get-tuple-element.41), channel_id=1, source_target_pairs={{0,6},{1,7},{2,4},{3,5},{4,2},{5,3},{6,0},{7,1},{8,14},{9,15},{10,... | collective-permute-start | bytes 393224 | tf_op jit(solution)/shard_map/ppermute | solution.py:214
  41.3 3.3 %copy-start.1 = (bf16[2,2,256,256]{3,2,1,0:T(8,128)(2,1)S(1)}, bf16[2,2,256,256]{3,2,1,0:T(8,128)(2,1)}, u32[]{:S(2)}) copy-start(bf16[2,2,256,256]{3,2,1,0:T(8,128)(2,1)} %get-tuple-element.34) | copy-start | bytes 1572868
  41.4 6.2 %collective-permute-start.9 = (bf16[2,2,2,16,256]{4,3,2,1,0:T(8,128)(2,1)S(1)}, bf16[2,2,2,16,256]{4,3,2,1,0:T(8,128)(2,1)S(1)}, u32[]{:S(2)}, u32[]{:S(2)}) collective-permute-start(bf16[2,2,2,16,256]{4,3,2,1,0:T(8,128)(2,1)S(1)} %slice.170), channel_id=1, source_target_pairs={{0,8},{1,9},{2,10},{3,11},{4,12},{5,13},{6,14},{7,15},{8,0},{9,1},... | collective-permute-start | bytes 196616 | tf_op jit(solution)/shard_map/ppermute | solution.py:214
  47.6 1.0 %copy-start.4 = (bf16[2,256,256]{2,1,0:T(8,128)(2,1)S(1)}, bf16[2,256,256]{2,1,0:T(8,128)(2,1)}, u32[]{:S(2)}) copy-start(bf16[2,256,256]{2,1,0:T(8,128)(2,1)} %cols_ref.1) | copy-start | bytes 786436
  47.6 1.0 %copy-start.3 = (bf16[2,256,256]{2,1,0:T(8,128)(2,1)S(1)}, bf16[2,256,256]{2,1,0:T(8,128)(2,1)}, u32[]{:S(2)}) copy-start(bf16[2,256,256]{2,1,0:T(8,128)(2,1)} %rows_ref.1) | copy-start | bytes 786436
  49.6 5.0 %collective-permute-start.10 = (bf16[65542]{0:T(1024)(128)(2,1)S(1)}, bf16[65542]{0:T(1024)(128)(2,1)S(1)}, u32[]{:S(2)}, u32[]{:S(2)}) collective-permute-start(bf16[65542]{0:T(1024)(128)(2,1)S(1)} %concatenate.16), channel_id=1, source_target_pairs={{0,16},{16,0},{1,17},{17,1},{2,18},{18,2},{3,19},{19,3},{4,20},{20... | collective-permute-start | bytes 393260 | tf_op jit(solution)/shard_map/ppermute | solution.py:245

commit v13 on v10

--- a/solution.py
+++ b/solution.py
@@ -59,18 +59,20 @@
             (weighted[pixels - OVL :].astype(jnp.float32), weighted[:OVL].astype(jnp.float32))
         )
 
+    kept_ref[...] = jnp.zeros_like(kept_ref)
     return_ref[...] = jnp.zeros_like(return_ref)
     for k in range(own_count):
         bottom_rows, top_rows = edge_rows[k]
-
         for j in range(neighbours):
             q = places[k][j]
             s = side_ref[k, j]
             rows = jnp.where(s == 0, bottom_rows, top_rows)
             part = (weight_ref[k, j] * rows).astype(jnp.bfloat16).astype(jnp.float32)
-            return_ref[q, s] = return_ref[q, s] + part
-    kept_ref[:, :, 0] = return_ref[:half]
-    sent_ref[:, :, 0] = return_ref[half:].astype(jnp.bfloat16)
+            kept_at = jnp.minimum(q, half - 1)
+            sent_at = jnp.maximum(q - half, 0)
+            kept_ref[kept_at, s, 0] = kept_ref[kept_at, s, 0] + jnp.where(q < half, part, 0.0)
+            return_ref[sent_at, s] = return_ref[sent_at, s] + jnp.where(q < half, 0.0, part)
+    sent_ref[:, :, 0] = return_ref[...].astype(jnp.bfloat16)
 
 
 def middle(owner, local, side, weight, images, projected, edges_low, edges_high, ctf_filter):
@@ -110,7 +112,7 @@
         ],
         scratch_shapes=[
             pltpu.VMEM((own_count, pixels, pixels), jnp.float32),
-            pltpu.VMEM((total, 2, OVL, pixels), jnp.float32),
+            pltpu.VMEM((half, 2, OVL, pixels), jnp.float32),
         ],
         compiler_params=pltpu.CompilerParams(dimension_semantics=("arbitrary",)),
         cost_estimate=pl.CostEstimate(flops=flops, transcendentals=0, bytes_accessed=moved),

time: 54.6 us -> 54.7 us (level)
  no operation moved by 1% of the time
where the time goes in v13:
time: 54.7 us; the launch traced here: 54.4 us
  waiting for transfers between devices  23.7 us (43%)
  starting transfers between devices  16.3 us (30%)
  Pallas kernels  5.35 us (10%)
  other arithmetic  3.82 us (7%)
  local copies, waits for them, and re-layouts  2.36 us (4%)
  matrix products  2.11 us (4%)
  between operations  0.85 us (2%)
    ppermute x4, waiting for transfers between devices, on_device(): pieces.append(lax.ppermute(edges_all, 'dom', pairs))  8.84 us
    ppermute x4, starting transfers between devices, on_device(): pieces.append(lax.ppermute(edges_all, 'dom', pairs))  7.65 us
    ppermute x4, waiting for transfers between devices, on_device(): kept = kept + lax.ppermute(given, 'dom', pairs).astype(jnp.float32)  7.51 us
    ppermute x4, starting transfers between devices, on_device(): kept = kept + lax.ppermute(given, 'dom', pairs).astype(jnp.float32)  6.81 us
    pallas_call x1, Pallas kernels, middle(): pl.pallas_call(middle_kernel, grid=(tilt_count,), in_specs=[smem, smem, s...  5.35 us
    ppermute x1, waiting for transfers between devices, on_device(): parcel = lax.ppermute(parcel, 'tilt', [(0, 1), (1, 0)]).astype(jnp.float32)  3.46 us
    ppermute x1, waiting for transfers between devices, on_device(): lax.ppermute(sent_half, 'dom', pairs).astype(jnp.float32)  1.96 us
    ppermute x1, waiting for transfers between devices, on_device(): lax.ppermute(edges_all, 'dom', [(i, i ^ 1) for i in range(peer_count)])  1.9 us
  transfers between devices with their start and end apart: 11, of which 10 were waited for; matrix products, arithmetic and copies ran while one was open for 2% of the time, Pallas kernels for 0%

profile of v13, /device:TPU:0, one launch (start us, length us, event | category | flops | bytes accessed | tf_op | source)
XLA Modules:
  0.0 54.4 jit_solution(4130586375326769739)
XLA Ops:
  0.7 0.9 %copy-done = bf16[2,256,256]{2,1,0:T(8,128)(2,1)S(1)} copy-done((bf16[2,256,256]{2,1,0:T(8,128)(2,1)S(1)}, bf16[2,256,256]{2,1,0:T(8,128)(2,1)}, u32[]{:S(2)}) %copy-start) | copy-done | bytes 262168
  1.6 1.3 %fusion = bf16[2,2,256,256]{3,2,0,1:T(8,128)(2,1)S(1)} fusion(bf16[2,256,256]{2,1,0:T(8,128)(2,1)S(1)} %copy-done, bf16[2,256,256]{2,1,0:T(8,128)(2,1)} %param.13), kind=kOutput, calls=%fused_computation.3 | convolution fusion | flops 134479872 | bytes 1048576 | tf_op jit(solution)/shard_map/kij,tlj->ktil/dot_general | solution.py:144
  3.2 4.1 %collective-permute-start = (bf16[2,2,2,16,256]{4,3,2,1,0:T(8,128)(2,1)S(1)}, bf16[2,2,2,16,256]{4,3,2,1,0:T(8,128)(2,1)S(1)}, u32[]{:S(2)}, u32[]{:S(2)}) collective-permute-start(bf16[2,2,2,16,256]{4,3,2,1,0:T(8,128)(2,1)S(1)} %get-tuple-element.41), channel_id=1, source_target_pairs={{0,8},{1,9},{2,10},{3,11},{4,12},{5,13},{6,14},{7,15},{8,0},{9,1},... | collective-permute-start | bytes 196616 | tf_op jit(solution)/shard_map/ppermute | solution.py:158
  7.3 3.6 %collective-permute-done = bf16[2,2,2,16,256]{4,3,2,1,0:T(8,128)(2,1)S(1)} collective-permute-done((bf16[2,2,2,16,256]{4,3,2,1,0:T(8,128)(2,1)S(1)}, bf16[2,2,2,16,256]{4,3,2,1,0:T(8,128)(2,1)S(1)}, u32[]{:S(2)}, u32[]{:S(2)}) %collective-permute-start) | collective-permute-done | bytes 65568 | tf_op jit(solution)/shard_map/ppermute | solution.py:158
  11.6 1.5 %collective-permute-start.2 = (bf16[4,2,2,16,256]{4,3,2,1,0:T(8,128)(2,1)S(1)}, bf16[4,2,2,16,256]{4,3,2,1,0:T(8,128)(2,1)S(1)}, u32[]{:S(2)}, u32[]{:S(2)}) collective-permute-start(bf16[4,2,2,16,256]{4,3,2,1,0:T(8,128)(2,1)S(1)} %pad_maximum_fusion), channel_id=1, source_target_pairs={{0,2},{1,3},{2,0},{3,1},{4,6},{5,7},{6,4},{7,5},{8,10},{9,11},{10,... | collective-permute-start | bytes 393224 | tf_op jit(solution)/shard_map/ppermute | solution.py:158
  13.1 1.4 %collective-permute-start.3 = (bf16[4,2,2,16,256]{4,3,2,1,0:T(8,128)(2,1)S(1)}, bf16[4,2,2,16,256]{4,3,2,1,0:T(8,128)(2,1)S(1)}, u32[]{:S(2)}, u32[]{:S(2)}) collective-permute-start(bf16[4,2,2,16,256]{4,3,2,1,0:T(8,128)(2,1)S(1)} %pad_maximum_fusion), channel_id=1, source_target_pairs={{0,6},{1,7},{2,4},{3,5},{4,2},{5,3},{6,0},{7,1},{8,14},{9,15},{10,... | collective-permute-start | bytes 393224 | tf_op jit(solution)/shard_map/ppermute | solution.py:158
  14.6 2.8 %collective-permute-done.1 = bf16[4,2,2,16,256]{4,3,2,1,0:T(8,128)(2,1)S(1)} collective-permute-done((bf16[4,2,2,16,256]{4,3,2,1,0:T(8,128)(2,1)S(1)}, bf16[4,2,2,16,256]{4,3,2,1,0:T(8,128)(2,1)S(1)}, u32[]{:S(2)}, u32[]{:S(2)}) %collective-permute-start.1) | collective-permute-done | bytes 131104 | tf_op jit(solution)/shard_map/ppermute | solution.py:158
  17.4 0.8 %collective-permute-done.2 = bf16[4,2,2,16,256]{4,3,2,1,0:T(8,128)(2,1)S(1)} collective-permute-done((bf16[4,2,2,16,256]{4,3,2,1,0:T(8,128)(2,1)S(1)}, bf16[4,2,2,16,256]{4,3,2,1,0:T(8,128)(2,1)S(1)}, u32[]{:S(2)}, u32[]{:S(2)}) %collective-permute-start.2) | collective-permute-done | bytes 131104 | tf_op jit(solution)/shard_map/ppermute | solution.py:158
  18.2 1.6 %collective-permute-done.3 = bf16[4,2,2,16,256]{4,3,2,1,0:T(8,128)(2,1)S(1)} collective-permute-done((bf16[4,2,2,16,256]{4,3,2,1,0:T(8,128)(2,1)S(1)}, bf16[4,2,2,16,256]{4,3,2,1,0:T(8,128)(2,1)S(1)}, u32[]{:S(2)}, u32[]{:S(2)}) %collective-permute-start.3) | collective-permute-done | bytes 131104 | tf_op jit(solution)/shard_map/ppermute | solution.py:158
  19.9 1.9 %collective-permute-done.4.high_ref = bf16[16,2,2,16,256]{4,3,2,1,0:T(8,128)(2,1)S(1)} collective-permute-done((bf16[16,2,2,16,256]{4,3,2,1,0:T(8,128)(2,1)S(1)}, bf16[16,2,2,16,256]{4,3,2,1,0:T(8,128)(2,1)S(1)}, u32[]{:S(2)}, u32[]{:S(2)}) %collective-permute-start.4) | collective-permute-done | bytes 524320 | tf_op jit(solution)/shard_map/ppermute | solution.py:160
  21.8 0.8 %copy-done.5 = bf16[16,2,2,16,256]{4,3,2,1,0:T(8,128)(2,1)} copy-done((bf16[16,2,2,16,256]{4,3,2,1,0:T(8,128)(2,1)}, bf16[16,2,2,16,256]{4,3,2,1,0:T(8,128)(2,1)S(1)}, u32[]{:S(2)}) %copy-start.5) | copy-done | bytes 524312
  22.6 5.3 %shard_map.104 = (bf16[2,2,256,256]{3,2,1,0:T(8,128)(2,1)}, f32[2,2,8,128]{3,2,1,0:T(8,128)}, f32[16,2,2,16,256]{4,3,2,1,0:T(8,128)}, bf16[16,2,2,16,256]{4,3,2,1,0:T(8,128)(2,1)}) custom-call(s32[2,2,8]{2,1,0:T(2,128)} %owner_ref.1, s32[2,16]{1,0:T(2,128)} %local_ref.1, s32[2,16]{1,0:T(2,128)} %side_ref.1, f32[2,16]{1,0:T(2,128)} %weight_ref.1, ...), custom_call_target="tpu_custom_call" | custom-call | flops 536870912 | bytes 4456448 | tf_op jit(solution)/shard_map/pallas_call | solution.py:87
  28.1 2.0 %collective-permute-done.5 = bf16[16,2,2,16,256]{4,3,2,1,0:T(8,128)(2,1)S(1)} collective-permute-done((bf16[16,2,2,16,256]{4,3,2,1,0:T(8,128)(2,1)}, bf16[16,2,2,16,256]{4,3,2,1,0:T(8,128)(2,1)S(1)}, u32[]{:S(2)}, u32[]{:S(2)}) %collective-permute-start.5) | collective-permute-done | bytes 524320 | tf_op jit(solution)/shard_map/ppermute | solution.py:170
  30.1 1.4 %fusion.23 = (bf16[16,2,2,16,256]{4,3,2,1,0:T(8,128)(2,1)S(1)}, f32[16,2,2,16,256]{4,3,2,1,0:T(8,128)S(1)}) fusion(f32[16,2,2,16,256]{4,3,2,1,0:T(8,128)} %get-tuple-element.31, bf16[16,2,2,16,256]{4,3,2,1,0:T(8,128)(2,1)S(1)} %collective-permute-done.5), kind=kLoop, calls=%fused_computation.46 | loop fusion | flops 786432 | bytes 3145728 | tf_op jit(solution)/shard_map/convert.3
  31.5 0.9 %collective-permute-start.6 = (bf16[4,2,2,16,256]{4,3,2,1,0:T(8,128)(2,1)S(1)}, bf16[4,2,2,16,256]{4,3,2,1,0:T(8,128)(2,1)S(1)}, u32[]{:S(2)}, u32[]{:S(2)}) collective-permute-start(bf16[4,2,2,16,256]{4,3,2,1,0:T(8,128)(2,1)S(1)} %get-tuple-element.36), channel_id=1, source_target_pairs={{0,4},{1,5},{2,6},{3,7},{4,0},{5,1},{6,2},{7,3},{8,12},{9,13},{10,... | collective-permute-start | bytes 393224 | tf_op jit(solution)/shard_map/ppermute | solution.py:181
  32.5 1.0 %collective-permute-start.7 = (bf16[4,2,2,16,256]{4,3,2,1,0:T(8,128)(2,1)S(1)}, bf16[4,2,2,16,256]{4,3,2,1,0:T(8,128)(2,1)S(1)}, u32[]{:S(2)}, u32[]{:S(2)}) collective-permute-start(bf16[4,2,2,16,256]{4,3,2,1,0:T(8,128)(2,1)S(1)} %get-tuple-element.38), channel_id=1, source_target_pairs={{0,2},{1,3},{2,0},{3,1},{4,6},{5,7},{6,4},{7,5},{8,10},{9,11},{10,... | collective-permute-start | bytes 393224 | tf_op jit(solution)/shard_map/ppermute | solution.py:181
  33.5 1.6 %collective-permute-start.8 = (bf16[4,2,2,16,256]{4,3,2,1,0:T(8,128)(2,1)S(1)}, bf16[4,2,2,16,256]{4,3,2,1,0:T(8,128)(2,1)S(1)}, u32[]{:S(2)}, u32[]{:S(2)}) collective-permute-start(bf16[4,2,2,16,256]{4,3,2,1,0:T(8,128)(2,1)S(1)} %get-tuple-element.37), channel_id=1, source_target_pairs={{0,6},{1,7},{2,4},{3,5},{4,2},{5,3},{6,0},{7,1},{8,14},{9,15},{10,... | collective-permute-start | bytes 393224 | tf_op jit(solution)/shard_map/ppermute | solution.py:181
  35.1 0.8 %slice_reduce_fusion = f32[2]{0:T(128)S(1)} fusion(f32[2,2,8,128]{3,2,1,0:T(8,128)} %get-tuple-element.33), kind=kLoop, calls=%fused_computation.38 | loop fusion | flops 2 | bytes 24 | tf_op jit(solution)/shard_map/reduce_sum | solution.py:166
  35.9 2.0 %collective-permute-done.6 = bf16[4,2,2,16,256]{4,3,2,1,0:T(8,128)(2,1)S(1)} collective-permute-done((bf16[4,2,2,16,256]{4,3,2,1,0:T(8,128)(2,1)S(1)}, bf16[4,2,2,16,256]{4,3,2,1,0:T(8,128)(2,1)S(1)}, u32[]{:S(2)}, u32[]{:S(2)}) %collective-permute-start.6) | collective-permute-done | bytes 131104 | tf_op jit(solution)/shard_map/ppermute | solution.py:181
  38.0 2.6 %collective-permute-done.7 = bf16[4,2,2,16,256]{4,3,2,1,0:T(8,128)(2,1)S(1)} collective-permute-done((bf16[4,2,2,16,256]{4,3,2,1,0:T(8,128)(2,1)S(1)}, bf16[4,2,2,16,256]{4,3,2,1,0:T(8,128)(2,1)S(1)}, u32[]{:S(2)}, u32[]{:S(2)}) %collective-permute-start.7) | collective-permute-done | bytes 131104 | tf_op jit(solution)/shard_map/ppermute | solution.py:181
  40.7 3.3 %collective-permute-start.9 = (bf16[2,2,2,16,256]{4,3,2,1,0:T(8,128)(2,1)S(1)}, bf16[2,2,2,16,256]{4,3,2,1,0:T(8,128)(2,1)S(1)}, u32[]{:S(2)}, u32[]{:S(2)}) collective-permute-start(bf16[2,2,2,16,256]{4,3,2,1,0:T(8,128)(2,1)S(1)} %slice.182), channel_id=1, source_target_pairs={{0,8},{1,9},{2,10},{3,11},{4,12},{5,13},{6,14},{7,15},{8,0},{9,1},... | collective-permute-start | bytes 196616 | tf_op jit(solution)/shard_map/ppermute | solution.py:181
  44.0 2.8 %collective-permute-done.9 = bf16[2,2,2,16,256]{4,3,2,1,0:T(8,128)(2,1)S(1)} collective-permute-done((bf16[2,2,2,16,256]{4,3,2,1,0:T(8,128)(2,1)S(1)}, bf16[2,2,2,16,256]{4,3,2,1,0:T(8,128)(2,1)S(1)}, u32[]{:S(2)}, u32[]{:S(2)}) %collective-permute-start.9) | collective-permute-done | bytes 65568 | tf_op jit(solution)/shard_map/ppermute | solution.py:181
  48.0 1.5 %collective-permute-start.10 = (bf16[65542]{0:T(1024)(128)(2,1)S(1)}, bf16[65542]{0:T(1024)(128)(2,1)S(1)}, u32[]{:S(2)}, u32[]{:S(2)}) collective-permute-start(bf16[65542]{0:T(1024)(128)(2,1)S(1)} %concatenate.16), channel_id=1, source_target_pairs={{0,16},{16,0},{1,17},{17,1},{2,18},{18,2},{3,19},{19,3},{4,20},{20... | collective-permute-start | bytes 393260 | tf_op jit(solution)/shard_map/ppermute | solution.py:212
  49.5 3.5 %collective-permute-done.10 = bf16[65542]{0:T(1024)(128)(2,1)S(1)} collective-permute-done((bf16[65542]{0:T(1024)(128)(2,1)S(1)}, bf16[65542]{0:T(1024)(128)(2,1)S(1)}, u32[]{:S(2)}, u32[]{:S(2)}) %collective-permute-start.10) | collective-permute-done | bytes 131116 | tf_op jit(solution)/shard_map/ppermute | solution.py:212
  (39 shorter events, 4.0 us)
Async XLA Ops:
  0.6 1.0 %copy-start = (bf16[2,256,256]{2,1,0:T(8,128)(2,1)S(1)}, bf16[2,256,256]{2,1,0:T(8,128)(2,1)}, u32[]{:S(2)}) copy-start(bf16[2,256,256]{2,1,0:T(8,128)(2,1)} %param.16) | copy-start | bytes 786436
  0.6 2.2 %copy-start.2 = (bf16[2,256,256]{2,1,0:T(8,128)(2,1)S(1)}, bf16[2,256,256]{2,1,0:T(8,128)(2,1)}, u32[]{:S(2)}) copy-start(bf16[2,256,256]{2,1,0:T(8,128)(2,1)} %param.15) | copy-start | bytes 786436
  3.2 15.0 %copy-start.1 = (bf16[2,2,256,256]{3,2,1,0:T(8,128)(2,1)}, bf16[2,2,256,256]{3,2,1,0:T(8,128)(2,1)S(1)}, u32[]{:S(2)}) copy-start(bf16[2,2,256,256]{3,2,1,0:T(8,128)(2,1)S(1)} %fusion.2.proj_ref) | copy-start | bytes 1572868
  3.2 7.7 %collective-permute-start = (bf16[2,2,2,16,256]{4,3,2,1,0:T(8,128)(2,1)S(1)}, bf16[2,2,2,16,256]{4,3,2,1,0:T(8,128)(2,1)S(1)}, u32[]{:S(2)}, u32[]{:S(2)}) collective-permute-start(bf16[2,2,2,16,256]{4,3,2,1,0:T(8,128)(2,1)S(1)} %get-tuple-element.41), channel_id=1, source_target_pairs={{0,8},{1,9},{2,10},{3,11},{4,12},{5,13},{6,14},{7,15},{8,0},{9,1},... | collective-permute-start | bytes 196616 | tf_op jit(solution)/shard_map/ppermute | solution.py:158
  11.0 6.4 %collective-permute-start.1 = (bf16[4,2,2,16,256]{4,3,2,1,0:T(8,128)(2,1)S(1)}, bf16[4,2,2,16,256]{4,3,2,1,0:T(8,128)(2,1)S(1)}, u32[]{:S(2)}, u32[]{:S(2)}) collective-permute-start(bf16[4,2,2,16,256]{4,3,2,1,0:T(8,128)(2,1)S(1)} %pad_maximum_fusion), channel_id=1, source_target_pairs={{0,4},{1,5},{2,6},{3,7},{4,0},{5,1},{6,2},{7,3},{8,12},{9,13},{10,... | collective-permute-start | bytes 393224 | tf_op jit(solution)/shard_map/ppermute | solution.py:158
  11.6 6.5 %collective-permute-start.2 = (bf16[4,2,2,16,256]{4,3,2,1,0:T(8,128)(2,1)S(1)}, bf16[4,2,2,16,256]{4,3,2,1,0:T(8,128)(2,1)S(1)}, u32[]{:S(2)}, u32[]{:S(2)}) collective-permute-start(bf16[4,2,2,16,256]{4,3,2,1,0:T(8,128)(2,1)S(1)} %pad_maximum_fusion), channel_id=1, source_target_pairs={{0,2},{1,3},{2,0},{3,1},{4,6},{5,7},{6,4},{7,5},{8,10},{9,11},{10,... | collective-permute-start | bytes 393224 | tf_op jit(solution)/shard_map/ppermute | solution.py:158
  13.1 6.7 %collective-permute-start.3 = (bf16[4,2,2,16,256]{4,3,2,1,0:T(8,128)(2,1)S(1)}, bf16[4,2,2,16,256]{4,3,2,1,0:T(8,128)(2,1)S(1)}, u32[]{:S(2)}, u32[]{:S(2)}) collective-permute-start(bf16[4,2,2,16,256]{4,3,2,1,0:T(8,128)(2,1)S(1)} %pad_maximum_fusion), channel_id=1, source_target_pairs={{0,6},{1,7},{2,4},{3,5},{4,2},{5,3},{6,0},{7,1},{8,14},{9,15},{10,... | collective-permute-start | bytes 393224 | tf_op jit(solution)/shard_map/ppermute | solution.py:158
  19.8 2.0 %copy-start.3 = (bf16[16,2,2,16,256]{4,3,2,1,0:T(8,128)(2,1)}, bf16[16,2,2,16,256]{4,3,2,1,0:T(8,128)(2,1)S(1)}, u32[]{:S(2)}) copy-start(bf16[16,2,2,16,256]{4,3,2,1,0:T(8,128)(2,1)S(1)} %constant_dynamic-update-slice_fusion.low_ref) | copy-start | bytes 1572868
  19.8 2.0 %collective-permute-start.4 = (bf16[16,2,2,16,256]{4,3,2,1,0:T(8,128)(2,1)S(1)}, bf16[16,2,2,16,256]{4,3,2,1,0:T(8,128)(2,1)S(1)}, u32[]{:S(2)}, u32[]{:S(2)}) collective-permute-start(bf16[16,2,2,16,256]{4,3,2,1,0:T(8,128)(2,1)S(1)} %constant_dynamic-update-slice_fusion.low_ref), channel_id=1, source_target_pairs={{0,1},{1,0},{2,3},{3,2},{4,5},{5,4},{6,7},{7,6},{8,9},{9,8},{10,11... | collective-permute-start | bytes 1572872 | tf_op jit(solution)/shard_map/ppermute | solution.py:160
  21.8 0.8 %copy-start.5 = (bf16[16,2,2,16,256]{4,3,2,1,0:T(8,128)(2,1)}, bf16[16,2,2,16,256]{4,3,2,1,0:T(8,128)(2,1)S(1)}, u32[]{:S(2)}) copy-start(bf16[16,2,2,16,256]{4,3,2,1,0:T(8,128)(2,1)S(1)} %collective-permute-done.4.high_ref) | copy-start | bytes 1572868
  27.9 2.2 %collective-permute-start.5 = (bf16[16,2,2,16,256]{4,3,2,1,0:T(8,128)(2,1)}, bf16[16,2,2,16,256]{4,3,2,1,0:T(8,128)(2,1)S(1)}, u32[]{:S(2)}, u32[]{:S(2)}) collective-permute-start(bf16[16,2,2,16,256]{4,3,2,1,0:T(8,128)(2,1)} %get-tuple-element.32), channel_id=1, source_target_pairs={{0,1},{1,0},{2,3},{3,2},{4,5},{5,4},{6,7},{7,6},{8,9},{9,8},{10,11... | collective-permute-start | bytes 1572872 | tf_op jit(solution)/shard_map/ppermute | solution.py:170
  31.5 6.4 %collective-permute-start.6 = (bf16[4,2,2,16,256]{4,3,2,1,0:T(8,128)(2,1)S(1)}, bf16[4,2,2,16,256]{4,3,2,1,0:T(8,128)(2,1)S(1)}, u32[]{:S(2)}, u32[]{:S(2)}) collective-permute-start(bf16[4,2,2,16,256]{4,3,2,1,0:T(8,128)(2,1)S(1)} %get-tuple-element.36), channel_id=1, source_target_pairs={{0,4},{1,5},{2,6},{3,7},{4,0},{5,1},{6,2},{7,3},{8,12},{9,13},{10,... | collective-permute-start | bytes 393224 | tf_op jit(solution)/shard_map/ppermute | solution.py:181
  32.5 8.1 %collective-permute-start.7 = (bf16[4,2,2,16,256]{4,3,2,1,0:T(8,128)(2,1)S(1)}, bf16[4,2,2,16,256]{4,3,2,1,0:T(8,128)(2,1)S(1)}, u32[]{:S(2)}, u32[]{:S(2)}) collective-permute-start(bf16[4,2,2,16,256]{4,3,2,1,0:T(8,128)(2,1)S(1)} %get-tuple-element.38), channel_id=1, source_target_pairs={{0,2},{1,3},{2,0},{3,1},{4,6},{5,7},{6,4},{7,5},{8,10},{9,11},{10,... | collective-permute-start | bytes 393224 | tf_op jit(solution)/shard_map/ppermute | solution.py:181
  33.5 7.1 %collective-permute-start.8 = (bf16[4,2,2,16,256]{4,3,2,1,0:T(8,128)(2,1)S(1)}, bf16[4,2,2,16,256]{4,3,2,1,0:T(8,128)(2,1)S(1)}, u32[]{:S(2)}, u32[]{:S(2)}) collective-permute-start(bf16[4,2,2,16,256]{4,3,2,1,0:T(8,128)(2,1)S(1)} %get-tuple-element.37), channel_id=1, source_target_pairs={{0,6},{1,7},{2,4},{3,5},{4,2},{5,3},{6,0},{7,1},{8,14},{9,15},{10,... | collective-permute-start | bytes 393224 | tf_op jit(solution)/shard_map/ppermute | solution.py:181
  40.6 3.4 %copy-start.4 = (bf16[2,2,256,256]{3,2,1,0:T(8,128)(2,1)S(1)}, bf16[2,2,256,256]{3,2,1,0:T(8,128)(2,1)}, u32[]{:S(2)}) copy-start(bf16[2,2,256,256]{3,2,1,0:T(8,128)(2,1)} %get-tuple-element.30) | copy-start | bytes 1572868
  40.7 6.2 %collective-permute-start.9 = (bf16[2,2,2,16,256]{4,3,2,1,0:T(8,128)(2,1)S(1)}, bf16[2,2,2,16,256]{4,3,2,1,0:T(8,128)(2,1)S(1)}, u32[]{:S(2)}, u32[]{:S(2)}) collective-permute-start(bf16[2,2,2,16,256]{4,3,2,1,0:T(8,128)(2,1)S(1)} %slice.182), channel_id=1, source_target_pairs={{0,8},{1,9},{2,10},{3,11},{4,12},{5,13},{6,14},{7,15},{8,0},{9,1},... | collective-permute-start | bytes 196616 | tf_op jit(solution)/shard_map/ppermute | solution.py:181
  48.0 5.0 %collective-permute-start.10 = (bf16[65542]{0:T(1024)(128)(2,1)S(1)}, bf16[65542]{0:T(1024)(128)(2,1)S(1)}, u32[]{:S(2)}, u32[]{:S(2)}) collective-permute-start(bf16[65542]{0:T(1024)(128)(2,1)S(1)} %concatenate.16), channel_id=1, source_target_pairs={{0,16},{16,0},{1,17},{17,1},{2,18},{18,2},{3,19},{19,3},{4,20},{20... | collective-permute-start | bytes 393260 | tf_op jit(solution)/shard_map/ppermute | solution.py:212

commit v14 on v10

--- a/solution.py
+++ b/solution.py
@@ -163,6 +163,15 @@
     )
     score_part = jnp.sum(score_tiles[:, :, 0, 0], axis=0)
     tilt_groups = lax.axis_size("tilt")
+    scale = 0.5 / (tilt_count * tilt_groups * pixels * pixels)
+    if tilt_groups == 2:
+        score_hi = score_part.astype(jnp.bfloat16)
+        score_rest = score_part - score_hi.astype(jnp.float32)
+        score_mid = score_rest.astype(jnp.bfloat16)
+        score_low = (score_rest - score_mid.astype(jnp.float32)).astype(jnp.bfloat16)
+        parts = jnp.stack((score_hi, score_mid, score_low))
+        parts = lax.ppermute(parts, "tilt", [(0, 1), (1, 0)]).astype(jnp.float32)
+        scores = scale * (score_part + (parts[0] + (parts[1] + parts[2])))
 
     pairs = [(i, i ^ 1) for i in range(peer_count)]
     returned = kept_half + lax.ppermute(sent_half, "dom", pairs).astype(jnp.float32)
@@ -191,7 +200,6 @@
     partial_grad = -jnp.einsum(
         "ktil,tlj->kij", upward, slice_cols, preferred_element_type=jnp.float32
     )
-    scale = 0.5 / (tilt_count * tilt_groups * pixels * pixels)
     if tilt_groups != 2:
         scores = scale * lax.psum(score_part, "tilt")
         section_grad = lax.psum_scatter(partial_grad, "tilt", scatter_dimension=1, tiled=True)
@@ -200,17 +208,8 @@
     side = lax.axis_index("tilt")
     kept = lax.dynamic_slice_in_dim(partial_grad, side * half, half, axis=1)
     given = lax.dynamic_slice_in_dim(partial_grad, (1 - side) * half, half, axis=1)
-    score_hi = score_part.astype(jnp.bfloat16)
-    score_rest = score_part - score_hi.astype(jnp.float32)
-    score_mid = score_rest.astype(jnp.bfloat16)
-    score_low = (score_rest - score_mid.astype(jnp.float32)).astype(jnp.bfloat16)
-    parcel = jnp.concatenate(
-        (given.reshape(-1).astype(jnp.bfloat16), score_hi, score_mid, score_low)
-    )
-    parcel = lax.ppermute(parcel, "tilt", [(0, 1), (1, 0)]).astype(jnp.float32)
-    section_grad = kept + parcel[: given.size].reshape(given.shape)
-    parts = parcel[given.size :].reshape(3, own_count)
-    scores = scale * (score_part + (parts[0] + (parts[1] + parts[2])))
+    given = lax.ppermute(given.astype(jnp.bfloat16), "tilt", [(0, 1), (1, 0)])
+    section_grad = kept + given.astype(jnp.float32)
     return (section_grad, scores)
 
 

time: 54.6 us -> 54.2 us (level)
  starting transfers between devices: 16.2 us -> 17.9 us
  waiting for transfers between devices: 23.7 us -> 22.2 us
    ppermute x4, waiting for transfers between devices: 7.5 us -> 5.45 us  [on_device(): kept = kept + lax.ppermute(given, 'dom', pairs).astype(jnp.float32)]
    ppermute x1 -> x2, starting transfers between devices: 1.53 us -> 3.19 us  [the longest x1 1.6 us: on_device(): parts = lax.ppermute(parts, 'tilt', [(0, 1), (1, 0)]).astype(jnp.float32)]
    ppermute x1 -> x2, waiting for transfers between devices: 3.46 us -> 4.86 us  [the longest x1 2.92 us: on_device(): given = lax.ppermute(given.astype(jnp.bfloat16), 'tilt', [(0, 1), (1, 0)])]
    ppermute x1, waiting for transfers between devices: 1.97 us -> 1.16 us  [on_device(): lax.ppermute(sent_half, 'dom', pairs).astype(jnp.float32)]
    unnamed x16 -> x15, local copies, waits for them, and re-layouts: 1.88 us -> 1.77 us
    another operation x1 -> x2, other arithmetic: 1.41 us -> 1.42 us
  transfers between devices with their start and end apart: 11 -> 12, of which waited for: 10 -> 10; matrix products, arithmetic and copies ran while one was open for 2% -> 3% of each run, Pallas kernels for 0% -> 0%
where the time goes in v14:
time: 54.2 us; the launch traced here: 53.9 us
  waiting for transfers between devices  22.2 us (41%)
  starting transfers between devices  17.9 us (33%)
  Pallas kernels  5.34 us (10%)
  other arithmetic  3.73 us (7%)
  matrix products  2.12 us (4%)
  local copies, waits for them, and re-layouts  1.85 us (3%)
  between operations  0.83 us (2%)
    ppermute x4, waiting for transfers between devices, on_device(): pieces.append(lax.ppermute(edges_all, 'dom', pairs))  8.84 us
    ppermute x4, starting transfers between devices, on_device(): pieces.append(lax.ppermute(edges_all, 'dom', pairs))  7.65 us
    ppermute x4, starting transfers between devices, on_device(): kept = kept + lax.ppermute(given, 'dom', pairs).astype(jnp.float32)  6.8 us
    ppermute x4, waiting for transfers between devices, on_device(): kept = kept + lax.ppermute(given, 'dom', pairs).astype(jnp.float32)  5.45 us
    pallas_call x1, Pallas kernels, middle(): pl.pallas_call(middle_kernel, grid=(tilt_count,), in_specs=[smem, smem, s...  5.34 us
    ppermute x1, waiting for transfers between devices, on_device(): given = lax.ppermute(given.astype(jnp.bfloat16), 'tilt', [(0, 1), (1, 0)])  2.92 us
    ppermute x1, waiting for transfers between devices, on_device(): parts = lax.ppermute(parts, 'tilt', [(0, 1), (1, 0)]).astype(jnp.float32)  1.94 us
    ppermute x1, waiting for transfers between devices, on_device(): lax.ppermute(edges_all, 'dom', [(i, i ^ 1) for i in range(peer_count)])  1.9 us
  transfers between devices with their start and end apart: 12, of which 10 were waited for; matrix products, arithmetic and copies ran while one was open for 3% of the time, Pallas kernels for 0%

profile of v14, /device:TPU:0, one launch (start us, length us, event | category | flops | bytes accessed | tf_op | source)
XLA Modules:
  0.0 53.9 jit_solution(15978307741031896062)
XLA Ops:
  0.7 0.9 %copy-done = bf16[2,256,256]{2,1,0:T(8,128)(2,1)S(1)} copy-done((bf16[2,256,256]{2,1,0:T(8,128)(2,1)S(1)}, bf16[2,256,256]{2,1,0:T(8,128)(2,1)}, u32[]{:S(2)}) %copy-start) | copy-done | bytes 262168
  1.6 1.3 %fusion = bf16[2,2,256,256]{3,2,0,1:T(8,128)(2,1)S(1)} fusion(bf16[2,256,256]{2,1,0:T(8,128)(2,1)S(1)} %copy-done, bf16[2,256,256]{2,1,0:T(8,128)(2,1)} %param.13), kind=kOutput, calls=%fused_computation.3 | convolution fusion | flops 134479872 | bytes 1048576 | tf_op jit(solution)/shard_map/kij,tlj->ktil/dot_general | solution.py:142
  3.2 4.1 %collective-permute-start = (bf16[2,2,2,16,256]{4,3,2,1,0:T(8,128)(2,1)S(1)}, bf16[2,2,2,16,256]{4,3,2,1,0:T(8,128)(2,1)S(1)}, u32[]{:S(2)}, u32[]{:S(2)}) collective-permute-start(bf16[2,2,2,16,256]{4,3,2,1,0:T(8,128)(2,1)S(1)} %get-tuple-element.41), channel_id=1, source_target_pairs={{0,8},{1,9},{2,10},{3,11},{4,12},{5,13},{6,14},{7,15},{8,0},{9,1},... | collective-permute-start | bytes 196616 | tf_op jit(solution)/shard_map/ppermute | solution.py:156
  7.3 3.6 %collective-permute-done = bf16[2,2,2,16,256]{4,3,2,1,0:T(8,128)(2,1)S(1)} collective-permute-done((bf16[2,2,2,16,256]{4,3,2,1,0:T(8,128)(2,1)S(1)}, bf16[2,2,2,16,256]{4,3,2,1,0:T(8,128)(2,1)S(1)}, u32[]{:S(2)}, u32[]{:S(2)}) %collective-permute-start) | collective-permute-done | bytes 65568 | tf_op jit(solution)/shard_map/ppermute | solution.py:156
  11.6 1.5 %collective-permute-start.2 = (bf16[4,2,2,16,256]{4,3,2,1,0:T(8,128)(2,1)S(1)}, bf16[4,2,2,16,256]{4,3,2,1,0:T(8,128)(2,1)S(1)}, u32[]{:S(2)}, u32[]{:S(2)}) collective-permute-start(bf16[4,2,2,16,256]{4,3,2,1,0:T(8,128)(2,1)S(1)} %pad_maximum_fusion), channel_id=1, source_target_pairs={{0,2},{1,3},{2,0},{3,1},{4,6},{5,7},{6,4},{7,5},{8,10},{9,11},{10,... | collective-permute-start | bytes 393224 | tf_op jit(solution)/shard_map/ppermute | solution.py:156
  13.1 1.4 %collective-permute-start.3 = (bf16[4,2,2,16,256]{4,3,2,1,0:T(8,128)(2,1)S(1)}, bf16[4,2,2,16,256]{4,3,2,1,0:T(8,128)(2,1)S(1)}, u32[]{:S(2)}, u32[]{:S(2)}) collective-permute-start(bf16[4,2,2,16,256]{4,3,2,1,0:T(8,128)(2,1)S(1)} %pad_maximum_fusion), channel_id=1, source_target_pairs={{0,6},{1,7},{2,4},{3,5},{4,2},{5,3},{6,0},{7,1},{8,14},{9,15},{10,... | collective-permute-start | bytes 393224 | tf_op jit(solution)/shard_map/ppermute | solution.py:156
  14.6 2.8 %collective-permute-done.1 = bf16[4,2,2,16,256]{4,3,2,1,0:T(8,128)(2,1)S(1)} collective-permute-done((bf16[4,2,2,16,256]{4,3,2,1,0:T(8,128)(2,1)S(1)}, bf16[4,2,2,16,256]{4,3,2,1,0:T(8,128)(2,1)S(1)}, u32[]{:S(2)}, u32[]{:S(2)}) %collective-permute-start.1) | collective-permute-done | bytes 131104 | tf_op jit(solution)/shard_map/ppermute | solution.py:156
  18.2 1.6 %collective-permute-done.3 = bf16[4,2,2,16,256]{4,3,2,1,0:T(8,128)(2,1)S(1)} collective-permute-done((bf16[4,2,2,16,256]{4,3,2,1,0:T(8,128)(2,1)S(1)}, bf16[4,2,2,16,256]{4,3,2,1,0:T(8,128)(2,1)S(1)}, u32[]{:S(2)}, u32[]{:S(2)}) %collective-permute-start.3) | collective-permute-done | bytes 131104 | tf_op jit(solution)/shard_map/ppermute | solution.py:156
  19.9 1.9 %collective-permute-done.4.high_ref = bf16[16,2,2,16,256]{4,3,2,1,0:T(8,128)(2,1)S(1)} collective-permute-done((bf16[16,2,2,16,256]{4,3,2,1,0:T(8,128)(2,1)S(1)}, bf16[16,2,2,16,256]{4,3,2,1,0:T(8,128)(2,1)S(1)}, u32[]{:S(2)}, u32[]{:S(2)}) %collective-permute-start.4) | collective-permute-done | bytes 524320 | tf_op jit(solution)/shard_map/ppermute | solution.py:158
  21.8 0.8 %copy-done.5 = bf16[16,2,2,16,256]{4,3,2,1,0:T(8,128)(2,1)} copy-done((bf16[16,2,2,16,256]{4,3,2,1,0:T(8,128)(2,1)}, bf16[16,2,2,16,256]{4,3,2,1,0:T(8,128)(2,1)S(1)}, u32[]{:S(2)}) %copy-start.5) | copy-done | bytes 524312
  22.6 5.3 %shard_map.104 = (bf16[2,2,256,256]{3,2,1,0:T(8,128)(2,1)}, f32[2,2,8,128]{3,2,1,0:T(8,128)}, f32[16,2,2,16,256]{4,3,2,1,0:T(8,128)}, bf16[16,2,2,16,256]{4,3,2,1,0:T(8,128)(2,1)}) custom-call(s32[2,2,8]{2,1,0:T(2,128)} %owner_ref.1, s32[2,16]{1,0:T(2,128)} %local_ref.1, s32[2,16]{1,0:T(2,128)} %side_ref.1, f32[2,16]{1,0:T(2,128)} %weight_ref.1, ...), custom_call_target="tpu_custom_call" | custom-call | flops 536870912 | bytes 4456448 | tf_op jit(solution)/shard_map/pallas_call | solution.py:85
  28.1 0.8 %slice_reduce_fusion = f32[2]{0:T(128)S(1)} fusion(f32[2,2,8,128]{3,2,1,0:T(8,128)} %get-tuple-element.33), kind=kLoop, calls=%fused_computation.38 | loop fusion | flops 2 | bytes 24 | tf_op jit(solution)/shard_map/reduce_sum | solution.py:164
  28.9 1.2 %collective-permute-done.5 = bf16[16,2,2,16,256]{4,3,2,1,0:T(8,128)(2,1)S(1)} collective-permute-done((bf16[16,2,2,16,256]{4,3,2,1,0:T(8,128)(2,1)}, bf16[16,2,2,16,256]{4,3,2,1,0:T(8,128)(2,1)S(1)}, u32[]{:S(2)}, u32[]{:S(2)}) %collective-permute-start.5) | collective-permute-done | bytes 524320 | tf_op jit(solution)/shard_map/ppermute | solution.py:177
  30.1 1.4 %fusion.21 = (bf16[16,2,2,16,256]{4,3,2,1,0:T(8,128)(2,1)S(1)}, f32[16,2,2,16,256]{4,3,2,1,0:T(8,128)S(1)}) fusion(f32[16,2,2,16,256]{4,3,2,1,0:T(8,128)} %get-tuple-element.31, bf16[16,2,2,16,256]{4,3,2,1,0:T(8,128)(2,1)S(1)} %collective-permute-done.5), kind=kLoop, calls=%fused_computation.46 | loop fusion | flops 786432 | bytes 3145728 | tf_op jit(solution)/shard_map/convert.3
  31.5 0.9 %collective-permute-start.6 = (bf16[4,2,2,16,256]{4,3,2,1,0:T(8,128)(2,1)S(1)}, bf16[4,2,2,16,256]{4,3,2,1,0:T(8,128)(2,1)S(1)}, u32[]{:S(2)}, u32[]{:S(2)}) collective-permute-start(bf16[4,2,2,16,256]{4,3,2,1,0:T(8,128)(2,1)S(1)} %get-tuple-element.36), channel_id=1, source_target_pairs={{0,4},{1,5},{2,6},{3,7},{4,0},{5,1},{6,2},{7,3},{8,12},{9,13},{10,... | collective-permute-start | bytes 393224 | tf_op jit(solution)/shard_map/ppermute | solution.py:188
  32.5 1.0 %collective-permute-start.7 = (bf16[4,2,2,16,256]{4,3,2,1,0:T(8,128)(2,1)S(1)}, bf16[4,2,2,16,256]{4,3,2,1,0:T(8,128)(2,1)S(1)}, u32[]{:S(2)}, u32[]{:S(2)}) collective-permute-start(bf16[4,2,2,16,256]{4,3,2,1,0:T(8,128)(2,1)S(1)} %get-tuple-element.38), channel_id=1, source_target_pairs={{0,2},{1,3},{2,0},{3,1},{4,6},{5,7},{6,4},{7,5},{8,10},{9,11},{10,... | collective-permute-start | bytes 393224 | tf_op jit(solution)/shard_map/ppermute | solution.py:188
  33.5 1.6 %collective-permute-start.8 = (bf16[4,2,2,16,256]{4,3,2,1,0:T(8,128)(2,1)S(1)}, bf16[4,2,2,16,256]{4,3,2,1,0:T(8,128)(2,1)S(1)}, u32[]{:S(2)}, u32[]{:S(2)}) collective-permute-start(bf16[4,2,2,16,256]{4,3,2,1,0:T(8,128)(2,1)S(1)} %get-tuple-element.37), channel_id=1, source_target_pairs={{0,6},{1,7},{2,4},{3,5},{4,2},{5,3},{6,0},{7,1},{8,14},{9,15},{10,... | collective-permute-start | bytes 393224 | tf_op jit(solution)/shard_map/ppermute | solution.py:188
  35.1 2.8 %collective-permute-done.6 = bf16[4,2,2,16,256]{4,3,2,1,0:T(8,128)(2,1)S(1)} collective-permute-done((bf16[4,2,2,16,256]{4,3,2,1,0:T(8,128)(2,1)S(1)}, bf16[4,2,2,16,256]{4,3,2,1,0:T(8,128)(2,1)S(1)}, u32[]{:S(2)}, u32[]{:S(2)}) %collective-permute-start.6) | collective-permute-done | bytes 131104 | tf_op jit(solution)/shard_map/ppermute | solution.py:188
  37.9 2.6 %collective-permute-done.7 = bf16[4,2,2,16,256]{4,3,2,1,0:T(8,128)(2,1)S(1)} collective-permute-done((bf16[4,2,2,16,256]{4,3,2,1,0:T(8,128)(2,1)S(1)}, bf16[4,2,2,16,256]{4,3,2,1,0:T(8,128)(2,1)S(1)}, u32[]{:S(2)}, u32[]{:S(2)}) %collective-permute-start.7) | collective-permute-done | bytes 131104 | tf_op jit(solution)/shard_map/ppermute | solution.py:188
  40.6 3.3 %collective-permute-start.9 = (bf16[2,2,2,16,256]{4,3,2,1,0:T(8,128)(2,1)S(1)}, bf16[2,2,2,16,256]{4,3,2,1,0:T(8,128)(2,1)S(1)}, u32[]{:S(2)}, u32[]{:S(2)}) collective-permute-start(bf16[2,2,2,16,256]{4,3,2,1,0:T(8,128)(2,1)S(1)} %slice.157), channel_id=1, source_target_pairs={{0,8},{1,9},{2,10},{3,11},{4,12},{5,13},{6,14},{7,15},{8,0},{9,1},... | collective-permute-start | bytes 196616 | tf_op jit(solution)/shard_map/ppermute | solution.py:188
  43.9 1.6 %collective-permute-start.11 = (bf16[3,2]{1,0:T(4,128)(2,1)S(1)}, bf16[3,2]{1,0:T(4,128)(2,1)S(1)}, u32[]{:S(2)}, u32[]{:S(2)}) collective-permute-start(bf16[3,2]{1,0:T(4,128)(2,1)S(1)} %pad_maximum_fusion.2), channel_id=1, source_target_pairs={{0,16},{16,0},{1,17},{17,1},{2,18},{18,2},{3,19},{19,3},{4,20},{20... | collective-permute-start | bytes 44 | tf_op jit(solution)/shard_map/ppermute | solution.py:173
  45.6 1.9 %collective-permute-done.11 = bf16[3,2]{1,0:T(4,128)(2,1)S(1)} collective-permute-done((bf16[3,2]{1,0:T(4,128)(2,1)S(1)}, bf16[3,2]{1,0:T(4,128)(2,1)S(1)}, u32[]{:S(2)}, u32[]{:S(2)}) %collective-permute-start.11) | collective-permute-done | bytes 44 | tf_op jit(solution)/shard_map/ppermute | solution.py:173
  48.2 1.6 %collective-permute-start.10 = (bf16[2,128,256]{2,1,0:T(8,128)(2,1)S(1)}, bf16[2,128,256]{2,1,0:T(8,128)(2,1)S(1)}, u32[]{:S(2)}, u32[]{:S(2)}) collective-permute-start(bf16[2,128,256]{2,1,0:T(8,128)(2,1)S(1)} %dynamic-slice_convert_fusion), channel_id=1, source_target_pairs={{0,16},{16,0},{1,17},{17,1},{2,18},{18,2},{3,19},{19,3},{4,20},{20... | collective-permute-start | bytes 393224 | tf_op jit(solution)/shard_map/ppermute | solution.py:211
  50.3 2.9 %collective-permute-done.10 = bf16[2,128,256]{2,1,0:T(8,128)(2,1)S(1)} collective-permute-done((bf16[2,128,256]{2,1,0:T(8,128)(2,1)S(1)}, bf16[2,128,256]{2,1,0:T(8,128)(2,1)S(1)}, u32[]{:S(2)}, u32[]{:S(2)}) %collective-permute-start.10) | collective-permute-done | bytes 131104 | tf_op jit(solution)/shard_map/ppermute | solution.py:211
  (39 shorter events, 4.1 us)
Async XLA Ops:
  0.6 1.0 %copy-start = (bf16[2,256,256]{2,1,0:T(8,128)(2,1)S(1)}, bf16[2,256,256]{2,1,0:T(8,128)(2,1)}, u32[]{:S(2)}) copy-start(bf16[2,256,256]{2,1,0:T(8,128)(2,1)} %param.16) | copy-start | bytes 786436
  0.6 2.2 %copy-start.2 = (bf16[2,256,256]{2,1,0:T(8,128)(2,1)S(1)}, bf16[2,256,256]{2,1,0:T(8,128)(2,1)}, u32[]{:S(2)}) copy-start(bf16[2,256,256]{2,1,0:T(8,128)(2,1)} %param.15) | copy-start | bytes 786436
  3.2 15.0 %copy-start.1 = (bf16[2,2,256,256]{3,2,1,0:T(8,128)(2,1)}, bf16[2,2,256,256]{3,2,1,0:T(8,128)(2,1)S(1)}, u32[]{:S(2)}) copy-start(bf16[2,2,256,256]{3,2,1,0:T(8,128)(2,1)S(1)} %fusion.2.proj_ref) | copy-start | bytes 1572868
  3.2 7.7 %collective-permute-start = (bf16[2,2,2,16,256]{4,3,2,1,0:T(8,128)(2,1)S(1)}, bf16[2,2,2,16,256]{4,3,2,1,0:T(8,128)(2,1)S(1)}, u32[]{:S(2)}, u32[]{:S(2)}) collective-permute-start(bf16[2,2,2,16,256]{4,3,2,1,0:T(8,128)(2,1)S(1)} %get-tuple-element.41), channel_id=1, source_target_pairs={{0,8},{1,9},{2,10},{3,11},{4,12},{5,13},{6,14},{7,15},{8,0},{9,1},... | collective-permute-start | bytes 196616 | tf_op jit(solution)/shard_map/ppermute | solution.py:156
  11.0 6.4 %collective-permute-start.1 = (bf16[4,2,2,16,256]{4,3,2,1,0:T(8,128)(2,1)S(1)}, bf16[4,2,2,16,256]{4,3,2,1,0:T(8,128)(2,1)S(1)}, u32[]{:S(2)}, u32[]{:S(2)}) collective-permute-start(bf16[4,2,2,16,256]{4,3,2,1,0:T(8,128)(2,1)S(1)} %pad_maximum_fusion), channel_id=1, source_target_pairs={{0,4},{1,5},{2,6},{3,7},{4,0},{5,1},{6,2},{7,3},{8,12},{9,13},{10,... | collective-permute-start | bytes 393224 | tf_op jit(solution)/shard_map/ppermute | solution.py:156
  11.6 6.5 %collective-permute-start.2 = (bf16[4,2,2,16,256]{4,3,2,1,0:T(8,128)(2,1)S(1)}, bf16[4,2,2,16,256]{4,3,2,1,0:T(8,128)(2,1)S(1)}, u32[]{:S(2)}, u32[]{:S(2)}) collective-permute-start(bf16[4,2,2,16,256]{4,3,2,1,0:T(8,128)(2,1)S(1)} %pad_maximum_fusion), channel_id=1, source_target_pairs={{0,2},{1,3},{2,0},{3,1},{4,6},{5,7},{6,4},{7,5},{8,10},{9,11},{10,... | collective-permute-start | bytes 393224 | tf_op jit(solution)/shard_map/ppermute | solution.py:156
  13.1 6.7 %collective-permute-start.3 = (bf16[4,2,2,16,256]{4,3,2,1,0:T(8,128)(2,1)S(1)}, bf16[4,2,2,16,256]{4,3,2,1,0:T(8,128)(2,1)S(1)}, u32[]{:S(2)}, u32[]{:S(2)}) collective-permute-start(bf16[4,2,2,16,256]{4,3,2,1,0:T(8,128)(2,1)S(1)} %pad_maximum_fusion), channel_id=1, source_target_pairs={{0,6},{1,7},{2,4},{3,5},{4,2},{5,3},{6,0},{7,1},{8,14},{9,15},{10,... | collective-permute-start | bytes 393224 | tf_op jit(solution)/shard_map/ppermute | solution.py:156
  19.8 2.0 %copy-start.3 = (bf16[16,2,2,16,256]{4,3,2,1,0:T(8,128)(2,1)}, bf16[16,2,2,16,256]{4,3,2,1,0:T(8,128)(2,1)S(1)}, u32[]{:S(2)}) copy-start(bf16[16,2,2,16,256]{4,3,2,1,0:T(8,128)(2,1)S(1)} %constant_dynamic-update-slice_fusion.low_ref) | copy-start | bytes 1572868
  19.8 2.0 %collective-permute-start.4 = (bf16[16,2,2,16,256]{4,3,2,1,0:T(8,128)(2,1)S(1)}, bf16[16,2,2,16,256]{4,3,2,1,0:T(8,128)(2,1)S(1)}, u32[]{:S(2)}, u32[]{:S(2)}) collective-permute-start(bf16[16,2,2,16,256]{4,3,2,1,0:T(8,128)(2,1)S(1)} %constant_dynamic-update-slice_fusion.low_ref), channel_id=1, source_target_pairs={{0,1},{1,0},{2,3},{3,2},{4,5},{5,4},{6,7},{7,6},{8,9},{9,8},{10,11... | collective-permute-start | bytes 1572872 | tf_op jit(solution)/shard_map/ppermute | solution.py:158
  21.8 0.8 %copy-start.5 = (bf16[16,2,2,16,256]{4,3,2,1,0:T(8,128)(2,1)}, bf16[16,2,2,16,256]{4,3,2,1,0:T(8,128)(2,1)S(1)}, u32[]{:S(2)}) copy-start(bf16[16,2,2,16,256]{4,3,2,1,0:T(8,128)(2,1)S(1)} %collective-permute-done.4.high_ref) | copy-start | bytes 1572868
  27.9 2.2 %collective-permute-start.5 = (bf16[16,2,2,16,256]{4,3,2,1,0:T(8,128)(2,1)}, bf16[16,2,2,16,256]{4,3,2,1,0:T(8,128)(2,1)S(1)}, u32[]{:S(2)}, u32[]{:S(2)}) collective-permute-start(bf16[16,2,2,16,256]{4,3,2,1,0:T(8,128)(2,1)} %get-tuple-element.32), channel_id=1, source_target_pairs={{0,1},{1,0},{2,3},{3,2},{4,5},{5,4},{6,7},{7,6},{8,9},{9,8},{10,11... | collective-permute-start | bytes 1572872 | tf_op jit(solution)/shard_map/ppermute | solution.py:177
  31.5 6.4 %collective-permute-start.6 = (bf16[4,2,2,16,256]{4,3,2,1,0:T(8,128)(2,1)S(1)}, bf16[4,2,2,16,256]{4,3,2,1,0:T(8,128)(2,1)S(1)}, u32[]{:S(2)}, u32[]{:S(2)}) collective-permute-start(bf16[4,2,2,16,256]{4,3,2,1,0:T(8,128)(2,1)S(1)} %get-tuple-element.36), channel_id=1, source_target_pairs={{0,4},{1,5},{2,6},{3,7},{4,0},{5,1},{6,2},{7,3},{8,12},{9,13},{10,... | collective-permute-start | bytes 393224 | tf_op jit(solution)/shard_map/ppermute | solution.py:188
  32.5 8.1 %collective-permute-start.7 = (bf16[4,2,2,16,256]{4,3,2,1,0:T(8,128)(2,1)S(1)}, bf16[4,2,2,16,256]{4,3,2,1,0:T(8,128)(2,1)S(1)}, u32[]{:S(2)}, u32[]{:S(2)}) collective-permute-start(bf16[4,2,2,16,256]{4,3,2,1,0:T(8,128)(2,1)S(1)} %get-tuple-element.38), channel_id=1, source_target_pairs={{0,2},{1,3},{2,0},{3,1},{4,6},{5,7},{6,4},{7,5},{8,10},{9,11},{10,... | collective-permute-start | bytes 393224 | tf_op jit(solution)/shard_map/ppermute | solution.py:188
  33.5 7.0 %collective-permute-start.8 = (bf16[4,2,2,16,256]{4,3,2,1,0:T(8,128)(2,1)S(1)}, bf16[4,2,2,16,256]{4,3,2,1,0:T(8,128)(2,1)S(1)}, u32[]{:S(2)}, u32[]{:S(2)}) collective-permute-start(bf16[4,2,2,16,256]{4,3,2,1,0:T(8,128)(2,1)S(1)} %get-tuple-element.37), channel_id=1, source_target_pairs={{0,6},{1,7},{2,4},{3,5},{4,2},{5,3},{6,0},{7,1},{8,14},{9,15},{10,... | collective-permute-start | bytes 393224 | tf_op jit(solution)/shard_map/ppermute | solution.py:188
  40.5 5.0 %copy-start.4 = (bf16[2,2,256,256]{3,2,1,0:T(8,128)(2,1)S(1)}, bf16[2,2,256,256]{3,2,1,0:T(8,128)(2,1)}, u32[]{:S(2)}) copy-start(bf16[2,2,256,256]{3,2,1,0:T(8,128)(2,1)} %get-tuple-element.30) | copy-start | bytes 1572868
  40.6 6.9 %collective-permute-start.9 = (bf16[2,2,2,16,256]{4,3,2,1,0:T(8,128)(2,1)S(1)}, bf16[2,2,2,16,256]{4,3,2,1,0:T(8,128)(2,1)S(1)}, u32[]{:S(2)}, u32[]{:S(2)}) collective-permute-start(bf16[2,2,2,16,256]{4,3,2,1,0:T(8,128)(2,1)S(1)} %slice.157), channel_id=1, source_target_pairs={{0,8},{1,9},{2,10},{3,11},{4,12},{5,13},{6,14},{7,15},{8,0},{9,1},... | collective-permute-start | bytes 196616 | tf_op jit(solution)/shard_map/ppermute | solution.py:188
  43.9 3.6 %collective-permute-start.11 = (bf16[3,2]{1,0:T(4,128)(2,1)S(1)}, bf16[3,2]{1,0:T(4,128)(2,1)S(1)}, u32[]{:S(2)}, u32[]{:S(2)}) collective-permute-start(bf16[3,2]{1,0:T(4,128)(2,1)S(1)} %pad_maximum_fusion.2), channel_id=1, source_target_pairs={{0,16},{16,0},{1,17},{17,1},{2,18},{18,2},{3,19},{19,3},{4,20},{20... | collective-permute-start | bytes 44 | tf_op jit(solution)/shard_map/ppermute | solution.py:173
  48.2 5.0 %collective-permute-start.10 = (bf16[2,128,256]{2,1,0:T(8,128)(2,1)S(1)}, bf16[2,128,256]{2,1,0:T(8,128)(2,1)S(1)}, u32[]{:S(2)}, u32[]{:S(2)}) collective-permute-start(bf16[2,128,256]{2,1,0:T(8,128)(2,1)S(1)} %dynamic-slice_convert_fusion), channel_id=1, source_target_pairs={{0,16},{16,0},{1,17},{17,1},{2,18},{18,2},{3,19},{19,3},{4,20},{20... | collective-permute-start | bytes 393224 | tf_op jit(solution)/shard_map/ppermute | solution.py:211

commit v15 on v14

--- a/solution.py
+++ b/solution.py
@@ -20,6 +20,7 @@
     steps = peer_count.bit_length() - 1
     me = lax.axis_index("dom")
     ctf = ctf_ref[0]
+    ctf_t = ctf.T
     zero = jnp.zeros((OVL, pixels), jnp.float32)
 
     def place_of(k, j):
@@ -45,13 +46,10 @@
         residual_ref[k, pixels - OVL :] = residual_ref[k, pixels - OVL :] - lower
         residual = residual_ref[k].astype(jnp.bfloat16)
         smoothed = jnp.dot(ctf, residual, preferred_element_type=jnp.float32).astype(jnp.bfloat16)
-        filtered = lax.dot_general(
-            smoothed, ctf, (((1,), (1,)), ((), ())), preferred_element_type=jnp.float32
-        )
+        filtered = jnp.dot(smoothed, ctf_t, preferred_element_type=jnp.float32)
         score_ref[0, k] = jnp.full(score_ref.shape[2:], jnp.sum(filtered * filtered), jnp.float32)
-        reverse = lax.dot_general(
-            ctf, filtered.astype(jnp.bfloat16), (((0,), (0,)), ((), ())),
-            preferred_element_type=jnp.float32,
+        reverse = jnp.dot(
+            ctf_t, filtered.astype(jnp.bfloat16), preferred_element_type=jnp.float32
         ).astype(jnp.bfloat16)
         weighted = jnp.dot(reverse, ctf, preferred_element_type=jnp.float32).astype(jnp.bfloat16)
         weighted_ref[k, 0] = weighted

time: 54.2 us -> 54.3 us (level)
  no operation moved by 1% of the time
where the time goes in v15:
time: 54.3 us; the launch traced here: 54 us
  waiting for transfers between devices  22.2 us (41%)
  starting transfers between devices  17.9 us (33%)
  Pallas kernels  5.42 us (10%)
  other arithmetic  3.73 us (7%)
  matrix products  2.12 us (4%)
  local copies, waits for them, and re-layouts  1.85 us (3%)
  between operations  0.83 us (2%)
    ppermute x4, waiting for transfers between devices, on_device(): pieces.append(lax.ppermute(edges_all, 'dom', pairs))  8.84 us
    ppermute x4, starting transfers between devices, on_device(): pieces.append(lax.ppermute(edges_all, 'dom', pairs))  7.65 us
    ppermute x4, starting transfers between devices, on_device(): kept = kept + lax.ppermute(given, 'dom', pairs).astype(jnp.float32)  6.8 us
    ppermute x4, waiting for transfers between devices, on_device(): kept = kept + lax.ppermute(given, 'dom', pairs).astype(jnp.float32)  5.46 us
    pallas_call x1, Pallas kernels, middle(): pl.pallas_call(middle_kernel, grid=(tilt_count,), in_specs=[smem, smem, s...  5.42 us
    ppermute x1, waiting for transfers between devices, on_device(): given = lax.ppermute(given.astype(jnp.bfloat16), 'tilt', [(0, 1), (1, 0)])  2.92 us
    ppermute x1, waiting for transfers between devices, on_device(): parts = lax.ppermute(parts, 'tilt', [(0, 1), (1, 0)]).astype(jnp.float32)  1.94 us
    ppermute x1, waiting for transfers between devices, on_device(): lax.ppermute(edges_all, 'dom', [(i, i ^ 1) for i in range(peer_count)])  1.9 us
  transfers between devices with their start and end apart: 12, of which 10 were waited for; matrix products, arithmetic and copies ran while one was open for 3% of the time, Pallas kernels for 0%

profile of v15, /device:TPU:0, one launch (start us, length us, event | category | flops | bytes accessed | tf_op | source)
XLA Modules:
  0.0 54.0 jit_solution(5633555837547671253)
XLA Ops:
  0.7 0.9 %copy-done = bf16[2,256,256]{2,1,0:T(8,128)(2,1)S(1)} copy-done((bf16[2,256,256]{2,1,0:T(8,128)(2,1)S(1)}, bf16[2,256,256]{2,1,0:T(8,128)(2,1)}, u32[]{:S(2)}) %copy-start) | copy-done | bytes 262168
  1.6 1.3 %fusion = bf16[2,2,256,256]{3,2,0,1:T(8,128)(2,1)S(1)} fusion(bf16[2,256,256]{2,1,0:T(8,128)(2,1)S(1)} %copy-done, bf16[2,256,256]{2,1,0:T(8,128)(2,1)} %param.13), kind=kOutput, calls=%fused_computation.3 | convolution fusion | flops 134479872 | bytes 1048576 | tf_op jit(solution)/shard_map/kij,tlj->ktil/dot_general | solution.py:140
  3.2 4.1 %collective-permute-start = (bf16[2,2,2,16,256]{4,3,2,1,0:T(8,128)(2,1)S(1)}, bf16[2,2,2,16,256]{4,3,2,1,0:T(8,128)(2,1)S(1)}, u32[]{:S(2)}, u32[]{:S(2)}) collective-permute-start(bf16[2,2,2,16,256]{4,3,2,1,0:T(8,128)(2,1)S(1)} %get-tuple-element.41), channel_id=1, source_target_pairs={{0,8},{1,9},{2,10},{3,11},{4,12},{5,13},{6,14},{7,15},{8,0},{9,1},... | collective-permute-start | bytes 196616 | tf_op jit(solution)/shard_map/ppermute | solution.py:154
  7.3 3.6 %collective-permute-done = bf16[2,2,2,16,256]{4,3,2,1,0:T(8,128)(2,1)S(1)} collective-permute-done((bf16[2,2,2,16,256]{4,3,2,1,0:T(8,128)(2,1)S(1)}, bf16[2,2,2,16,256]{4,3,2,1,0:T(8,128)(2,1)S(1)}, u32[]{:S(2)}, u32[]{:S(2)}) %collective-permute-start) | collective-permute-done | bytes 65568 | tf_op jit(solution)/shard_map/ppermute | solution.py:154
  11.6 1.5 %collective-permute-start.2 = (bf16[4,2,2,16,256]{4,3,2,1,0:T(8,128)(2,1)S(1)}, bf16[4,2,2,16,256]{4,3,2,1,0:T(8,128)(2,1)S(1)}, u32[]{:S(2)}, u32[]{:S(2)}) collective-permute-start(bf16[4,2,2,16,256]{4,3,2,1,0:T(8,128)(2,1)S(1)} %pad_maximum_fusion), channel_id=1, source_target_pairs={{0,2},{1,3},{2,0},{3,1},{4,6},{5,7},{6,4},{7,5},{8,10},{9,11},{10,... | collective-permute-start | bytes 393224 | tf_op jit(solution)/shard_map/ppermute | solution.py:154
  13.1 1.4 %collective-permute-start.3 = (bf16[4,2,2,16,256]{4,3,2,1,0:T(8,128)(2,1)S(1)}, bf16[4,2,2,16,256]{4,3,2,1,0:T(8,128)(2,1)S(1)}, u32[]{:S(2)}, u32[]{:S(2)}) collective-permute-start(bf16[4,2,2,16,256]{4,3,2,1,0:T(8,128)(2,1)S(1)} %pad_maximum_fusion), channel_id=1, source_target_pairs={{0,6},{1,7},{2,4},{3,5},{4,2},{5,3},{6,0},{7,1},{8,14},{9,15},{10,... | collective-permute-start | bytes 393224 | tf_op jit(solution)/shard_map/ppermute | solution.py:154
  14.6 2.8 %collective-permute-done.1 = bf16[4,2,2,16,256]{4,3,2,1,0:T(8,128)(2,1)S(1)} collective-permute-done((bf16[4,2,2,16,256]{4,3,2,1,0:T(8,128)(2,1)S(1)}, bf16[4,2,2,16,256]{4,3,2,1,0:T(8,128)(2,1)S(1)}, u32[]{:S(2)}, u32[]{:S(2)}) %collective-permute-start.1) | collective-permute-done | bytes 131104 | tf_op jit(solution)/shard_map/ppermute | solution.py:154
  18.2 1.6 %collective-permute-done.3 = bf16[4,2,2,16,256]{4,3,2,1,0:T(8,128)(2,1)S(1)} collective-permute-done((bf16[4,2,2,16,256]{4,3,2,1,0:T(8,128)(2,1)S(1)}, bf16[4,2,2,16,256]{4,3,2,1,0:T(8,128)(2,1)S(1)}, u32[]{:S(2)}, u32[]{:S(2)}) %collective-permute-start.3) | collective-permute-done | bytes 131104 | tf_op jit(solution)/shard_map/ppermute | solution.py:154
  19.9 1.9 %collective-permute-done.4.high_ref = bf16[16,2,2,16,256]{4,3,2,1,0:T(8,128)(2,1)S(1)} collective-permute-done((bf16[16,2,2,16,256]{4,3,2,1,0:T(8,128)(2,1)S(1)}, bf16[16,2,2,16,256]{4,3,2,1,0:T(8,128)(2,1)S(1)}, u32[]{:S(2)}, u32[]{:S(2)}) %collective-permute-start.4) | collective-permute-done | bytes 524320 | tf_op jit(solution)/shard_map/ppermute | solution.py:156
  21.8 0.8 %copy-done.5 = bf16[16,2,2,16,256]{4,3,2,1,0:T(8,128)(2,1)} copy-done((bf16[16,2,2,16,256]{4,3,2,1,0:T(8,128)(2,1)}, bf16[16,2,2,16,256]{4,3,2,1,0:T(8,128)(2,1)S(1)}, u32[]{:S(2)}) %copy-start.5) | copy-done | bytes 524312
  22.6 5.4 %shard_map.104 = (bf16[2,2,256,256]{3,2,1,0:T(8,128)(2,1)}, f32[2,2,8,128]{3,2,1,0:T(8,128)}, f32[16,2,2,16,256]{4,3,2,1,0:T(8,128)}, bf16[16,2,2,16,256]{4,3,2,1,0:T(8,128)(2,1)}) custom-call(s32[2,2,8]{2,1,0:T(2,128)} %owner_ref.1, s32[2,16]{1,0:T(2,128)} %local_ref.1, s32[2,16]{1,0:T(2,128)} %side_ref.1, f32[2,16]{1,0:T(2,128)} %weight_ref.1, ...), custom_call_target="tpu_custom_call" | custom-call | flops 536870912 | bytes 4456448 | tf_op jit(solution)/shard_map/pallas_call | solution.py:83
  28.2 0.8 %slice_reduce_fusion = f32[2]{0:T(128)S(1)} fusion(f32[2,2,8,128]{3,2,1,0:T(8,128)} %get-tuple-element.33), kind=kLoop, calls=%fused_computation.38 | loop fusion | flops 2 | bytes 24 | tf_op jit(solution)/shard_map/reduce_sum | solution.py:162
  29.0 1.2 %collective-permute-done.5 = bf16[16,2,2,16,256]{4,3,2,1,0:T(8,128)(2,1)S(1)} collective-permute-done((bf16[16,2,2,16,256]{4,3,2,1,0:T(8,128)(2,1)}, bf16[16,2,2,16,256]{4,3,2,1,0:T(8,128)(2,1)S(1)}, u32[]{:S(2)}, u32[]{:S(2)}) %collective-permute-start.5) | collective-permute-done | bytes 524320 | tf_op jit(solution)/shard_map/ppermute | solution.py:175
  30.2 1.4 %fusion.21 = (bf16[16,2,2,16,256]{4,3,2,1,0:T(8,128)(2,1)S(1)}, f32[16,2,2,16,256]{4,3,2,1,0:T(8,128)S(1)}) fusion(f32[16,2,2,16,256]{4,3,2,1,0:T(8,128)} %get-tuple-element.31, bf16[16,2,2,16,256]{4,3,2,1,0:T(8,128)(2,1)S(1)} %collective-permute-done.5), kind=kLoop, calls=%fused_computation.46 | loop fusion | flops 786432 | bytes 3145728 | tf_op jit(solution)/shard_map/convert.3
  31.6 0.9 %collective-permute-start.6 = (bf16[4,2,2,16,256]{4,3,2,1,0:T(8,128)(2,1)S(1)}, bf16[4,2,2,16,256]{4,3,2,1,0:T(8,128)(2,1)S(1)}, u32[]{:S(2)}, u32[]{:S(2)}) collective-permute-start(bf16[4,2,2,16,256]{4,3,2,1,0:T(8,128)(2,1)S(1)} %get-tuple-element.36), channel_id=1, source_target_pairs={{0,4},{1,5},{2,6},{3,7},{4,0},{5,1},{6,2},{7,3},{8,12},{9,13},{10,... | collective-permute-start | bytes 393224 | tf_op jit(solution)/shard_map/ppermute | solution.py:186
  32.6 1.0 %collective-permute-start.7 = (bf16[4,2,2,16,256]{4,3,2,1,0:T(8,128)(2,1)S(1)}, bf16[4,2,2,16,256]{4,3,2,1,0:T(8,128)(2,1)S(1)}, u32[]{:S(2)}, u32[]{:S(2)}) collective-permute-start(bf16[4,2,2,16,256]{4,3,2,1,0:T(8,128)(2,1)S(1)} %get-tuple-element.38), channel_id=1, source_target_pairs={{0,2},{1,3},{2,0},{3,1},{4,6},{5,7},{6,4},{7,5},{8,10},{9,11},{10,... | collective-permute-start | bytes 393224 | tf_op jit(solution)/shard_map/ppermute | solution.py:186
  33.6 1.6 %collective-permute-start.8 = (bf16[4,2,2,16,256]{4,3,2,1,0:T(8,128)(2,1)S(1)}, bf16[4,2,2,16,256]{4,3,2,1,0:T(8,128)(2,1)S(1)}, u32[]{:S(2)}, u32[]{:S(2)}) collective-permute-start(bf16[4,2,2,16,256]{4,3,2,1,0:T(8,128)(2,1)S(1)} %get-tuple-element.37), channel_id=1, source_target_pairs={{0,6},{1,7},{2,4},{3,5},{4,2},{5,3},{6,0},{7,1},{8,14},{9,15},{10,... | collective-permute-start | bytes 393224 | tf_op jit(solution)/shard_map/ppermute | solution.py:186
  35.2 2.8 %collective-permute-done.6 = bf16[4,2,2,16,256]{4,3,2,1,0:T(8,128)(2,1)S(1)} collective-permute-done((bf16[4,2,2,16,256]{4,3,2,1,0:T(8,128)(2,1)S(1)}, bf16[4,2,2,16,256]{4,3,2,1,0:T(8,128)(2,1)S(1)}, u32[]{:S(2)}, u32[]{:S(2)}) %collective-permute-start.6) | collective-permute-done | bytes 131104 | tf_op jit(solution)/shard_map/ppermute | solution.py:186
  38.0 2.6 %collective-permute-done.7 = bf16[4,2,2,16,256]{4,3,2,1,0:T(8,128)(2,1)S(1)} collective-permute-done((bf16[4,2,2,16,256]{4,3,2,1,0:T(8,128)(2,1)S(1)}, bf16[4,2,2,16,256]{4,3,2,1,0:T(8,128)(2,1)S(1)}, u32[]{:S(2)}, u32[]{:S(2)}) %collective-permute-start.7) | collective-permute-done | bytes 131104 | tf_op jit(solution)/shard_map/ppermute | solution.py:186
  40.7 3.2 %collective-permute-start.9 = (bf16[2,2,2,16,256]{4,3,2,1,0:T(8,128)(2,1)S(1)}, bf16[2,2,2,16,256]{4,3,2,1,0:T(8,128)(2,1)S(1)}, u32[]{:S(2)}, u32[]{:S(2)}) collective-permute-start(bf16[2,2,2,16,256]{4,3,2,1,0:T(8,128)(2,1)S(1)} %slice.157), channel_id=1, source_target_pairs={{0,8},{1,9},{2,10},{3,11},{4,12},{5,13},{6,14},{7,15},{8,0},{9,1},... | collective-permute-start | bytes 196616 | tf_op jit(solution)/shard_map/ppermute | solution.py:186
  44.0 1.6 %collective-permute-start.11 = (bf16[3,2]{1,0:T(4,128)(2,1)S(1)}, bf16[3,2]{1,0:T(4,128)(2,1)S(1)}, u32[]{:S(2)}, u32[]{:S(2)}) collective-permute-start(bf16[3,2]{1,0:T(4,128)(2,1)S(1)} %pad_maximum_fusion.2), channel_id=1, source_target_pairs={{0,16},{16,0},{1,17},{17,1},{2,18},{18,2},{3,19},{19,3},{4,20},{20... | collective-permute-start | bytes 44 | tf_op jit(solution)/shard_map/ppermute | solution.py:171
  45.7 1.9 %collective-permute-done.11 = bf16[3,2]{1,0:T(4,128)(2,1)S(1)} collective-permute-done((bf16[3,2]{1,0:T(4,128)(2,1)S(1)}, bf16[3,2]{1,0:T(4,128)(2,1)S(1)}, u32[]{:S(2)}, u32[]{:S(2)}) %collective-permute-start.11) | collective-permute-done | bytes 44 | tf_op jit(solution)/shard_map/ppermute | solution.py:171
  48.3 1.6 %collective-permute-start.10 = (bf16[2,128,256]{2,1,0:T(8,128)(2,1)S(1)}, bf16[2,128,256]{2,1,0:T(8,128)(2,1)S(1)}, u32[]{:S(2)}, u32[]{:S(2)}) collective-permute-start(bf16[2,128,256]{2,1,0:T(8,128)(2,1)S(1)} %dynamic-slice_convert_fusion), channel_id=1, source_target_pairs={{0,16},{16,0},{1,17},{17,1},{2,18},{18,2},{3,19},{19,3},{4,20},{20... | collective-permute-start | bytes 393224 | tf_op jit(solution)/shard_map/ppermute | solution.py:209
  50.4 2.9 %collective-permute-done.10 = bf16[2,128,256]{2,1,0:T(8,128)(2,1)S(1)} collective-permute-done((bf16[2,128,256]{2,1,0:T(8,128)(2,1)S(1)}, bf16[2,128,256]{2,1,0:T(8,128)(2,1)S(1)}, u32[]{:S(2)}, u32[]{:S(2)}) %collective-permute-start.10) | collective-permute-done | bytes 131104 | tf_op jit(solution)/shard_map/ppermute | solution.py:209
  (39 shorter events, 4.1 us)
Async XLA Ops:
  0.6 1.0 %copy-start = (bf16[2,256,256]{2,1,0:T(8,128)(2,1)S(1)}, bf16[2,256,256]{2,1,0:T(8,128)(2,1)}, u32[]{:S(2)}) copy-start(bf16[2,256,256]{2,1,0:T(8,128)(2,1)} %param.16) | copy-start | bytes 786436
  0.6 2.2 %copy-start.2 = (bf16[2,256,256]{2,1,0:T(8,128)(2,1)S(1)}, bf16[2,256,256]{2,1,0:T(8,128)(2,1)}, u32[]{:S(2)}) copy-start(bf16[2,256,256]{2,1,0:T(8,128)(2,1)} %param.15) | copy-start | bytes 786436
  3.2 15.0 %copy-start.1 = (bf16[2,2,256,256]{3,2,1,0:T(8,128)(2,1)}, bf16[2,2,256,256]{3,2,1,0:T(8,128)(2,1)S(1)}, u32[]{:S(2)}) copy-start(bf16[2,2,256,256]{3,2,1,0:T(8,128)(2,1)S(1)} %fusion.2.proj_ref) | copy-start | bytes 1572868
  3.2 7.7 %collective-permute-start = (bf16[2,2,2,16,256]{4,3,2,1,0:T(8,128)(2,1)S(1)}, bf16[2,2,2,16,256]{4,3,2,1,0:T(8,128)(2,1)S(1)}, u32[]{:S(2)}, u32[]{:S(2)}) collective-permute-start(bf16[2,2,2,16,256]{4,3,2,1,0:T(8,128)(2,1)S(1)} %get-tuple-element.41), channel_id=1, source_target_pairs={{0,8},{1,9},{2,10},{3,11},{4,12},{5,13},{6,14},{7,15},{8,0},{9,1},... | collective-permute-start | bytes 196616 | tf_op jit(solution)/shard_map/ppermute | solution.py:154
  11.0 6.4 %collective-permute-start.1 = (bf16[4,2,2,16,256]{4,3,2,1,0:T(8,128)(2,1)S(1)}, bf16[4,2,2,16,256]{4,3,2,1,0:T(8,128)(2,1)S(1)}, u32[]{:S(2)}, u32[]{:S(2)}) collective-permute-start(bf16[4,2,2,16,256]{4,3,2,1,0:T(8,128)(2,1)S(1)} %pad_maximum_fusion), channel_id=1, source_target_pairs={{0,4},{1,5},{2,6},{3,7},{4,0},{5,1},{6,2},{7,3},{8,12},{9,13},{10,... | collective-permute-start | bytes 393224 | tf_op jit(solution)/shard_map/ppermute | solution.py:154
  11.6 6.5 %collective-permute-start.2 = (bf16[4,2,2,16,256]{4,3,2,1,0:T(8,128)(2,1)S(1)}, bf16[4,2,2,16,256]{4,3,2,1,0:T(8,128)(2,1)S(1)}, u32[]{:S(2)}, u32[]{:S(2)}) collective-permute-start(bf16[4,2,2,16,256]{4,3,2,1,0:T(8,128)(2,1)S(1)} %pad_maximum_fusion), channel_id=1, source_target_pairs={{0,2},{1,3},{2,0},{3,1},{4,6},{5,7},{6,4},{7,5},{8,10},{9,11},{10,... | collective-permute-start | bytes 393224 | tf_op jit(solution)/shard_map/ppermute | solution.py:154
  13.1 6.7 %collective-permute-start.3 = (bf16[4,2,2,16,256]{4,3,2,1,0:T(8,128)(2,1)S(1)}, bf16[4,2,2,16,256]{4,3,2,1,0:T(8,128)(2,1)S(1)}, u32[]{:S(2)}, u32[]{:S(2)}) collective-permute-start(bf16[4,2,2,16,256]{4,3,2,1,0:T(8,128)(2,1)S(1)} %pad_maximum_fusion), channel_id=1, source_target_pairs={{0,6},{1,7},{2,4},{3,5},{4,2},{5,3},{6,0},{7,1},{8,14},{9,15},{10,... | collective-permute-start | bytes 393224 | tf_op jit(solution)/shard_map/ppermute | solution.py:154
  19.8 2.0 %copy-start.3 = (bf16[16,2,2,16,256]{4,3,2,1,0:T(8,128)(2,1)}, bf16[16,2,2,16,256]{4,3,2,1,0:T(8,128)(2,1)S(1)}, u32[]{:S(2)}) copy-start(bf16[16,2,2,16,256]{4,3,2,1,0:T(8,128)(2,1)S(1)} %constant_dynamic-update-slice_fusion.low_ref) | copy-start | bytes 1572868
  19.8 2.0 %collective-permute-start.4 = (bf16[16,2,2,16,256]{4,3,2,1,0:T(8,128)(2,1)S(1)}, bf16[16,2,2,16,256]{4,3,2,1,0:T(8,128)(2,1)S(1)}, u32[]{:S(2)}, u32[]{:S(2)}) collective-permute-start(bf16[16,2,2,16,256]{4,3,2,1,0:T(8,128)(2,1)S(1)} %constant_dynamic-update-slice_fusion.low_ref), channel_id=1, source_target_pairs={{0,1},{1,0},{2,3},{3,2},{4,5},{5,4},{6,7},{7,6},{8,9},{9,8},{10,11... | collective-permute-start | bytes 1572872 | tf_op jit(solution)/shard_map/ppermute | solution.py:156
  21.8 0.8 %copy-start.5 = (bf16[16,2,2,16,256]{4,3,2,1,0:T(8,128)(2,1)}, bf16[16,2,2,16,256]{4,3,2,1,0:T(8,128)(2,1)S(1)}, u32[]{:S(2)}) copy-start(bf16[16,2,2,16,256]{4,3,2,1,0:T(8,128)(2,1)S(1)} %collective-permute-done.4.high_ref) | copy-start | bytes 1572868
  28.0 2.2 %collective-permute-start.5 = (bf16[16,2,2,16,256]{4,3,2,1,0:T(8,128)(2,1)}, bf16[16,2,2,16,256]{4,3,2,1,0:T(8,128)(2,1)S(1)}, u32[]{:S(2)}, u32[]{:S(2)}) collective-permute-start(bf16[16,2,2,16,256]{4,3,2,1,0:T(8,128)(2,1)} %get-tuple-element.32), channel_id=1, source_target_pairs={{0,1},{1,0},{2,3},{3,2},{4,5},{5,4},{6,7},{7,6},{8,9},{9,8},{10,11... | collective-permute-start | bytes 1572872 | tf_op jit(solution)/shard_map/ppermute | solution.py:175
  31.6 6.4 %collective-permute-start.6 = (bf16[4,2,2,16,256]{4,3,2,1,0:T(8,128)(2,1)S(1)}, bf16[4,2,2,16,256]{4,3,2,1,0:T(8,128)(2,1)S(1)}, u32[]{:S(2)}, u32[]{:S(2)}) collective-permute-start(bf16[4,2,2,16,256]{4,3,2,1,0:T(8,128)(2,1)S(1)} %get-tuple-element.36), channel_id=1, source_target_pairs={{0,4},{1,5},{2,6},{3,7},{4,0},{5,1},{6,2},{7,3},{8,12},{9,13},{10,... | collective-permute-start | bytes 393224 | tf_op jit(solution)/shard_map/ppermute | solution.py:186
  32.6 8.1 %collective-permute-start.7 = (bf16[4,2,2,16,256]{4,3,2,1,0:T(8,128)(2,1)S(1)}, bf16[4,2,2,16,256]{4,3,2,1,0:T(8,128)(2,1)S(1)}, u32[]{:S(2)}, u32[]{:S(2)}) collective-permute-start(bf16[4,2,2,16,256]{4,3,2,1,0:T(8,128)(2,1)S(1)} %get-tuple-element.38), channel_id=1, source_target_pairs={{0,2},{1,3},{2,0},{3,1},{4,6},{5,7},{6,4},{7,5},{8,10},{9,11},{10,... | collective-permute-start | bytes 393224 | tf_op jit(solution)/shard_map/ppermute | solution.py:186
  33.6 7.0 %collective-permute-start.8 = (bf16[4,2,2,16,256]{4,3,2,1,0:T(8,128)(2,1)S(1)}, bf16[4,2,2,16,256]{4,3,2,1,0:T(8,128)(2,1)S(1)}, u32[]{:S(2)}, u32[]{:S(2)}) collective-permute-start(bf16[4,2,2,16,256]{4,3,2,1,0:T(8,128)(2,1)S(1)} %get-tuple-element.37), channel_id=1, source_target_pairs={{0,6},{1,7},{2,4},{3,5},{4,2},{5,3},{6,0},{7,1},{8,14},{9,15},{10,... | collective-permute-start | bytes 393224 | tf_op jit(solution)/shard_map/ppermute | solution.py:186
  40.6 5.0 %copy-start.4 = (bf16[2,2,256,256]{3,2,1,0:T(8,128)(2,1)S(1)}, bf16[2,2,256,256]{3,2,1,0:T(8,128)(2,1)}, u32[]{:S(2)}) copy-start(bf16[2,2,256,256]{3,2,1,0:T(8,128)(2,1)} %get-tuple-element.30) | copy-start | bytes 1572868
  40.7 6.9 %collective-permute-start.9 = (bf16[2,2,2,16,256]{4,3,2,1,0:T(8,128)(2,1)S(1)}, bf16[2,2,2,16,256]{4,3,2,1,0:T(8,128)(2,1)S(1)}, u32[]{:S(2)}, u32[]{:S(2)}) collective-permute-start(bf16[2,2,2,16,256]{4,3,2,1,0:T(8,128)(2,1)S(1)} %slice.157), channel_id=1, source_target_pairs={{0,8},{1,9},{2,10},{3,11},{4,12},{5,13},{6,14},{7,15},{8,0},{9,1},... | collective-permute-start | bytes 196616 | tf_op jit(solution)/shard_map/ppermute | solution.py:186
  44.0 3.6 %collective-permute-start.11 = (bf16[3,2]{1,0:T(4,128)(2,1)S(1)}, bf16[3,2]{1,0:T(4,128)(2,1)S(1)}, u32[]{:S(2)}, u32[]{:S(2)}) collective-permute-start(bf16[3,2]{1,0:T(4,128)(2,1)S(1)} %pad_maximum_fusion.2), channel_id=1, source_target_pairs={{0,16},{16,0},{1,17},{17,1},{2,18},{18,2},{3,19},{19,3},{4,20},{20... | collective-permute-start | bytes 44 | tf_op jit(solution)/shard_map/ppermute | solution.py:171
  48.3 5.0 %collective-permute-start.10 = (bf16[2,128,256]{2,1,0:T(8,128)(2,1)S(1)}, bf16[2,128,256]{2,1,0:T(8,128)(2,1)S(1)}, u32[]{:S(2)}, u32[]{:S(2)}) collective-permute-start(bf16[2,128,256]{2,1,0:T(8,128)(2,1)S(1)} %dynamic-slice_convert_fusion), channel_id=1, source_target_pairs={{0,16},{16,0},{1,17},{17,1},{2,18},{18,2},{3,19},{19,3},{4,20},{20... | collective-permute-start | bytes 393224 | tf_op jit(solution)/shard_map/ppermute | solution.py:209

commit v16 on v15

--- a/solution.py
+++ b/solution.py
@@ -192,24 +192,29 @@
     proj_grad = proj_grad.at[:, :, :OVL].add(add_top)
     proj_grad = proj_grad.at[:, :, pixels - OVL :].add(add_bottom)
     proj_half = proj_grad.astype(jnp.bfloat16)
-    upward = jnp.einsum(
-        "tai,ktal->ktil", slice_rows, proj_half, preferred_element_type=jnp.float32
-    ).astype(jnp.bfloat16)
-    partial_grad = -jnp.einsum(
-        "ktil,tlj->kij", upward, slice_cols, preferred_element_type=jnp.float32
-    )
     if tilt_groups != 2:
+        upward = jnp.einsum(
+            "tai,ktal->ktil", slice_rows, proj_half, preferred_element_type=jnp.float32
+        ).astype(jnp.bfloat16)
+        partial_grad = -jnp.einsum(
+            "ktil,tlj->kij", upward, slice_cols, preferred_element_type=jnp.float32
+        )
         scores = scale * lax.psum(score_part, "tilt")
         section_grad = lax.psum_scatter(partial_grad, "tilt", scatter_dimension=1, tiled=True)
         return (section_grad, scores)
-    half = pixels // 2
+
+    def grad_rows(start):
+        rows_weight = lax.dynamic_slice_in_dim(slice_rows, start, pixels // 2, axis=2)
+        upward = jnp.einsum(
+            "tai,ktal->ktil", rows_weight, proj_half, preferred_element_type=jnp.float32
+        ).astype(jnp.bfloat16)
+        return -jnp.einsum("ktil,tlj->kij", upward, slice_cols, preferred_element_type=jnp.float32)
+
     side = lax.axis_index("tilt")
-    kept = lax.dynamic_slice_in_dim(partial_grad, side * half, half, axis=1)
-    given = lax.dynamic_slice_in_dim(partial_grad, (1 - side) * half, half, axis=1)
-    given = lax.ppermute(given.astype(jnp.bfloat16), "tilt", [(0, 1), (1, 0)])
-    section_grad = kept + given.astype(jnp.float32)
+    given = grad_rows((1 - side) * (pixels // 2)).astype(jnp.bfloat16)
+    given = lax.ppermute(given, "tilt", [(0, 1), (1, 0)])
+    section_grad = grad_rows(side * (pixels // 2)) + given.astype(jnp.float32)
     return (section_grad, scores)
-
 
 def solution(mesh):
     in_specs = (

time: 54.3 us -> 54.6 us (level)
  matrix products: 2.12 us -> 3.16 us
  other arithmetic: 3.73 us -> 3 us
    dot_general x1 -> x2, matrix products: 0.54 us -> 1.58 us  [grad_rows(): jnp.einsum('ktil,tlj->kij', upward, slice_cols, preferred_element_type=jn...]
    add x1 -> x0, other arithmetic: 0.73 us -> none  [on_device(): section_grad = kept + given.astype(jnp.float32)]
where the time goes in v16:
time: 54.6 us; the launch traced here: 54.3 us
  waiting for transfers between devices  22.2 us (41%)
  starting transfers between devices  17.9 us (33%)
  Pallas kernels  5.42 us (10%)
  matrix products  3.16 us (6%)
  other arithmetic  3 us (5%)
  local copies, waits for them, and re-layouts  1.82 us (3%)
  between operations  0.81 us (1%)
    ppermute x4, waiting for transfers between devices, on_device(): pieces.append(lax.ppermute(edges_all, 'dom', pairs))  8.84 us
    ppermute x4, starting transfers between devices, on_device(): pieces.append(lax.ppermute(edges_all, 'dom', pairs))  7.65 us
    ppermute x4, starting transfers between devices, on_device(): kept = kept + lax.ppermute(given, 'dom', pairs).astype(jnp.float32)  6.8 us
    ppermute x4, waiting for transfers between devices, on_device(): kept = kept + lax.ppermute(given, 'dom', pairs).astype(jnp.float32)  5.46 us
    pallas_call x1, Pallas kernels, middle(): pl.pallas_call(middle_kernel, grid=(tilt_count,), in_specs=[smem, smem, s...  5.42 us
    ppermute x1, waiting for transfers between devices, on_device(): given = lax.ppermute(given, 'tilt', [(0, 1), (1, 0)])  2.92 us
    ppermute x1, waiting for transfers between devices, on_device(): parts = lax.ppermute(parts, 'tilt', [(0, 1), (1, 0)]).astype(jnp.float32)  1.95 us
    ppermute x1, waiting for transfers between devices, on_device(): lax.ppermute(edges_all, 'dom', [(i, i ^ 1) for i in range(peer_count)])  1.9 us
  transfers between devices with their start and end apart: 12, of which 10 were waited for; matrix products, arithmetic and copies ran while one was open for 3% of the time, Pallas kernels for 0%

profile of v16, /device:TPU:0, one launch (start us, length us, event | category | flops | bytes accessed | tf_op | source)
XLA Modules:
  0.0 54.3 jit_solution(5257352864684224710)
XLA Ops:
  0.7 0.9 %copy-done = bf16[2,256,256]{2,1,0:T(8,128)(2,1)S(1)} copy-done((bf16[2,256,256]{2,1,0:T(8,128)(2,1)S(1)}, bf16[2,256,256]{2,1,0:T(8,128)(2,1)}, u32[]{:S(2)}) %copy-start) | copy-done | bytes 262168
  1.6 1.3 %fusion = bf16[2,2,256,256]{3,2,0,1:T(8,128)(2,1)S(1)} fusion(bf16[2,256,256]{2,1,0:T(8,128)(2,1)S(1)} %copy-done, bf16[2,256,256]{2,1,0:T(8,128)(2,1)} %param.13), kind=kOutput, calls=%fused_computation.2 | convolution fusion | flops 134479872 | bytes 1048576 | tf_op jit(solution)/shard_map/kij,tlj->ktil/dot_general | solution.py:140
  3.2 4.1 %collective-permute-start = (bf16[2,2,2,16,256]{4,3,2,1,0:T(8,128)(2,1)S(1)}, bf16[2,2,2,16,256]{4,3,2,1,0:T(8,128)(2,1)S(1)}, u32[]{:S(2)}, u32[]{:S(2)}) collective-permute-start(bf16[2,2,2,16,256]{4,3,2,1,0:T(8,128)(2,1)S(1)} %get-tuple-element.41), channel_id=1, source_target_pairs={{0,8},{1,9},{2,10},{3,11},{4,12},{5,13},{6,14},{7,15},{8,0},{9,1},... | collective-permute-start | bytes 196616 | tf_op jit(solution)/shard_map/ppermute | solution.py:154
  7.3 3.6 %collective-permute-done = bf16[2,2,2,16,256]{4,3,2,1,0:T(8,128)(2,1)S(1)} collective-permute-done((bf16[2,2,2,16,256]{4,3,2,1,0:T(8,128)(2,1)S(1)}, bf16[2,2,2,16,256]{4,3,2,1,0:T(8,128)(2,1)S(1)}, u32[]{:S(2)}, u32[]{:S(2)}) %collective-permute-start) | collective-permute-done | bytes 65568 | tf_op jit(solution)/shard_map/ppermute | solution.py:154
  11.6 1.5 %collective-permute-start.2 = (bf16[4,2,2,16,256]{4,3,2,1,0:T(8,128)(2,1)S(1)}, bf16[4,2,2,16,256]{4,3,2,1,0:T(8,128)(2,1)S(1)}, u32[]{:S(2)}, u32[]{:S(2)}) collective-permute-start(bf16[4,2,2,16,256]{4,3,2,1,0:T(8,128)(2,1)S(1)} %pad_maximum_fusion), channel_id=1, source_target_pairs={{0,2},{1,3},{2,0},{3,1},{4,6},{5,7},{6,4},{7,5},{8,10},{9,11},{10,... | collective-permute-start | bytes 393224 | tf_op jit(solution)/shard_map/ppermute | solution.py:154
  13.1 1.4 %collective-permute-start.3 = (bf16[4,2,2,16,256]{4,3,2,1,0:T(8,128)(2,1)S(1)}, bf16[4,2,2,16,256]{4,3,2,1,0:T(8,128)(2,1)S(1)}, u32[]{:S(2)}, u32[]{:S(2)}) collective-permute-start(bf16[4,2,2,16,256]{4,3,2,1,0:T(8,128)(2,1)S(1)} %pad_maximum_fusion), channel_id=1, source_target_pairs={{0,6},{1,7},{2,4},{3,5},{4,2},{5,3},{6,0},{7,1},{8,14},{9,15},{10,... | collective-permute-start | bytes 393224 | tf_op jit(solution)/shard_map/ppermute | solution.py:154
  14.6 2.8 %collective-permute-done.1 = bf16[4,2,2,16,256]{4,3,2,1,0:T(8,128)(2,1)S(1)} collective-permute-done((bf16[4,2,2,16,256]{4,3,2,1,0:T(8,128)(2,1)S(1)}, bf16[4,2,2,16,256]{4,3,2,1,0:T(8,128)(2,1)S(1)}, u32[]{:S(2)}, u32[]{:S(2)}) %collective-permute-start.1) | collective-permute-done | bytes 131104 | tf_op jit(solution)/shard_map/ppermute | solution.py:154
  18.2 1.6 %collective-permute-done.3 = bf16[4,2,2,16,256]{4,3,2,1,0:T(8,128)(2,1)S(1)} collective-permute-done((bf16[4,2,2,16,256]{4,3,2,1,0:T(8,128)(2,1)S(1)}, bf16[4,2,2,16,256]{4,3,2,1,0:T(8,128)(2,1)S(1)}, u32[]{:S(2)}, u32[]{:S(2)}) %collective-permute-start.3) | collective-permute-done | bytes 131104 | tf_op jit(solution)/shard_map/ppermute | solution.py:154
  19.9 1.9 %collective-permute-done.4.high_ref = bf16[16,2,2,16,256]{4,3,2,1,0:T(8,128)(2,1)S(1)} collective-permute-done((bf16[16,2,2,16,256]{4,3,2,1,0:T(8,128)(2,1)S(1)}, bf16[16,2,2,16,256]{4,3,2,1,0:T(8,128)(2,1)S(1)}, u32[]{:S(2)}, u32[]{:S(2)}) %collective-permute-start.4) | collective-permute-done | bytes 524320 | tf_op jit(solution)/shard_map/ppermute | solution.py:156
  22.6 5.4 %shard_map.104 = (bf16[2,2,256,256]{3,2,1,0:T(8,128)(2,1)}, f32[2,2,8,128]{3,2,1,0:T(8,128)}, f32[16,2,2,16,256]{4,3,2,1,0:T(8,128)}, bf16[16,2,2,16,256]{4,3,2,1,0:T(8,128)(2,1)}) custom-call(s32[2,2,8]{2,1,0:T(2,128)} %owner_ref.1, s32[2,16]{1,0:T(2,128)} %local_ref.1, s32[2,16]{1,0:T(2,128)} %side_ref.1, f32[2,16]{1,0:T(2,128)} %weight_ref.1, ...), custom_call_target="tpu_custom_call" | custom-call | flops 536870912 | bytes 4456448 | tf_op jit(solution)/shard_map/pallas_call | solution.py:83
  28.2 0.8 %slice_reduce_fusion = f32[2]{0:T(128)S(1)} fusion(f32[2,2,8,128]{3,2,1,0:T(8,128)} %get-tuple-element.33), kind=kLoop, calls=%fused_computation.49 | loop fusion | flops 2 | bytes 24 | tf_op jit(solution)/shard_map/reduce_sum | solution.py:162
  29.0 1.2 %collective-permute-done.5 = bf16[16,2,2,16,256]{4,3,2,1,0:T(8,128)(2,1)S(1)} collective-permute-done((bf16[16,2,2,16,256]{4,3,2,1,0:T(8,128)(2,1)}, bf16[16,2,2,16,256]{4,3,2,1,0:T(8,128)(2,1)S(1)}, u32[]{:S(2)}, u32[]{:S(2)}) %collective-permute-start.5) | collective-permute-done | bytes 524320 | tf_op jit(solution)/shard_map/ppermute | solution.py:175
  30.1 1.4 %fusion.45 = (bf16[16,2,2,16,256]{4,3,2,1,0:T(8,128)(2,1)S(1)}, f32[16,2,2,16,256]{4,3,2,1,0:T(8,128)S(1)}) fusion(f32[16,2,2,16,256]{4,3,2,1,0:T(8,128)} %get-tuple-element.31, bf16[16,2,2,16,256]{4,3,2,1,0:T(8,128)(2,1)S(1)} %collective-permute-done.5), kind=kLoop, calls=%fused_computation.59 | loop fusion | flops 786432 | bytes 3145728 | tf_op jit(solution)/shard_map/convert.3
  31.6 0.9 %collective-permute-start.6 = (bf16[4,2,2,16,256]{4,3,2,1,0:T(8,128)(2,1)S(1)}, bf16[4,2,2,16,256]{4,3,2,1,0:T(8,128)(2,1)S(1)}, u32[]{:S(2)}, u32[]{:S(2)}) collective-permute-start(bf16[4,2,2,16,256]{4,3,2,1,0:T(8,128)(2,1)S(1)} %get-tuple-element.36), channel_id=1, source_target_pairs={{0,4},{1,5},{2,6},{3,7},{4,0},{5,1},{6,2},{7,3},{8,12},{9,13},{10,... | collective-permute-start | bytes 393224 | tf_op jit(solution)/shard_map/ppermute | solution.py:186
  32.6 1.0 %collective-permute-start.7 = (bf16[4,2,2,16,256]{4,3,2,1,0:T(8,128)(2,1)S(1)}, bf16[4,2,2,16,256]{4,3,2,1,0:T(8,128)(2,1)S(1)}, u32[]{:S(2)}, u32[]{:S(2)}) collective-permute-start(bf16[4,2,2,16,256]{4,3,2,1,0:T(8,128)(2,1)S(1)} %get-tuple-element.38), channel_id=1, source_target_pairs={{0,2},{1,3},{2,0},{3,1},{4,6},{5,7},{6,4},{7,5},{8,10},{9,11},{10,... | collective-permute-start | bytes 393224 | tf_op jit(solution)/shard_map/ppermute | solution.py:186
  33.6 1.6 %collective-permute-start.8 = (bf16[4,2,2,16,256]{4,3,2,1,0:T(8,128)(2,1)S(1)}, bf16[4,2,2,16,256]{4,3,2,1,0:T(8,128)(2,1)S(1)}, u32[]{:S(2)}, u32[]{:S(2)}) collective-permute-start(bf16[4,2,2,16,256]{4,3,2,1,0:T(8,128)(2,1)S(1)} %get-tuple-element.37), channel_id=1, source_target_pairs={{0,6},{1,7},{2,4},{3,5},{4,2},{5,3},{6,0},{7,1},{8,14},{9,15},{10,... | collective-permute-start | bytes 393224 | tf_op jit(solution)/shard_map/ppermute | solution.py:186
  35.2 2.8 %collective-permute-done.6 = bf16[4,2,2,16,256]{4,3,2,1,0:T(8,128)(2,1)S(1)} collective-permute-done((bf16[4,2,2,16,256]{4,3,2,1,0:T(8,128)(2,1)S(1)}, bf16[4,2,2,16,256]{4,3,2,1,0:T(8,128)(2,1)S(1)}, u32[]{:S(2)}, u32[]{:S(2)}) %collective-permute-start.6) | collective-permute-done | bytes 131104 | tf_op jit(solution)/shard_map/ppermute | solution.py:186
  38.0 2.6 %collective-permute-done.7 = bf16[4,2,2,16,256]{4,3,2,1,0:T(8,128)(2,1)S(1)} collective-permute-done((bf16[4,2,2,16,256]{4,3,2,1,0:T(8,128)(2,1)S(1)}, bf16[4,2,2,16,256]{4,3,2,1,0:T(8,128)(2,1)S(1)}, u32[]{:S(2)}, u32[]{:S(2)}) %collective-permute-start.7) | collective-permute-done | bytes 131104 | tf_op jit(solution)/shard_map/ppermute | solution.py:186
  40.7 3.2 %collective-permute-start.9 = (bf16[2,2,2,16,256]{4,3,2,1,0:T(8,128)(2,1)S(1)}, bf16[2,2,2,16,256]{4,3,2,1,0:T(8,128)(2,1)S(1)}, u32[]{:S(2)}, u32[]{:S(2)}) collective-permute-start(bf16[2,2,2,16,256]{4,3,2,1,0:T(8,128)(2,1)S(1)} %slice.157), channel_id=1, source_target_pairs={{0,8},{1,9},{2,10},{3,11},{4,12},{5,13},{6,14},{7,15},{8,0},{9,1},... | collective-permute-start | bytes 196616 | tf_op jit(solution)/shard_map/ppermute | solution.py:186
  44.0 1.6 %collective-permute-start.11 = (bf16[3,2]{1,0:T(4,128)(2,1)S(1)}, bf16[3,2]{1,0:T(4,128)(2,1)S(1)}, u32[]{:S(2)}, u32[]{:S(2)}) collective-permute-start(bf16[3,2]{1,0:T(4,128)(2,1)S(1)} %pad_maximum_fusion.2), channel_id=1, source_target_pairs={{0,16},{16,0},{1,17},{17,1},{2,18},{18,2},{3,19},{19,3},{4,20},{20... | collective-permute-start | bytes 44 | tf_op jit(solution)/shard_map/ppermute | solution.py:171
  45.7 1.9 %collective-permute-done.11 = bf16[3,2]{1,0:T(4,128)(2,1)S(1)} collective-permute-done((bf16[3,2]{1,0:T(4,128)(2,1)S(1)}, bf16[3,2]{1,0:T(4,128)(2,1)S(1)}, u32[]{:S(2)}, u32[]{:S(2)}) %collective-permute-start.11) | collective-permute-done | bytes 44 | tf_op jit(solution)/shard_map/ppermute | solution.py:171
  48.1 1.6 %collective-permute-start.10 = (bf16[2,128,256]{2,1,0:T(8,128)(2,1)S(1)}, bf16[2,128,256]{2,1,0:T(8,128)(2,1)S(1)}, u32[]{:S(2)}, u32[]{:S(2)}) collective-permute-start(bf16[2,128,256]{2,1,0:T(8,128)(2,1)S(1)} %fusion.10), channel_id=1, source_target_pairs={{0,16},{16,0},{1,17},{17,1},{2,18},{18,2},{3,19},{19,3},{4,20},{20... | collective-permute-start | bytes 393224 | tf_op jit(solution)/shard_map/ppermute | solution.py:215
  50.2 2.9 %collective-permute-done.10 = bf16[2,128,256]{2,1,0:T(8,128)(2,1)S(1)} collective-permute-done((bf16[2,128,256]{2,1,0:T(8,128)(2,1)S(1)}, bf16[2,128,256]{2,1,0:T(8,128)(2,1)S(1)}, u32[]{:S(2)}, u32[]{:S(2)}) %collective-permute-start.10) | collective-permute-done | bytes 131104 | tf_op jit(solution)/shard_map/ppermute | solution.py:215
  53.2 1.1 %convert_add_fusion.1 = f32[2,128,256]{2,1,0:T(8,128)} fusion(bf16[2,128,256]{2,1,0:T(8,128)(2,1)S(1)} %collective-permute-done.10, bf16[2,256,256]{2,1,0:T(8,128)(2,1)S(1)} %copy-done, f32[2,2,256,256]{3,2,1,0:T(8,128)S(1)} %fusion.36, bf16[2,256,256]{2,1,0:T(8,128)(2,1)S(1)} %copy-done.2, s32[]{:T(128)S(6)} %select_n.6), kind=kOutput, calls=%fused_computation.25 | convolution fusion | flops 134807552 | bytes 1835012 | tf_op jit(solution)/shard_map/ktil,tlj->kij/dot_general | solution.py:211
  (38 shorter events, 4.0 us)
Async XLA Ops:
  0.6 1.0 %copy-start = (bf16[2,256,256]{2,1,0:T(8,128)(2,1)S(1)}, bf16[2,256,256]{2,1,0:T(8,128)(2,1)}, u32[]{:S(2)}) copy-start(bf16[2,256,256]{2,1,0:T(8,128)(2,1)} %param.16) | copy-start | bytes 786436
  0.6 2.2 %copy-start.2 = (bf16[2,256,256]{2,1,0:T(8,128)(2,1)S(1)}, bf16[2,256,256]{2,1,0:T(8,128)(2,1)}, u32[]{:S(2)}) copy-start(bf16[2,256,256]{2,1,0:T(8,128)(2,1)} %param.15) | copy-start | bytes 786436
  3.2 15.0 %copy-start.1 = (bf16[2,2,256,256]{3,2,1,0:T(8,128)(2,1)}, bf16[2,2,256,256]{3,2,1,0:T(8,128)(2,1)S(1)}, u32[]{:S(2)}) copy-start(bf16[2,2,256,256]{3,2,1,0:T(8,128)(2,1)S(1)} %fusion.1.proj_ref) | copy-start | bytes 1572868
  3.2 7.7 %collective-permute-start = (bf16[2,2,2,16,256]{4,3,2,1,0:T(8,128)(2,1)S(1)}, bf16[2,2,2,16,256]{4,3,2,1,0:T(8,128)(2,1)S(1)}, u32[]{:S(2)}, u32[]{:S(2)}) collective-permute-start(bf16[2,2,2,16,256]{4,3,2,1,0:T(8,128)(2,1)S(1)} %get-tuple-element.41), channel_id=1, source_target_pairs={{0,8},{1,9},{2,10},{3,11},{4,12},{5,13},{6,14},{7,15},{8,0},{9,1},... | collective-permute-start | bytes 196616 | tf_op jit(solution)/shard_map/ppermute | solution.py:154
  11.0 6.4 %collective-permute-start.1 = (bf16[4,2,2,16,256]{4,3,2,1,0:T(8,128)(2,1)S(1)}, bf16[4,2,2,16,256]{4,3,2,1,0:T(8,128)(2,1)S(1)}, u32[]{:S(2)}, u32[]{:S(2)}) collective-permute-start(bf16[4,2,2,16,256]{4,3,2,1,0:T(8,128)(2,1)S(1)} %pad_maximum_fusion), channel_id=1, source_target_pairs={{0,4},{1,5},{2,6},{3,7},{4,0},{5,1},{6,2},{7,3},{8,12},{9,13},{10,... | collective-permute-start | bytes 393224 | tf_op jit(solution)/shard_map/ppermute | solution.py:154
  11.6 6.5 %collective-permute-start.2 = (bf16[4,2,2,16,256]{4,3,2,1,0:T(8,128)(2,1)S(1)}, bf16[4,2,2,16,256]{4,3,2,1,0:T(8,128)(2,1)S(1)}, u32[]{:S(2)}, u32[]{:S(2)}) collective-permute-start(bf16[4,2,2,16,256]{4,3,2,1,0:T(8,128)(2,1)S(1)} %pad_maximum_fusion), channel_id=1, source_target_pairs={{0,2},{1,3},{2,0},{3,1},{4,6},{5,7},{6,4},{7,5},{8,10},{9,11},{10,... | collective-permute-start | bytes 393224 | tf_op jit(solution)/shard_map/ppermute | solution.py:154
  13.1 6.7 %collective-permute-start.3 = (bf16[4,2,2,16,256]{4,3,2,1,0:T(8,128)(2,1)S(1)}, bf16[4,2,2,16,256]{4,3,2,1,0:T(8,128)(2,1)S(1)}, u32[]{:S(2)}, u32[]{:S(2)}) collective-permute-start(bf16[4,2,2,16,256]{4,3,2,1,0:T(8,128)(2,1)S(1)} %pad_maximum_fusion), channel_id=1, source_target_pairs={{0,6},{1,7},{2,4},{3,5},{4,2},{5,3},{6,0},{7,1},{8,14},{9,15},{10,... | collective-permute-start | bytes 393224 | tf_op jit(solution)/shard_map/ppermute | solution.py:154
  19.8 2.0 %copy-start.3 = (bf16[16,2,2,16,256]{4,3,2,1,0:T(8,128)(2,1)}, bf16[16,2,2,16,256]{4,3,2,1,0:T(8,128)(2,1)S(1)}, u32[]{:S(2)}) copy-start(bf16[16,2,2,16,256]{4,3,2,1,0:T(8,128)(2,1)S(1)} %constant_dynamic-update-slice_fusion.low_ref) | copy-start | bytes 1572868
  19.8 2.0 %collective-permute-start.4 = (bf16[16,2,2,16,256]{4,3,2,1,0:T(8,128)(2,1)S(1)}, bf16[16,2,2,16,256]{4,3,2,1,0:T(8,128)(2,1)S(1)}, u32[]{:S(2)}, u32[]{:S(2)}) collective-permute-start(bf16[16,2,2,16,256]{4,3,2,1,0:T(8,128)(2,1)S(1)} %constant_dynamic-update-slice_fusion.low_ref), channel_id=1, source_target_pairs={{0,1},{1,0},{2,3},{3,2},{4,5},{5,4},{6,7},{7,6},{8,9},{9,8},{10,11... | collective-permute-start | bytes 1572872 | tf_op jit(solution)/shard_map/ppermute | solution.py:156
  21.8 0.8 %copy-start.5 = (bf16[16,2,2,16,256]{4,3,2,1,0:T(8,128)(2,1)}, bf16[16,2,2,16,256]{4,3,2,1,0:T(8,128)(2,1)S(1)}, u32[]{:S(2)}) copy-start(bf16[16,2,2,16,256]{4,3,2,1,0:T(8,128)(2,1)S(1)} %collective-permute-done.4.high_ref) | copy-start | bytes 1572868
  28.0 2.2 %collective-permute-start.5 = (bf16[16,2,2,16,256]{4,3,2,1,0:T(8,128)(2,1)}, bf16[16,2,2,16,256]{4,3,2,1,0:T(8,128)(2,1)S(1)}, u32[]{:S(2)}, u32[]{:S(2)}) collective-permute-start(bf16[16,2,2,16,256]{4,3,2,1,0:T(8,128)(2,1)} %get-tuple-element.32), channel_id=1, source_target_pairs={{0,1},{1,0},{2,3},{3,2},{4,5},{5,4},{6,7},{7,6},{8,9},{9,8},{10,11... | collective-permute-start | bytes 1572872 | tf_op jit(solution)/shard_map/ppermute | solution.py:175
  31.6 6.4 %collective-permute-start.6 = (bf16[4,2,2,16,256]{4,3,2,1,0:T(8,128)(2,1)S(1)}, bf16[4,2,2,16,256]{4,3,2,1,0:T(8,128)(2,1)S(1)}, u32[]{:S(2)}, u32[]{:S(2)}) collective-permute-start(bf16[4,2,2,16,256]{4,3,2,1,0:T(8,128)(2,1)S(1)} %get-tuple-element.36), channel_id=1, source_target_pairs={{0,4},{1,5},{2,6},{3,7},{4,0},{5,1},{6,2},{7,3},{8,12},{9,13},{10,... | collective-permute-start | bytes 393224 | tf_op jit(solution)/shard_map/ppermute | solution.py:186
  32.6 8.1 %collective-permute-start.7 = (bf16[4,2,2,16,256]{4,3,2,1,0:T(8,128)(2,1)S(1)}, bf16[4,2,2,16,256]{4,3,2,1,0:T(8,128)(2,1)S(1)}, u32[]{:S(2)}, u32[]{:S(2)}) collective-permute-start(bf16[4,2,2,16,256]{4,3,2,1,0:T(8,128)(2,1)S(1)} %get-tuple-element.38), channel_id=1, source_target_pairs={{0,2},{1,3},{2,0},{3,1},{4,6},{5,7},{6,4},{7,5},{8,10},{9,11},{10,... | collective-permute-start | bytes 393224 | tf_op jit(solution)/shard_map/ppermute | solution.py:186
  33.6 7.0 %collective-permute-start.8 = (bf16[4,2,2,16,256]{4,3,2,1,0:T(8,128)(2,1)S(1)}, bf16[4,2,2,16,256]{4,3,2,1,0:T(8,128)(2,1)S(1)}, u32[]{:S(2)}, u32[]{:S(2)}) collective-permute-start(bf16[4,2,2,16,256]{4,3,2,1,0:T(8,128)(2,1)S(1)} %get-tuple-element.37), channel_id=1, source_target_pairs={{0,6},{1,7},{2,4},{3,5},{4,2},{5,3},{6,0},{7,1},{8,14},{9,15},{10,... | collective-permute-start | bytes 393224 | tf_op jit(solution)/shard_map/ppermute | solution.py:186
  40.6 4.9 %copy-start.4 = (bf16[2,2,256,256]{3,2,1,0:T(8,128)(2,1)S(1)}, bf16[2,2,256,256]{3,2,1,0:T(8,128)(2,1)}, u32[]{:S(2)}) copy-start(bf16[2,2,256,256]{3,2,1,0:T(8,128)(2,1)} %get-tuple-element.30) | copy-start | bytes 1572868
  40.7 6.9 %collective-permute-start.9 = (bf16[2,2,2,16,256]{4,3,2,1,0:T(8,128)(2,1)S(1)}, bf16[2,2,2,16,256]{4,3,2,1,0:T(8,128)(2,1)S(1)}, u32[]{:S(2)}, u32[]{:S(2)}) collective-permute-start(bf16[2,2,2,16,256]{4,3,2,1,0:T(8,128)(2,1)S(1)} %slice.157), channel_id=1, source_target_pairs={{0,8},{1,9},{2,10},{3,11},{4,12},{5,13},{6,14},{7,15},{8,0},{9,1},... | collective-permute-start | bytes 196616 | tf_op jit(solution)/shard_map/ppermute | solution.py:186
  44.0 3.6 %collective-permute-start.11 = (bf16[3,2]{1,0:T(4,128)(2,1)S(1)}, bf16[3,2]{1,0:T(4,128)(2,1)S(1)}, u32[]{:S(2)}, u32[]{:S(2)}) collective-permute-start(bf16[3,2]{1,0:T(4,128)(2,1)S(1)} %pad_maximum_fusion.2), channel_id=1, source_target_pairs={{0,16},{16,0},{1,17},{17,1},{2,18},{18,2},{3,19},{19,3},{4,20},{20... | collective-permute-start | bytes 44 | tf_op jit(solution)/shard_map/ppermute | solution.py:171
  48.1 5.0 %collective-permute-start.10 = (bf16[2,128,256]{2,1,0:T(8,128)(2,1)S(1)}, bf16[2,128,256]{2,1,0:T(8,128)(2,1)S(1)}, u32[]{:S(2)}, u32[]{:S(2)}) collective-permute-start(bf16[2,128,256]{2,1,0:T(8,128)(2,1)S(1)} %fusion.10), channel_id=1, source_target_pairs={{0,16},{16,0},{1,17},{17,1},{2,18},{18,2},{3,19},{19,3},{4,20},{20... | collective-permute-start | bytes 393224 | tf_op jit(solution)/shard_map/ppermute | solution.py:215

commit v17 on v15

--- a/solution.py
+++ b/solution.py
@@ -19,6 +19,7 @@
     peer_count = lax.axis_size("dom")
     steps = peer_count.bit_length() - 1
     me = lax.axis_index("dom")
+    tilt = pl.program_id(0)
     ctf = ctf_ref[0]
     ctf_t = ctf.T
     zero = jnp.zeros((OVL, pixels), jnp.float32)
@@ -36,8 +37,8 @@
             q = places[k][j]
             s = side_ref[k, j]
             w = weight_ref[k, j]
-            low_band = low_ref[jnp.minimum(q, half - 1), s, 0]
-            high_band = high_ref[jnp.maximum(q - half, 0), s, 0]
+            low_band = low_ref[jnp.minimum(q, half - 1), s, tilt]
+            high_band = high_ref[jnp.maximum(q - half, 0), s, tilt]
             band = jnp.where(q < half, low_band, high_band).astype(jnp.float32)
             lower = lower + jnp.where(s == 0, w, 0.0) * band
             upper = upper + jnp.where(s == 1, w, 0.0) * band
@@ -78,6 +79,7 @@
     tiles = pl.BlockSpec((own_count, 1, pixels, pixels), lambda t: (0, t, 0, 0))
     halves = pl.BlockSpec((half, 2, 1, OVL, pixels), lambda t: (0, 0, t, 0, 0))
     smem = pl.BlockSpec(memory_space=pltpu.SMEM)
+    whole = pl.BlockSpec(memory_space=pltpu.VMEM)
     flops = own_count * tilt_count * 8 * pixels**3
     moved = 2 * images.size * 3 + 10 * edges_low.size + 2 * ctf_filter.size
     return pl.pallas_call(
@@ -90,8 +92,8 @@
             smem,
             tiles,
             tiles,
-            halves,
-            halves,
+            whole,
+            whole,
             pl.BlockSpec((1, pixels, pixels), lambda t: (t, 0, 0)),
         ],
         out_specs=[

time: 54.3 us -> 54.5 us (level)
  no operation moved by 1% of the time
where the time goes in v17:
time: 54.5 us; the launch traced here: 54.2 us
  waiting for transfers between devices  22.2 us (41%)
  starting transfers between devices  17.9 us (33%)
  Pallas kernels  5.63 us (10%)
  other arithmetic  3.73 us (7%)
  matrix products  2.12 us (4%)
  local copies, waits for them, and re-layouts  1.85 us (3%)
  between operations  0.83 us (2%)
    ppermute x4, waiting for transfers between devices, on_device(): pieces.append(lax.ppermute(edges_all, 'dom', pairs))  8.84 us
    ppermute x4, starting transfers between devices, on_device(): pieces.append(lax.ppermute(edges_all, 'dom', pairs))  7.65 us
    ppermute x4, starting transfers between devices, on_device(): kept = kept + lax.ppermute(given, 'dom', pairs).astype(jnp.float32)  6.8 us
    pallas_call x1, Pallas kernels, middle(): pl.pallas_call(middle_kernel, grid=(tilt_count,), in_specs=[smem, smem, s...  5.63 us
    ppermute x4, waiting for transfers between devices, on_device(): kept = kept + lax.ppermute(given, 'dom', pairs).astype(jnp.float32)  5.46 us
    ppermute x1, waiting for transfers between devices, on_device(): given = lax.ppermute(given.astype(jnp.bfloat16), 'tilt', [(0, 1), (1, 0)])  2.92 us
    ppermute x1, waiting for transfers between devices, on_device(): parts = lax.ppermute(parts, 'tilt', [(0, 1), (1, 0)]).astype(jnp.float32)  1.94 us
    ppermute x1, waiting for transfers between devices, on_device(): lax.ppermute(edges_all, 'dom', [(i, i ^ 1) for i in range(peer_count)])  1.9 us
  transfers between devices with their start and end apart: 12, of which 10 were waited for; matrix products, arithmetic and copies ran while one was open for 3% of the time, Pallas kernels for 0%

profile of v17, /device:TPU:0, one launch (start us, length us, event | category | flops | bytes accessed | tf_op | source)
XLA Modules:
  0.0 54.2 jit_solution(16900684301493364249)
XLA Ops:
  0.7 0.9 %copy-done = bf16[2,256,256]{2,1,0:T(8,128)(2,1)S(1)} copy-done((bf16[2,256,256]{2,1,0:T(8,128)(2,1)S(1)}, bf16[2,256,256]{2,1,0:T(8,128)(2,1)}, u32[]{:S(2)}) %copy-start) | copy-done | bytes 262168
  1.6 1.3 %fusion = bf16[2,2,256,256]{3,2,0,1:T(8,128)(2,1)S(1)} fusion(bf16[2,256,256]{2,1,0:T(8,128)(2,1)S(1)} %copy-done, bf16[2,256,256]{2,1,0:T(8,128)(2,1)} %param.13), kind=kOutput, calls=%fused_computation.3 | convolution fusion | flops 134479872 | bytes 1048576 | tf_op jit(solution)/shard_map/kij,tlj->ktil/dot_general | solution.py:142
  3.2 4.1 %collective-permute-start = (bf16[2,2,2,16,256]{4,3,2,1,0:T(8,128)(2,1)S(1)}, bf16[2,2,2,16,256]{4,3,2,1,0:T(8,128)(2,1)S(1)}, u32[]{:S(2)}, u32[]{:S(2)}) collective-permute-start(bf16[2,2,2,16,256]{4,3,2,1,0:T(8,128)(2,1)S(1)} %get-tuple-element.41), channel_id=1, source_target_pairs={{0,8},{1,9},{2,10},{3,11},{4,12},{5,13},{6,14},{7,15},{8,0},{9,1},... | collective-permute-start | bytes 196616 | tf_op jit(solution)/shard_map/ppermute | solution.py:156
  7.3 3.6 %collective-permute-done = bf16[2,2,2,16,256]{4,3,2,1,0:T(8,128)(2,1)S(1)} collective-permute-done((bf16[2,2,2,16,256]{4,3,2,1,0:T(8,128)(2,1)S(1)}, bf16[2,2,2,16,256]{4,3,2,1,0:T(8,128)(2,1)S(1)}, u32[]{:S(2)}, u32[]{:S(2)}) %collective-permute-start) | collective-permute-done | bytes 65568 | tf_op jit(solution)/shard_map/ppermute | solution.py:156
  11.6 1.5 %collective-permute-start.2 = (bf16[4,2,2,16,256]{4,3,2,1,0:T(8,128)(2,1)S(1)}, bf16[4,2,2,16,256]{4,3,2,1,0:T(8,128)(2,1)S(1)}, u32[]{:S(2)}, u32[]{:S(2)}) collective-permute-start(bf16[4,2,2,16,256]{4,3,2,1,0:T(8,128)(2,1)S(1)} %pad_maximum_fusion), channel_id=1, source_target_pairs={{0,2},{1,3},{2,0},{3,1},{4,6},{5,7},{6,4},{7,5},{8,10},{9,11},{10,... | collective-permute-start | bytes 393224 | tf_op jit(solution)/shard_map/ppermute | solution.py:156
  13.1 1.4 %collective-permute-start.3 = (bf16[4,2,2,16,256]{4,3,2,1,0:T(8,128)(2,1)S(1)}, bf16[4,2,2,16,256]{4,3,2,1,0:T(8,128)(2,1)S(1)}, u32[]{:S(2)}, u32[]{:S(2)}) collective-permute-start(bf16[4,2,2,16,256]{4,3,2,1,0:T(8,128)(2,1)S(1)} %pad_maximum_fusion), channel_id=1, source_target_pairs={{0,6},{1,7},{2,4},{3,5},{4,2},{5,3},{6,0},{7,1},{8,14},{9,15},{10,... | collective-permute-start | bytes 393224 | tf_op jit(solution)/shard_map/ppermute | solution.py:156
  14.6 2.8 %collective-permute-done.1 = bf16[4,2,2,16,256]{4,3,2,1,0:T(8,128)(2,1)S(1)} collective-permute-done((bf16[4,2,2,16,256]{4,3,2,1,0:T(8,128)(2,1)S(1)}, bf16[4,2,2,16,256]{4,3,2,1,0:T(8,128)(2,1)S(1)}, u32[]{:S(2)}, u32[]{:S(2)}) %collective-permute-start.1) | collective-permute-done | bytes 131104 | tf_op jit(solution)/shard_map/ppermute | solution.py:156
  18.2 1.6 %collective-permute-done.3 = bf16[4,2,2,16,256]{4,3,2,1,0:T(8,128)(2,1)S(1)} collective-permute-done((bf16[4,2,2,16,256]{4,3,2,1,0:T(8,128)(2,1)S(1)}, bf16[4,2,2,16,256]{4,3,2,1,0:T(8,128)(2,1)S(1)}, u32[]{:S(2)}, u32[]{:S(2)}) %collective-permute-start.3) | collective-permute-done | bytes 131104 | tf_op jit(solution)/shard_map/ppermute | solution.py:156
  19.9 1.9 %collective-permute-done.4.high_ref = bf16[16,2,2,16,256]{4,3,2,1,0:T(8,128)(2,1)S(1)} collective-permute-done((bf16[16,2,2,16,256]{4,3,2,1,0:T(8,128)(2,1)S(1)}, bf16[16,2,2,16,256]{4,3,2,1,0:T(8,128)(2,1)S(1)}, u32[]{:S(2)}, u32[]{:S(2)}) %collective-permute-start.4) | collective-permute-done | bytes 524320 | tf_op jit(solution)/shard_map/ppermute | solution.py:158
  21.8 0.8 %copy-done.5 = bf16[16,2,2,16,256]{4,3,2,1,0:T(8,128)(2,1)} copy-done((bf16[16,2,2,16,256]{4,3,2,1,0:T(8,128)(2,1)}, bf16[16,2,2,16,256]{4,3,2,1,0:T(8,128)(2,1)S(1)}, u32[]{:S(2)}) %copy-start.5) | copy-done | bytes 524312
  22.6 5.6 %shard_map.104 = (bf16[2,2,256,256]{3,2,1,0:T(8,128)(2,1)}, f32[2,2,8,128]{3,2,1,0:T(8,128)}, f32[16,2,2,16,256]{4,3,2,1,0:T(8,128)}, bf16[16,2,2,16,256]{4,3,2,1,0:T(8,128)(2,1)}) custom-call(s32[2,2,8]{2,1,0:T(2,128)} %owner_ref.1, s32[2,16]{1,0:T(2,128)} %local_ref.1, s32[2,16]{1,0:T(2,128)} %side_ref.1, f32[2,16]{1,0:T(2,128)} %weight_ref.1, ...), custom_call_target="tpu_custom_call" | custom-call | flops 536870912 | bytes 4456448 | tf_op jit(solution)/shard_map/pallas_call | solution.py:85
  28.4 0.8 %slice_reduce_fusion = f32[2]{0:T(128)S(1)} fusion(f32[2,2,8,128]{3,2,1,0:T(8,128)} %get-tuple-element.33), kind=kLoop, calls=%fused_computation.38 | loop fusion | flops 2 | bytes 24 | tf_op jit(solution)/shard_map/reduce_sum | solution.py:164
  29.2 1.2 %collective-permute-done.5 = bf16[16,2,2,16,256]{4,3,2,1,0:T(8,128)(2,1)S(1)} collective-permute-done((bf16[16,2,2,16,256]{4,3,2,1,0:T(8,128)(2,1)}, bf16[16,2,2,16,256]{4,3,2,1,0:T(8,128)(2,1)S(1)}, u32[]{:S(2)}, u32[]{:S(2)}) %collective-permute-start.5) | collective-permute-done | bytes 524320 | tf_op jit(solution)/shard_map/ppermute | solution.py:177
  30.4 1.4 %fusion.21 = (bf16[16,2,2,16,256]{4,3,2,1,0:T(8,128)(2,1)S(1)}, f32[16,2,2,16,256]{4,3,2,1,0:T(8,128)S(1)}) fusion(f32[16,2,2,16,256]{4,3,2,1,0:T(8,128)} %get-tuple-element.31, bf16[16,2,2,16,256]{4,3,2,1,0:T(8,128)(2,1)S(1)} %collective-permute-done.5), kind=kLoop, calls=%fused_computation.46 | loop fusion | flops 786432 | bytes 3145728 | tf_op jit(solution)/shard_map/convert.3
  31.8 0.9 %collective-permute-start.6 = (bf16[4,2,2,16,256]{4,3,2,1,0:T(8,128)(2,1)S(1)}, bf16[4,2,2,16,256]{4,3,2,1,0:T(8,128)(2,1)S(1)}, u32[]{:S(2)}, u32[]{:S(2)}) collective-permute-start(bf16[4,2,2,16,256]{4,3,2,1,0:T(8,128)(2,1)S(1)} %get-tuple-element.36), channel_id=1, source_target_pairs={{0,4},{1,5},{2,6},{3,7},{4,0},{5,1},{6,2},{7,3},{8,12},{9,13},{10,... | collective-permute-start | bytes 393224 | tf_op jit(solution)/shard_map/ppermute | solution.py:188
  32.8 1.0 %collective-permute-start.7 = (bf16[4,2,2,16,256]{4,3,2,1,0:T(8,128)(2,1)S(1)}, bf16[4,2,2,16,256]{4,3,2,1,0:T(8,128)(2,1)S(1)}, u32[]{:S(2)}, u32[]{:S(2)}) collective-permute-start(bf16[4,2,2,16,256]{4,3,2,1,0:T(8,128)(2,1)S(1)} %get-tuple-element.38), channel_id=1, source_target_pairs={{0,2},{1,3},{2,0},{3,1},{4,6},{5,7},{6,4},{7,5},{8,10},{9,11},{10,... | collective-permute-start | bytes 393224 | tf_op jit(solution)/shard_map/ppermute | solution.py:188
  33.8 1.6 %collective-permute-start.8 = (bf16[4,2,2,16,256]{4,3,2,1,0:T(8,128)(2,1)S(1)}, bf16[4,2,2,16,256]{4,3,2,1,0:T(8,128)(2,1)S(1)}, u32[]{:S(2)}, u32[]{:S(2)}) collective-permute-start(bf16[4,2,2,16,256]{4,3,2,1,0:T(8,128)(2,1)S(1)} %get-tuple-element.37), channel_id=1, source_target_pairs={{0,6},{1,7},{2,4},{3,5},{4,2},{5,3},{6,0},{7,1},{8,14},{9,15},{10,... | collective-permute-start | bytes 393224 | tf_op jit(solution)/shard_map/ppermute | solution.py:188
  35.4 2.8 %collective-permute-done.6 = bf16[4,2,2,16,256]{4,3,2,1,0:T(8,128)(2,1)S(1)} collective-permute-done((bf16[4,2,2,16,256]{4,3,2,1,0:T(8,128)(2,1)S(1)}, bf16[4,2,2,16,256]{4,3,2,1,0:T(8,128)(2,1)S(1)}, u32[]{:S(2)}, u32[]{:S(2)}) %collective-permute-start.6) | collective-permute-done | bytes 131104 | tf_op jit(solution)/shard_map/ppermute | solution.py:188
  38.2 2.6 %collective-permute-done.7 = bf16[4,2,2,16,256]{4,3,2,1,0:T(8,128)(2,1)S(1)} collective-permute-done((bf16[4,2,2,16,256]{4,3,2,1,0:T(8,128)(2,1)S(1)}, bf16[4,2,2,16,256]{4,3,2,1,0:T(8,128)(2,1)S(1)}, u32[]{:S(2)}, u32[]{:S(2)}) %collective-permute-start.7) | collective-permute-done | bytes 131104 | tf_op jit(solution)/shard_map/ppermute | solution.py:188
  40.9 3.2 %collective-permute-start.9 = (bf16[2,2,2,16,256]{4,3,2,1,0:T(8,128)(2,1)S(1)}, bf16[2,2,2,16,256]{4,3,2,1,0:T(8,128)(2,1)S(1)}, u32[]{:S(2)}, u32[]{:S(2)}) collective-permute-start(bf16[2,2,2,16,256]{4,3,2,1,0:T(8,128)(2,1)S(1)} %slice.157), channel_id=1, source_target_pairs={{0,8},{1,9},{2,10},{3,11},{4,12},{5,13},{6,14},{7,15},{8,0},{9,1},... | collective-permute-start | bytes 196616 | tf_op jit(solution)/shard_map/ppermute | solution.py:188
  44.2 1.6 %collective-permute-start.11 = (bf16[3,2]{1,0:T(4,128)(2,1)S(1)}, bf16[3,2]{1,0:T(4,128)(2,1)S(1)}, u32[]{:S(2)}, u32[]{:S(2)}) collective-permute-start(bf16[3,2]{1,0:T(4,128)(2,1)S(1)} %pad_maximum_fusion.2), channel_id=1, source_target_pairs={{0,16},{16,0},{1,17},{17,1},{2,18},{18,2},{3,19},{19,3},{4,20},{20... | collective-permute-start | bytes 44 | tf_op jit(solution)/shard_map/ppermute | solution.py:173
  45.9 1.9 %collective-permute-done.11 = bf16[3,2]{1,0:T(4,128)(2,1)S(1)} collective-permute-done((bf16[3,2]{1,0:T(4,128)(2,1)S(1)}, bf16[3,2]{1,0:T(4,128)(2,1)S(1)}, u32[]{:S(2)}, u32[]{:S(2)}) %collective-permute-start.11) | collective-permute-done | bytes 44 | tf_op jit(solution)/shard_map/ppermute | solution.py:173
  48.5 1.6 %collective-permute-start.10 = (bf16[2,128,256]{2,1,0:T(8,128)(2,1)S(1)}, bf16[2,128,256]{2,1,0:T(8,128)(2,1)S(1)}, u32[]{:S(2)}, u32[]{:S(2)}) collective-permute-start(bf16[2,128,256]{2,1,0:T(8,128)(2,1)S(1)} %dynamic-slice_convert_fusion), channel_id=1, source_target_pairs={{0,16},{16,0},{1,17},{17,1},{2,18},{18,2},{3,19},{19,3},{4,20},{20... | collective-permute-start | bytes 393224 | tf_op jit(solution)/shard_map/ppermute | solution.py:211
  50.6 2.9 %collective-permute-done.10 = bf16[2,128,256]{2,1,0:T(8,128)(2,1)S(1)} collective-permute-done((bf16[2,128,256]{2,1,0:T(8,128)(2,1)S(1)}, bf16[2,128,256]{2,1,0:T(8,128)(2,1)S(1)}, u32[]{:S(2)}, u32[]{:S(2)}) %collective-permute-start.10) | collective-permute-done | bytes 131104 | tf_op jit(solution)/shard_map/ppermute | solution.py:211
  (39 shorter events, 4.1 us)
Async XLA Ops:
  0.6 1.0 %copy-start = (bf16[2,256,256]{2,1,0:T(8,128)(2,1)S(1)}, bf16[2,256,256]{2,1,0:T(8,128)(2,1)}, u32[]{:S(2)}) copy-start(bf16[2,256,256]{2,1,0:T(8,128)(2,1)} %param.16) | copy-start | bytes 786436
  0.6 2.2 %copy-start.2 = (bf16[2,256,256]{2,1,0:T(8,128)(2,1)S(1)}, bf16[2,256,256]{2,1,0:T(8,128)(2,1)}, u32[]{:S(2)}) copy-start(bf16[2,256,256]{2,1,0:T(8,128)(2,1)} %param.15) | copy-start | bytes 786436
  3.2 15.0 %copy-start.1 = (bf16[2,2,256,256]{3,2,1,0:T(8,128)(2,1)}, bf16[2,2,256,256]{3,2,1,0:T(8,128)(2,1)S(1)}, u32[]{:S(2)}) copy-start(bf16[2,2,256,256]{3,2,1,0:T(8,128)(2,1)S(1)} %fusion.2.proj_ref) | copy-start | bytes 1572868
  3.2 7.7 %collective-permute-start = (bf16[2,2,2,16,256]{4,3,2,1,0:T(8,128)(2,1)S(1)}, bf16[2,2,2,16,256]{4,3,2,1,0:T(8,128)(2,1)S(1)}, u32[]{:S(2)}, u32[]{:S(2)}) collective-permute-start(bf16[2,2,2,16,256]{4,3,2,1,0:T(8,128)(2,1)S(1)} %get-tuple-element.41), channel_id=1, source_target_pairs={{0,8},{1,9},{2,10},{3,11},{4,12},{5,13},{6,14},{7,15},{8,0},{9,1},... | collective-permute-start | bytes 196616 | tf_op jit(solution)/shard_map/ppermute | solution.py:156
  11.0 6.4 %collective-permute-start.1 = (bf16[4,2,2,16,256]{4,3,2,1,0:T(8,128)(2,1)S(1)}, bf16[4,2,2,16,256]{4,3,2,1,0:T(8,128)(2,1)S(1)}, u32[]{:S(2)}, u32[]{:S(2)}) collective-permute-start(bf16[4,2,2,16,256]{4,3,2,1,0:T(8,128)(2,1)S(1)} %pad_maximum_fusion), channel_id=1, source_target_pairs={{0,4},{1,5},{2,6},{3,7},{4,0},{5,1},{6,2},{7,3},{8,12},{9,13},{10,... | collective-permute-start | bytes 393224 | tf_op jit(solution)/shard_map/ppermute | solution.py:156
  11.6 6.5 %collective-permute-start.2 = (bf16[4,2,2,16,256]{4,3,2,1,0:T(8,128)(2,1)S(1)}, bf16[4,2,2,16,256]{4,3,2,1,0:T(8,128)(2,1)S(1)}, u32[]{:S(2)}, u32[]{:S(2)}) collective-permute-start(bf16[4,2,2,16,256]{4,3,2,1,0:T(8,128)(2,1)S(1)} %pad_maximum_fusion), channel_id=1, source_target_pairs={{0,2},{1,3},{2,0},{3,1},{4,6},{5,7},{6,4},{7,5},{8,10},{9,11},{10,... | collective-permute-start | bytes 393224 | tf_op jit(solution)/shard_map/ppermute | solution.py:156
  13.1 6.7 %collective-permute-start.3 = (bf16[4,2,2,16,256]{4,3,2,1,0:T(8,128)(2,1)S(1)}, bf16[4,2,2,16,256]{4,3,2,1,0:T(8,128)(2,1)S(1)}, u32[]{:S(2)}, u32[]{:S(2)}) collective-permute-start(bf16[4,2,2,16,256]{4,3,2,1,0:T(8,128)(2,1)S(1)} %pad_maximum_fusion), channel_id=1, source_target_pairs={{0,6},{1,7},{2,4},{3,5},{4,2},{5,3},{6,0},{7,1},{8,14},{9,15},{10,... | collective-permute-start | bytes 393224 | tf_op jit(solution)/shard_map/ppermute | solution.py:156
  19.8 2.0 %copy-start.3 = (bf16[16,2,2,16,256]{4,3,2,1,0:T(8,128)(2,1)}, bf16[16,2,2,16,256]{4,3,2,1,0:T(8,128)(2,1)S(1)}, u32[]{:S(2)}) copy-start(bf16[16,2,2,16,256]{4,3,2,1,0:T(8,128)(2,1)S(1)} %constant_dynamic-update-slice_fusion.low_ref) | copy-start | bytes 1572868
  19.8 2.0 %collective-permute-start.4 = (bf16[16,2,2,16,256]{4,3,2,1,0:T(8,128)(2,1)S(1)}, bf16[16,2,2,16,256]{4,3,2,1,0:T(8,128)(2,1)S(1)}, u32[]{:S(2)}, u32[]{:S(2)}) collective-permute-start(bf16[16,2,2,16,256]{4,3,2,1,0:T(8,128)(2,1)S(1)} %constant_dynamic-update-slice_fusion.low_ref), channel_id=1, source_target_pairs={{0,1},{1,0},{2,3},{3,2},{4,5},{5,4},{6,7},{7,6},{8,9},{9,8},{10,11... | collective-permute-start | bytes 1572872 | tf_op jit(solution)/shard_map/ppermute | solution.py:158
  21.8 0.8 %copy-start.5 = (bf16[16,2,2,16,256]{4,3,2,1,0:T(8,128)(2,1)}, bf16[16,2,2,16,256]{4,3,2,1,0:T(8,128)(2,1)S(1)}, u32[]{:S(2)}) copy-start(bf16[16,2,2,16,256]{4,3,2,1,0:T(8,128)(2,1)S(1)} %collective-permute-done.4.high_ref) | copy-start | bytes 1572868
  28.2 2.2 %collective-permute-start.5 = (bf16[16,2,2,16,256]{4,3,2,1,0:T(8,128)(2,1)}, bf16[16,2,2,16,256]{4,3,2,1,0:T(8,128)(2,1)S(1)}, u32[]{:S(2)}, u32[]{:S(2)}) collective-permute-start(bf16[16,2,2,16,256]{4,3,2,1,0:T(8,128)(2,1)} %get-tuple-element.32), channel_id=1, source_target_pairs={{0,1},{1,0},{2,3},{3,2},{4,5},{5,4},{6,7},{7,6},{8,9},{9,8},{10,11... | collective-permute-start | bytes 1572872 | tf_op jit(solution)/shard_map/ppermute | solution.py:177
  31.8 6.4 %collective-permute-start.6 = (bf16[4,2,2,16,256]{4,3,2,1,0:T(8,128)(2,1)S(1)}, bf16[4,2,2,16,256]{4,3,2,1,0:T(8,128)(2,1)S(1)}, u32[]{:S(2)}, u32[]{:S(2)}) collective-permute-start(bf16[4,2,2,16,256]{4,3,2,1,0:T(8,128)(2,1)S(1)} %get-tuple-element.36), channel_id=1, source_target_pairs={{0,4},{1,5},{2,6},{3,7},{4,0},{5,1},{6,2},{7,3},{8,12},{9,13},{10,... | collective-permute-start | bytes 393224 | tf_op jit(solution)/shard_map/ppermute | solution.py:188
  32.8 8.1 %collective-permute-start.7 = (bf16[4,2,2,16,256]{4,3,2,1,0:T(8,128)(2,1)S(1)}, bf16[4,2,2,16,256]{4,3,2,1,0:T(8,128)(2,1)S(1)}, u32[]{:S(2)}, u32[]{:S(2)}) collective-permute-start(bf16[4,2,2,16,256]{4,3,2,1,0:T(8,128)(2,1)S(1)} %get-tuple-element.38), channel_id=1, source_target_pairs={{0,2},{1,3},{2,0},{3,1},{4,6},{5,7},{6,4},{7,5},{8,10},{9,11},{10,... | collective-permute-start | bytes 393224 | tf_op jit(solution)/shard_map/ppermute | solution.py:188
  33.8 7.0 %collective-permute-start.8 = (bf16[4,2,2,16,256]{4,3,2,1,0:T(8,128)(2,1)S(1)}, bf16[4,2,2,16,256]{4,3,2,1,0:T(8,128)(2,1)S(1)}, u32[]{:S(2)}, u32[]{:S(2)}) collective-permute-start(bf16[4,2,2,16,256]{4,3,2,1,0:T(8,128)(2,1)S(1)} %get-tuple-element.37), channel_id=1, source_target_pairs={{0,6},{1,7},{2,4},{3,5},{4,2},{5,3},{6,0},{7,1},{8,14},{9,15},{10,... | collective-permute-start | bytes 393224 | tf_op jit(solution)/shard_map/ppermute | solution.py:188
  40.8 5.0 %copy-start.4 = (bf16[2,2,256,256]{3,2,1,0:T(8,128)(2,1)S(1)}, bf16[2,2,256,256]{3,2,1,0:T(8,128)(2,1)}, u32[]{:S(2)}) copy-start(bf16[2,2,256,256]{3,2,1,0:T(8,128)(2,1)} %get-tuple-element.30) | copy-start | bytes 1572868
  40.9 6.9 %collective-permute-start.9 = (bf16[2,2,2,16,256]{4,3,2,1,0:T(8,128)(2,1)S(1)}, bf16[2,2,2,16,256]{4,3,2,1,0:T(8,128)(2,1)S(1)}, u32[]{:S(2)}, u32[]{:S(2)}) collective-permute-start(bf16[2,2,2,16,256]{4,3,2,1,0:T(8,128)(2,1)S(1)} %slice.157), channel_id=1, source_target_pairs={{0,8},{1,9},{2,10},{3,11},{4,12},{5,13},{6,14},{7,15},{8,0},{9,1},... | collective-permute-start | bytes 196616 | tf_op jit(solution)/shard_map/ppermute | solution.py:188
  44.2 3.6 %collective-permute-start.11 = (bf16[3,2]{1,0:T(4,128)(2,1)S(1)}, bf16[3,2]{1,0:T(4,128)(2,1)S(1)}, u32[]{:S(2)}, u32[]{:S(2)}) collective-permute-start(bf16[3,2]{1,0:T(4,128)(2,1)S(1)} %pad_maximum_fusion.2), channel_id=1, source_target_pairs={{0,16},{16,0},{1,17},{17,1},{2,18},{18,2},{3,19},{19,3},{4,20},{20... | collective-permute-start | bytes 44 | tf_op jit(solution)/shard_map/ppermute | solution.py:173
  48.5 5.0 %collective-permute-start.10 = (bf16[2,128,256]{2,1,0:T(8,128)(2,1)S(1)}, bf16[2,128,256]{2,1,0:T(8,128)(2,1)S(1)}, u32[]{:S(2)}, u32[]{:S(2)}) collective-permute-start(bf16[2,128,256]{2,1,0:T(8,128)(2,1)S(1)} %dynamic-slice_convert_fusion), channel_id=1, source_target_pairs={{0,16},{16,0},{1,17},{17,1},{2,18},{18,2},{3,19},{19,3},{4,20},{20... | collective-permute-start | bytes 393224 | tf_op jit(solution)/shard_map/ppermute | solution.py:211

commit v18 on v15

--- a/solution.py
+++ b/solution.py
@@ -143,7 +143,14 @@
     projected = jnp.einsum(
         "tai,ktil->ktal", slice_rows, halfway, preferred_element_type=jnp.float32
     ).astype(jnp.bfloat16)
-    edges = jnp.stack((projected[:, :, :OVL], projected[:, :, pixels - OVL :]), axis=1)
+    band_weight = jnp.concatenate((slice_rows[:, :OVL], slice_rows[:, pixels - OVL :]), axis=1)
+    inner = jnp.einsum(
+        "tai,kij->ktaj", band_weight, sections, preferred_element_type=jnp.float32
+    ).astype(jnp.bfloat16)
+    edge_rows = jnp.einsum(
+        "ktaj,tlj->ktal", inner, slice_cols, preferred_element_type=jnp.float32
+    ).astype(jnp.bfloat16)
+    edges = jnp.stack((edge_rows[:, :, :OVL], edge_rows[:, :, OVL:]), axis=1)
     stages = gather_stages(peer_count)
     edges_all = edges
     for stage in stages[:-1]:

time: 54.3 us -> 54.2 us (level)
  waiting for transfers between devices: 22.2 us -> 20.4 us
  matrix products: 2.12 us -> 3.32 us
  local copies, waits for them, and re-layouts: 1.85 us -> 2.41 us
    ppermute x1, waiting for transfers between devices: 1.9 us -> 0.01 us  [on_device(): lax.ppermute(edges_all, 'dom', [(i, i ^ 1) for i in range(peer_count)])]
    dot_general x0 -> x2, matrix products: none -> 1.32 us  [the longest x1 1.12 us: on_device(): jnp.einsum('tai,kij->ktaj', band_weight, sections, preferred_element_type...]
    dot_general x1, matrix products: 1.28 us -> 0.33 us  [on_device(): jnp.einsum('kij,tlj->ktil', sections, slice_cols, preferred_element_type=...]
    dot_general x1, matrix products: 0.3 us -> 1.13 us  [on_device(): jnp.einsum('tai,ktil->ktal', slice_rows, halfway, preferred_element_type=...]
    slice x0 -> x1, local copies, waits for them, and re-layouts: none -> 0.78 us  [on_device(): slice_rows[:, :OVL]]
  transfers between devices with their start and end apart: 12 -> 12, of which waited for: 10 -> 9; matrix products, arithmetic and copies ran while one was open for 3% -> 5% of each run, Pallas kernels for 0% -> 0%
where the time goes in v18:
time: 54.2 us; the launch traced here: 53.9 us
  waiting for transfers between devices  20.4 us (38%)
  starting transfers between devices  17.7 us (33%)
  Pallas kernels  5.42 us (10%)
  other arithmetic  3.73 us (7%)
  matrix products  3.32 us (6%)
  local copies, waits for them, and re-layouts  2.41 us (4%)
  between operations  0.83 us (2%)
    ppermute x4, waiting for transfers between devices, on_device(): pieces.append(lax.ppermute(edges_all, 'dom', pairs))  8.84 us
    ppermute x4, starting transfers between devices, on_device(): pieces.append(lax.ppermute(edges_all, 'dom', pairs))  7.65 us
    ppermute x4, starting transfers between devices, on_device(): kept = kept + lax.ppermute(given, 'dom', pairs).astype(jnp.float32)  6.81 us
    ppermute x4, waiting for transfers between devices, on_device(): kept = kept + lax.ppermute(given, 'dom', pairs).astype(jnp.float32)  5.43 us
    pallas_call x1, Pallas kernels, middle(): pl.pallas_call(middle_kernel, grid=(tilt_count,), in_specs=[smem, smem, s...  5.42 us
    ppermute x1, waiting for transfers between devices, on_device(): given = lax.ppermute(given.astype(jnp.bfloat16), 'tilt', [(0, 1), (1, 0)])  2.93 us
    ppermute x1, waiting for transfers between devices, on_device(): parts = lax.ppermute(parts, 'tilt', [(0, 1), (1, 0)]).astype(jnp.float32)  1.96 us
    ppermute x1, starting transfers between devices, on_device(): parts = lax.ppermute(parts, 'tilt', [(0, 1), (1, 0)]).astype(jnp.float32)  1.58 us
  transfers between devices with their start and end apart: 12, of which 9 were waited for; matrix products, arithmetic and copies ran while one was open for 5% of the time, Pallas kernels for 0%

profile of v18, /device:TPU:0, one launch (start us, length us, event | category | flops | bytes accessed | tf_op | source)
XLA Modules:
  0.0 53.9 jit_solution(7224318462866092228)
XLA Ops:
  0.6 0.8 %fusion.31 = (bf16[2,16,256]{2,1,0:T(8,128)(2,1)S(1)}, bf16[2,16,256]{2,1,0:T(8,128)(2,1)S(1)}) fusion(bf16[2,256,256]{2,1,0:T(8,128)(2,1)} %param.15), kind=kLoop, calls=%fused_computation.59 | loop fusion | bytes 65536 | tf_op jit(solution)/shard_map/slice | solution.py:146
  1.4 1.1 %fusion.4 = bf16[2,2,32,256]{3,2,0,1:T(8,128)(2,1)S(1)} fusion(bf16[2,256,256]{2,1,0:T(8,128)(2,1)} %param.13, bf16[2,16,256]{2,1,0:T(8,128)(2,1)S(1)} %get-tuple-element.40, bf16[2,16,256]{2,1,0:T(8,128)(2,1)S(1)} %get-tuple-element.39), kind=kOutput, calls=%fused_computation.10 | convolution fusion | flops 16875520 | bytes 360448 | tf_op jit(solution)/shard_map/tai,kij->ktaj/dot_general | solution.py:147
  2.8 4.1 %collective-permute-start = (bf16[2,2,2,16,256]{4,3,2,1,0:T(8,128)(2,1)S(1)}, bf16[2,2,2,16,256]{4,3,2,1,0:T(8,128)(2,1)S(1)}, u32[]{:S(2)}, u32[]{:S(2)}) collective-permute-start(bf16[2,2,2,16,256]{4,3,2,1,0:T(8,128)(2,1)S(1)} %get-tuple-element.41), channel_id=1, source_target_pairs={{0,8},{1,9},{2,10},{3,11},{4,12},{5,13},{6,14},{7,15},{8,0},{9,1},... | collective-permute-start | bytes 196616 | tf_op jit(solution)/shard_map/ppermute | solution.py:161
  6.9 3.6 %collective-permute-done = bf16[2,2,2,16,256]{4,3,2,1,0:T(8,128)(2,1)S(1)} collective-permute-done((bf16[2,2,2,16,256]{4,3,2,1,0:T(8,128)(2,1)S(1)}, bf16[2,2,2,16,256]{4,3,2,1,0:T(8,128)(2,1)S(1)}, u32[]{:S(2)}, u32[]{:S(2)}) %collective-permute-start) | collective-permute-done | bytes 65568 | tf_op jit(solution)/shard_map/ppermute | solution.py:161
  11.2 1.5 %collective-permute-start.2 = (bf16[4,2,2,16,256]{4,3,2,1,0:T(8,128)(2,1)S(1)}, bf16[4,2,2,16,256]{4,3,2,1,0:T(8,128)(2,1)S(1)}, u32[]{:S(2)}, u32[]{:S(2)}) collective-permute-start(bf16[4,2,2,16,256]{4,3,2,1,0:T(8,128)(2,1)S(1)} %pad_maximum_fusion), channel_id=1, source_target_pairs={{0,2},{1,3},{2,0},{3,1},{4,6},{5,7},{6,4},{7,5},{8,10},{9,11},{10,... | collective-permute-start | bytes 393224 | tf_op jit(solution)/shard_map/ppermute | solution.py:161
  12.7 1.4 %collective-permute-start.3 = (bf16[4,2,2,16,256]{4,3,2,1,0:T(8,128)(2,1)S(1)}, bf16[4,2,2,16,256]{4,3,2,1,0:T(8,128)(2,1)S(1)}, u32[]{:S(2)}, u32[]{:S(2)}) collective-permute-start(bf16[4,2,2,16,256]{4,3,2,1,0:T(8,128)(2,1)S(1)} %pad_maximum_fusion), channel_id=1, source_target_pairs={{0,6},{1,7},{2,4},{3,5},{4,2},{5,3},{6,0},{7,1},{8,14},{9,15},{10,... | collective-permute-start | bytes 393224 | tf_op jit(solution)/shard_map/ppermute | solution.py:161
  14.1 2.8 %collective-permute-done.1 = bf16[4,2,2,16,256]{4,3,2,1,0:T(8,128)(2,1)S(1)} collective-permute-done((bf16[4,2,2,16,256]{4,3,2,1,0:T(8,128)(2,1)S(1)}, bf16[4,2,2,16,256]{4,3,2,1,0:T(8,128)(2,1)S(1)}, u32[]{:S(2)}, u32[]{:S(2)}) %collective-permute-start.1) | collective-permute-done | bytes 131104 | tf_op jit(solution)/shard_map/ppermute | solution.py:161
  17.7 1.6 %collective-permute-done.3 = bf16[4,2,2,16,256]{4,3,2,1,0:T(8,128)(2,1)S(1)} collective-permute-done((bf16[4,2,2,16,256]{4,3,2,1,0:T(8,128)(2,1)S(1)}, bf16[4,2,2,16,256]{4,3,2,1,0:T(8,128)(2,1)S(1)}, u32[]{:S(2)}, u32[]{:S(2)}) %collective-permute-start.3) | collective-permute-done | bytes 131104 | tf_op jit(solution)/shard_map/ppermute | solution.py:161
  20.5 1.1 %fusion.1.proj_ref = bf16[2,2,256,256]{3,2,1,0:T(8,128)(2,1)} fusion(bf16[2,2,256,256]{2,3,0,1:T(8,128)(2,1)S(1)} %fusion, bf16[2,256,256]{2,1,0:T(8,128)(2,1)S(1)} %copy-done.1), kind=kOutput, calls=%fused_computation.4 | convolution fusion | flops 134479872 | bytes 1310720 | tf_op jit(solution)/shard_map/tai,ktil->ktal/dot_general | solution.py:143
  21.7 0.8 %copy-done.5 = bf16[16,2,2,16,256]{4,3,2,1,0:T(8,128)(2,1)} copy-done((bf16[16,2,2,16,256]{4,3,2,1,0:T(8,128)(2,1)}, bf16[16,2,2,16,256]{4,3,2,1,0:T(8,128)(2,1)S(1)}, u32[]{:S(2)}) %copy-start.5) | copy-done | bytes 524312
  22.5 5.4 %shard_map.104 = (bf16[2,2,256,256]{3,2,1,0:T(8,128)(2,1)}, f32[2,2,8,128]{3,2,1,0:T(8,128)}, f32[16,2,2,16,256]{4,3,2,1,0:T(8,128)}, bf16[16,2,2,16,256]{4,3,2,1,0:T(8,128)(2,1)}) custom-call(s32[2,2,8]{2,1,0:T(2,128)} %owner_ref.1, s32[2,16]{1,0:T(2,128)} %local_ref.1, s32[2,16]{1,0:T(2,128)} %side_ref.1, f32[2,16]{1,0:T(2,128)} %weight_ref.1, ...), custom_call_target="tpu_custom_call" | custom-call | flops 536870912 | bytes 4456448 | tf_op jit(solution)/shard_map/pallas_call | solution.py:83
  27.9 0.8 %slice_reduce_fusion = f32[2]{0:T(128)S(1)} fusion(f32[2,2,8,128]{3,2,1,0:T(8,128)} %get-tuple-element.33), kind=kLoop, calls=%fused_computation.48 | loop fusion | flops 2 | bytes 24 | tf_op jit(solution)/shard_map/reduce_sum | solution.py:169
  28.8 1.3 %collective-permute-done.5 = bf16[16,2,2,16,256]{4,3,2,1,0:T(8,128)(2,1)S(1)} collective-permute-done((bf16[16,2,2,16,256]{4,3,2,1,0:T(8,128)(2,1)}, bf16[16,2,2,16,256]{4,3,2,1,0:T(8,128)(2,1)S(1)}, u32[]{:S(2)}, u32[]{:S(2)}) %collective-permute-start.5) | collective-permute-done | bytes 524320 | tf_op jit(solution)/shard_map/ppermute | solution.py:182
  30.0 1.4 %fusion.29 = (bf16[16,2,2,16,256]{4,3,2,1,0:T(8,128)(2,1)S(1)}, f32[16,2,2,16,256]{4,3,2,1,0:T(8,128)S(1)}) fusion(f32[16,2,2,16,256]{4,3,2,1,0:T(8,128)} %get-tuple-element.31, bf16[16,2,2,16,256]{4,3,2,1,0:T(8,128)(2,1)S(1)} %collective-permute-done.5), kind=kLoop, calls=%fused_computation.57 | loop fusion | flops 786432 | bytes 3145728 | tf_op jit(solution)/shard_map/convert.3
  31.5 0.9 %collective-permute-start.6 = (bf16[4,2,2,16,256]{4,3,2,1,0:T(8,128)(2,1)S(1)}, bf16[4,2,2,16,256]{4,3,2,1,0:T(8,128)(2,1)S(1)}, u32[]{:S(2)}, u32[]{:S(2)}) collective-permute-start(bf16[4,2,2,16,256]{4,3,2,1,0:T(8,128)(2,1)S(1)} %get-tuple-element.36), channel_id=1, source_target_pairs={{0,4},{1,5},{2,6},{3,7},{4,0},{5,1},{6,2},{7,3},{8,12},{9,13},{10,... | collective-permute-start | bytes 393224 | tf_op jit(solution)/shard_map/ppermute | solution.py:193
  32.4 1.0 %collective-permute-start.7 = (bf16[4,2,2,16,256]{4,3,2,1,0:T(8,128)(2,1)S(1)}, bf16[4,2,2,16,256]{4,3,2,1,0:T(8,128)(2,1)S(1)}, u32[]{:S(2)}, u32[]{:S(2)}) collective-permute-start(bf16[4,2,2,16,256]{4,3,2,1,0:T(8,128)(2,1)S(1)} %get-tuple-element.38), channel_id=1, source_target_pairs={{0,2},{1,3},{2,0},{3,1},{4,6},{5,7},{6,4},{7,5},{8,10},{9,11},{10,... | collective-permute-start | bytes 393224 | tf_op jit(solution)/shard_map/ppermute | solution.py:193
  33.4 1.6 %collective-permute-start.8 = (bf16[4,2,2,16,256]{4,3,2,1,0:T(8,128)(2,1)S(1)}, bf16[4,2,2,16,256]{4,3,2,1,0:T(8,128)(2,1)S(1)}, u32[]{:S(2)}, u32[]{:S(2)}) collective-permute-start(bf16[4,2,2,16,256]{4,3,2,1,0:T(8,128)(2,1)S(1)} %get-tuple-element.37), channel_id=1, source_target_pairs={{0,6},{1,7},{2,4},{3,5},{4,2},{5,3},{6,0},{7,1},{8,14},{9,15},{10,... | collective-permute-start | bytes 393224 | tf_op jit(solution)/shard_map/ppermute | solution.py:193
  35.0 2.8 %collective-permute-done.6 = bf16[4,2,2,16,256]{4,3,2,1,0:T(8,128)(2,1)S(1)} collective-permute-done((bf16[4,2,2,16,256]{4,3,2,1,0:T(8,128)(2,1)S(1)}, bf16[4,2,2,16,256]{4,3,2,1,0:T(8,128)(2,1)S(1)}, u32[]{:S(2)}, u32[]{:S(2)}) %collective-permute-start.6) | collective-permute-done | bytes 131104 | tf_op jit(solution)/shard_map/ppermute | solution.py:193
  37.9 2.6 %collective-permute-done.7 = bf16[4,2,2,16,256]{4,3,2,1,0:T(8,128)(2,1)S(1)} collective-permute-done((bf16[4,2,2,16,256]{4,3,2,1,0:T(8,128)(2,1)S(1)}, bf16[4,2,2,16,256]{4,3,2,1,0:T(8,128)(2,1)S(1)}, u32[]{:S(2)}, u32[]{:S(2)}) %collective-permute-start.7) | collective-permute-done | bytes 131104 | tf_op jit(solution)/shard_map/ppermute | solution.py:193
  40.6 3.3 %collective-permute-start.9 = (bf16[2,2,2,16,256]{4,3,2,1,0:T(8,128)(2,1)S(1)}, bf16[2,2,2,16,256]{4,3,2,1,0:T(8,128)(2,1)S(1)}, u32[]{:S(2)}, u32[]{:S(2)}) collective-permute-start(bf16[2,2,2,16,256]{4,3,2,1,0:T(8,128)(2,1)S(1)} %slice.165), channel_id=1, source_target_pairs={{0,8},{1,9},{2,10},{3,11},{4,12},{5,13},{6,14},{7,15},{8,0},{9,1},... | collective-permute-start | bytes 196616 | tf_op jit(solution)/shard_map/ppermute | solution.py:193
  43.8 1.6 %collective-permute-start.11 = (bf16[3,2]{1,0:T(4,128)(2,1)S(1)}, bf16[3,2]{1,0:T(4,128)(2,1)S(1)}, u32[]{:S(2)}, u32[]{:S(2)}) collective-permute-start(bf16[3,2]{1,0:T(4,128)(2,1)S(1)} %pad_maximum_fusion.2), channel_id=1, source_target_pairs={{0,16},{16,0},{1,17},{17,1},{2,18},{18,2},{3,19},{19,3},{4,20},{20... | collective-permute-start | bytes 44 | tf_op jit(solution)/shard_map/ppermute | solution.py:178
  45.5 2.0 %collective-permute-done.11 = bf16[3,2]{1,0:T(4,128)(2,1)S(1)} collective-permute-done((bf16[3,2]{1,0:T(4,128)(2,1)S(1)}, bf16[3,2]{1,0:T(4,128)(2,1)S(1)}, u32[]{:S(2)}, u32[]{:S(2)}) %collective-permute-start.11) | collective-permute-done | bytes 44 | tf_op jit(solution)/shard_map/ppermute | solution.py:178
  48.1 1.6 %collective-permute-start.10 = (bf16[2,128,256]{2,1,0:T(8,128)(2,1)S(1)}, bf16[2,128,256]{2,1,0:T(8,128)(2,1)S(1)}, u32[]{:S(2)}, u32[]{:S(2)}) collective-permute-start(bf16[2,128,256]{2,1,0:T(8,128)(2,1)S(1)} %dynamic-slice_convert_fusion), channel_id=1, source_target_pairs={{0,16},{16,0},{1,17},{17,1},{2,18},{18,2},{3,19},{19,3},{4,20},{20... | collective-permute-start | bytes 393224 | tf_op jit(solution)/shard_map/ppermute | solution.py:216
  50.2 2.9 %collective-permute-done.10 = bf16[2,128,256]{2,1,0:T(8,128)(2,1)S(1)} collective-permute-done((bf16[2,128,256]{2,1,0:T(8,128)(2,1)S(1)}, bf16[2,128,256]{2,1,0:T(8,128)(2,1)S(1)}, u32[]{:S(2)}, u32[]{:S(2)}) %collective-permute-start.10) | collective-permute-done | bytes 131104 | tf_op jit(solution)/shard_map/ppermute | solution.py:216
  (42 shorter events, 4.9 us)
Async XLA Ops:
  0.6 1.9 %copy-start = (bf16[2,256,256]{2,1,0:T(8,128)(2,1)S(1)}, bf16[2,256,256]{2,1,0:T(8,128)(2,1)}, u32[]{:S(2)}) copy-start(bf16[2,256,256]{2,1,0:T(8,128)(2,1)} %param.16) | copy-start | bytes 786436
  2.8 7.8 %collective-permute-start = (bf16[2,2,2,16,256]{4,3,2,1,0:T(8,128)(2,1)S(1)}, bf16[2,2,2,16,256]{4,3,2,1,0:T(8,128)(2,1)S(1)}, u32[]{:S(2)}, u32[]{:S(2)}) collective-permute-start(bf16[2,2,2,16,256]{4,3,2,1,0:T(8,128)(2,1)S(1)} %get-tuple-element.41), channel_id=1, source_target_pairs={{0,8},{1,9},{2,10},{3,11},{4,12},{5,13},{6,14},{7,15},{8,0},{9,1},... | collective-permute-start | bytes 196616 | tf_op jit(solution)/shard_map/ppermute | solution.py:161
  10.6 6.4 %collective-permute-start.1 = (bf16[4,2,2,16,256]{4,3,2,1,0:T(8,128)(2,1)S(1)}, bf16[4,2,2,16,256]{4,3,2,1,0:T(8,128)(2,1)S(1)}, u32[]{:S(2)}, u32[]{:S(2)}) collective-permute-start(bf16[4,2,2,16,256]{4,3,2,1,0:T(8,128)(2,1)S(1)} %pad_maximum_fusion), channel_id=1, source_target_pairs={{0,4},{1,5},{2,6},{3,7},{4,0},{5,1},{6,2},{7,3},{8,12},{9,13},{10,... | collective-permute-start | bytes 393224 | tf_op jit(solution)/shard_map/ppermute | solution.py:161
  11.2 6.5 %collective-permute-start.2 = (bf16[4,2,2,16,256]{4,3,2,1,0:T(8,128)(2,1)S(1)}, bf16[4,2,2,16,256]{4,3,2,1,0:T(8,128)(2,1)S(1)}, u32[]{:S(2)}, u32[]{:S(2)}) collective-permute-start(bf16[4,2,2,16,256]{4,3,2,1,0:T(8,128)(2,1)S(1)} %pad_maximum_fusion), channel_id=1, source_target_pairs={{0,2},{1,3},{2,0},{3,1},{4,6},{5,7},{6,4},{7,5},{8,10},{9,11},{10,... | collective-permute-start | bytes 393224 | tf_op jit(solution)/shard_map/ppermute | solution.py:161
  12.7 6.7 %collective-permute-start.3 = (bf16[4,2,2,16,256]{4,3,2,1,0:T(8,128)(2,1)S(1)}, bf16[4,2,2,16,256]{4,3,2,1,0:T(8,128)(2,1)S(1)}, u32[]{:S(2)}, u32[]{:S(2)}) collective-permute-start(bf16[4,2,2,16,256]{4,3,2,1,0:T(8,128)(2,1)S(1)} %pad_maximum_fusion), channel_id=1, source_target_pairs={{0,6},{1,7},{2,4},{3,5},{4,2},{5,3},{6,0},{7,1},{8,14},{9,15},{10,... | collective-permute-start | bytes 393224 | tf_op jit(solution)/shard_map/ppermute | solution.py:161
  17.0 2.5 %copy-start.2 = (bf16[2,256,256]{2,1,0:T(8,128)(2,1)S(1)}, bf16[2,256,256]{2,1,0:T(8,128)(2,1)}, u32[]{:S(2)}) copy-start(bf16[2,256,256]{2,1,0:T(8,128)(2,1)} %param.13) | copy-start | bytes 786436
  19.4 2.3 %copy-start.3 = (bf16[16,2,2,16,256]{4,3,2,1,0:T(8,128)(2,1)}, bf16[16,2,2,16,256]{4,3,2,1,0:T(8,128)(2,1)S(1)}, u32[]{:S(2)}) copy-start(bf16[16,2,2,16,256]{4,3,2,1,0:T(8,128)(2,1)S(1)} %constant_dynamic-update-slice_fusion.low_ref) | copy-start | bytes 1572868
  19.4 1.1 %copy-start.1 = (bf16[2,256,256]{2,1,0:T(8,128)(2,1)S(1)}, bf16[2,256,256]{2,1,0:T(8,128)(2,1)}, u32[]{:S(2)}) copy-start(bf16[2,256,256]{2,1,0:T(8,128)(2,1)} %param.15) | copy-start | bytes 786436
  19.4 2.3 %collective-permute-start.4 = (bf16[16,2,2,16,256]{4,3,2,1,0:T(8,128)(2,1)S(1)}, bf16[16,2,2,16,256]{4,3,2,1,0:T(8,128)(2,1)S(1)}, u32[]{:S(2)}, u32[]{:S(2)}) collective-permute-start(bf16[16,2,2,16,256]{4,3,2,1,0:T(8,128)(2,1)S(1)} %constant_dynamic-update-slice_fusion.low_ref), channel_id=1, source_target_pairs={{0,1},{1,0},{2,3},{3,2},{4,5},{5,4},{6,7},{7,6},{8,9},{9,8},{10,11... | collective-permute-start | bytes 1572872 | tf_op jit(solution)/shard_map/ppermute | solution.py:163
  21.7 0.8 %copy-start.5 = (bf16[16,2,2,16,256]{4,3,2,1,0:T(8,128)(2,1)}, bf16[16,2,2,16,256]{4,3,2,1,0:T(8,128)(2,1)S(1)}, u32[]{:S(2)}) copy-start(bf16[16,2,2,16,256]{4,3,2,1,0:T(8,128)(2,1)S(1)} %collective-permute-done.4.high_ref) | copy-start | bytes 1572868
  27.9 2.2 %collective-permute-start.5 = (bf16[16,2,2,16,256]{4,3,2,1,0:T(8,128)(2,1)}, bf16[16,2,2,16,256]{4,3,2,1,0:T(8,128)(2,1)S(1)}, u32[]{:S(2)}, u32[]{:S(2)}) collective-permute-start(bf16[16,2,2,16,256]{4,3,2,1,0:T(8,128)(2,1)} %get-tuple-element.32), channel_id=1, source_target_pairs={{0,1},{1,0},{2,3},{3,2},{4,5},{5,4},{6,7},{7,6},{8,9},{9,8},{10,11... | collective-permute-start | bytes 1572872 | tf_op jit(solution)/shard_map/ppermute | solution.py:182
  31.5 6.4 %collective-permute-start.6 = (bf16[4,2,2,16,256]{4,3,2,1,0:T(8,128)(2,1)S(1)}, bf16[4,2,2,16,256]{4,3,2,1,0:T(8,128)(2,1)S(1)}, u32[]{:S(2)}, u32[]{:S(2)}) collective-permute-start(bf16[4,2,2,16,256]{4,3,2,1,0:T(8,128)(2,1)S(1)} %get-tuple-element.36), channel_id=1, source_target_pairs={{0,4},{1,5},{2,6},{3,7},{4,0},{5,1},{6,2},{7,3},{8,12},{9,13},{10,... | collective-permute-start | bytes 393224 | tf_op jit(solution)/shard_map/ppermute | solution.py:193
  32.4 8.1 %collective-permute-start.7 = (bf16[4,2,2,16,256]{4,3,2,1,0:T(8,128)(2,1)S(1)}, bf16[4,2,2,16,256]{4,3,2,1,0:T(8,128)(2,1)S(1)}, u32[]{:S(2)}, u32[]{:S(2)}) collective-permute-start(bf16[4,2,2,16,256]{4,3,2,1,0:T(8,128)(2,1)S(1)} %get-tuple-element.38), channel_id=1, source_target_pairs={{0,2},{1,3},{2,0},{3,1},{4,6},{5,7},{6,4},{7,5},{8,10},{9,11},{10,... | collective-permute-start | bytes 393224 | tf_op jit(solution)/shard_map/ppermute | solution.py:193
  33.4 7.0 %collective-permute-start.8 = (bf16[4,2,2,16,256]{4,3,2,1,0:T(8,128)(2,1)S(1)}, bf16[4,2,2,16,256]{4,3,2,1,0:T(8,128)(2,1)S(1)}, u32[]{:S(2)}, u32[]{:S(2)}) collective-permute-start(bf16[4,2,2,16,256]{4,3,2,1,0:T(8,128)(2,1)S(1)} %get-tuple-element.37), channel_id=1, source_target_pairs={{0,6},{1,7},{2,4},{3,5},{4,2},{5,3},{6,0},{7,1},{8,14},{9,15},{10,... | collective-permute-start | bytes 393224 | tf_op jit(solution)/shard_map/ppermute | solution.py:193
  40.5 5.0 %copy-start.4 = (bf16[2,2,256,256]{3,2,1,0:T(8,128)(2,1)S(1)}, bf16[2,2,256,256]{3,2,1,0:T(8,128)(2,1)}, u32[]{:S(2)}) copy-start(bf16[2,2,256,256]{3,2,1,0:T(8,128)(2,1)} %get-tuple-element.30) | copy-start | bytes 1572868
  40.6 6.9 %collective-permute-start.9 = (bf16[2,2,2,16,256]{4,3,2,1,0:T(8,128)(2,1)S(1)}, bf16[2,2,2,16,256]{4,3,2,1,0:T(8,128)(2,1)S(1)}, u32[]{:S(2)}, u32[]{:S(2)}) collective-permute-start(bf16[2,2,2,16,256]{4,3,2,1,0:T(8,128)(2,1)S(1)} %slice.165), channel_id=1, source_target_pairs={{0,8},{1,9},{2,10},{3,11},{4,12},{5,13},{6,14},{7,15},{8,0},{9,1},... | collective-permute-start | bytes 196616 | tf_op jit(solution)/shard_map/ppermute | solution.py:193
  43.8 3.6 %collective-permute-start.11 = (bf16[3,2]{1,0:T(4,128)(2,1)S(1)}, bf16[3,2]{1,0:T(4,128)(2,1)S(1)}, u32[]{:S(2)}, u32[]{:S(2)}) collective-permute-start(bf16[3,2]{1,0:T(4,128)(2,1)S(1)} %pad_maximum_fusion.2), channel_id=1, source_target_pairs={{0,16},{16,0},{1,17},{17,1},{2,18},{18,2},{3,19},{19,3},{4,20},{20... | collective-permute-start | bytes 44 | tf_op jit(solution)/shard_map/ppermute | solution.py:178
  48.1 5.0 %collective-permute-start.10 = (bf16[2,128,256]{2,1,0:T(8,128)(2,1)S(1)}, bf16[2,128,256]{2,1,0:T(8,128)(2,1)S(1)}, u32[]{:S(2)}, u32[]{:S(2)}) collective-permute-start(bf16[2,128,256]{2,1,0:T(8,128)(2,1)S(1)} %dynamic-slice_convert_fusion), channel_id=1, source_target_pairs={{0,16},{16,0},{1,17},{17,1},{2,18},{18,2},{3,19},{19,3},{4,20},{20... | collective-permute-start | bytes 393224 | tf_op jit(solution)/shard_map/ppermute | solution.py:216

commit v19 on v15

--- a/solution.py
+++ b/solution.py
@@ -19,8 +19,6 @@
     peer_count = lax.axis_size("dom")
     steps = peer_count.bit_length() - 1
     me = lax.axis_index("dom")
-    ctf = ctf_ref[0]
-    ctf_t = ctf.T
     zero = jnp.zeros((OVL, pixels), jnp.float32)
 
     def place_of(k, j):
@@ -29,60 +27,61 @@
         return flipped * own_count + local_ref[k, j]
 
     places = [[place_of(k, j) for j in range(neighbours)] for k in range(own_count)]
-    edge_rows = []
-    for k in range(own_count):
-        lower, upper = zero, zero
-        for j in range(neighbours):
-            q = places[k][j]
-            s = side_ref[k, j]
-            w = weight_ref[k, j]
-            low_band = low_ref[jnp.minimum(q, half - 1), s, 0]
-            high_band = high_ref[jnp.maximum(q - half, 0), s, 0]
-            band = jnp.where(q < half, low_band, high_band).astype(jnp.float32)
-            lower = lower + jnp.where(s == 0, w, 0.0) * band
-            upper = upper + jnp.where(s == 1, w, 0.0) * band
-        residual_ref[k] = image_ref[k, 0].astype(jnp.float32) - proj_ref[k, 0].astype(jnp.float32)
-        residual_ref[k, :OVL] = residual_ref[k, :OVL] - upper
-        residual_ref[k, pixels - OVL :] = residual_ref[k, pixels - OVL :] - lower
-        residual = residual_ref[k].astype(jnp.bfloat16)
-        smoothed = jnp.dot(ctf, residual, preferred_element_type=jnp.float32).astype(jnp.bfloat16)
-        filtered = jnp.dot(smoothed, ctf_t, preferred_element_type=jnp.float32)
-        score_ref[0, k] = jnp.full(score_ref.shape[2:], jnp.sum(filtered * filtered), jnp.float32)
-        reverse = jnp.dot(
-            ctf_t, filtered.astype(jnp.bfloat16), preferred_element_type=jnp.float32
-        ).astype(jnp.bfloat16)
-        weighted = jnp.dot(reverse, ctf, preferred_element_type=jnp.float32).astype(jnp.bfloat16)
-        weighted_ref[k, 0] = weighted
-        edge_rows.append(
-            (weighted[pixels - OVL :].astype(jnp.float32), weighted[:OVL].astype(jnp.float32))
-        )
-
-    return_ref[...] = jnp.zeros_like(return_ref)
-    for k in range(own_count):
-        bottom_rows, top_rows = edge_rows[k]
-
-        for j in range(neighbours):
-            q = places[k][j]
-            s = side_ref[k, j]
-            rows = jnp.where(s == 0, bottom_rows, top_rows)
-            part = (weight_ref[k, j] * rows).astype(jnp.bfloat16).astype(jnp.float32)
-            return_ref[q, s] = return_ref[q, s] + part
-    kept_ref[:, :, 0] = return_ref[:half]
-    sent_ref[:, :, 0] = return_ref[half:].astype(jnp.bfloat16)
-
+    for t in range(ctf_ref.shape[0]):
+        ctf = ctf_ref[t]
+        ctf_t = ctf.T
+        edge_rows = []
+        for k in range(own_count):
+            lower, upper = zero, zero
+            for j in range(neighbours):
+                q = places[k][j]
+                s = side_ref[k, j]
+                w = weight_ref[k, j]
+                low_band = low_ref[jnp.minimum(q, half - 1), s, t]
+                high_band = high_ref[jnp.maximum(q - half, 0), s, t]
+                band = jnp.where(q < half, low_band, high_band).astype(jnp.float32)
+                lower = lower + jnp.where(s == 0, w, 0.0) * band
+                upper = upper + jnp.where(s == 1, w, 0.0) * band
+            residual_ref[k] = image_ref[k, t].astype(jnp.float32) - proj_ref[k, t].astype(jnp.float32)
+            residual_ref[k, :OVL] = residual_ref[k, :OVL] - upper
+            residual_ref[k, pixels - OVL :] = residual_ref[k, pixels - OVL :] - lower
+            residual = residual_ref[k].astype(jnp.bfloat16)
+            smoothed = jnp.dot(ctf, residual, preferred_element_type=jnp.float32).astype(jnp.bfloat16)
+            filtered = jnp.dot(smoothed, ctf_t, preferred_element_type=jnp.float32)
+            score_ref[t, k] = jnp.full(score_ref.shape[2:], jnp.sum(filtered * filtered), jnp.float32)
+            reverse = jnp.dot(
+                ctf_t, filtered.astype(jnp.bfloat16), preferred_element_type=jnp.float32
+            ).astype(jnp.bfloat16)
+            weighted = jnp.dot(reverse, ctf, preferred_element_type=jnp.float32).astype(jnp.bfloat16)
+            weighted_ref[k, t] = weighted
+            edge_rows.append(
+                (weighted[pixels - OVL :].astype(jnp.float32), weighted[:OVL].astype(jnp.float32))
+            )
+
+        return_ref[...] = jnp.zeros_like(return_ref)
+        for k in range(own_count):
+            bottom_rows, top_rows = edge_rows[k]
+            for j in range(neighbours):
+                q = places[k][j]
+                s = side_ref[k, j]
+                rows = jnp.where(s == 0, bottom_rows, top_rows)
+                part = (weight_ref[k, j] * rows).astype(jnp.bfloat16).astype(jnp.float32)
+                return_ref[q, s] = return_ref[q, s] + part
+        kept_ref[:, :, t] = return_ref[:half]
+        sent_ref[:, :, t] = return_ref[half:].astype(jnp.bfloat16)
 
 def middle(owner, local, side, weight, images, projected, edges_low, edges_high, ctf_filter):
     own_count, tilt_count, pixels, _ = images.shape
     half = edges_low.shape[0]
     total = 2 * half
-    tiles = pl.BlockSpec((own_count, 1, pixels, pixels), lambda t: (0, t, 0, 0))
-    halves = pl.BlockSpec((half, 2, 1, OVL, pixels), lambda t: (0, 0, t, 0, 0))
+    tiles = pl.BlockSpec(images.shape, lambda t: (0, 0, 0, 0))
+    halves = pl.BlockSpec(edges_low.shape, lambda t: (0, 0, 0, 0, 0))
     smem = pl.BlockSpec(memory_space=pltpu.SMEM)
     flops = own_count * tilt_count * 8 * pixels**3
     moved = 2 * images.size * 3 + 10 * edges_low.size + 2 * ctf_filter.size
     return pl.pallas_call(
         middle_kernel,
-        grid=(tilt_count,),
+        grid=(1,),
         in_specs=[
             smem,
             smem,
@@ -92,11 +91,11 @@
             tiles,
             halves,
             halves,
-            pl.BlockSpec((1, pixels, pixels), lambda t: (t, 0, 0)),
+            pl.BlockSpec(ctf_filter.shape, lambda t: (0, 0, 0)),
         ],
         out_specs=[
             tiles,
-            pl.BlockSpec((1, own_count, 8, 128), lambda t: (t, 0, 0, 0)),
+            pl.BlockSpec((tilt_count, own_count, 8, 128), lambda t: (0, 0, 0, 0)),
             halves,
             halves,
         ],

time: 54.3 us -> 54 us (level)
  no operation moved by 1% of the time
where the time goes in v19:
time: 54 us; the launch traced here: 53.8 us
  waiting for transfers between devices  22.2 us (41%)
  starting transfers between devices  17.8 us (33%)
  Pallas kernels  5.19 us (10%)
  other arithmetic  3.73 us (7%)
  matrix products  2.12 us (4%)
  local copies, waits for them, and re-layouts  1.85 us (3%)
  between operations  0.83 us (2%)
    ppermute x4, waiting for transfers between devices, on_device(): pieces.append(lax.ppermute(edges_all, 'dom', pairs))  8.84 us
    ppermute x4, starting transfers between devices, on_device(): pieces.append(lax.ppermute(edges_all, 'dom', pairs))  7.65 us
    ppermute x4, starting transfers between devices, on_device(): kept = kept + lax.ppermute(given, 'dom', pairs).astype(jnp.float32)  6.8 us
    ppermute x4, waiting for transfers between devices, on_device(): kept = kept + lax.ppermute(given, 'dom', pairs).astype(jnp.float32)  5.46 us
    pallas_call x1, Pallas kernels, middle(): pl.pallas_call(middle_kernel, grid=(1,), in_specs=[smem, smem, smem, smem...  5.19 us
    ppermute x1, waiting for transfers between devices, on_device(): given = lax.ppermute(given.astype(jnp.bfloat16), 'tilt', [(0, 1), (1, 0)])  2.92 us
    ppermute x1, waiting for transfers between devices, on_device(): parts = lax.ppermute(parts, 'tilt', [(0, 1), (1, 0)]).astype(jnp.float32)  1.94 us
    ppermute x1, waiting for transfers between devices, on_device(): lax.ppermute(edges_all, 'dom', [(i, i ^ 1) for i in range(peer_count)])  1.9 us
  transfers between devices with their start and end apart: 12, of which 10 were waited for; matrix products, arithmetic and copies ran while one was open for 3% of the time, Pallas kernels for 0%

profile of v19, /device:TPU:0, one launch (start us, length us, event | category | flops | bytes accessed | tf_op | source)
XLA Modules:
  0.0 53.8 jit_solution(3917440720326382836)
XLA Ops:
  0.7 0.9 %copy-done = bf16[2,256,256]{2,1,0:T(8,128)(2,1)S(1)} copy-done((bf16[2,256,256]{2,1,0:T(8,128)(2,1)S(1)}, bf16[2,256,256]{2,1,0:T(8,128)(2,1)}, u32[]{:S(2)}) %copy-start) | copy-done | bytes 262168
  1.6 1.3 %fusion = bf16[2,2,256,256]{3,2,0,1:T(8,128)(2,1)S(1)} fusion(bf16[2,256,256]{2,1,0:T(8,128)(2,1)S(1)} %copy-done, bf16[2,256,256]{2,1,0:T(8,128)(2,1)} %param.13), kind=kOutput, calls=%fused_computation.3 | convolution fusion | flops 134479872 | bytes 1048576 | tf_op jit(solution)/shard_map/kij,tlj->ktil/dot_general | solution.py:139
  3.2 4.1 %collective-permute-start = (bf16[2,2,2,16,256]{4,3,2,1,0:T(8,128)(2,1)S(1)}, bf16[2,2,2,16,256]{4,3,2,1,0:T(8,128)(2,1)S(1)}, u32[]{:S(2)}, u32[]{:S(2)}) collective-permute-start(bf16[2,2,2,16,256]{4,3,2,1,0:T(8,128)(2,1)S(1)} %get-tuple-element.41), channel_id=1, source_target_pairs={{0,8},{1,9},{2,10},{3,11},{4,12},{5,13},{6,14},{7,15},{8,0},{9,1},... | collective-permute-start | bytes 196616 | tf_op jit(solution)/shard_map/ppermute | solution.py:153
  7.3 3.6 %collective-permute-done = bf16[2,2,2,16,256]{4,3,2,1,0:T(8,128)(2,1)S(1)} collective-permute-done((bf16[2,2,2,16,256]{4,3,2,1,0:T(8,128)(2,1)S(1)}, bf16[2,2,2,16,256]{4,3,2,1,0:T(8,128)(2,1)S(1)}, u32[]{:S(2)}, u32[]{:S(2)}) %collective-permute-start) | collective-permute-done | bytes 65568 | tf_op jit(solution)/shard_map/ppermute | solution.py:153
  11.6 1.5 %collective-permute-start.2 = (bf16[4,2,2,16,256]{4,3,2,1,0:T(8,128)(2,1)S(1)}, bf16[4,2,2,16,256]{4,3,2,1,0:T(8,128)(2,1)S(1)}, u32[]{:S(2)}, u32[]{:S(2)}) collective-permute-start(bf16[4,2,2,16,256]{4,3,2,1,0:T(8,128)(2,1)S(1)} %pad_maximum_fusion), channel_id=1, source_target_pairs={{0,2},{1,3},{2,0},{3,1},{4,6},{5,7},{6,4},{7,5},{8,10},{9,11},{10,... | collective-permute-start | bytes 393224 | tf_op jit(solution)/shard_map/ppermute | solution.py:153
  13.1 1.4 %collective-permute-start.3 = (bf16[4,2,2,16,256]{4,3,2,1,0:T(8,128)(2,1)S(1)}, bf16[4,2,2,16,256]{4,3,2,1,0:T(8,128)(2,1)S(1)}, u32[]{:S(2)}, u32[]{:S(2)}) collective-permute-start(bf16[4,2,2,16,256]{4,3,2,1,0:T(8,128)(2,1)S(1)} %pad_maximum_fusion), channel_id=1, source_target_pairs={{0,6},{1,7},{2,4},{3,5},{4,2},{5,3},{6,0},{7,1},{8,14},{9,15},{10,... | collective-permute-start | bytes 393224 | tf_op jit(solution)/shard_map/ppermute | solution.py:153
  14.6 2.8 %collective-permute-done.1 = bf16[4,2,2,16,256]{4,3,2,1,0:T(8,128)(2,1)S(1)} collective-permute-done((bf16[4,2,2,16,256]{4,3,2,1,0:T(8,128)(2,1)S(1)}, bf16[4,2,2,16,256]{4,3,2,1,0:T(8,128)(2,1)S(1)}, u32[]{:S(2)}, u32[]{:S(2)}) %collective-permute-start.1) | collective-permute-done | bytes 131104 | tf_op jit(solution)/shard_map/ppermute | solution.py:153
  18.2 1.6 %collective-permute-done.3 = bf16[4,2,2,16,256]{4,3,2,1,0:T(8,128)(2,1)S(1)} collective-permute-done((bf16[4,2,2,16,256]{4,3,2,1,0:T(8,128)(2,1)S(1)}, bf16[4,2,2,16,256]{4,3,2,1,0:T(8,128)(2,1)S(1)}, u32[]{:S(2)}, u32[]{:S(2)}) %collective-permute-start.3) | collective-permute-done | bytes 131104 | tf_op jit(solution)/shard_map/ppermute | solution.py:153
  19.9 1.9 %collective-permute-done.4.high_ref = bf16[16,2,2,16,256]{4,3,2,1,0:T(8,128)(2,1)S(1)} collective-permute-done((bf16[16,2,2,16,256]{4,3,2,1,0:T(8,128)(2,1)S(1)}, bf16[16,2,2,16,256]{4,3,2,1,0:T(8,128)(2,1)S(1)}, u32[]{:S(2)}, u32[]{:S(2)}) %collective-permute-start.4) | collective-permute-done | bytes 524320 | tf_op jit(solution)/shard_map/ppermute | solution.py:155
  21.8 0.8 %copy-done.5 = bf16[16,2,2,16,256]{4,3,2,1,0:T(8,128)(2,1)} copy-done((bf16[16,2,2,16,256]{4,3,2,1,0:T(8,128)(2,1)}, bf16[16,2,2,16,256]{4,3,2,1,0:T(8,128)(2,1)S(1)}, u32[]{:S(2)}) %copy-start.5) | copy-done | bytes 524312
  22.6 5.2 %shard_map.104 = (bf16[2,2,256,256]{3,2,1,0:T(8,128)(2,1)}, f32[2,2,8,128]{3,2,1,0:T(8,128)}, f32[16,2,2,16,256]{4,3,2,1,0:T(8,128)}, bf16[16,2,2,16,256]{4,3,2,1,0:T(8,128)(2,1)}) custom-call(s32[2,2,8]{2,1,0:T(2,128)} %owner_ref.1, s32[2,16]{1,0:T(2,128)} %local_ref.1, s32[2,16]{1,0:T(2,128)} %side_ref.1, f32[2,16]{1,0:T(2,128)} %weight_ref.1, ...), custom_call_target="tpu_custom_call" | custom-call | flops 536870912 | bytes 4456448 | tf_op jit(solution)/shard_map/pallas_call | solution.py:82
  27.9 0.8 %slice_reduce_fusion = f32[2]{0:T(128)S(1)} fusion(f32[2,2,8,128]{3,2,1,0:T(8,128)} %get-tuple-element.33), kind=kLoop, calls=%fused_computation.38 | loop fusion | flops 2 | bytes 24 | tf_op jit(solution)/shard_map/reduce_sum | solution.py:161
  28.7 1.2 %collective-permute-done.5 = bf16[16,2,2,16,256]{4,3,2,1,0:T(8,128)(2,1)S(1)} collective-permute-done((bf16[16,2,2,16,256]{4,3,2,1,0:T(8,128)(2,1)}, bf16[16,2,2,16,256]{4,3,2,1,0:T(8,128)(2,1)S(1)}, u32[]{:S(2)}, u32[]{:S(2)}) %collective-permute-start.5) | collective-permute-done | bytes 524320 | tf_op jit(solution)/shard_map/ppermute | solution.py:174
  29.9 1.4 %fusion.21 = (bf16[16,2,2,16,256]{4,3,2,1,0:T(8,128)(2,1)S(1)}, f32[16,2,2,16,256]{4,3,2,1,0:T(8,128)S(1)}) fusion(f32[16,2,2,16,256]{4,3,2,1,0:T(8,128)} %get-tuple-element.31, bf16[16,2,2,16,256]{4,3,2,1,0:T(8,128)(2,1)S(1)} %collective-permute-done.5), kind=kLoop, calls=%fused_computation.46 | loop fusion | flops 786432 | bytes 3145728 | tf_op jit(solution)/shard_map/convert.3
  31.3 0.9 %collective-permute-start.6 = (bf16[4,2,2,16,256]{4,3,2,1,0:T(8,128)(2,1)S(1)}, bf16[4,2,2,16,256]{4,3,2,1,0:T(8,128)(2,1)S(1)}, u32[]{:S(2)}, u32[]{:S(2)}) collective-permute-start(bf16[4,2,2,16,256]{4,3,2,1,0:T(8,128)(2,1)S(1)} %get-tuple-element.36), channel_id=1, source_target_pairs={{0,4},{1,5},{2,6},{3,7},{4,0},{5,1},{6,2},{7,3},{8,12},{9,13},{10,... | collective-permute-start | bytes 393224 | tf_op jit(solution)/shard_map/ppermute | solution.py:185
  32.3 1.0 %collective-permute-start.7 = (bf16[4,2,2,16,256]{4,3,2,1,0:T(8,128)(2,1)S(1)}, bf16[4,2,2,16,256]{4,3,2,1,0:T(8,128)(2,1)S(1)}, u32[]{:S(2)}, u32[]{:S(2)}) collective-permute-start(bf16[4,2,2,16,256]{4,3,2,1,0:T(8,128)(2,1)S(1)} %get-tuple-element.38), channel_id=1, source_target_pairs={{0,2},{1,3},{2,0},{3,1},{4,6},{5,7},{6,4},{7,5},{8,10},{9,11},{10,... | collective-permute-start | bytes 393224 | tf_op jit(solution)/shard_map/ppermute | solution.py:185
  33.3 1.6 %collective-permute-start.8 = (bf16[4,2,2,16,256]{4,3,2,1,0:T(8,128)(2,1)S(1)}, bf16[4,2,2,16,256]{4,3,2,1,0:T(8,128)(2,1)S(1)}, u32[]{:S(2)}, u32[]{:S(2)}) collective-permute-start(bf16[4,2,2,16,256]{4,3,2,1,0:T(8,128)(2,1)S(1)} %get-tuple-element.37), channel_id=1, source_target_pairs={{0,6},{1,7},{2,4},{3,5},{4,2},{5,3},{6,0},{7,1},{8,14},{9,15},{10,... | collective-permute-start | bytes 393224 | tf_op jit(solution)/shard_map/ppermute | solution.py:185
  34.9 2.8 %collective-permute-done.6 = bf16[4,2,2,16,256]{4,3,2,1,0:T(8,128)(2,1)S(1)} collective-permute-done((bf16[4,2,2,16,256]{4,3,2,1,0:T(8,128)(2,1)S(1)}, bf16[4,2,2,16,256]{4,3,2,1,0:T(8,128)(2,1)S(1)}, u32[]{:S(2)}, u32[]{:S(2)}) %collective-permute-start.6) | collective-permute-done | bytes 131104 | tf_op jit(solution)/shard_map/ppermute | solution.py:185
  37.8 2.6 %collective-permute-done.7 = bf16[4,2,2,16,256]{4,3,2,1,0:T(8,128)(2,1)S(1)} collective-permute-done((bf16[4,2,2,16,256]{4,3,2,1,0:T(8,128)(2,1)S(1)}, bf16[4,2,2,16,256]{4,3,2,1,0:T(8,128)(2,1)S(1)}, u32[]{:S(2)}, u32[]{:S(2)}) %collective-permute-start.7) | collective-permute-done | bytes 131104 | tf_op jit(solution)/shard_map/ppermute | solution.py:185
  40.5 3.2 %collective-permute-start.9 = (bf16[2,2,2,16,256]{4,3,2,1,0:T(8,128)(2,1)S(1)}, bf16[2,2,2,16,256]{4,3,2,1,0:T(8,128)(2,1)S(1)}, u32[]{:S(2)}, u32[]{:S(2)}) collective-permute-start(bf16[2,2,2,16,256]{4,3,2,1,0:T(8,128)(2,1)S(1)} %slice.157), channel_id=1, source_target_pairs={{0,8},{1,9},{2,10},{3,11},{4,12},{5,13},{6,14},{7,15},{8,0},{9,1},... | collective-permute-start | bytes 196616 | tf_op jit(solution)/shard_map/ppermute | solution.py:185
  43.7 1.6 %collective-permute-start.11 = (bf16[3,2]{1,0:T(4,128)(2,1)S(1)}, bf16[3,2]{1,0:T(4,128)(2,1)S(1)}, u32[]{:S(2)}, u32[]{:S(2)}) collective-permute-start(bf16[3,2]{1,0:T(4,128)(2,1)S(1)} %pad_maximum_fusion.2), channel_id=1, source_target_pairs={{0,16},{16,0},{1,17},{17,1},{2,18},{18,2},{3,19},{19,3},{4,20},{20... | collective-permute-start | bytes 44 | tf_op jit(solution)/shard_map/ppermute | solution.py:170
  45.4 1.9 %collective-permute-done.11 = bf16[3,2]{1,0:T(4,128)(2,1)S(1)} collective-permute-done((bf16[3,2]{1,0:T(4,128)(2,1)S(1)}, bf16[3,2]{1,0:T(4,128)(2,1)S(1)}, u32[]{:S(2)}, u32[]{:S(2)}) %collective-permute-start.11) | collective-permute-done | bytes 44 | tf_op jit(solution)/shard_map/ppermute | solution.py:170
  48.0 1.6 %collective-permute-start.10 = (bf16[2,128,256]{2,1,0:T(8,128)(2,1)S(1)}, bf16[2,128,256]{2,1,0:T(8,128)(2,1)S(1)}, u32[]{:S(2)}, u32[]{:S(2)}) collective-permute-start(bf16[2,128,256]{2,1,0:T(8,128)(2,1)S(1)} %dynamic-slice_convert_fusion), channel_id=1, source_target_pairs={{0,16},{16,0},{1,17},{17,1},{2,18},{18,2},{3,19},{19,3},{4,20},{20... | collective-permute-start | bytes 393224 | tf_op jit(solution)/shard_map/ppermute | solution.py:208
  50.1 2.9 %collective-permute-done.10 = bf16[2,128,256]{2,1,0:T(8,128)(2,1)S(1)} collective-permute-done((bf16[2,128,256]{2,1,0:T(8,128)(2,1)S(1)}, bf16[2,128,256]{2,1,0:T(8,128)(2,1)S(1)}, u32[]{:S(2)}, u32[]{:S(2)}) %collective-permute-start.10) | collective-permute-done | bytes 131104 | tf_op jit(solution)/shard_map/ppermute | solution.py:208
  (39 shorter events, 4.1 us)
Async XLA Ops:
  0.6 1.0 %copy-start = (bf16[2,256,256]{2,1,0:T(8,128)(2,1)S(1)}, bf16[2,256,256]{2,1,0:T(8,128)(2,1)}, u32[]{:S(2)}) copy-start(bf16[2,256,256]{2,1,0:T(8,128)(2,1)} %param.16) | copy-start | bytes 786436
  0.6 2.2 %copy-start.2 = (bf16[2,256,256]{2,1,0:T(8,128)(2,1)S(1)}, bf16[2,256,256]{2,1,0:T(8,128)(2,1)}, u32[]{:S(2)}) copy-start(bf16[2,256,256]{2,1,0:T(8,128)(2,1)} %param.15) | copy-start | bytes 786436
  3.2 15.0 %copy-start.1 = (bf16[2,2,256,256]{3,2,1,0:T(8,128)(2,1)}, bf16[2,2,256,256]{3,2,1,0:T(8,128)(2,1)S(1)}, u32[]{:S(2)}) copy-start(bf16[2,2,256,256]{3,2,1,0:T(8,128)(2,1)S(1)} %fusion.2.proj_ref) | copy-start | bytes 1572868
  3.2 7.7 %collective-permute-start = (bf16[2,2,2,16,256]{4,3,2,1,0:T(8,128)(2,1)S(1)}, bf16[2,2,2,16,256]{4,3,2,1,0:T(8,128)(2,1)S(1)}, u32[]{:S(2)}, u32[]{:S(2)}) collective-permute-start(bf16[2,2,2,16,256]{4,3,2,1,0:T(8,128)(2,1)S(1)} %get-tuple-element.41), channel_id=1, source_target_pairs={{0,8},{1,9},{2,10},{3,11},{4,12},{5,13},{6,14},{7,15},{8,0},{9,1},... | collective-permute-start | bytes 196616 | tf_op jit(solution)/shard_map/ppermute | solution.py:153
  11.0 6.4 %collective-permute-start.1 = (bf16[4,2,2,16,256]{4,3,2,1,0:T(8,128)(2,1)S(1)}, bf16[4,2,2,16,256]{4,3,2,1,0:T(8,128)(2,1)S(1)}, u32[]{:S(2)}, u32[]{:S(2)}) collective-permute-start(bf16[4,2,2,16,256]{4,3,2,1,0:T(8,128)(2,1)S(1)} %pad_maximum_fusion), channel_id=1, source_target_pairs={{0,4},{1,5},{2,6},{3,7},{4,0},{5,1},{6,2},{7,3},{8,12},{9,13},{10,... | collective-permute-start | bytes 393224 | tf_op jit(solution)/shard_map/ppermute | solution.py:153
  11.6 6.5 %collective-permute-start.2 = (bf16[4,2,2,16,256]{4,3,2,1,0:T(8,128)(2,1)S(1)}, bf16[4,2,2,16,256]{4,3,2,1,0:T(8,128)(2,1)S(1)}, u32[]{:S(2)}, u32[]{:S(2)}) collective-permute-start(bf16[4,2,2,16,256]{4,3,2,1,0:T(8,128)(2,1)S(1)} %pad_maximum_fusion), channel_id=1, source_target_pairs={{0,2},{1,3},{2,0},{3,1},{4,6},{5,7},{6,4},{7,5},{8,10},{9,11},{10,... | collective-permute-start | bytes 393224 | tf_op jit(solution)/shard_map/ppermute | solution.py:153
  13.1 6.7 %collective-permute-start.3 = (bf16[4,2,2,16,256]{4,3,2,1,0:T(8,128)(2,1)S(1)}, bf16[4,2,2,16,256]{4,3,2,1,0:T(8,128)(2,1)S(1)}, u32[]{:S(2)}, u32[]{:S(2)}) collective-permute-start(bf16[4,2,2,16,256]{4,3,2,1,0:T(8,128)(2,1)S(1)} %pad_maximum_fusion), channel_id=1, source_target_pairs={{0,6},{1,7},{2,4},{3,5},{4,2},{5,3},{6,0},{7,1},{8,14},{9,15},{10,... | collective-permute-start | bytes 393224 | tf_op jit(solution)/shard_map/ppermute | solution.py:153
  19.8 2.0 %copy-start.3 = (bf16[16,2,2,16,256]{4,3,2,1,0:T(8,128)(2,1)}, bf16[16,2,2,16,256]{4,3,2,1,0:T(8,128)(2,1)S(1)}, u32[]{:S(2)}) copy-start(bf16[16,2,2,16,256]{4,3,2,1,0:T(8,128)(2,1)S(1)} %constant_dynamic-update-slice_fusion.low_ref) | copy-start | bytes 1572868
  19.8 2.0 %collective-permute-start.4 = (bf16[16,2,2,16,256]{4,3,2,1,0:T(8,128)(2,1)S(1)}, bf16[16,2,2,16,256]{4,3,2,1,0:T(8,128)(2,1)S(1)}, u32[]{:S(2)}, u32[]{:S(2)}) collective-permute-start(bf16[16,2,2,16,256]{4,3,2,1,0:T(8,128)(2,1)S(1)} %constant_dynamic-update-slice_fusion.low_ref), channel_id=1, source_target_pairs={{0,1},{1,0},{2,3},{3,2},{4,5},{5,4},{6,7},{7,6},{8,9},{9,8},{10,11... | collective-permute-start | bytes 1572872 | tf_op jit(solution)/shard_map/ppermute | solution.py:155
  21.8 0.8 %copy-start.5 = (bf16[16,2,2,16,256]{4,3,2,1,0:T(8,128)(2,1)}, bf16[16,2,2,16,256]{4,3,2,1,0:T(8,128)(2,1)S(1)}, u32[]{:S(2)}) copy-start(bf16[16,2,2,16,256]{4,3,2,1,0:T(8,128)(2,1)S(1)} %collective-permute-done.4.high_ref) | copy-start | bytes 1572868
  27.8 2.1 %collective-permute-start.5 = (bf16[16,2,2,16,256]{4,3,2,1,0:T(8,128)(2,1)}, bf16[16,2,2,16,256]{4,3,2,1,0:T(8,128)(2,1)S(1)}, u32[]{:S(2)}, u32[]{:S(2)}) collective-permute-start(bf16[16,2,2,16,256]{4,3,2,1,0:T(8,128)(2,1)} %get-tuple-element.32), channel_id=1, source_target_pairs={{0,1},{1,0},{2,3},{3,2},{4,5},{5,4},{6,7},{7,6},{8,9},{9,8},{10,11... | collective-permute-start | bytes 1572872 | tf_op jit(solution)/shard_map/ppermute | solution.py:174
  31.3 6.4 %collective-permute-start.6 = (bf16[4,2,2,16,256]{4,3,2,1,0:T(8,128)(2,1)S(1)}, bf16[4,2,2,16,256]{4,3,2,1,0:T(8,128)(2,1)S(1)}, u32[]{:S(2)}, u32[]{:S(2)}) collective-permute-start(bf16[4,2,2,16,256]{4,3,2,1,0:T(8,128)(2,1)S(1)} %get-tuple-element.36), channel_id=1, source_target_pairs={{0,4},{1,5},{2,6},{3,7},{4,0},{5,1},{6,2},{7,3},{8,12},{9,13},{10,... | collective-permute-start | bytes 393224 | tf_op jit(solution)/shard_map/ppermute | solution.py:185
  32.3 8.1 %collective-permute-start.7 = (bf16[4,2,2,16,256]{4,3,2,1,0:T(8,128)(2,1)S(1)}, bf16[4,2,2,16,256]{4,3,2,1,0:T(8,128)(2,1)S(1)}, u32[]{:S(2)}, u32[]{:S(2)}) collective-permute-start(bf16[4,2,2,16,256]{4,3,2,1,0:T(8,128)(2,1)S(1)} %get-tuple-element.38), channel_id=1, source_target_pairs={{0,2},{1,3},{2,0},{3,1},{4,6},{5,7},{6,4},{7,5},{8,10},{9,11},{10,... | collective-permute-start | bytes 393224 | tf_op jit(solution)/shard_map/ppermute | solution.py:185
  33.3 7.0 %collective-permute-start.8 = (bf16[4,2,2,16,256]{4,3,2,1,0:T(8,128)(2,1)S(1)}, bf16[4,2,2,16,256]{4,3,2,1,0:T(8,128)(2,1)S(1)}, u32[]{:S(2)}, u32[]{:S(2)}) collective-permute-start(bf16[4,2,2,16,256]{4,3,2,1,0:T(8,128)(2,1)S(1)} %get-tuple-element.37), channel_id=1, source_target_pairs={{0,6},{1,7},{2,4},{3,5},{4,2},{5,3},{6,0},{7,1},{8,14},{9,15},{10,... | collective-permute-start | bytes 393224 | tf_op jit(solution)/shard_map/ppermute | solution.py:185
  40.4 5.0 %copy-start.4 = (bf16[2,2,256,256]{3,2,1,0:T(8,128)(2,1)S(1)}, bf16[2,2,256,256]{3,2,1,0:T(8,128)(2,1)}, u32[]{:S(2)}) copy-start(bf16[2,2,256,256]{3,2,1,0:T(8,128)(2,1)} %get-tuple-element.30) | copy-start | bytes 1572868
  40.5 6.9 %collective-permute-start.9 = (bf16[2,2,2,16,256]{4,3,2,1,0:T(8,128)(2,1)S(1)}, bf16[2,2,2,16,256]{4,3,2,1,0:T(8,128)(2,1)S(1)}, u32[]{:S(2)}, u32[]{:S(2)}) collective-permute-start(bf16[2,2,2,16,256]{4,3,2,1,0:T(8,128)(2,1)S(1)} %slice.157), channel_id=1, source_target_pairs={{0,8},{1,9},{2,10},{3,11},{4,12},{5,13},{6,14},{7,15},{8,0},{9,1},... | collective-permute-start | bytes 196616 | tf_op jit(solution)/shard_map/ppermute | solution.py:185
  43.7 3.6 %collective-permute-start.11 = (bf16[3,2]{1,0:T(4,128)(2,1)S(1)}, bf16[3,2]{1,0:T(4,128)(2,1)S(1)}, u32[]{:S(2)}, u32[]{:S(2)}) collective-permute-start(bf16[3,2]{1,0:T(4,128)(2,1)S(1)} %pad_maximum_fusion.2), channel_id=1, source_target_pairs={{0,16},{16,0},{1,17},{17,1},{2,18},{18,2},{3,19},{19,3},{4,20},{20... | collective-permute-start | bytes 44 | tf_op jit(solution)/shard_map/ppermute | solution.py:170
  48.0 5.0 %collective-permute-start.10 = (bf16[2,128,256]{2,1,0:T(8,128)(2,1)S(1)}, bf16[2,128,256]{2,1,0:T(8,128)(2,1)S(1)}, u32[]{:S(2)}, u32[]{:S(2)}) collective-permute-start(bf16[2,128,256]{2,1,0:T(8,128)(2,1)S(1)} %dynamic-slice_convert_fusion), channel_id=1, source_target_pairs={{0,16},{16,0},{1,17},{17,1},{2,18},{18,2},{3,19},{19,3},{4,20},{20... | collective-permute-start | bytes 393224 | tf_op jit(solution)/shard_map/ppermute | solution.py:208

commit v20 on v19

--- a/solution.py
+++ b/solution.py
@@ -67,7 +67,7 @@
                 rows = jnp.where(s == 0, bottom_rows, top_rows)
                 part = (weight_ref[k, j] * rows).astype(jnp.bfloat16).astype(jnp.float32)
                 return_ref[q, s] = return_ref[q, s] + part
-        kept_ref[:, :, t] = return_ref[:half]
+        kept_ref[:, :, t] = return_ref[:half].astype(jnp.bfloat16)
         sent_ref[:, :, t] = return_ref[half:].astype(jnp.bfloat16)
 
 def middle(owner, local, side, weight, images, projected, edges_low, edges_high, ctf_filter):
@@ -102,7 +102,7 @@
         out_shape=[
             jax.ShapeDtypeStruct(images.shape, jnp.bfloat16),
             jax.ShapeDtypeStruct((tilt_count, own_count, 8, 128), jnp.float32),
-            jax.ShapeDtypeStruct(edges_low.shape, jnp.float32),
+            jax.ShapeDtypeStruct(edges_low.shape, jnp.bfloat16),
             jax.ShapeDtypeStruct(edges_low.shape, jnp.bfloat16),
         ],
         scratch_shapes=[
@@ -171,7 +171,9 @@
         scores = scale * (score_part + (parts[0] + (parts[1] + parts[2])))
 
     pairs = [(i, i ^ 1) for i in range(peer_count)]
-    returned = kept_half + lax.ppermute(sent_half, "dom", pairs).astype(jnp.float32)
+    returned = kept_half.astype(jnp.float32) + lax.ppermute(sent_half, "dom", pairs).astype(
+        jnp.float32
+    )
     for stage in [tuple(reversed(stage)) for stage in reversed(stages[:-1])]:
         count = 2 ** len(stage)
         share = returned.shape[0] // count

time: 54 us -> 53.8 us (level)
  no operation moved by 1% of the time
where the time goes in v20:
time: 53.8 us; the launch traced here: 53.5 us
  waiting for transfers between devices  22.2 us (41%)
  starting transfers between devices  17.8 us (33%)
  Pallas kernels  5.06 us (9%)
  other arithmetic  3.57 us (7%)
  matrix products  2.11 us (4%)
  local copies, waits for them, and re-layouts  1.86 us (3%)
  between operations  0.83 us (2%)
    ppermute x4, waiting for transfers between devices, on_device(): pieces.append(lax.ppermute(edges_all, 'dom', pairs))  8.84 us
    ppermute x4, starting transfers between devices, on_device(): pieces.append(lax.ppermute(edges_all, 'dom', pairs))  7.65 us
    ppermute x4, starting transfers between devices, on_device(): kept = kept + lax.ppermute(given, 'dom', pairs).astype(jnp.float32)  6.8 us
    ppermute x4, waiting for transfers between devices, on_device(): kept = kept + lax.ppermute(given, 'dom', pairs).astype(jnp.float32)  5.46 us
    pallas_call x1, Pallas kernels, middle(): pl.pallas_call(middle_kernel, grid=(1,), in_specs=[smem, smem, smem, smem...  5.06 us
    ppermute x1, waiting for transfers between devices, on_device(): given = lax.ppermute(given.astype(jnp.bfloat16), 'tilt', [(0, 1), (1, 0)])  2.93 us
    ppermute x1, waiting for transfers between devices, on_device(): parts = lax.ppermute(parts, 'tilt', [(0, 1), (1, 0)]).astype(jnp.float32)  1.94 us
    ppermute x1, waiting for transfers between devices, on_device(): lax.ppermute(edges_all, 'dom', [(i, i ^ 1) for i in range(peer_count)])  1.9 us
  transfers between devices with their start and end apart: 12, of which 10 were waited for; matrix products, arithmetic and copies ran while one was open for 3% of the time, Pallas kernels for 0%

profile of v20, /device:TPU:0, one launch (start us, length us, event | category | flops | bytes accessed | tf_op | source)
XLA Modules:
  0.0 53.5 jit_solution(11037859413465382029)
XLA Ops:
  0.7 0.9 %copy-done = bf16[2,256,256]{2,1,0:T(8,128)(2,1)S(1)} copy-done((bf16[2,256,256]{2,1,0:T(8,128)(2,1)S(1)}, bf16[2,256,256]{2,1,0:T(8,128)(2,1)}, u32[]{:S(2)}) %copy-start) | copy-done | bytes 262168
  1.6 1.3 %fusion = bf16[2,2,256,256]{3,2,0,1:T(8,128)(2,1)S(1)} fusion(bf16[2,256,256]{2,1,0:T(8,128)(2,1)S(1)} %copy-done, bf16[2,256,256]{2,1,0:T(8,128)(2,1)} %param.13), kind=kOutput, calls=%fused_computation.3 | convolution fusion | flops 134479872 | bytes 1048576 | tf_op jit(solution)/shard_map/kij,tlj->ktil/dot_general | solution.py:139
  3.2 4.1 %collective-permute-start = (bf16[2,2,2,16,256]{4,3,2,1,0:T(8,128)(2,1)S(1)}, bf16[2,2,2,16,256]{4,3,2,1,0:T(8,128)(2,1)S(1)}, u32[]{:S(2)}, u32[]{:S(2)}) collective-permute-start(bf16[2,2,2,16,256]{4,3,2,1,0:T(8,128)(2,1)S(1)} %get-tuple-element.41), channel_id=1, source_target_pairs={{0,8},{1,9},{2,10},{3,11},{4,12},{5,13},{6,14},{7,15},{8,0},{9,1},... | collective-permute-start | bytes 196616 | tf_op jit(solution)/shard_map/ppermute | solution.py:153
  7.3 3.6 %collective-permute-done = bf16[2,2,2,16,256]{4,3,2,1,0:T(8,128)(2,1)S(1)} collective-permute-done((bf16[2,2,2,16,256]{4,3,2,1,0:T(8,128)(2,1)S(1)}, bf16[2,2,2,16,256]{4,3,2,1,0:T(8,128)(2,1)S(1)}, u32[]{:S(2)}, u32[]{:S(2)}) %collective-permute-start) | collective-permute-done | bytes 65568 | tf_op jit(solution)/shard_map/ppermute | solution.py:153
  11.6 1.5 %collective-permute-start.2 = (bf16[4,2,2,16,256]{4,3,2,1,0:T(8,128)(2,1)S(1)}, bf16[4,2,2,16,256]{4,3,2,1,0:T(8,128)(2,1)S(1)}, u32[]{:S(2)}, u32[]{:S(2)}) collective-permute-start(bf16[4,2,2,16,256]{4,3,2,1,0:T(8,128)(2,1)S(1)} %pad_maximum_fusion), channel_id=1, source_target_pairs={{0,2},{1,3},{2,0},{3,1},{4,6},{5,7},{6,4},{7,5},{8,10},{9,11},{10,... | collective-permute-start | bytes 393224 | tf_op jit(solution)/shard_map/ppermute | solution.py:153
  13.1 1.4 %collective-permute-start.3 = (bf16[4,2,2,16,256]{4,3,2,1,0:T(8,128)(2,1)S(1)}, bf16[4,2,2,16,256]{4,3,2,1,0:T(8,128)(2,1)S(1)}, u32[]{:S(2)}, u32[]{:S(2)}) collective-permute-start(bf16[4,2,2,16,256]{4,3,2,1,0:T(8,128)(2,1)S(1)} %pad_maximum_fusion), channel_id=1, source_target_pairs={{0,6},{1,7},{2,4},{3,5},{4,2},{5,3},{6,0},{7,1},{8,14},{9,15},{10,... | collective-permute-start | bytes 393224 | tf_op jit(solution)/shard_map/ppermute | solution.py:153
  14.6 2.8 %collective-permute-done.1 = bf16[4,2,2,16,256]{4,3,2,1,0:T(8,128)(2,1)S(1)} collective-permute-done((bf16[4,2,2,16,256]{4,3,2,1,0:T(8,128)(2,1)S(1)}, bf16[4,2,2,16,256]{4,3,2,1,0:T(8,128)(2,1)S(1)}, u32[]{:S(2)}, u32[]{:S(2)}) %collective-permute-start.1) | collective-permute-done | bytes 131104 | tf_op jit(solution)/shard_map/ppermute | solution.py:153
  18.2 1.6 %collective-permute-done.3 = bf16[4,2,2,16,256]{4,3,2,1,0:T(8,128)(2,1)S(1)} collective-permute-done((bf16[4,2,2,16,256]{4,3,2,1,0:T(8,128)(2,1)S(1)}, bf16[4,2,2,16,256]{4,3,2,1,0:T(8,128)(2,1)S(1)}, u32[]{:S(2)}, u32[]{:S(2)}) %collective-permute-start.3) | collective-permute-done | bytes 131104 | tf_op jit(solution)/shard_map/ppermute | solution.py:153
  19.9 1.9 %collective-permute-done.4.high_ref = bf16[16,2,2,16,256]{4,3,2,1,0:T(8,128)(2,1)S(1)} collective-permute-done((bf16[16,2,2,16,256]{4,3,2,1,0:T(8,128)(2,1)S(1)}, bf16[16,2,2,16,256]{4,3,2,1,0:T(8,128)(2,1)S(1)}, u32[]{:S(2)}, u32[]{:S(2)}) %collective-permute-start.4) | collective-permute-done | bytes 524320 | tf_op jit(solution)/shard_map/ppermute | solution.py:155
  21.8 0.8 %copy-done.5 = bf16[16,2,2,16,256]{4,3,2,1,0:T(8,128)(2,1)} copy-done((bf16[16,2,2,16,256]{4,3,2,1,0:T(8,128)(2,1)}, bf16[16,2,2,16,256]{4,3,2,1,0:T(8,128)(2,1)S(1)}, u32[]{:S(2)}) %copy-start.5) | copy-done | bytes 524312
  22.6 5.1 %shard_map.104 = (bf16[2,2,256,256]{3,2,1,0:T(8,128)(2,1)}, f32[2,2,8,128]{3,2,1,0:T(8,128)}, bf16[16,2,2,16,256]{4,3,2,1,0:T(8,128)(2,1)}, bf16[16,2,2,16,256]{4,3,2,1,0:T(8,128)(2,1)}) custom-call(s32[2,2,8]{2,1,0:T(2,128)} %owner_ref.1, s32[2,16]{1,0:T(2,128)} %local_ref.1, s32[2,16]{1,0:T(2,128)} %side_ref.1, f32[2,16]{1,0:T(2,128)} %weight_ref.1, ...), custom_call_target="tpu_custom_call" | custom-call | flops 536870912 | bytes 4456448 | tf_op jit(solution)/shard_map/pallas_call | solution.py:82
  27.8 0.8 %slice_reduce_fusion = f32[2]{0:T(128)S(1)} fusion(f32[2,2,8,128]{3,2,1,0:T(8,128)} %get-tuple-element.33), kind=kLoop, calls=%fused_computation.38 | loop fusion | flops 2 | bytes 24 | tf_op jit(solution)/shard_map/reduce_sum | solution.py:161
  28.6 1.2 %collective-permute-done.5 = bf16[16,2,2,16,256]{4,3,2,1,0:T(8,128)(2,1)S(1)} collective-permute-done((bf16[16,2,2,16,256]{4,3,2,1,0:T(8,128)(2,1)}, bf16[16,2,2,16,256]{4,3,2,1,0:T(8,128)(2,1)S(1)}, u32[]{:S(2)}, u32[]{:S(2)}) %collective-permute-start.5) | collective-permute-done | bytes 524320 | tf_op jit(solution)/shard_map/ppermute | solution.py:174
  29.8 1.3 %fusion.21 = (bf16[16,2,2,16,256]{4,3,2,1,0:T(8,128)(2,1)S(1)}, f32[16,2,2,16,256]{4,3,2,1,0:T(8,128)S(1)}) fusion(bf16[16,2,2,16,256]{4,3,2,1,0:T(8,128)(2,1)S(1)} %collective-permute-done.5, bf16[16,2,2,16,256]{4,3,2,1,0:T(8,128)(2,1)} %get-tuple-element.31), kind=kLoop, calls=%fused_computation.46 | loop fusion | flops 1048576 | bytes 2621440 | tf_op jit(solution)/shard_map/convert.3
  31.1 0.9 %collective-permute-start.6 = (bf16[4,2,2,16,256]{4,3,2,1,0:T(8,128)(2,1)S(1)}, bf16[4,2,2,16,256]{4,3,2,1,0:T(8,128)(2,1)S(1)}, u32[]{:S(2)}, u32[]{:S(2)}) collective-permute-start(bf16[4,2,2,16,256]{4,3,2,1,0:T(8,128)(2,1)S(1)} %get-tuple-element.36), channel_id=1, source_target_pairs={{0,4},{1,5},{2,6},{3,7},{4,0},{5,1},{6,2},{7,3},{8,12},{9,13},{10,... | collective-permute-start | bytes 393224 | tf_op jit(solution)/shard_map/ppermute | solution.py:187
  32.0 1.0 %collective-permute-start.7 = (bf16[4,2,2,16,256]{4,3,2,1,0:T(8,128)(2,1)S(1)}, bf16[4,2,2,16,256]{4,3,2,1,0:T(8,128)(2,1)S(1)}, u32[]{:S(2)}, u32[]{:S(2)}) collective-permute-start(bf16[4,2,2,16,256]{4,3,2,1,0:T(8,128)(2,1)S(1)} %get-tuple-element.38), channel_id=1, source_target_pairs={{0,2},{1,3},{2,0},{3,1},{4,6},{5,7},{6,4},{7,5},{8,10},{9,11},{10,... | collective-permute-start | bytes 393224 | tf_op jit(solution)/shard_map/ppermute | solution.py:187
  33.0 1.6 %collective-permute-start.8 = (bf16[4,2,2,16,256]{4,3,2,1,0:T(8,128)(2,1)S(1)}, bf16[4,2,2,16,256]{4,3,2,1,0:T(8,128)(2,1)S(1)}, u32[]{:S(2)}, u32[]{:S(2)}) collective-permute-start(bf16[4,2,2,16,256]{4,3,2,1,0:T(8,128)(2,1)S(1)} %get-tuple-element.37), channel_id=1, source_target_pairs={{0,6},{1,7},{2,4},{3,5},{4,2},{5,3},{6,0},{7,1},{8,14},{9,15},{10,... | collective-permute-start | bytes 393224 | tf_op jit(solution)/shard_map/ppermute | solution.py:187
  34.6 2.8 %collective-permute-done.6 = bf16[4,2,2,16,256]{4,3,2,1,0:T(8,128)(2,1)S(1)} collective-permute-done((bf16[4,2,2,16,256]{4,3,2,1,0:T(8,128)(2,1)S(1)}, bf16[4,2,2,16,256]{4,3,2,1,0:T(8,128)(2,1)S(1)}, u32[]{:S(2)}, u32[]{:S(2)}) %collective-permute-start.6) | collective-permute-done | bytes 131104 | tf_op jit(solution)/shard_map/ppermute | solution.py:187
  37.5 2.6 %collective-permute-done.7 = bf16[4,2,2,16,256]{4,3,2,1,0:T(8,128)(2,1)S(1)} collective-permute-done((bf16[4,2,2,16,256]{4,3,2,1,0:T(8,128)(2,1)S(1)}, bf16[4,2,2,16,256]{4,3,2,1,0:T(8,128)(2,1)S(1)}, u32[]{:S(2)}, u32[]{:S(2)}) %collective-permute-start.7) | collective-permute-done | bytes 131104 | tf_op jit(solution)/shard_map/ppermute | solution.py:187
  40.2 3.2 %collective-permute-start.9 = (bf16[2,2,2,16,256]{4,3,2,1,0:T(8,128)(2,1)S(1)}, bf16[2,2,2,16,256]{4,3,2,1,0:T(8,128)(2,1)S(1)}, u32[]{:S(2)}, u32[]{:S(2)}) collective-permute-start(bf16[2,2,2,16,256]{4,3,2,1,0:T(8,128)(2,1)S(1)} %slice.157), channel_id=1, source_target_pairs={{0,8},{1,9},{2,10},{3,11},{4,12},{5,13},{6,14},{7,15},{8,0},{9,1},... | collective-permute-start | bytes 196616 | tf_op jit(solution)/shard_map/ppermute | solution.py:187
  43.4 1.6 %collective-permute-start.11 = (bf16[3,2]{1,0:T(4,128)(2,1)S(1)}, bf16[3,2]{1,0:T(4,128)(2,1)S(1)}, u32[]{:S(2)}, u32[]{:S(2)}) collective-permute-start(bf16[3,2]{1,0:T(4,128)(2,1)S(1)} %pad_maximum_fusion.2), channel_id=1, source_target_pairs={{0,16},{16,0},{1,17},{17,1},{2,18},{18,2},{3,19},{19,3},{4,20},{20... | collective-permute-start | bytes 44 | tf_op jit(solution)/shard_map/ppermute | solution.py:170
  45.1 1.9 %collective-permute-done.11 = bf16[3,2]{1,0:T(4,128)(2,1)S(1)} collective-permute-done((bf16[3,2]{1,0:T(4,128)(2,1)S(1)}, bf16[3,2]{1,0:T(4,128)(2,1)S(1)}, u32[]{:S(2)}, u32[]{:S(2)}) %collective-permute-start.11) | collective-permute-done | bytes 44 | tf_op jit(solution)/shard_map/ppermute | solution.py:170
  47.7 1.6 %collective-permute-start.10 = (bf16[2,128,256]{2,1,0:T(8,128)(2,1)S(1)}, bf16[2,128,256]{2,1,0:T(8,128)(2,1)S(1)}, u32[]{:S(2)}, u32[]{:S(2)}) collective-permute-start(bf16[2,128,256]{2,1,0:T(8,128)(2,1)S(1)} %dynamic-slice_convert_fusion), channel_id=1, source_target_pairs={{0,16},{16,0},{1,17},{17,1},{2,18},{18,2},{3,19},{19,3},{4,20},{20... | collective-permute-start | bytes 393224 | tf_op jit(solution)/shard_map/ppermute | solution.py:210
  49.8 2.9 %collective-permute-done.10 = bf16[2,128,256]{2,1,0:T(8,128)(2,1)S(1)} collective-permute-done((bf16[2,128,256]{2,1,0:T(8,128)(2,1)S(1)}, bf16[2,128,256]{2,1,0:T(8,128)(2,1)S(1)}, u32[]{:S(2)}, u32[]{:S(2)}) %collective-permute-start.10) | collective-permute-done | bytes 131104 | tf_op jit(solution)/shard_map/ppermute | solution.py:210
  (39 shorter events, 4.1 us)
Async XLA Ops:
  0.6 1.0 %copy-start = (bf16[2,256,256]{2,1,0:T(8,128)(2,1)S(1)}, bf16[2,256,256]{2,1,0:T(8,128)(2,1)}, u32[]{:S(2)}) copy-start(bf16[2,256,256]{2,1,0:T(8,128)(2,1)} %param.16) | copy-start | bytes 786436
  0.6 2.2 %copy-start.2 = (bf16[2,256,256]{2,1,0:T(8,128)(2,1)S(1)}, bf16[2,256,256]{2,1,0:T(8,128)(2,1)}, u32[]{:S(2)}) copy-start(bf16[2,256,256]{2,1,0:T(8,128)(2,1)} %param.15) | copy-start | bytes 786436
  3.2 15.0 %copy-start.1 = (bf16[2,2,256,256]{3,2,1,0:T(8,128)(2,1)}, bf16[2,2,256,256]{3,2,1,0:T(8,128)(2,1)S(1)}, u32[]{:S(2)}) copy-start(bf16[2,2,256,256]{3,2,1,0:T(8,128)(2,1)S(1)} %fusion.2.proj_ref) | copy-start | bytes 1572868
  3.2 7.7 %collective-permute-start = (bf16[2,2,2,16,256]{4,3,2,1,0:T(8,128)(2,1)S(1)}, bf16[2,2,2,16,256]{4,3,2,1,0:T(8,128)(2,1)S(1)}, u32[]{:S(2)}, u32[]{:S(2)}) collective-permute-start(bf16[2,2,2,16,256]{4,3,2,1,0:T(8,128)(2,1)S(1)} %get-tuple-element.41), channel_id=1, source_target_pairs={{0,8},{1,9},{2,10},{3,11},{4,12},{5,13},{6,14},{7,15},{8,0},{9,1},... | collective-permute-start | bytes 196616 | tf_op jit(solution)/shard_map/ppermute | solution.py:153
  11.0 6.4 %collective-permute-start.1 = (bf16[4,2,2,16,256]{4,3,2,1,0:T(8,128)(2,1)S(1)}, bf16[4,2,2,16,256]{4,3,2,1,0:T(8,128)(2,1)S(1)}, u32[]{:S(2)}, u32[]{:S(2)}) collective-permute-start(bf16[4,2,2,16,256]{4,3,2,1,0:T(8,128)(2,1)S(1)} %pad_maximum_fusion), channel_id=1, source_target_pairs={{0,4},{1,5},{2,6},{3,7},{4,0},{5,1},{6,2},{7,3},{8,12},{9,13},{10,... | collective-permute-start | bytes 393224 | tf_op jit(solution)/shard_map/ppermute | solution.py:153
  11.6 6.5 %collective-permute-start.2 = (bf16[4,2,2,16,256]{4,3,2,1,0:T(8,128)(2,1)S(1)}, bf16[4,2,2,16,256]{4,3,2,1,0:T(8,128)(2,1)S(1)}, u32[]{:S(2)}, u32[]{:S(2)}) collective-permute-start(bf16[4,2,2,16,256]{4,3,2,1,0:T(8,128)(2,1)S(1)} %pad_maximum_fusion), channel_id=1, source_target_pairs={{0,2},{1,3},{2,0},{3,1},{4,6},{5,7},{6,4},{7,5},{8,10},{9,11},{10,... | collective-permute-start | bytes 393224 | tf_op jit(solution)/shard_map/ppermute | solution.py:153
  13.1 6.7 %collective-permute-start.3 = (bf16[4,2,2,16,256]{4,3,2,1,0:T(8,128)(2,1)S(1)}, bf16[4,2,2,16,256]{4,3,2,1,0:T(8,128)(2,1)S(1)}, u32[]{:S(2)}, u32[]{:S(2)}) collective-permute-start(bf16[4,2,2,16,256]{4,3,2,1,0:T(8,128)(2,1)S(1)} %pad_maximum_fusion), channel_id=1, source_target_pairs={{0,6},{1,7},{2,4},{3,5},{4,2},{5,3},{6,0},{7,1},{8,14},{9,15},{10,... | collective-permute-start | bytes 393224 | tf_op jit(solution)/shard_map/ppermute | solution.py:153
  19.8 2.0 %copy-start.3 = (bf16[16,2,2,16,256]{4,3,2,1,0:T(8,128)(2,1)}, bf16[16,2,2,16,256]{4,3,2,1,0:T(8,128)(2,1)S(1)}, u32[]{:S(2)}) copy-start(bf16[16,2,2,16,256]{4,3,2,1,0:T(8,128)(2,1)S(1)} %constant_dynamic-update-slice_fusion.low_ref) | copy-start | bytes 1572868
  19.8 2.0 %collective-permute-start.4 = (bf16[16,2,2,16,256]{4,3,2,1,0:T(8,128)(2,1)S(1)}, bf16[16,2,2,16,256]{4,3,2,1,0:T(8,128)(2,1)S(1)}, u32[]{:S(2)}, u32[]{:S(2)}) collective-permute-start(bf16[16,2,2,16,256]{4,3,2,1,0:T(8,128)(2,1)S(1)} %constant_dynamic-update-slice_fusion.low_ref), channel_id=1, source_target_pairs={{0,1},{1,0},{2,3},{3,2},{4,5},{5,4},{6,7},{7,6},{8,9},{9,8},{10,11... | collective-permute-start | bytes 1572872 | tf_op jit(solution)/shard_map/ppermute | solution.py:155
  21.8 0.8 %copy-start.5 = (bf16[16,2,2,16,256]{4,3,2,1,0:T(8,128)(2,1)}, bf16[16,2,2,16,256]{4,3,2,1,0:T(8,128)(2,1)S(1)}, u32[]{:S(2)}) copy-start(bf16[16,2,2,16,256]{4,3,2,1,0:T(8,128)(2,1)S(1)} %collective-permute-done.4.high_ref) | copy-start | bytes 1572868
  27.6 2.1 %collective-permute-start.5 = (bf16[16,2,2,16,256]{4,3,2,1,0:T(8,128)(2,1)}, bf16[16,2,2,16,256]{4,3,2,1,0:T(8,128)(2,1)S(1)}, u32[]{:S(2)}, u32[]{:S(2)}) collective-permute-start(bf16[16,2,2,16,256]{4,3,2,1,0:T(8,128)(2,1)} %get-tuple-element.32), channel_id=1, source_target_pairs={{0,1},{1,0},{2,3},{3,2},{4,5},{5,4},{6,7},{7,6},{8,9},{9,8},{10,11... | collective-permute-start | bytes 1572872 | tf_op jit(solution)/shard_map/ppermute | solution.py:174
  31.1 6.4 %collective-permute-start.6 = (bf16[4,2,2,16,256]{4,3,2,1,0:T(8,128)(2,1)S(1)}, bf16[4,2,2,16,256]{4,3,2,1,0:T(8,128)(2,1)S(1)}, u32[]{:S(2)}, u32[]{:S(2)}) collective-permute-start(bf16[4,2,2,16,256]{4,3,2,1,0:T(8,128)(2,1)S(1)} %get-tuple-element.36), channel_id=1, source_target_pairs={{0,4},{1,5},{2,6},{3,7},{4,0},{5,1},{6,2},{7,3},{8,12},{9,13},{10,... | collective-permute-start | bytes 393224 | tf_op jit(solution)/shard_map/ppermute | solution.py:187
  32.0 8.1 %collective-permute-start.7 = (bf16[4,2,2,16,256]{4,3,2,1,0:T(8,128)(2,1)S(1)}, bf16[4,2,2,16,256]{4,3,2,1,0:T(8,128)(2,1)S(1)}, u32[]{:S(2)}, u32[]{:S(2)}) collective-permute-start(bf16[4,2,2,16,256]{4,3,2,1,0:T(8,128)(2,1)S(1)} %get-tuple-element.38), channel_id=1, source_target_pairs={{0,2},{1,3},{2,0},{3,1},{4,6},{5,7},{6,4},{7,5},{8,10},{9,11},{10,... | collective-permute-start | bytes 393224 | tf_op jit(solution)/shard_map/ppermute | solution.py:187
  33.0 7.0 %collective-permute-start.8 = (bf16[4,2,2,16,256]{4,3,2,1,0:T(8,128)(2,1)S(1)}, bf16[4,2,2,16,256]{4,3,2,1,0:T(8,128)(2,1)S(1)}, u32[]{:S(2)}, u32[]{:S(2)}) collective-permute-start(bf16[4,2,2,16,256]{4,3,2,1,0:T(8,128)(2,1)S(1)} %get-tuple-element.37), channel_id=1, source_target_pairs={{0,6},{1,7},{2,4},{3,5},{4,2},{5,3},{6,0},{7,1},{8,14},{9,15},{10,... | collective-permute-start | bytes 393224 | tf_op jit(solution)/shard_map/ppermute | solution.py:187
  40.1 5.0 %copy-start.4 = (bf16[2,2,256,256]{3,2,1,0:T(8,128)(2,1)S(1)}, bf16[2,2,256,256]{3,2,1,0:T(8,128)(2,1)}, u32[]{:S(2)}) copy-start(bf16[2,2,256,256]{3,2,1,0:T(8,128)(2,1)} %get-tuple-element.30) | copy-start | bytes 1572868
  40.2 6.9 %collective-permute-start.9 = (bf16[2,2,2,16,256]{4,3,2,1,0:T(8,128)(2,1)S(1)}, bf16[2,2,2,16,256]{4,3,2,1,0:T(8,128)(2,1)S(1)}, u32[]{:S(2)}, u32[]{:S(2)}) collective-permute-start(bf16[2,2,2,16,256]{4,3,2,1,0:T(8,128)(2,1)S(1)} %slice.157), channel_id=1, source_target_pairs={{0,8},{1,9},{2,10},{3,11},{4,12},{5,13},{6,14},{7,15},{8,0},{9,1},... | collective-permute-start | bytes 196616 | tf_op jit(solution)/shard_map/ppermute | solution.py:187
  43.4 3.6 %collective-permute-start.11 = (bf16[3,2]{1,0:T(4,128)(2,1)S(1)}, bf16[3,2]{1,0:T(4,128)(2,1)S(1)}, u32[]{:S(2)}, u32[]{:S(2)}) collective-permute-start(bf16[3,2]{1,0:T(4,128)(2,1)S(1)} %pad_maximum_fusion.2), channel_id=1, source_target_pairs={{0,16},{16,0},{1,17},{17,1},{2,18},{18,2},{3,19},{19,3},{4,20},{20... | collective-permute-start | bytes 44 | tf_op jit(solution)/shard_map/ppermute | solution.py:170
  47.7 5.0 %collective-permute-start.10 = (bf16[2,128,256]{2,1,0:T(8,128)(2,1)S(1)}, bf16[2,128,256]{2,1,0:T(8,128)(2,1)S(1)}, u32[]{:S(2)}, u32[]{:S(2)}) collective-permute-start(bf16[2,128,256]{2,1,0:T(8,128)(2,1)S(1)} %dynamic-slice_convert_fusion), channel_id=1, source_target_pairs={{0,16},{16,0},{1,17},{17,1},{2,18},{18,2},{3,19},{19,3},{4,20},{20... | collective-permute-start | bytes 393224 | tf_op jit(solution)/shard_map/ppermute | solution.py:210
